TPU v7x, 256 devices: a whole 4x4x8 slice. The times are simulated.
256 devices in a mesh: freq: 32 (over y_hi, z, core), tm: 4 (over x), grp: 2 (over y_lo).
Axes of the slice: x: 4, y: 4 (y_hi: 2, y_lo: 2; y = y_hi * 2 + y_lo), z: 8, core: 2. Of those that a mesh axis runs over, the one named last changes fastest.
Arguments:
- voltages: bfloat16 [32, 2, 1024, 4096], P(None, None, ('freq', 'grp'), 'tm'), may hold values from -6 to 6
- prior_gains: float32 [32, 2, 1024], P('freq'), may hold values from -4.2 to 4.2
- station_flags: int32 [512], replicated, may hold values 0 or 1
- ingest_map: int32 [512], replicated, may hold values from 0 to 511, each once
- station_coords: float32 [2, 512], replicated, may hold values from -40 to 40
- pointing: int32 [2, 256], replicated, may hold values from 0 to 63
- corr_channels: int32 [32], replicated, may hold values from 0 to 31, each once
- beam_channels: int32 [32], replicated, may hold values from 0 to 31, each once
Outputs:
- visibilities: float32 [32, 2, 1024, 1024], P('freq', None, 'grp', 'tm')
- solved_gains: float32 [32, 2, 1024], P('freq')
- tied_beams: bfloat16 [32, 2, 2, 256, 4096], P('freq', None, None, 'grp', 'tm')
Inputs may be any that keep to these rules, and one draw needn't show every extreme that they name: `ingest_map`: each station appears in exactly one ingest slot. `corr_channels`: each channel is handled by exactly one correlator slot. `beam_channels`: each channel is handled by exactly one beamformer slot.
All inputs are finite; a program needn't handle non-finite values.
Results may differ from a plain program's by a relative error of at most 0.0049.
Values may be sent and summed in bfloat16 or wider, within the bound.
No kernel may reach another device: no remote copies, remote signals or barrier semaphores. Data moves between devices by JAX's collectives and lax.ppermute only.
A program may use at most 64 MiB of HBM per device.

v0:
```python
import math

import jax
import jax.numpy as jnp
from jax import lax
from jax.sharding import PartitionSpec as P

S = 512
ITERS = 4


grid_cells = 64.0


def weights_for(gains_sel, ratio, pointing_part, slot_coords):
    east_dir = (pointing_part[0].astype(jnp.float32) + 0.5) / grid_cells - 0.5
    north_dir = (pointing_part[1].astype(jnp.float32) + 0.5) / grid_cells - 0.5
    phase = (
        2.0
        * math.pi
        * ratio
        * (
            east_dir[:, None] * slot_coords[0][None, :]
            + north_dir[:, None] * slot_coords[1][None, :]
        )
    )
    cosine = jnp.cos(phase)
    sine = jnp.sin(phase)
    gain_real = gains_sel[0].reshape(2, S)
    gain_imag = gains_sel[1].reshape(2, S)
    denom = jnp.maximum(gain_real * gain_real + gain_imag * gain_imag, 0.5)
    along_real = gain_real / denom
    along_imag = gain_imag / denom
    factor = 1.0 / math.sqrt(S)
    w_real = (cosine[None] * along_real[:, None, :] - sine[None] * along_imag[:, None, :]) * factor
    w_imag = -(cosine[None] * along_imag[:, None, :] + sine[None] * along_real[:, None, :]) * factor
    upper = jnp.stack([w_real, -w_imag], axis=2)
    lower = jnp.stack([w_imag, w_real], axis=2)
    return jnp.stack([upper, lower], axis=1).astype(jnp.bfloat16)


def body(
    voltages,
    prior_gains,
    station_flags,
    ingest_map,
    station_coords,
    pointing,
    corr_channels,
    beam_channels,
):
    highest = lax.Precision.HIGHEST
    n_freq = lax.axis_size("freq")
    n_time = lax.axis_size("tm")
    n_group = lax.axis_size("grp")
    freq_index = lax.axis_index("freq")
    time_index = lax.axis_index("tm")
    group_index = lax.axis_index("grp")
    channels_all = voltages.shape[0]
    per_device = channels_all // n_freq
    samples = voltages.shape[3]
    inputs_all = 2 * S
    paired = lax.all_gather(voltages, "grp", axis=2, tiled=True)
    corr_source = jnp.take(paired, corr_channels, axis=0)
    beam_source = jnp.take(paired, beam_channels, axis=0)
    corr_volts, beam_volts = (
        lax.all_to_all(corr_source, "freq", split_axis=0, concat_axis=2, tiled=True),
        lax.all_to_all(beam_source, "freq", split_axis=0, concat_axis=2, tiled=True),
    )
    slot_keep = 1 - jnp.take(station_flags, ingest_map)
    keep = jnp.concatenate([slot_keep, slot_keep]).astype(jnp.bfloat16)
    corr_volts = corr_volts * keep[None, None, :, None]
    beam_volts = beam_volts * keep[None, None, :, None]
    rows = inputs_all // n_group
    row_start = group_index * rows
    mine = lax.dynamic_slice_in_dim(corr_volts, row_start, rows, 2)
    left = jnp.stack([mine, jnp.stack([mine[:, 1], -mine[:, 0]], axis=1)], axis=1)
    partial_value = jnp.einsum(
        "corit,crjt->coij", left, corr_volts, preferred_element_type=jnp.float32
    )
    partial_value = partial_value * (1.0 / (samples * n_time))
    columns = inputs_all // n_time
    vis_block = lax.psum_scatter(partial_value, "tm", scatter_dimension=3, tiled=True)
    gains = prior_gains
    for iteration in range(ITERS):
        power = jnp.sum(gains * gains, axis=(1, 2)) + 1e-06
        along = lax.dynamic_slice_in_dim(gains, time_index * columns, columns, 2)
        real_real = jnp.einsum("cij,cj->ci", vis_block[:, 0], along[:, 0], precision=highest)
        imag_imag = jnp.einsum("cij,cj->ci", vis_block[:, 1], along[:, 1], precision=highest)
        real_imag = jnp.einsum("cij,cj->ci", vis_block[:, 0], along[:, 1], precision=highest)
        imag_real = jnp.einsum("cij,cj->ci", vis_block[:, 1], along[:, 0], precision=highest)
        update = jnp.stack([real_real - imag_imag, imag_real + real_imag], axis=1)
        update = lax.psum(update, "tm")
        own_rows = lax.dynamic_slice_in_dim(gains, row_start, rows, 2)
        fresh = 0.5 * (own_rows + inputs_all * update / power[:, None, None])
        gains = lax.all_gather(fresh, "grp", axis=2, tiled=True)
    all_gains = lax.all_gather(gains, "freq", axis=0, tiled=True)
    my_beam = lax.dynamic_slice_in_dim(beam_channels, freq_index * per_device, per_device, 0)
    onehot = (corr_channels[None, :] == my_beam[:, None]).astype(jnp.float32)
    selected = jnp.einsum("ck,kri->cri", onehot, all_gains, precision=highest)
    ratio = 0.875 + 0.25 * (my_beam.astype(jnp.float32) + 0.5) / channels_all
    beams_mine = pointing.shape[1] // n_group
    pointing_part = lax.dynamic_slice_in_dim(pointing, group_index * beams_mine, beams_mine, 1)
    slot_coords = jnp.take(station_coords, ingest_map, axis=1)
    weights = jax.vmap(weights_for, in_axes=(0, 0, None, None))(
        selected, ratio, pointing_part, slot_coords
    )
    block = beam_volts.reshape(per_device, 2, 2, S, samples)
    beams = jnp.einsum("cpobrq,crpqt->cpobt", weights, block, preferred_element_type=jnp.float32)
    return (vis_block, gains, beams.astype(jnp.bfloat16))


def solution(mesh):
    return jax.shard_map(
        body,
        mesh=mesh,
        in_specs=(
            P(None, None, ("freq", "grp"), "tm"),
            P("freq", None, None),
            P(),
            P(),
            P(),
            P(),
            P(),
            P(),
        ),
        out_specs=(
            P("freq", None, "grp", "tm"),
            P("freq", None, None),
            P("freq", None, None, "grp", "tm"),
        ),
        check_vma=False,
    )
```

profile of v0, /device:TPU:1, one launch (start us, length us, event | category | flops | bytes accessed | tf_op | source)
XLA Modules:
  0.0 446.5 jit_solution(17262730501101874338)
XLA Ops:
  9.3 66.2 %all-gather.2.cloned.1.call-done = bf16[32,2,32,1024]{3,2,1,0:T(8,128)(2,1)} async-done(((bf16[32,2,16,1024]{3,2,1,0:T(8,128)(2,1)}), bf16[32,2,32,1024]{3,2,1,0:T(8,128)(2,1)}) %all-gather.2.cloned.1.call-update) | async-done | bytes 4194320 | tf_op jit(solution)/shard_map/all_gather | solution.py:63
  75.5 5.0 %gather_fusion.2 = bf16[32,2,32,1024]{3,2,1,0:T(8,128)(2,1)} fusion(bf16[32,2,32,1024]{3,2,1,0:T(8,128)(2,1)} %all-gather.2.cloned.1.call-done, s32[1024]{0:T(1024)S(1)} %pad_clamp_fusion.2), kind=kCustom, calls=%fused_computation.clone | custom fusion | bytes 8388736 | tf_op jit(solution)/shard_map/jit(_take)/gather | solution.py:64
  80.4 4.6 %broadcast_select_fusion.1 = bf16[32,2,32,1024]{3,2,1,0:T(8,128)(2,1)} fusion(bf16[32,2,32,1024]{3,2,1,0:T(8,128)(2,1)} %gather_fusion.2, pred[32]{0:T(512)(128)(4,1)S(1)} %get-tuple-element.27), kind=kLoop, calls=%fused_computation.14 | loop fusion | flops 2097152 | bytes 8388640 | tf_op jit(solution)/shard_map/jit(_take)/select_n | solution.py:64
  85.1 10.2 %all-to-all-start = ((bf16[32,2,32,1024]{3,2,1,0:T(8,128)(2,1)}), bf16[32,2,32,1024]{3,2,1,0:T(8,128)(2,1)}, u32[]{:S(2)}, u32[]{:S(2)}) async-start(bf16[32,2,32,1024]{3,2,1,0:T(8,128)(2,1)} %broadcast_select_fusion.1), calls=%async_computation | async-start | bytes 8388608 | tf_op jit(solution)/shard_map/all_to_all | solution.py:67
  95.3 3.5 gather_fusion
  99.1 5.0 %gather_fusion.3 = bf16[32,2,32,1024]{3,2,1,0:T(8,128)(2,1)} fusion(bf16[32,2,32,1024]{3,2,1,0:T(8,128)(2,1)} %all-gather.2.cloned.1.call-done, s32[1024]{0:T(1024)S(1)} %pad_clamp_fusion), kind=kCustom, calls=%fused_computation.1.clone | custom fusion | bytes 8388736 | tf_op jit(solution)/shard_map/jit(_take)/gather | solution.py:65
  104.1 87.4 %all-to-all-done = bf16[32,2,32,1024]{3,2,1,0:T(8,128)(2,1)} async-done(((bf16[32,2,32,1024]{3,2,1,0:T(8,128)(2,1)}), bf16[32,2,32,1024]{3,2,1,0:T(8,128)(2,1)}, u32[]{:S(2)}, u32[]{:S(2)}) %all-to-all-start) | async-done | bytes 4194336 | tf_op jit(solution)/shard_map/all_to_all | solution.py:67
  191.4 2.6 copy.23
  194.9 2.5 broadcast_multiply_fusion
  198.6 6.1 %fusion.5 = f32[1,2,512,1024]{3,2,1,0:T(8,128)} fusion(bf16[2,1024,1024,1]{2,1,0,3:T(8,128)(2,1)S(1)} %bitcast.170, bf16[1,1,2,512,1024]{4,3,2,1,0:T(8,128)(2,1)S(1)} %maximum_bitcast_fusion.4, bf16[1,1,2,512,1024]{4,3,2,1,0:T(8,128)(2,1)S(1)} %fusion.76), kind=kOutput, calls=%fused_computation.11 | convolution fusion | flops 4298113024 | bytes 12582912 | tf_op jit(solution)/shard_map/corit,crjt->coij/dot_general | solution.py:78
  204.7 4.6 %broadcast_select_fusion = bf16[32,2,32,1024]{3,2,1,0:T(8,128)(2,1)} fusion(bf16[32,2,32,1024]{3,2,1,0:T(8,128)(2,1)} %gather_fusion.3, pred[32]{0:T(512)(128)(4,1)S(1)} %get-tuple-element.26), kind=kLoop, calls=%fused_computation.13 | loop fusion | flops 2097152 | bytes 8388640 | tf_op jit(solution)/shard_map/jit(_take)/select_n | solution.py:65
  209.4 7.4 %all-to-all-start.1 = ((bf16[32,2,32,1024]{3,2,1,0:T(8,128)(2,1)}), bf16[32,2,32,1024]{3,2,1,0:T(8,128)(2,1)}, u32[]{:S(2)}, u32[]{:S(2)}) async-start(bf16[32,2,32,1024]{3,2,1,0:T(8,128)(2,1)} %broadcast_select_fusion), calls=%async_computation.2 | async-start | bytes 8388608 | tf_op jit(solution)/shard_map/all_to_all | solution.py:68
  222.1 90.9 %all-to-all-done.1 = bf16[32,2,32,1024]{3,2,1,0:T(8,128)(2,1)} async-done(((bf16[32,2,32,1024]{3,2,1,0:T(8,128)(2,1)}), bf16[32,2,32,1024]{3,2,1,0:T(8,128)(2,1)}, u32[]{:S(2)}, u32[]{:S(2)}) %all-to-all-start.1) | async-done | bytes 4194336 | tf_op jit(solution)/shard_map/all_to_all | solution.py:68
  313.0 5.0 %copy.27 = bf16[1,2,32,32,1024]{4,3,2,1,0:T(8,128)(2,1)} copy(bf16[1,2,32,32,1024]{4,3,1,2,0:T(8,128)(2,1)} %bitcast.74) | data formatting | bytes 8388608 | tf_op jit(solution)/shard_map/all_to_all | solution.py:68
  317.9 1.7 fusion.29
  319.6 1.6 fusion.21
  321.2 1.6 fusion.22
  322.8 1.6 fusion.30
  324.5 8.4 %psum.28 = f32[1,2,512]{2,1,0:T(2,128)S(1)} all-reduce(f32[1,2,512]{2,1,0:T(2,128)S(1)} %pad_maximum_fusion), channel_id=1, replica_groups=mesh['freq'=32,'tm'=4,'grp'=2] {'tm'}, use_global_device_ids=true, to_apply=%region_1.3 | all-reduce | flops 1024 | bytes 8192 | tf_op jit(solution)/shard_map/psum | solution.py:93
  332.9 3.4 all_gather.19
  336.9 1.6 fusion.27
  338.4 1.6 fusion.19
  340.0 1.6 fusion.20
  341.6 1.6 fusion.28
  343.3 6.0 %psum.29 = f32[1,2,512]{2,1,0:T(2,128)S(1)} all-reduce(f32[1,2,512]{2,1,0:T(2,128)S(1)} %pad_maximum_fusion.1), channel_id=1, replica_groups=mesh['freq'=32,'tm'=4,'grp'=2] {'tm'}, use_global_device_ids=true, to_apply=%region_3.5 | all-reduce | flops 1024 | bytes 8192 | tf_op jit(solution)/shard_map/psum | solution.py:93
  350.0 3.2 all_gather.20
  356.0 7.4 %psum.30 = f32[1,2,512]{2,1,0:T(2,128)S(1)} all-reduce(f32[1,2,512]{2,1,0:T(2,128)S(1)} %pad_maximum_fusion.2), channel_id=1, replica_groups=mesh['freq'=32,'tm'=4,'grp'=2] {'tm'}, use_global_device_ids=true, to_apply=%region_5.7 | all-reduce | flops 1024 | bytes 8192 | tf_op jit(solution)/shard_map/psum | solution.py:93
  364.1 3.4 all_gather.21
  370.4 6.0 %psum.31 = f32[1,2,512]{2,1,0:T(2,128)S(1)} all-reduce(f32[1,2,512]{2,1,0:T(2,128)S(1)} %pad_maximum_fusion.3), channel_id=1, replica_groups=mesh['freq'=32,'tm'=4,'grp'=2] {'tm'}, use_global_device_ids=true, to_apply=%region_7.9 | all-reduce | flops 1024 | bytes 8192 | tf_op jit(solution)/shard_map/psum | solution.py:93
  377.1 3.2 all_gather.22
  380.3 52.9 %all_gather.23 = f32[32,2,1024]{2,1,0:T(2,128)S(1)} all-gather(f32[1,2,1024]{2,1,0:T(2,128)S(1)} %all_gather.22), channel_id=1, replica_groups=mesh['freq'=32,'tm'=4,'grp'=2] {'freq'}, dimensions={0}, use_global_device_ids=true | all-gather | bytes 270336 | tf_op jit(solution)/shard_map/all_gather | solution.py:97
  434.5 4.6 %fusion.8 = bf16[1,2,2,128,1024]{4,3,2,1,0:T(8,128)(2,1)} fusion(bf16[2,1,128,2,512]{4,2,3,1,0:T(8,128)(2,1)S(1)} %get-tuple-element.17, bf16[2,1,128,2,512]{4,2,3,1,0:T(8,128)(2,1)S(1)} %get-tuple-element.16, bf16[2,2,512,1024]{3,2,1,0:T(8,128)(2,1)} %bitcast.169, bf16[2,512]{1,0:T(2,128)(2,1)S(1)} %convert_element_type.50), kind=kOutput, calls=%fused_computation.19 | convolution fusion | flops 1076887552 | bytes 6293504 | tf_op jit(solution)/shard_map/cpobrq,crpqt->cpobt/dot_general | solution.py:109
  (82 shorter events, 16.4 us)
Async XLA Ops:
  7.2 88.2 %copy-start = (s32[512]{0:T(512)S(1)}, s32[512]{0:T(512)}, u32[]{:S(2)}) copy-start(s32[512]{0:T(512)} %param.12) | copy-start | bytes 6148
  7.2 68.3 %all-gather.2.cloned.1.call-start = ((), (), s32[]{:S(2)}) async-start(), calls=%async_computation.3 | async-start | bytes 6291456 | tf_op jit(solution)/shard_map/all_gather | solution.py:63
  85.1 10.2 %copy-start.3 = (s32[512]{0:T(512)S(1)}, s32[512]{0:T(512)}, u32[]{:S(2)}) copy-start(s32[512]{0:T(512)} %param.13) | copy-start | bytes 6148
  85.1 106.3 %all-to-all-start = ((bf16[32,2,32,1024]{3,2,1,0:T(8,128)(2,1)}), bf16[32,2,32,1024]{3,2,1,0:T(8,128)(2,1)}, u32[]{:S(2)}, u32[]{:S(2)}) async-start(bf16[32,2,32,1024]{3,2,1,0:T(8,128)(2,1)} %broadcast_select_fusion.1), calls=%async_computation | async-start | bytes 8388608 | tf_op jit(solution)/shard_map/all_to_all | solution.py:67
  95.2 222.7 %reduce-scatter.2.cloned.1.call-start = ((), (), s32[]{:S(2)}) async-start(), calls=%async_computation.4 | async-start | bytes 5242880 | tf_op jit(solution)/shard_map/reduce_scatter | solution.py:83
  209.4 7.5 %copy-start.6 = (s32[32]{0:T(128)S(1)}, s32[32]{0:T(128)}, u32[]{:S(2)}) copy-start(s32[32]{0:T(128)} %param.17) | copy-start | bytes 388
  209.4 8.1 %copy-start.5 = (f32[2,512]{1,0:T(2,128)S(1)}, f32[2,512]{1,0:T(2,128)}, u32[]{:S(2)}) copy-start(f32[2,512]{1,0:T(2,128)} %param.14) | copy-start | bytes 12292
  209.4 9.9 %copy-start.2 = (f32[1,2,1024]{2,1,0:T(2,128)S(1)}, f32[1,2,1024]{2,1,0:T(2,128)}, u32[]{:S(2)}) copy-start(f32[1,2,1024]{2,1,0:T(2,128)} %param.11) | copy-start | bytes 24580
  209.4 11.2 %copy-start.7 = (s32[2,256]{1,0:T(2,128)S(1)}, s32[2,256]{1,0:T(2,128)}, u32[]{:S(2)}) copy-start(s32[2,256]{1,0:T(2,128)} %param.15) | copy-start | bytes 6148
  209.4 103.6 %all-to-all-start.1 = ((bf16[32,2,32,1024]{3,2,1,0:T(8,128)(2,1)}), bf16[32,2,32,1024]{3,2,1,0:T(8,128)(2,1)}, u32[]{:S(2)}, u32[]{:S(2)}) async-start(bf16[32,2,32,1024]{3,2,1,0:T(8,128)(2,1)} %broadcast_select_fusion), calls=%async_computation.2 | async-start | bytes 8388608 | tf_op jit(solution)/shard_map/all_to_all | solution.py:68
  317.9 35.8 %copy-start.1 = (f32[1,2,512,256]{3,2,1,0:T(8,128)S(1)}, f32[1,2,512,256]{3,2,1,0:T(8,128)}, u32[]{:S(2)}) copy-start(f32[1,2,512,256]{3,2,1,0:T(8,128)} %reduce-scatter.2.cloned.1.call-done) | copy-start | bytes 3145732
  319.6 113.6 %copy-start.4 = (s32[32]{0:T(128)S(1)}, s32[32]{0:T(128)}, u32[]{:S(2)}) copy-start(s32[32]{0:T(128)} %param.16) | copy-start | bytes 388
Sparse Core Ops, SparseCore 0:
  9.8 65.6 all-gather.1
  204.8 47.6 reduce-scatter.1
where the time goes:
time: 448 us; the launch traced here: 446 us
  waiting for transfers between devices  245 us (55%)
  blocking collectives  94 us (21%)
  matrix products  28.9 us (6%)
  local copies, waits for them, and re-layouts  24.8 us (6%)
  other arithmetic  18.4 us (4%)
  starting transfers between devices  17.7 us (4%)
  between operations  17.6 us (4%)
    all_to_all x1, waiting for transfers between devices, body(): lax.all_to_all(beam_source, 'freq', split_axis=0, concat_axis=2, tiled=True)  90.9 us
    all_to_all x1, waiting for transfers between devices, body(): lax.all_to_all(corr_source, 'freq', split_axis=0, concat_axis=2, tiled=True)  87.4 us
    all_gather x1, waiting for transfers between devices, body(): paired = lax.all_gather(voltages, 'grp', axis=2, tiled=True)  66.2 us
    all_gather x1, blocking collectives, body(): all_gains = lax.all_gather(gains, 'freq', axis=0, tiled=True)  52.9 us
    psum x4, blocking collectives, body(): update = lax.psum(update, 'tm')  27.9 us
    all_gather x4, blocking collectives, body(): gains = lax.all_gather(fresh, 'grp', axis=2, tiled=True)  13.2 us
    all_to_all x1, starting transfers between devices, body(): lax.all_to_all(corr_source, 'freq', split_axis=0, concat_axis=2, tiled=True)  10.2 us
  transfers between devices with their start and end apart: 4, of which 3 were waited for; matrix products, arithmetic and copies ran while one was open for 5% of the time, Pallas kernels for 0%

commit v1 on v0

v1 whole, which is shorter than its diff:
```python
import functools
import math

import jax
import jax.numpy as jnp
from jax import lax
from jax.experimental import pallas as pl
from jax.experimental.pallas import tpu as pltpu
from jax.sharding import PartitionSpec as P

ITERS = 4
GRID_CELLS = 64.0
F32 = jnp.float32
BF16 = jnp.bfloat16
WIDE = ("freq", "grp")
TEAM = ("tm", "grp")
VMEM = pltpu.VMEM
SMEM = pltpu.SMEM


def whole(space=VMEM):
    return pl.BlockSpec(memory_space=space)


def params(mib=48):
    return pltpu.CompilerParams(vmem_limit_bytes=mib << 20)


def ingest_kernel(stations, chan_ref, map_ref, flag_ref, base_ref, volts_ref, out_ref):
    step = pl.program_id(0)
    per_step = out_ref.shape[0]
    rows, half = out_ref.shape[3], out_ref.shape[4]
    line = lax.broadcasted_iota(jnp.int32, (rows, half), 0)
    keep = jnp.zeros((rows, half), F32)
    for row in range(rows):
        slot = lax.rem(base_ref[0] + row, stations)
        good = (1 - flag_ref[map_ref[slot]]).astype(F32)
        keep = jnp.where(line == row, good, keep)
    keep = keep.astype(BF16)
    for i in range(per_step):
        channel = chan_ref[step * per_step + i]
        for part in range(2):
            for g in range(out_ref.shape[1]):
                piece = volts_ref[channel, part, :, g * half : (g + 1) * half]
                out_ref[i, g, part] = piece * keep


def ingest(voltages, channels, ingest_map, station_flags, base, groups):
    slots, parts, rows, samples = voltages.shape
    stations = ingest_map.shape[0]
    per_step = 8
    half = samples // groups
    out = pl.pallas_call(
        functools.partial(ingest_kernel, stations),
        grid=(slots // per_step,),
        in_specs=[whole(SMEM)] * 4 + [whole(VMEM)],
        out_specs=pl.BlockSpec(
            (per_step, groups, parts, rows, half), lambda s: (s, 0, 0, 0, 0)
        ),
        out_shape=jax.ShapeDtypeStruct((slots, groups, parts, rows, half), BF16),
        compiler_params=params(),
        name="ingest",
    )(channels, ingest_map, station_flags, base, voltages)
    return out.reshape(slots * groups, parts, rows, half)


def load_part(ref, part):
    blocks, _, rows, samples = ref.shape
    return ref[:, part].reshape(blocks * rows, samples)


def nt_dot(a, b):
    return lax.dot_general(a, b, (((1,), (1,)), ((), ())), preferred_element_type=F32)


def correlate_kernel(scale, row_blocks, y_ref, out_ref, real_ref, imag_ref):
    col, row = pl.program_id(0), pl.program_id(1)

    @pl.when((col == 0) & (row == 0))
    def _():
        real_ref[...] = load_part(y_ref, 0)
        imag_ref[...] = load_part(y_ref, 1)

    height, width = out_ref.shape[1], out_ref.shape[2]
    rows = pl.ds(pl.multiple_of(row * height, height), height)
    cols = pl.ds(pl.multiple_of(col * width, width), width)
    left_r, left_i = real_ref[rows, :], imag_ref[rows, :]
    right_r, right_i = real_ref[cols, :], imag_ref[cols, :]
    out_ref[0] = ((nt_dot(left_r, right_r) + nt_dot(left_i, right_i)) * scale).astype(BF16)
    out_ref[1] = ((nt_dot(left_i, right_r) - nt_dot(left_r, right_i)) * scale).astype(BF16)


def correlate(y, scale, n_time, n_group):
    blocks, _, rows, samples = y.shape
    inputs = blocks * rows
    height, width = inputs // n_group, inputs // n_time
    return pl.pallas_call(
        functools.partial(correlate_kernel, scale, n_group),
        grid=(n_time, n_group),
        in_specs=[whole(VMEM)],
        out_specs=pl.BlockSpec((2, height, width), lambda t, g: (0, g, t)),
        out_shape=jax.ShapeDtypeStruct((2, inputs, inputs), BF16),
        scratch_shapes=[VMEM((inputs, samples), BF16)] * 2,
        compiler_params=params(),
        name="correlate",
    )(y)


def in_terms(x):
    high = x.astype(BF16).astype(F32)
    rest = x - high
    mid = rest.astype(BF16).astype(F32)
    low = rest - mid
    pad = jnp.zeros_like(x)
    return jnp.concatenate([high, mid, low, pad], axis=0).astype(BF16)


def add_terms(x):
    return x[0:2] + x[2:4] + x[4:6]


def advance(scale, z, partials):
    power = jnp.sum(z * z) + 1e-06
    update = partials[0]
    for i in range(1, partials.shape[0]):
        update = update + partials[i]
    return 0.5 * (z + scale * update / power)


def apply_kernel(scale, first, y_ref, z_ref, *refs):
    z = z_ref[...]
    if first:
        (out_ref,) = refs
    else:
        sums_ref, out_ref, fresh_ref = refs
        z = advance(scale, z, sums_ref[...])
        fresh_ref[...] = z
    real, imag = load_part(y_ref, 0), load_part(y_ref, 1)
    terms = in_terms(z)
    a = add_terms(jnp.dot(terms, real, preferred_element_type=F32))
    b = add_terms(jnp.dot(terms, imag, preferred_element_type=F32))
    w = jnp.concatenate([a[0:1] + b[1:2], a[1:2] - b[0:1]], axis=0)
    terms = in_terms(w)
    c = add_terms(nt_dot(terms, real))
    d = add_terms(nt_dot(terms, imag))
    u = jnp.concatenate([c[0:1] - d[1:2], c[1:2] + d[0:1]], axis=0)
    for i in range(out_ref.shape[0]):
        out_ref[i] = u


def apply_visibilities(y, z, sums, scale, team):
    first = sums is None
    part = jax.ShapeDtypeStruct((team,) + z.shape, F32)
    return pl.pallas_call(
        functools.partial(apply_kernel, scale, first),
        in_specs=[whole(VMEM)] * (2 if first else 3),
        out_specs=whole(VMEM) if first else [whole(VMEM)] * 2,
        out_shape=part if first else [part, jax.ShapeDtypeStruct(z.shape, F32)],
        compiler_params=params(),
        name="apply",
    )(*((y, z) if first else (y, z, sums)))


def finish_kernel(scale, z_ref, sums_ref, fresh_ref, copies_ref):
    z = advance(scale, z_ref[...], sums_ref[...])
    fresh_ref[...] = z
    for i in range(copies_ref.shape[0]):
        copies_ref[i] = z


def finish(z, sums, scale, copies):
    return pl.pallas_call(
        functools.partial(finish_kernel, scale),
        in_specs=[whole(VMEM)] * 2,
        out_specs=[whole(VMEM)] * 2,
        out_shape=[
            jax.ShapeDtypeStruct(z.shape, F32),
            jax.ShapeDtypeStruct((copies,) + z.shape, F32),
        ],
        compiler_params=params(),
        name="finish",
    )(z, sums)


def beam_kernel(corr_ref, beam_ref, me_ref, gains_ref, cos_ref, sin_ref, y_ref, out_ref):
    slots = gains_ref.shape[0]
    mine = beam_ref[me_ref[0]]
    source = jnp.int32(0)
    for k in range(slots):
        source = jnp.where(corr_ref[k] == mine, k, source)
    blocks, _, rows, samples = y_ref.shape
    stations = blocks // 2 * rows
    beams = out_ref.shape[3]
    factor = 1.0 / math.sqrt(stations)
    for pol in range(2):
        chunk = pl.ds(pol * stations, stations)
        gain_r = gains_ref[source, 0:1, chunk]
        gain_i = gains_ref[source, 1:2, chunk]
        denom = jnp.maximum(gain_r * gain_r + gain_i * gain_i, 0.5)
        along_r, along_i = gain_r / denom, gain_i / denom
        y_r = y_ref[pol * blocks // 2 : (pol + 1) * blocks // 2, 0].reshape(stations, samples)
        y_i = y_ref[pol * blocks // 2 : (pol + 1) * blocks // 2, 1].reshape(stations, samples)
        for g in range(out_ref.shape[0]):
            cosine = cos_ref[g * beams : (g + 1) * beams]
            sine = sin_ref[g * beams : (g + 1) * beams]
            w_r = ((cosine * along_r - sine * along_i) * factor).astype(BF16)
            w_i = (-(cosine * along_i + sine * along_r) * factor).astype(BF16)
            dot = functools.partial(jnp.dot, preferred_element_type=F32)
            out_ref[g, pol, 0] = (dot(w_r, y_r) - dot(w_i, y_i)).astype(BF16)
            out_ref[g, pol, 1] = (dot(w_i, y_r) + dot(w_r, y_i)).astype(BF16)


def beamform(corr_channels, beam_channels, me, gains, cosine, sine, y, groups):
    samples = y.shape[3]
    beams = cosine.shape[0] // groups
    return pl.pallas_call(
        beam_kernel,
        in_specs=[whole(SMEM)] * 3 + [whole(VMEM)] * 4,
        out_specs=whole(VMEM),
        out_shape=jax.ShapeDtypeStruct((groups, 2, 2, beams, samples), BF16),
        compiler_params=params(),
        name="beamform",
    )(corr_channels, beam_channels, me, gains, cosine, sine, y)


def swap(x, axis, mask):
    n = lax.axis_size(axis)
    return lax.ppermute(x, axis, [(i, i ^ mask) for i in range(n)])


def exchange(part):
    part = part[0]
    part = part + swap(part, "grp", 1)
    part = part + swap(part, "tm", 1)
    part = part + swap(part, "tm", 2)
    return part[None]


def body(
    voltages,
    prior_gains,
    station_flags,
    ingest_map,
    station_coords,
    pointing,
    corr_channels,
    beam_channels,
):
    n_freq = lax.axis_size("freq")
    n_time = lax.axis_size("tm")
    n_group = lax.axis_size("grp")
    freq_index = lax.axis_index("freq")
    group_index = lax.axis_index("grp")
    slots, _, rows, samples = voltages.shape
    stations = ingest_map.shape[0]
    inputs = 2 * stations
    team = n_time * n_group
    total = samples * n_time

    me = freq_index.astype(jnp.int32).reshape(1)
    base = ((freq_index * n_group + group_index) * rows).astype(jnp.int32).reshape(1)

    corr_send = ingest(voltages, corr_channels, ingest_map, station_flags, base, n_group)
    corr_y = lax.all_to_all(corr_send, WIDE, split_axis=0, concat_axis=0, tiled=True)
    beam_send = ingest(voltages, beam_channels, ingest_map, station_flags, base, n_group)
    beam_send, corr_y = lax.optimization_barrier((beam_send, corr_y))
    beam_y = lax.all_to_all(beam_send, WIDE, split_axis=0, concat_axis=0, tiled=True)

    my_beam = lax.dynamic_slice_in_dim(beam_channels, freq_index, 1, 0)[0]
    ratio = 0.875 + 0.25 * (my_beam.astype(F32) + 0.5) / slots
    slot_coords = jnp.take(station_coords, ingest_map, axis=1, mode="clip")
    east = (pointing[0].astype(F32) + 0.5) / GRID_CELLS - 0.5
    north = (pointing[1].astype(F32) + 0.5) / GRID_CELLS - 0.5
    phase = (2.0 * math.pi * ratio) * (
        east[:, None] * slot_coords[0][None, :] + north[:, None] * slot_coords[1][None, :]
    )
    cosine, sine = jnp.cos(phase), jnp.sin(phase)

    parts = correlate(corr_y, 1.0 / total, n_time, n_group)
    parts = lax.psum_scatter(parts, "tm", scatter_dimension=2, tiled=True)
    parts = lax.psum_scatter(parts, "grp", scatter_dimension=1, tiled=True)
    visibilities = parts.astype(F32)[None]

    z = prior_gains[0]
    scale = float(inputs) / total
    sums = None
    for _ in range(ITERS):
        if sums is None:
            part = apply_visibilities(corr_y, z, None, scale, team)
        else:
            part, z = apply_visibilities(corr_y, z, sums, scale, team)
        sums = exchange(part)
    z, copies = finish(z, sums, scale, n_freq)
    copies, beam_y = lax.optimization_barrier((copies, beam_y))
    all_gains = lax.all_to_all(copies, "freq", split_axis=0, concat_axis=0, tiled=True)

    beams = beamform(
        corr_channels, beam_channels, me, all_gains, cosine, sine, beam_y, n_group
    )
    own = lax.dynamic_index_in_dim(beams, group_index, 0, keepdims=False)
    away = lax.dynamic_index_in_dim(beams, 1 - group_index, 0, keepdims=False)
    other = swap(away, "grp", 1)
    first = jnp.where(group_index == 0, own, other)
    second = jnp.where(group_index == 0, other, own)
    return visibilities, z[None], jnp.concatenate([first, second], axis=3)[None]


def solution(mesh):
    return jax.shard_map(
        body,
        mesh=mesh,
        in_specs=(
            P(None, None, ("freq", "grp"), "tm"),
            P("freq", None, None),
            P(),
            P(),
            P(),
            P(),
            P(),
            P(),
        ),
        out_specs=(
            P("freq", None, "grp", "tm"),
            P("freq", None, None),
            P("freq", None, None, "grp", "tm"),
        ),
        check_vma=False,
    )
```

time: 448 us -> 200 us (0.45)
  waiting for transfers between devices: 245 us -> 90.4 us
  blocking collectives: 94 us -> 0 us
  starting transfers between devices: 17.7 us -> 59.8 us
  matrix products: 28.9 us -> 0 us
  Pallas kernels: 0 us -> 17.7 us
  local copies, waits for them, and re-layouts: 24.8 us -> 10.1 us
  other arithmetic: 18.4 us -> 5.3 us
    all_to_all x2 -> x3, waiting for transfers between devices: 178 us -> 56.4 us  [the longest x1 45.8 us: body(): lax.all_to_all(corr_send, WIDE, split_axis=0, concat_axis=0, tiled=True)]
    all_gather x1 -> x0, waiting for transfers between devices: 66.2 us -> none  [body(): paired = lax.all_gather(voltages, 'grp', axis=2, tiled=True)]
    all_gather x5 -> x0, blocking collectives: 66.1 us -> none  [the longest x1 52.9 us: body(): all_gains = lax.all_gather(gains, 'freq', axis=0, tiled=True)]
    ppermute x0 -> x13, waiting for transfers between devices: none -> 32.7 us  [swap(): return lax.ppermute(x, axis, [(i, i ^ mask) for i in range(n)])]
    dot_general x19 -> x0, matrix products: 28.9 us -> none  [the longest x1 6.15 us: body(): jnp.einsum('corit,crjt->coij', left, corr_volts, preferred_element_type=j...]
    psum x4 -> x0, blocking collectives: 27.9 us -> none  [body(): update = lax.psum(update, 'tm')]
    all_to_all x2 -> x3, starting transfers between devices: 17.6 us -> 39.1 us  [the longest x1 18.5 us: body(): lax.all_to_all(copies, 'freq', split_axis=0, concat_axis=0, tiled=True)]
    ppermute x0 -> x13, starting transfers between devices: none -> 20.6 us  [swap(): return lax.ppermute(x, axis, [(i, i ^ mask) for i in range(n)])]
  transfers between devices with their start and end apart: 4 -> 18, of which waited for: 3 -> 17; matrix products, arithmetic and copies ran while one was open for 5% -> 3% of each run, Pallas kernels for 0% -> 5%
where the time goes in v1:
time: 200 us; the launch traced here: 198 us
  waiting for transfers between devices  90.4 us (45%)
  starting transfers between devices  59.8 us (30%)
  Pallas kernels  17.7 us (9%)
  between operations  14.9 us (7%)
  local copies, waits for them, and re-layouts  10.1 us (5%)
  other arithmetic  5.3 us (3%)
    all_to_all x1, waiting for transfers between devices, body(): lax.all_to_all(corr_send, WIDE, split_axis=0, concat_axis=0, tiled=True)  45.8 us
    ppermute x13, waiting for transfers between devices, swap(): return lax.ppermute(x, axis, [(i, i ^ mask) for i in range(n)])  32.7 us
    ppermute x13, starting transfers between devices, swap(): return lax.ppermute(x, axis, [(i, i ^ mask) for i in range(n)])  20.6 us
    all_to_all x1, starting transfers between devices, body(): lax.all_to_all(copies, 'freq', split_axis=0, concat_axis=0, tiled=True)  18.5 us
    all_to_all x1, starting transfers between devices, body(): lax.all_to_all(corr_send, WIDE, split_axis=0, concat_axis=0, tiled=True)  13.3 us
    all_to_all x1, waiting for transfers between devices, body(): lax.all_to_all(copies, 'freq', split_axis=0, concat_axis=0, tiled=True)  9.98 us
    unnamed x29, local copies, waits for them, and re-layouts  8.09 us
    all_to_all x1, starting transfers between devices, body(): lax.all_to_all(beam_send, WIDE, split_axis=0, concat_axis=0, tiled=True)  7.36 us
  transfers between devices with their start and end apart: 18, of which 17 were waited for; matrix products, arithmetic and copies ran while one was open for 3% of the time, Pallas kernels for 5%

profile of v1, /device:TPU:1, one launch (start us, length us, event | category | flops | bytes accessed | tf_op | source)
XLA Modules:
  0.0 198.2 jit_solution(1753890897154256821)
XLA Ops:
  7.2 1.6 copy-done
  11.9 1.3 copy-done.3
  13.2 13.3 %all-to-all-start = ((bf16[64,2,16,512]{3,2,1,0:T(8,128)(2,1)}), bf16[64,2,16,512]{3,2,1,0:T(8,128)(2,1)S(1)}, u32[]{:S(2)}, u32[]{:S(2)}) async-start(bf16[64,2,16,512]{3,2,1,0:T(8,128)(2,1)} %bitcast.45), calls=%async_computation | async-start | bytes 4194304 | tf_op jit(solution)/shard_map/all_to_all | solution.py:264
  26.6 1.6 copy-done.1
  29.3 1.4 copy-done.2
  30.7 45.8 %all-to-all-done.y_ref = bf16[64,2,16,512]{3,2,1,0:T(8,128)(2,1)S(1)} async-done(((bf16[64,2,16,512]{3,2,1,0:T(8,128)(2,1)}), bf16[64,2,16,512]{3,2,1,0:T(8,128)(2,1)S(1)}, u32[]{:S(2)}, u32[]{:S(2)}) %all-to-all-start) | async-done | bytes 2097184 | tf_op jit(solution)/shard_map/all_to_all | solution.py:264
  76.5 7.3 %correlate.1 = bf16[2,1024,1024]{2,1,0:T(8,128)(2,1)} custom-call(bf16[64,2,16,512]{3,2,1,0:T(8,128)(2,1)S(1)} %all-to-all-done.y_ref), custom_call_target="tpu_custom_call" | custom-call | tf_op jit(solution)/shard_map/correlate/pallas_call | solution.py:97
  83.8 7.4 %all-to-all-start.1 = ((bf16[64,2,16,512]{3,2,1,0:T(8,128)(2,1)}), bf16[64,2,16,512]{3,2,1,0:T(8,128)(2,1)}, u32[]{:S(2)}, u32[]{:S(2)}) async-start(bf16[64,2,16,512]{3,2,1,0:T(8,128)(2,1)} %bitcast.44), calls=%async_computation.3 | async-start | bytes 4194304 | tf_op jit(solution)/shard_map/all_to_all | solution.py:267
  92.2 1.5 collective-permute-start
  93.7 2.4 %collective-permute-done = f32[2,1024]{1,0:T(2,128)S(1)} collective-permute-done((f32[2,1024]{1,0:T(2,128)S(1)}, f32[2,1024]{1,0:T(2,128)S(1)}, u32[]{:S(2)}, u32[]{:S(2)}) %collective-permute-start) | collective-permute-done | bytes 8224 | tf_op jit(solution)/shard_map/ppermute | solution.py:228
  97.3 1.8 collective-permute-done.1
  99.1 2.8 %collective-permute-start.2 = (f32[2,1024]{1,0:T(2,128)S(1)}, f32[2,1024]{1,0:T(2,128)S(1)}, u32[]{:S(2)}, u32[]{:S(2)}) collective-permute-start(f32[2,1024]{1,0:T(2,128)S(1)} %add.91), channel_id=1, source_target_pairs={{0,4},{2,6},{4,0},{6,2},{1,5},{3,7},{5,1},{7,3},{8,12},{10,14},{12... | collective-permute-start | bytes 24584 | tf_op jit(solution)/shard_map/ppermute | solution.py:228
  101.9 1.8 collective-permute-done.2
  105.7 2.2 %collective-permute-done.3 = f32[2,1024]{1,0:T(2,128)S(1)} collective-permute-done((f32[2,1024]{1,0:T(2,128)S(1)}, f32[2,1024]{1,0:T(2,128)S(1)}, u32[]{:S(2)}, u32[]{:S(2)}) %collective-permute-start.3) | collective-permute-done | bytes 8224 | tf_op jit(solution)/shard_map/ppermute | solution.py:228
  107.9 1.3 collective-permute-start.4
  109.2 1.9 collective-permute-done.4
  111.2 2.7 %collective-permute-start.5 = (f32[2,1024]{1,0:T(2,128)S(1)}, f32[2,1024]{1,0:T(2,128)S(1)}, u32[]{:S(2)}, u32[]{:S(2)}) collective-permute-start(f32[2,1024]{1,0:T(2,128)S(1)} %add.94), channel_id=1, source_target_pairs={{0,4},{2,6},{4,0},{6,2},{1,5},{3,7},{5,1},{7,3},{8,12},{10,14},{12... | collective-permute-start | bytes 24584 | tf_op jit(solution)/shard_map/ppermute | solution.py:228
  113.9 2.0 %collective-permute-done.5 = f32[2,1024]{1,0:T(2,128)S(1)} collective-permute-done((f32[2,1024]{1,0:T(2,128)S(1)}, f32[2,1024]{1,0:T(2,128)S(1)}, u32[]{:S(2)}, u32[]{:S(2)}) %collective-permute-start.5) | collective-permute-done | bytes 8224 | tf_op jit(solution)/shard_map/ppermute | solution.py:228
  118.2 1.9 collective-permute-done.6
  120.1 1.3 collective-permute-start.7
  121.4 1.9 collective-permute-done.7
  123.3 2.6 %collective-permute-start.8 = (f32[2,1024]{1,0:T(2,128)S(1)}, f32[2,1024]{1,0:T(2,128)S(1)}, u32[]{:S(2)}, u32[]{:S(2)}) collective-permute-start(f32[2,1024]{1,0:T(2,128)S(1)} %add.97), channel_id=1, source_target_pairs={{0,4},{2,6},{4,0},{6,2},{1,5},{3,7},{5,1},{7,3},{8,12},{10,14},{12... | collective-permute-start | bytes 24584 | tf_op jit(solution)/shard_map/ppermute | solution.py:228
  125.9 2.2 %collective-permute-done.8 = f32[2,1024]{1,0:T(2,128)S(1)} collective-permute-done((f32[2,1024]{1,0:T(2,128)S(1)}, f32[2,1024]{1,0:T(2,128)S(1)}, u32[]{:S(2)}, u32[]{:S(2)}) %collective-permute-start.8) | collective-permute-done | bytes 8224 | tf_op jit(solution)/shard_map/ppermute | solution.py:228
  132.3 1.3 collective-permute-start.10
  133.6 1.6 collective-permute-done.10
  135.2 2.6 %collective-permute-start.11 = (f32[2,1024]{1,0:T(2,128)S(1)}, f32[2,1024]{1,0:T(2,128)S(1)}, u32[]{:S(2)}, u32[]{:S(2)}) collective-permute-start(f32[2,1024]{1,0:T(2,128)S(1)} %add.100), channel_id=1, source_target_pairs={{0,4},{2,6},{4,0},{6,2},{1,5},{3,7},{5,1},{7,3},{8,12},{10,14},{12... | collective-permute-start | bytes 24584 | tf_op jit(solution)/shard_map/ppermute | solution.py:228
  141.1 18.5 %all-to-all-start.2 = ((f32[32,2,1024]{2,1,0:T(2,128)}), f32[32,2,1024]{2,1,0:T(2,128)S(1)}, u32[]{:S(2)}, u32[]{:S(2)}) async-start(f32[32,2,1024]{2,1,0:T(2,128)} %get-tuple-element.25), calls=%async_computation.4 | async-start | bytes 524288 | tf_op jit(solution)/shard_map/all_to_all | solution.py:295
  161.0 2.0 fusion
  163.0 10.0 %all-to-all-done.2.gains_ref = f32[32,2,1024]{2,1,0:T(2,128)S(1)} async-done(((f32[32,2,1024]{2,1,0:T(2,128)}), f32[32,2,1024]{2,1,0:T(2,128)S(1)}, u32[]{:S(2)}, u32[]{:S(2)}) %all-to-all-start.2) | async-done | bytes 262176 | tf_op jit(solution)/shard_map/all_to_all | solution.py:295
  172.9 3.1 %beamform.1 = bf16[2,2,2,128,512]{4,3,2,1,0:T(8,128)(2,1)S(1)} custom-call(s32[32]{0:T(128)S(1)} %copy-done.10, s32[32]{0:T(128)S(1)} %copy-done.11, s32[1]{0:T(128)} %bitcast.14.me_ref, f32[32,2,1024]{2,1,0:T(2,128)S(1)} %all-to-all-done.2.gains_ref, f32[256,512]{1,0:T(8,128)S(1)} %get-tuple-element.32.cos_ref, f32[256,512]{1,0:T(8,128)S(1)} %get-tuple-element.31.sin_ref, ...), custom_call_target="tpu_custom_call" | custom-call | tf_op jit(solution)/shard_map/beamform/pallas_call | solution.py:216
  176.4 11.7 %collective-permute-done.12 = bf16[2,2,128,512]{3,2,1,0:T(8,128)(2,1)S(1)} collective-permute-done((bf16[2,2,128,512]{3,2,1,0:T(8,128)(2,1)S(1)}, bf16[2,2,128,512]{3,2,1,0:T(8,128)(2,1)S(1)}, u32[]{:S(2)}, u32[]{:S(2)}) %collective-permute-start.12) | collective-permute-done | bytes 524320 | tf_op jit(solution)/shard_map/ppermute | solution.py:228
  189.3 2.1 %bitcast_convert_fusion = f32[1,2,512,256]{3,2,1,0:T(8,128)} fusion(bf16[2,512,256]{2,1,0:T(8,128)(2,1)} %reduce-scatter.5.cloned.1.call-done), kind=kLoop, calls=%fused_computation.2 | loop fusion | flops 262144 | bytes 1572864 | tf_op jit(solution)/shard_map/broadcast_in_dim | solution.py:282
  (70 shorter events, 20.6 us)
Async XLA Ops:
  7.2 1.6 copy-start
  8.8 0.7 copy-start.5
  9.5 0.7 copy-start.7
  10.1 0.7 copy-start.9
  11.9 1.3 copy-start.3
  13.2 13.4 %copy-start.6 = (s32[512]{0:T(512)S(1)}, s32[512]{0:T(512)}, u32[]{:S(2)}) copy-start(s32[512]{0:T(512)} %map_ref.3) | copy-start | bytes 6148
  13.2 13.4 %copy-start.8 = (s32[512]{0:T(512)S(1)}, s32[512]{0:T(512)}, u32[]{:S(2)}) copy-start(s32[512]{0:T(512)} %flag_ref.3) | copy-start | bytes 6148
  13.2 13.4 %copy-start.11 = (s32[32]{0:T(128)S(1)}, s32[32]{0:T(128)}, u32[]{:S(2)}) copy-start(s32[32]{0:T(128)} %beam_ref.1) | copy-start | bytes 388
  13.2 63.3 %all-to-all-start = ((bf16[64,2,16,512]{3,2,1,0:T(8,128)(2,1)}), bf16[64,2,16,512]{3,2,1,0:T(8,128)(2,1)S(1)}, u32[]{:S(2)}, u32[]{:S(2)}) async-start(bf16[64,2,16,512]{3,2,1,0:T(8,128)(2,1)} %bitcast.45), calls=%async_computation | async-start | bytes 4194304 | tf_op jit(solution)/shard_map/all_to_all | solution.py:264
  26.5 105.1 %reduce-scatter.3.cloned.1.call-start = ((), (), s32[]{:S(2)}) async-start(), calls=%async_computation.5 | async-start | bytes 5242880 | tf_op jit(solution)/shard_map/reduce_scatter | solution.py:280
  26.6 1.6 copy-start.1
  29.3 1.4 copy-start.2
  83.8 7.4 %copy-start.4 = (f32[1,2,1024]{2,1,0:T(2,128)S(1)}, f32[1,2,1024]{2,1,0:T(2,128)}, u32[]{:S(2)}) copy-start(f32[1,2,1024]{2,1,0:T(2,128)} %param.9) | copy-start | bytes 24580
  83.8 57.3 %all-to-all-start.1 = ((bf16[64,2,16,512]{3,2,1,0:T(8,128)(2,1)}), bf16[64,2,16,512]{3,2,1,0:T(8,128)(2,1)}, u32[]{:S(2)}, u32[]{:S(2)}) async-start(bf16[64,2,16,512]{3,2,1,0:T(8,128)(2,1)} %bitcast.44), calls=%async_computation.3 | async-start | bytes 4194304 | tf_op jit(solution)/shard_map/all_to_all | solution.py:267
  91.2 98.1 %reduce-scatter.5.cloned.1.call-start = ((), (), s32[]{:S(2)}) async-start(), calls=%async_computation.6 | async-start | bytes 1572864 | tf_op jit(solution)/shard_map/reduce_scatter | solution.py:281
  92.2 3.8 %collective-permute-start = (f32[2,1024]{1,0:T(2,128)S(1)}, f32[2,1024]{1,0:T(2,128)S(1)}, u32[]{:S(2)}, u32[]{:S(2)}) collective-permute-start(f32[2,1024]{1,0:T(2,128)S(1)} %slice_bitcast_fusion), channel_id=1, source_target_pairs={{0,1},{1,0},{2,3},{3,2},{4,5},{5,4},{6,7},{7,6},{8,9},{9,8},{10,11... | collective-permute-start | bytes 24584 | tf_op jit(solution)/shard_map/ppermute | solution.py:228
  96.1 3.0 %collective-permute-start.1 = (f32[2,1024]{1,0:T(2,128)S(1)}, f32[2,1024]{1,0:T(2,128)S(1)}, u32[]{:S(2)}, u32[]{:S(2)}) collective-permute-start(f32[2,1024]{1,0:T(2,128)S(1)} %fusion.5), channel_id=1, source_target_pairs={{0,2},{2,0},{4,6},{6,4},{1,3},{3,1},{5,7},{7,5},{8,10},{10,8},{12,... | collective-permute-start | bytes 24584 | tf_op jit(solution)/shard_map/ppermute | solution.py:228
  99.1 4.6 %collective-permute-start.2 = (f32[2,1024]{1,0:T(2,128)S(1)}, f32[2,1024]{1,0:T(2,128)S(1)}, u32[]{:S(2)}, u32[]{:S(2)}) collective-permute-start(f32[2,1024]{1,0:T(2,128)S(1)} %add.91), channel_id=1, source_target_pairs={{0,4},{2,6},{4,0},{6,2},{1,5},{3,7},{5,1},{7,3},{8,12},{10,14},{12... | collective-permute-start | bytes 24584 | tf_op jit(solution)/shard_map/ppermute | solution.py:228
  104.9 3.0 %collective-permute-start.3 = (f32[2,1024]{1,0:T(2,128)S(1)}, f32[2,1024]{1,0:T(2,128)S(1)}, u32[]{:S(2)}, u32[]{:S(2)}) collective-permute-start(f32[2,1024]{1,0:T(2,128)S(1)} %slice_bitcast_fusion.3), channel_id=1, source_target_pairs={{0,1},{1,0},{2,3},{3,2},{4,5},{5,4},{6,7},{7,6},{8,9},{9,8},{10,11... | collective-permute-start | bytes 24584 | tf_op jit(solution)/shard_map/ppermute | solution.py:228
  107.9 3.2 %collective-permute-start.4 = (f32[2,1024]{1,0:T(2,128)S(1)}, f32[2,1024]{1,0:T(2,128)S(1)}, u32[]{:S(2)}, u32[]{:S(2)}) collective-permute-start(f32[2,1024]{1,0:T(2,128)S(1)} %fusion.2), channel_id=1, source_target_pairs={{0,2},{2,0},{4,6},{6,4},{1,3},{3,1},{5,7},{7,5},{8,10},{10,8},{12,... | collective-permute-start | bytes 24584 | tf_op jit(solution)/shard_map/ppermute | solution.py:228
  111.2 4.7 %collective-permute-start.5 = (f32[2,1024]{1,0:T(2,128)S(1)}, f32[2,1024]{1,0:T(2,128)S(1)}, u32[]{:S(2)}, u32[]{:S(2)}) collective-permute-start(f32[2,1024]{1,0:T(2,128)S(1)} %add.94), channel_id=1, source_target_pairs={{0,4},{2,6},{4,0},{6,2},{1,5},{3,7},{5,1},{7,3},{8,12},{10,14},{12... | collective-permute-start | bytes 24584 | tf_op jit(solution)/shard_map/ppermute | solution.py:228
  117.0 20.7 %copy-start.12 = (f32[2,512]{1,0:T(2,128)S(1)}, f32[2,512]{1,0:T(2,128)}, u32[]{:S(2)}) copy-start(f32[2,512]{1,0:T(2,128)} %param.12) | copy-start | bytes 12292
  117.1 3.0 %collective-permute-start.6 = (f32[2,1024]{1,0:T(2,128)S(1)}, f32[2,1024]{1,0:T(2,128)S(1)}, u32[]{:S(2)}, u32[]{:S(2)}) collective-permute-start(f32[2,1024]{1,0:T(2,128)S(1)} %slice_bitcast_fusion.2), channel_id=1, source_target_pairs={{0,1},{1,0},{2,3},{3,2},{4,5},{5,4},{6,7},{7,6},{8,9},{9,8},{10,11... | collective-permute-start | bytes 24584 | tf_op jit(solution)/shard_map/ppermute | solution.py:228
  120.1 3.2 %collective-permute-start.7 = (f32[2,1024]{1,0:T(2,128)S(1)}, f32[2,1024]{1,0:T(2,128)S(1)}, u32[]{:S(2)}, u32[]{:S(2)}) collective-permute-start(f32[2,1024]{1,0:T(2,128)S(1)} %fusion.3), channel_id=1, source_target_pairs={{0,2},{2,0},{4,6},{6,4},{1,3},{3,1},{5,7},{7,5},{8,10},{10,8},{12,... | collective-permute-start | bytes 24584 | tf_op jit(solution)/shard_map/ppermute | solution.py:228
  123.3 4.7 %collective-permute-start.8 = (f32[2,1024]{1,0:T(2,128)S(1)}, f32[2,1024]{1,0:T(2,128)S(1)}, u32[]{:S(2)}, u32[]{:S(2)}) collective-permute-start(f32[2,1024]{1,0:T(2,128)S(1)} %add.97), channel_id=1, source_target_pairs={{0,4},{2,6},{4,0},{6,2},{1,5},{3,7},{5,1},{7,3},{8,12},{10,14},{12... | collective-permute-start | bytes 24584 | tf_op jit(solution)/shard_map/ppermute | solution.py:228
  128.1 32.9 %copy-start.13 = (s32[2,256]{1,0:T(2,128)S(1)}, s32[2,256]{1,0:T(2,128)}, u32[]{:S(2)}) copy-start(s32[2,256]{1,0:T(2,128)} %param.13) | copy-start | bytes 6148
  129.2 43.7 %copy-start.10 = (s32[32]{0:T(128)S(1)}, s32[32]{0:T(128)}, u32[]{:S(2)}) copy-start(s32[32]{0:T(128)} %corr_ref.1) | copy-start | bytes 388
  129.2 3.0 %collective-permute-start.9 = (f32[2,1024]{1,0:T(2,128)S(1)}, f32[2,1024]{1,0:T(2,128)S(1)}, u32[]{:S(2)}, u32[]{:S(2)}) collective-permute-start(f32[2,1024]{1,0:T(2,128)S(1)} %slice_bitcast_fusion.1), channel_id=1, source_target_pairs={{0,1},{1,0},{2,3},{3,2},{4,5},{5,4},{6,7},{7,6},{8,9},{9,8},{10,11... | collective-permute-start | bytes 24584 | tf_op jit(solution)/shard_map/ppermute | solution.py:228
  132.3 2.9 %collective-permute-start.10 = (f32[2,1024]{1,0:T(2,128)S(1)}, f32[2,1024]{1,0:T(2,128)S(1)}, u32[]{:S(2)}, u32[]{:S(2)}) collective-permute-start(f32[2,1024]{1,0:T(2,128)S(1)} %fusion.4), channel_id=1, source_target_pairs={{0,2},{2,0},{4,6},{6,4},{1,3},{3,1},{5,7},{7,5},{8,10},{10,8},{12,... | collective-permute-start | bytes 24584 | tf_op jit(solution)/shard_map/ppermute | solution.py:228
  135.2 4.4 %collective-permute-start.11 = (f32[2,1024]{1,0:T(2,128)S(1)}, f32[2,1024]{1,0:T(2,128)S(1)}, u32[]{:S(2)}, u32[]{:S(2)}) collective-permute-start(f32[2,1024]{1,0:T(2,128)S(1)} %add.100), channel_id=1, source_target_pairs={{0,4},{2,6},{4,0},{6,2},{1,5},{3,7},{5,1},{7,3},{8,12},{10,14},{12... | collective-permute-start | bytes 24584 | tf_op jit(solution)/shard_map/ppermute | solution.py:228
  141.1 31.9 %all-to-all-start.2 = ((f32[32,2,1024]{2,1,0:T(2,128)}), f32[32,2,1024]{2,1,0:T(2,128)S(1)}, u32[]{:S(2)}, u32[]{:S(2)}) async-start(f32[32,2,1024]{2,1,0:T(2,128)} %get-tuple-element.25), calls=%async_computation.4 | async-start | bytes 524288 | tf_op jit(solution)/shard_map/all_to_all | solution.py:295
  176.1 12.0 %collective-permute-start.12 = (bf16[2,2,128,512]{3,2,1,0:T(8,128)(2,1)S(1)}, bf16[2,2,128,512]{3,2,1,0:T(8,128)(2,1)S(1)}, u32[]{:S(2)}, u32[]{:S(2)}) collective-permute-start(bf16[2,2,128,512]{3,2,1,0:T(8,128)(2,1)S(1)} %dynamic-slice_bitcast_fusion), channel_id=1, source_target_pairs={{0,1},{1,0},{2,3},{3,2},{4,5},{5,4},{6,7},{7,6},{8,9},{9,8},{10,11... | collective-permute-start | bytes 1572872 | tf_op jit(solution)/shard_map/ppermute | solution.py:228
Sparse Core Ops, SparseCore 0:
  83.9 47.6 reduce-scatter.2
  134.2 30.2 reduce-scatter.4

commit v2 on v1

v2 whole, which is shorter than its diff:
```python
import functools
import math

import jax
import jax.numpy as jnp
from jax import lax
from jax.experimental import pallas as pl
from jax.experimental.pallas import tpu as pltpu
from jax.sharding import PartitionSpec as P

ITERS = 4
GRID_CELLS = 64.0
F32 = jnp.float32
BF16 = jnp.bfloat16
WIDE = ("freq", "grp")
TEAM = ("tm", "grp")
VMEM = pltpu.VMEM
SMEM = pltpu.SMEM


def whole(space=VMEM):
    return pl.BlockSpec(memory_space=space)


def params(mib=48):
    return pltpu.CompilerParams(vmem_limit_bytes=mib << 20)


def ingest_kernel(
    stations,
    pick,
    base_ref,
    chan_hbm,
    map_hbm,
    flag_hbm,
    volts_hbm,
    out_hbm,
    chan_ref,
    map_ref,
    flag_ref,
    volts_ref,
    out_ref,
    table_sem,
    volts_sem,
    out_sem,
):
    slots, groups, _, rows, half = out_ref.shape
    steps = out_sem.shape[0]
    per_step = slots // steps
    load = pltpu.make_async_copy(volts_hbm, volts_ref, volts_sem)
    load.start()
    tables = [
        pltpu.make_async_copy(source, target, table_sem.at[i])
        for i, (source, target) in enumerate(
            ((chan_hbm, chan_ref), (map_hbm, map_ref), (flag_hbm, flag_ref))
        )
    ]
    for copy in tables:
        copy.start()
    for copy in tables:
        copy.wait()
    line = lax.broadcasted_iota(jnp.int32, (rows, half), 0)
    keep = jnp.zeros((rows, half), F32)
    for row in range(rows):
        slot = lax.rem(base_ref[0] + row, stations)
        good = (1 - flag_ref[map_ref[slot]]).astype(F32)
        keep = jnp.where(line == row, good, keep)
    keep = keep.astype(BF16)
    load.wait()
    stores = []
    for step in range(steps):
        for slot in range(step * per_step, (step + 1) * per_step):
            for g in range(groups):
                index, cut = pick(slot, g)
                channel = chan_ref[index]
                for part in range(2):
                    piece = volts_ref[channel, part, :, cut * half : (cut + 1) * half]
                    out_ref[slot, g, part] = piece * keep
        span = pl.ds(step * per_step, per_step)
        store = pltpu.make_async_copy(out_ref.at[span], out_hbm.at[span], out_sem.at[step])
        store.start()
        stores.append(store)
    for store in stores:
        store.wait()


def ingest(voltages, channels, ingest_map, station_flags, base, groups, pick):
    slots, parts, rows, samples = voltages.shape
    stations = ingest_map.shape[0]
    half = samples // 2
    shape = (slots, groups, parts, rows, half)
    steps = 8
    out = pl.pallas_call(
        functools.partial(ingest_kernel, stations, pick),
        in_specs=[whole(SMEM)] + [whole(pltpu.HBM)] * 4,
        out_specs=whole(pltpu.HBM),
        out_shape=jax.ShapeDtypeStruct(shape, BF16),
        scratch_shapes=[
            SMEM(channels.shape, jnp.int32),
            SMEM(ingest_map.shape, jnp.int32),
            SMEM(station_flags.shape, jnp.int32),
            VMEM(voltages.shape, BF16),
            VMEM(shape, BF16),
            pltpu.SemaphoreType.DMA((3,)),
            pltpu.SemaphoreType.DMA,
            pltpu.SemaphoreType.DMA((steps,)),
        ],
        compiler_params=params(62),
        name="ingest",
    )(base, channels, ingest_map, station_flags, voltages)
    return out.reshape(slots * groups, parts, rows, half)


def load_part(ref, part):
    blocks, _, rows, samples = ref.shape
    return ref[:, part].reshape(blocks * rows, samples)


def nt_dot(a, b):
    return lax.dot_general(a, b, (((1,), (1,)), ((), ())), preferred_element_type=F32)


def correlate_kernel(scale, y_ref, out_ref, left_ref, turn_ref):
    row, col = pl.program_id(0), pl.program_id(1)
    samples = y_ref.shape[3]

    @pl.when((col == 0) & (row == 0))
    def _():
        real, imag = load_part(y_ref, 0), load_part(y_ref, 1)
        left_ref[:, :samples] = real
        left_ref[:, samples:] = imag
        turn_ref[:, :samples] = imag
        turn_ref[:, samples:] = -real

    height, width = out_ref.shape[1], out_ref.shape[2]
    rows = pl.ds(pl.multiple_of(row * height, height), height)
    cols = pl.ds(pl.multiple_of(col * width, width), width)
    right = left_ref[cols, :]
    out_ref[0] = (nt_dot(left_ref[rows, :], right) * scale).astype(BF16)
    out_ref[1] = (nt_dot(turn_ref[rows, :], right) * scale).astype(BF16)


def correlate(y, scale):
    blocks, _, rows, samples = y.shape
    inputs = blocks * rows
    height, width = inputs // 2, inputs // 4
    return pl.pallas_call(
        functools.partial(correlate_kernel, scale),
        grid=(inputs // height, inputs // width),
        in_specs=[whole(VMEM)],
        out_specs=pl.BlockSpec((2, height, width), lambda i, j: (0, i, j)),
        out_shape=jax.ShapeDtypeStruct((2, inputs, inputs), BF16),
        scratch_shapes=[VMEM((inputs, 2 * samples), BF16)] * 2,
        compiler_params=params(60),
        name="correlate",
    )(y)


def in_terms(x):
    high = x.astype(BF16).astype(F32)
    rest = x - high
    mid = rest.astype(BF16).astype(F32)
    low = rest - mid
    pad = jnp.zeros_like(x)
    return jnp.concatenate([high, mid, low, pad], axis=0).astype(BF16)


def add_terms(x):
    return x[0:2] + x[2:4] + x[4:6]


def advance(scale, z, update):
    power = jnp.sum(z * z) + 1e-06
    return 0.5 * (z + scale * update / power)


def apply_kernel(scale, first, y_ref, z_ref, *refs):
    z = z_ref[...]
    if first:
        (out_ref,) = refs
    else:
        near_ref, far_ref, out_ref, fresh_ref = refs
        z = advance(scale, z, near_ref[...] + far_ref[...])
        fresh_ref[...] = z
    real, imag = load_part(y_ref, 0), load_part(y_ref, 1)
    terms = in_terms(z)
    a = add_terms(jnp.dot(terms, real, preferred_element_type=F32))
    b = add_terms(jnp.dot(terms, imag, preferred_element_type=F32))
    w = jnp.concatenate([a[0:1] + b[1:2], a[1:2] - b[0:1]], axis=0)
    terms = in_terms(w)
    c = add_terms(nt_dot(terms, real))
    d = add_terms(nt_dot(terms, imag))
    out_ref[...] = jnp.concatenate([c[0:1] - d[1:2], c[1:2] + d[0:1]], axis=0)


def apply_visibilities(y, z, sums, scale):
    first = sums is None
    vector = jax.ShapeDtypeStruct(z.shape, F32)
    return pl.pallas_call(
        functools.partial(apply_kernel, scale, first),
        in_specs=[whole(VMEM)] * (2 if first else 4),
        out_specs=whole(VMEM) if first else [whole(VMEM)] * 2,
        out_shape=vector if first else [vector] * 2,
        compiler_params=params(16),
        name="apply",
    )(y, z, *(sums or ()))


def finish_kernel(scale, z_ref, near_ref, far_ref, fresh_ref, copies_ref):
    z = advance(scale, z_ref[...], near_ref[...] + far_ref[...])
    fresh_ref[...] = z
    for i in range(copies_ref.shape[0]):
        copies_ref[i] = z


def finish(z, sums, scale, copies):
    return pl.pallas_call(
        functools.partial(finish_kernel, scale),
        in_specs=[whole(VMEM)] * 3,
        out_specs=[whole(VMEM)] * 2,
        out_shape=[
            jax.ShapeDtypeStruct(z.shape, F32),
            jax.ShapeDtypeStruct((copies,) + z.shape, F32),
        ],
        compiler_params=params(8),
        name="finish",
    )(z, *sums)


def find_slot(corr_ref, channel):
    slot = jnp.int32(0)
    for k in range(corr_ref.shape[0]):
        slot = jnp.where(corr_ref[k] == channel, k, slot)
    return slot


def choose_kernel(reach, corr_ref, beam_ref, me_ref, line_ref, *out_refs):
    column, chip = me_ref[0] // 2, me_ref[0]
    for (high, _), out_ref in zip(reach, out_refs):
        peer = chip ^ (high * 2 * line_ref.shape[0])
        slot = find_slot(corr_ref, beam_ref[peer])
        out_ref[...] = line_ref[(slot // 2) % line_ref.shape[0]]


def choose(corr_channels, beam_channels, me, line, reach):
    vector = jax.ShapeDtypeStruct(line.shape[1:], F32)
    return pl.pallas_call(
        functools.partial(choose_kernel, reach),
        in_specs=[whole(SMEM)] * 3 + [whole(VMEM)],
        out_specs=[whole(VMEM)] * len(reach),
        out_shape=[vector] * len(reach),
        compiler_params=params(8),
        name="choose",
    )(corr_channels, beam_channels, me, line)


def beam_kernel(
    reach, corr_ref, beam_ref, me_ref, *refs
):
    gain_refs, (cos_ref, sin_ref, y_ref, out_ref) = refs[: len(reach)], refs[len(reach) :]
    slot = find_slot(corr_ref, beam_ref[me_ref[0]])
    half_ring = corr_ref.shape[0] // 2
    far = (slot // half_ring) ^ (me_ref[0] // half_ring)
    side = (slot % 2) ^ me_ref[1]
    gains = gain_refs[0][...]
    for (high, low), ref in zip(reach[1:], gain_refs[1:]):
        hit = ((far == high) & (side == low)).astype(jnp.int32)
        gains = jnp.where(jnp.full(gains.shape, hit) == 1, ref[...], gains)
    blocks, _, rows, samples = y_ref.shape
    stations = blocks // 2 * rows
    beams = out_ref.shape[3]
    factor = 1.0 / math.sqrt(stations)
    for pol in range(2):
        gain_r = gains[0:1, pol * stations : (pol + 1) * stations]
        gain_i = gains[1:2, pol * stations : (pol + 1) * stations]
        denom = jnp.maximum(gain_r * gain_r + gain_i * gain_i, 0.5)
        along_r, along_i = gain_r / denom, gain_i / denom
        y_r = y_ref[pol * blocks // 2 : (pol + 1) * blocks // 2, 0].reshape(stations, samples)
        y_i = y_ref[pol * blocks // 2 : (pol + 1) * blocks // 2, 1].reshape(stations, samples)
        for g in range(out_ref.shape[0]):
            cosine = cos_ref[g * beams : (g + 1) * beams]
            sine = sin_ref[g * beams : (g + 1) * beams]
            w_r = ((cosine * along_r - sine * along_i) * factor).astype(BF16)
            w_i = (-(cosine * along_i + sine * along_r) * factor).astype(BF16)
            dot = functools.partial(jnp.dot, preferred_element_type=F32)
            out_ref[g, pol, 0] = (dot(w_r, y_r) - dot(w_i, y_i)).astype(BF16)
            out_ref[g, pol, 1] = (dot(w_i, y_r) + dot(w_r, y_i)).astype(BF16)


def beamform(reach, corr_channels, beam_channels, me, gains, cosine, sine, y, groups):
    samples = y.shape[3]
    beams = cosine.shape[0] // groups
    return pl.pallas_call(
        functools.partial(beam_kernel, reach),
        in_specs=[whole(SMEM)] * 3 + [whole(VMEM)] * (3 + len(reach)),
        out_specs=whole(VMEM),
        out_shape=jax.ShapeDtypeStruct((groups, 2, 2, beams, samples), BF16),
        compiler_params=params(24),
        name="beamform",
    )(corr_channels, beam_channels, me, *gains, cosine, sine, y)


def swap(x, axis, mask):
    n = lax.axis_size(axis)
    return lax.ppermute(x, axis, [(i, i ^ mask) for i in range(n)])


def exchange(part):
    part = part + swap(part, "freq", 1)
    part = part + swap(part, "tm", 1)
    return part, swap(part, "tm", 3)


def cross(x, turn):
    pairs = []
    for i in range(lax.axis_size("freq") // 2):
        for core in range(2):
            for g in range(2):
                pairs.append(((2 * i + core) * 2 + g, (2 * i + g) * 2 + (core ^ turn)))
    return lax.ppermute(x, WIDE, pairs)


def body(
    voltages,
    prior_gains,
    station_flags,
    ingest_map,
    station_coords,
    pointing,
    corr_channels,
    beam_channels,
):
    n_freq = lax.axis_size("freq")
    n_time = lax.axis_size("tm")
    n_group = lax.axis_size("grp")
    freq_index = lax.axis_index("freq")
    group_index = lax.axis_index("grp")
    slots, _, rows, samples = voltages.shape
    stations = ingest_map.shape[0]
    inputs = 2 * stations
    total = samples * n_time
    core = freq_index % 2

    me = jnp.stack([freq_index, group_index]).astype(jnp.int32)
    base = ((freq_index * n_group + group_index) * rows).astype(jnp.int32).reshape(1)

    corr_send = ingest(
        voltages, corr_channels, ingest_map, station_flags, base, n_group,
        lambda slot, g: (slot // 2 * 2 + g, slot % 2),
    )
    corr_y = lax.all_to_all(corr_send, WIDE, split_axis=0, concat_axis=0, tiled=True)
    beam_send = ingest(
        voltages, beam_channels, ingest_map, station_flags, base, n_group,
        lambda slot, g: (slot, g),
    )
    z = cross(prior_gains[0], 0)
    beam_send, corr_y, z = lax.optimization_barrier((beam_send, corr_y, z))
    beam_y = lax.all_to_all(beam_send, WIDE, split_axis=0, concat_axis=0, tiled=True)

    my_beam = lax.dynamic_slice_in_dim(beam_channels, freq_index, 1, 0)[0]
    ratio = 0.875 + 0.25 * (my_beam.astype(F32) + 0.5) / slots
    slot_coords = jnp.take(station_coords, ingest_map, axis=1, mode="clip")
    east = (pointing[0].astype(F32) + 0.5) / GRID_CELLS - 0.5
    north = (pointing[1].astype(F32) + 0.5) / GRID_CELLS - 0.5
    phase = (2.0 * math.pi * ratio) * (
        east[:, None] * slot_coords[0][None, :] + north[:, None] * slot_coords[1][None, :]
    )
    cosine, sine = jnp.cos(phase), jnp.sin(phase)

    parts = correlate(corr_y, 1.0 / total)
    parts = lax.psum_scatter(parts, "tm", scatter_dimension=2, tiled=True)
    height = inputs // n_group
    near = lax.dynamic_slice_in_dim(parts, core * height, height, 1)
    far = lax.dynamic_slice_in_dim(parts, (1 - core) * height, height, 1)
    near, far = cross(near, 0), cross(far, 1)

    scale = float(inputs) / total
    sums = None
    for _ in range(ITERS):
        if sums is None:
            part = apply_visibilities(corr_y, z, None, scale)
        else:
            part, z = apply_visibilities(corr_y, z, sums, scale)
        sums = exchange(part)
    depth = slots // 4
    z, copies = finish(z, sums, scale, depth)
    copies, beam_y, cosine, sine = lax.optimization_barrier((copies, beam_y, cosine, sine))
    line = [
        [high * 2 * depth + 2 * i + c for i in range(depth)]
        for high in range(2)
        for c in range(2)
    ]
    line = lax.all_to_all(
        copies, "freq", split_axis=0, concat_axis=0, axis_index_groups=line, tiled=True
    )
    reach = [(0, 0), (0, 1), (1, 0), (1, 1)]
    picks = choose(corr_channels, beam_channels, me, line, reach)
    gains = [picks[0]] + [
        swap(pick, WIDE, high * 8 * depth // 2 + low)
        for (high, low), pick in zip(reach[1:], picks[1:])
    ]
    solved = cross(z, 0)
    gains, near, far, solved = lax.optimization_barrier((gains, near, far, solved))
    visibilities = (near.astype(F32) + far.astype(F32))[None]

    beams = beamform(
        reach, corr_channels, beam_channels, me, gains, cosine, sine, beam_y, n_group
    )
    own = lax.dynamic_index_in_dim(beams, group_index, 0, keepdims=False)
    away = lax.dynamic_index_in_dim(beams, 1 - group_index, 0, keepdims=False)
    other = swap(away, "grp", 1)
    first = jnp.where(group_index == 0, own, other)
    second = jnp.where(group_index == 0, other, own)
    return visibilities, solved[None], jnp.concatenate([first, second], axis=3)[None]


def solution(mesh):
    return jax.shard_map(
        body,
        mesh=mesh,
        in_specs=(
            P(None, None, ("freq", "grp"), "tm"),
            P("freq", None, None),
            P(),
            P(),
            P(),
            P(),
            P(),
            P(),
        ),
        out_specs=(
            P("freq", None, "grp", "tm"),
            P("freq", None, None),
            P("freq", None, None, "grp", "tm"),
        ),
        check_vma=False,
    )
```

time: 200 us -> 198 us (0.990)
  waiting for transfers between devices: 90.4 us -> 72.9 us
  Pallas kernels: 17.7 us -> 29.5 us
  starting transfers between devices: 59.8 us -> 62.9 us
  local copies, waits for them, and re-layouts: 10.1 us -> 7.87 us
    ppermute x0 -> x4, starting transfers between devices: none -> 14.1 us  [cross(): return lax.ppermute(x, WIDE, pairs)]
    all_to_all x1, starting transfers between devices: 18.5 us -> 6.52 us  [body(): lax.all_to_all(copies, 'freq', split_axis=0, concat_axis=0, axis_index_gr...]
    all_to_all x1, waiting for transfers between devices: 9.98 us -> 2.11 us  [body(): lax.all_to_all(copies, 'freq', split_axis=0, concat_axis=0, axis_index_gr...]
    pallas_call x4, Pallas kernels: 4.37 us -> 10.8 us  [apply_visibilities(): pl.pallas_call(functools.partial(apply_kernel, scale, first), in_specs=[w...]
    pallas_call x4 -> x5, Pallas kernels: 12.5 us -> 17.9 us  [the longest x1 9.02 us: correlate(): pl.pallas_call(functools.partial(correlate_kernel, scale), grid=(inputs /...]
    ppermute x13 -> x16, waiting for transfers between devices: 32.7 us -> 27.6 us  [swap(): return lax.ppermute(x, axis, [(i, i ^ mask) for i in range(n)])]
    unnamed x29 -> x20, local copies, waits for them, and re-layouts: 8.09 us -> 3.64 us
    all_to_all x1, waiting for transfers between devices: 45.8 us -> 43.1 us  [body(): lax.all_to_all(corr_send, WIDE, split_axis=0, concat_axis=0, tiled=True)]
  transfers between devices with their start and end apart: 18 -> 24, of which waited for: 17 -> 15; matrix products, arithmetic and copies ran while one was open for 3% -> 5% of each run, Pallas kernels for 5% -> 8%
where the time goes in v2:
time: 198 us; the launch traced here: 195 us
  waiting for transfers between devices  72.9 us (37%)
  starting transfers between devices  62.9 us (32%)
  Pallas kernels  29.5 us (15%)
  between operations  15 us (8%)
  local copies, waits for them, and re-layouts  7.87 us (4%)
  other arithmetic  6.67 us (3%)
    all_to_all x1, waiting for transfers between devices, body(): lax.all_to_all(corr_send, WIDE, split_axis=0, concat_axis=0, tiled=True)  43.1 us
    ppermute x16, waiting for transfers between devices, swap(): return lax.ppermute(x, axis, [(i, i ^ mask) for i in range(n)])  27.6 us
    ppermute x16, starting transfers between devices, swap(): return lax.ppermute(x, axis, [(i, i ^ mask) for i in range(n)])  21.7 us
    ppermute x4, starting transfers between devices, cross(): return lax.ppermute(x, WIDE, pairs)  14.1 us
    all_to_all x1, starting transfers between devices, body(): lax.all_to_all(corr_send, WIDE, split_axis=0, concat_axis=0, tiled=True)  13.4 us
    pallas_call x4, Pallas kernels, apply_visibilities(): pl.pallas_call(functools.partial(apply_kernel, scale, first), in_specs=[w...  10.8 us
    pallas_call x1, Pallas kernels, correlate(): pl.pallas_call(functools.partial(correlate_kernel, scale), grid=(inputs /...  9.02 us
    all_to_all x1, starting transfers between devices, body(): lax.all_to_all(beam_send, WIDE, split_axis=0, concat_axis=0, tiled=True)  7.17 us
  transfers between devices with their start and end apart: 24, of which 15 were waited for; matrix products, arithmetic and copies ran while one was open for 5% of the time, Pallas kernels for 8%

profile of v2, /device:TPU:1, one launch (start us, length us, event | category | flops | bytes accessed | tf_op | source)
XLA Modules:
  0.0 194.7 jit_solution(17521346829999522730)
XLA Ops:
  7.2 3.1 %ingest.3 = bf16[32,2,2,16,512]{4,3,2,1,0:T(8,128)(2,1)} custom-call(s32[1]{0:T(128)} %bitcast.2.base_ref, s32[32]{0:T(128)} %corr_ref.3, s32[512]{0:T(512)} %map_hbm.3, s32[512]{0:T(512)} %flag_hbm.3, bf16[32,2,16,1024]{3,2,1,0:T(8,128)(2,1)} %volts_hbm.3), custom_call_target="tpu_custom_call" | custom-call | tf_op jit(solution)/shard_map/ingest/pallas_call | solution.py:93
  10.3 13.4 %all-to-all-start = ((bf16[64,2,16,512]{3,2,1,0:T(8,128)(2,1)}), bf16[64,2,16,512]{3,2,1,0:T(8,128)(2,1)}, u32[]{:S(2)}, u32[]{:S(2)}) async-start(bf16[64,2,16,512]{3,2,1,0:T(8,128)(2,1)} %bitcast.21), calls=%async_computation | async-start | bytes 4194304 | tf_op jit(solution)/shard_map/all_to_all | solution.py:351
  23.7 3.5 %collective-permute-start = (f32[2,1024]{1,0:T(2,128)S(1)}, f32[2,1024]{1,0:T(2,128)S(1)}, u32[]{:S(2)}, u32[]{:S(2)}) collective-permute-start(f32[2,1024]{1,0:T(2,128)S(1)} %bitcast.26), channel_id=1, source_target_pairs={{0,0},{1,8},{8,1},{9,9},{16,16},{17,24},{24,17},{25,25},{32,32},{3... | collective-permute-start | bytes 24584 | tf_op jit(solution)/shard_map/ppermute | solution.py:320
  27.2 3.1 %ingest.2 = bf16[32,2,2,16,512]{4,3,2,1,0:T(8,128)(2,1)} custom-call(s32[1]{0:T(128)} %bitcast.2.base_ref, s32[32]{0:T(128)} %beam_ref.3, s32[512]{0:T(512)} %map_hbm.3, s32[512]{0:T(512)} %flag_hbm.3, bf16[32,2,16,1024]{3,2,1,0:T(8,128)(2,1)} %volts_hbm.3), custom_call_target="tpu_custom_call" | custom-call | tf_op jit(solution)/shard_map/ingest/pallas_call | solution.py:93
  30.4 43.1 %all-to-all-done.y_ref = bf16[64,2,16,512]{3,2,1,0:T(8,128)(2,1)} async-done(((bf16[64,2,16,512]{3,2,1,0:T(8,128)(2,1)}), bf16[64,2,16,512]{3,2,1,0:T(8,128)(2,1)}, u32[]{:S(2)}, u32[]{:S(2)}) %all-to-all-start) | async-done | bytes 2097184 | tf_op jit(solution)/shard_map/all_to_all | solution.py:351
  73.5 9.0 %correlate.1 = bf16[2,1024,1024]{2,1,0:T(8,128)(2,1)} custom-call(bf16[64,2,16,512]{3,2,1,0:T(8,128)(2,1)} %all-to-all-done.y_ref), custom_call_target="tpu_custom_call" | custom-call | tf_op jit(solution)/shard_map/correlate/pallas_call | solution.py:147
  82.6 7.2 %all-to-all-start.1 = ((bf16[64,2,16,512]{3,2,1,0:T(8,128)(2,1)}), bf16[64,2,16,512]{3,2,1,0:T(8,128)(2,1)S(1)}, u32[]{:S(2)}, u32[]{:S(2)}) async-start(bf16[64,2,16,512]{3,2,1,0:T(8,128)(2,1)} %bitcast.20), calls=%async_computation.1 | async-start | bytes 4194304 | tf_op jit(solution)/shard_map/all_to_all | solution.py:358
  89.8 2.6 %apply.4 = f32[2,1024]{1,0:T(2,128)S(1)} custom-call(bf16[64,2,16,512]{3,2,1,0:T(8,128)(2,1)} %all-to-all-done.y_ref, f32[2,1024]{1,0:T(2,128)S(1)} %collective-permute-done.z_ref), custom_call_target="tpu_custom_call" | custom-call | tf_op jit(solution)/shard_map/apply/pallas_call | solution.py:199
  96.8 2.6 %collective-permute-start.3 = (f32[2,1024]{1,0:T(2,128)S(1)}, f32[2,1024]{1,0:T(2,128)S(1)}, u32[]{:S(2)}, u32[]{:S(2)}) collective-permute-start(f32[2,1024]{1,0:T(2,128)S(1)} %add.90.refs_0_), channel_id=1, source_target_pairs={{0,6},{2,4},{4,2},{6,0},{1,7},{3,5},{5,3},{7,1},{8,14},{10,12},{12... | collective-permute-start | bytes 24584 | tf_op jit(solution)/shard_map/ppermute | solution.py:305
  101.1 2.8 %apply.5 = (f32[2,1024]{1,0:T(2,128)S(1)}, f32[2,1024]{1,0:T(2,128)S(1)}) custom-call(bf16[64,2,16,512]{3,2,1,0:T(8,128)(2,1)} %all-to-all-done.y_ref, f32[2,1024]{1,0:T(2,128)S(1)} %collective-permute-done.z_ref, f32[2,1024]{1,0:T(2,128)S(1)} %add.90.refs_0_, f32[2,1024]{1,0:T(2,128)S(1)} %collective-permute-done.3.refs_1_), custom_call_target="tpu_custom_call" | custom-call | tf_op jit(solution)/shard_map/apply/pallas_call | solution.py:199
  106.6 3.2 %collective-permute-done.5 = f32[2,1024]{1,0:T(2,128)S(1)} collective-permute-done((f32[2,1024]{1,0:T(2,128)S(1)}, f32[2,1024]{1,0:T(2,128)S(1)}, u32[]{:S(2)}, u32[]{:S(2)}) %collective-permute-start.5) | collective-permute-done | bytes 8224 | tf_op jit(solution)/shard_map/ppermute | solution.py:305
  109.9 2.6 %collective-permute-start.6 = (f32[2,1024]{1,0:T(2,128)S(1)}, f32[2,1024]{1,0:T(2,128)S(1)}, u32[]{:S(2)}, u32[]{:S(2)}) collective-permute-start(f32[2,1024]{1,0:T(2,128)S(1)} %add.92.refs_0_), channel_id=1, source_target_pairs={{0,6},{2,4},{4,2},{6,0},{1,7},{3,5},{5,3},{7,1},{8,14},{10,12},{12... | collective-permute-start | bytes 24584 | tf_op jit(solution)/shard_map/ppermute | solution.py:305
  114.3 2.7 %apply.6 = (f32[2,1024]{1,0:T(2,128)S(1)}, f32[2,1024]{1,0:T(2,128)S(1)}) custom-call(bf16[64,2,16,512]{3,2,1,0:T(8,128)(2,1)} %all-to-all-done.y_ref, f32[2,1024]{1,0:T(2,128)S(1)} %get-tuple-element.31.z_ref, f32[2,1024]{1,0:T(2,128)S(1)} %add.92.refs_0_, f32[2,1024]{1,0:T(2,128)S(1)} %collective-permute-done.6.refs_1_), custom_call_target="tpu_custom_call" | custom-call | tf_op jit(solution)/shard_map/apply/pallas_call | solution.py:199
  117.0 2.0 %collective-permute-start.7 = (f32[2,1024]{1,0:T(2,128)S(1)}, f32[2,1024]{1,0:T(2,128)S(1)}, u32[]{:S(2)}, u32[]{:S(2)}) collective-permute-start(f32[2,1024]{1,0:T(2,128)S(1)} %get-tuple-element.34), channel_id=1, source_target_pairs={{0,8},{8,0},{16,24},{24,16},{32,40},{40,32},{48,56},{56,48},{64,72... | collective-permute-start | bytes 24584 | tf_op jit(solution)/shard_map/ppermute | solution.py:305
  119.9 3.2 %collective-permute-done.8 = f32[2,1024]{1,0:T(2,128)S(1)} collective-permute-done((f32[2,1024]{1,0:T(2,128)S(1)}, f32[2,1024]{1,0:T(2,128)S(1)}, u32[]{:S(2)}, u32[]{:S(2)}) %collective-permute-start.8) | collective-permute-done | bytes 8224 | tf_op jit(solution)/shard_map/ppermute | solution.py:305
  123.1 2.5 %collective-permute-start.9 = (f32[2,1024]{1,0:T(2,128)S(1)}, f32[2,1024]{1,0:T(2,128)S(1)}, u32[]{:S(2)}, u32[]{:S(2)}) collective-permute-start(f32[2,1024]{1,0:T(2,128)S(1)} %add.94.refs_0_), channel_id=1, source_target_pairs={{0,6},{2,4},{4,2},{6,0},{1,7},{3,5},{5,3},{7,1},{8,14},{10,12},{12... | collective-permute-start | bytes 24584 | tf_op jit(solution)/shard_map/ppermute | solution.py:305
  125.6 1.9 collective-permute-done.9.refs_1_
  127.6 2.8 %apply.7 = (f32[2,1024]{1,0:T(2,128)S(1)}, f32[2,1024]{1,0:T(2,128)S(1)}) custom-call(bf16[64,2,16,512]{3,2,1,0:T(8,128)(2,1)} %all-to-all-done.y_ref, f32[2,1024]{1,0:T(2,128)S(1)} %get-tuple-element.33.z_ref, f32[2,1024]{1,0:T(2,128)S(1)} %add.94.refs_0_, f32[2,1024]{1,0:T(2,128)S(1)} %collective-permute-done.9.refs_1_), custom_call_target="tpu_custom_call" | custom-call | tf_op jit(solution)/shard_map/apply/pallas_call | solution.py:199
  130.3 1.9 collective-permute-start.10
  132.3 2.2 %constant_dynamic-slice_fusion = (bf16[2,512,256]{2,1,0:T(8,128)(2,1)}, bf16[2,512,256]{2,1,0:T(8,128)(2,1)}) fusion(bf16[2,1024,256]{2,1,0:T(8,128)(2,1)} %reduce-scatter.2.cloned.1.call-done, s32[]{:T(128)S(6)} %select_n.38, s32[]{:T(128)S(6)} %select_n.37), kind=kLoop, calls=%fused_computation.14 | loop fusion | bytes 2097160 | tf_op jit(solution)/shard_map/dynamic_slice | solution.py:374
  134.5 3.1 %collective-permute-start.16 = (bf16[2,512,256]{2,1,0:T(8,128)(2,1)}, bf16[2,512,256]{2,1,0:T(8,128)(2,1)}, u32[]{:S(2)}, u32[]{:S(2)}) collective-permute-start(bf16[2,512,256]{2,1,0:T(8,128)(2,1)} %get-tuple-element.60), channel_id=1, source_target_pairs={{0,0},{1,8},{8,1},{9,9},{16,16},{17,24},{24,17},{25,25},{32,32},{3... | collective-permute-start | bytes 1572872 | tf_op jit(solution)/shard_map/ppermute | solution.py:320
  137.6 2.3 %collective-permute-start.17 = (bf16[2,512,256]{2,1,0:T(8,128)(2,1)}, bf16[2,512,256]{2,1,0:T(8,128)(2,1)S(1)}, u32[]{:S(2)}, u32[]{:S(2)}) collective-permute-start(bf16[2,512,256]{2,1,0:T(8,128)(2,1)} %get-tuple-element.59), channel_id=1, source_target_pairs={{0,1},{1,9},{8,0},{9,8},{16,17},{17,25},{24,16},{25,24},{32,33},{3... | collective-permute-start | bytes 1572872 | tf_op jit(solution)/shard_map/ppermute | solution.py:320
  143.8 2.1 %collective-permute-start.12 = (f32[2,1024]{1,0:T(2,128)S(1)}, f32[2,1024]{1,0:T(2,128)S(1)}, u32[]{:S(2)}, u32[]{:S(2)}) collective-permute-start(f32[2,1024]{1,0:T(2,128)S(1)} %add.96.near_ref), channel_id=1, source_target_pairs={{0,6},{2,4},{4,2},{6,0},{1,7},{3,5},{5,3},{7,1},{8,14},{10,12},{12... | collective-permute-start | bytes 24584 | tf_op jit(solution)/shard_map/ppermute | solution.py:305
  145.9 3.1 %fusion = (f32[256,512]{1,0:T(8,128)}, f32[256,512]{1,0:T(8,128)}) fusion(f32[512]{0:T(512)S(1)} %get-tuple-element.56, f32[256]{0:T(256)S(1)} %bitcast.25, f32[512]{0:T(512)S(1)} %get-tuple-element.55, f32[256]{0:T(256)S(1)} %bitcast.24, f32[]{:T(128)} %bitcast.6), kind=kLoop, calls=%fused_computation.7 | loop fusion | flops 524288 | bytes 1054724 | tf_op jit(solution)/shard_map/sin | solution.py:368
  149.7 6.5 %all-to-all-start.2 = ((f32[8,2,1024]{2,1,0:T(2,128)}), f32[8,2,1024]{2,1,0:T(2,128)S(1)}, u32[]{:S(2)}, u32[]{:S(2)}) async-start(f32[8,2,1024]{2,1,0:T(2,128)} %get-tuple-element.39), calls=%async_computation.2 | async-start | bytes 131072 | tf_op jit(solution)/shard_map/all_to_all | solution.py:393
  156.3 5.1 %collective-permute-start.18 = (f32[2,1024]{1,0:T(2,128)S(1)}, f32[2,1024]{1,0:T(2,128)S(1)}, u32[]{:S(2)}, u32[]{:S(2)}) collective-permute-start(f32[2,1024]{1,0:T(2,128)S(1)} %get-tuple-element.44), channel_id=1, source_target_pairs={{0,0},{1,8},{8,1},{9,9},{16,16},{17,24},{24,17},{25,25},{32,32},{3... | collective-permute-start | bytes 24584 | tf_op jit(solution)/shard_map/ppermute | solution.py:320
  161.5 2.1 %all-to-all-done.2.line_ref = f32[8,2,1024]{2,1,0:T(2,128)S(1)} async-done(((f32[8,2,1024]{2,1,0:T(2,128)}), f32[8,2,1024]{2,1,0:T(2,128)S(1)}, u32[]{:S(2)}, u32[]{:S(2)}) %all-to-all-start.2) | async-done | bytes 65568 | tf_op jit(solution)/shard_map/all_to_all | solution.py:393
  165.9 2.6 %collective-permute-start.14 = (f32[2,1024]{1,0:T(2,128)S(1)}, f32[2,1024]{1,0:T(2,128)S(1)}, u32[]{:S(2)}, u32[]{:S(2)}) collective-permute-start(f32[2,1024]{1,0:T(2,128)S(1)} %get-tuple-element.42), channel_id=1, source_target_pairs={{0,128},{1,129},{8,136},{9,137},{16,144},{17,145},{24,152},{25,153... | collective-permute-start | bytes 24584 | tf_op jit(solution)/shard_map/ppermute | solution.py:305
  169.9 2.3 %collective-permute-done.15.refs_3_ = f32[2,1024]{1,0:T(2,128)S(1)} collective-permute-done((f32[2,1024]{1,0:T(2,128)S(1)}, f32[2,1024]{1,0:T(2,128)S(1)}, u32[]{:S(2)}, u32[]{:S(2)}) %collective-permute-start.15) | collective-permute-done | bytes 8224 | tf_op jit(solution)/shard_map/ppermute | solution.py:305
  175.1 2.0 %beamform.1 = bf16[2,2,2,128,512]{4,3,2,1,0:T(8,128)(2,1)S(1)} custom-call(s32[32]{0:T(128)S(1)} %copy-done.2, s32[32]{0:T(128)S(1)} %copy-done.3, s32[2]{0:T(128)S(1)} %pad_add_fusion.me_ref, f32[2,1024]{1,0:T(2,128)S(1)} %get-tuple-element.48.refs_0_, f32[2,1024]{1,0:T(2,128)S(1)} %collective-permute-done.13.refs_1_, ...), custom_call_target="tpu_custom_call" | custom-call | tf_op jit(solution)/shard_map/beamform/pallas_call | solution.py:293
  177.3 2.3 %add_bitcast_fusion = f32[1,2,512,256]{3,2,1,0:T(8,128)} fusion(bf16[2,512,256]{2,1,0:T(8,128)(2,1)} %copy-done.4, bf16[2,512,256]{2,1,0:T(8,128)(2,1)} %collective-permute-done.16), kind=kLoop, calls=%fused_computation.2 | loop fusion | flops 786432 | bytes 2097152 | tf_op jit(solution)/shard_map/broadcast_in_dim | solution.py:404
  179.5 6.5 %collective-permute-done.19 = bf16[2,2,128,512]{3,2,1,0:T(8,128)(2,1)S(1)} collective-permute-done((bf16[2,2,128,512]{3,2,1,0:T(8,128)(2,1)S(1)}, bf16[2,2,128,512]{3,2,1,0:T(8,128)(2,1)S(1)}, u32[]{:S(2)}, u32[]{:S(2)}) %collective-permute-start.19) | collective-permute-done | bytes 524320 | tf_op jit(solution)/shard_map/ppermute | solution.py:305
  (67 shorter events, 24.2 us)
Async XLA Ops:
  10.3 13.4 %copy-start.8 = (f32[1,2,1024]{2,1,0:T(2,128)S(1)}, f32[1,2,1024]{2,1,0:T(2,128)}, u32[]{:S(2)}) copy-start(f32[1,2,1024]{2,1,0:T(2,128)} %param.9) | copy-start | bytes 24580
  10.3 63.2 %all-to-all-start = ((bf16[64,2,16,512]{3,2,1,0:T(8,128)(2,1)}), bf16[64,2,16,512]{3,2,1,0:T(8,128)(2,1)}, u32[]{:S(2)}, u32[]{:S(2)}) async-start(bf16[64,2,16,512]{3,2,1,0:T(8,128)(2,1)} %bitcast.21), calls=%async_computation | async-start | bytes 4194304 | tf_op jit(solution)/shard_map/all_to_all | solution.py:351
  23.6 108.6 %reduce-scatter.2.cloned.1.call-start = ((), (), s32[]{:S(2)}) async-start(), calls=%async_computation.4 | async-start | bytes 5242880 | tf_op jit(solution)/shard_map/reduce_scatter | solution.py:371
  23.7 6.7 %collective-permute-start = (f32[2,1024]{1,0:T(2,128)S(1)}, f32[2,1024]{1,0:T(2,128)S(1)}, u32[]{:S(2)}, u32[]{:S(2)}) collective-permute-start(f32[2,1024]{1,0:T(2,128)S(1)} %bitcast.26), channel_id=1, source_target_pairs={{0,0},{1,8},{8,1},{9,9},{16,16},{17,24},{24,17},{25,25},{32,32},{3... | collective-permute-start | bytes 24584 | tf_op jit(solution)/shard_map/ppermute | solution.py:320
  82.6 67.2 %all-to-all-start.1 = ((bf16[64,2,16,512]{3,2,1,0:T(8,128)(2,1)}), bf16[64,2,16,512]{3,2,1,0:T(8,128)(2,1)S(1)}, u32[]{:S(2)}, u32[]{:S(2)}) async-start(bf16[64,2,16,512]{3,2,1,0:T(8,128)(2,1)} %bitcast.20), calls=%async_computation.1 | async-start | bytes 4194304 | tf_op jit(solution)/shard_map/all_to_all | solution.py:358
  92.3 1.4 collective-permute-start.1
  93.7 3.0 %collective-permute-start.2 = (f32[2,1024]{1,0:T(2,128)S(1)}, f32[2,1024]{1,0:T(2,128)S(1)}, u32[]{:S(2)}, u32[]{:S(2)}) collective-permute-start(f32[2,1024]{1,0:T(2,128)S(1)} %add.89), channel_id=1, source_target_pairs={{0,2},{2,0},{4,6},{6,4},{1,3},{3,1},{5,7},{7,5},{8,10},{10,8},{12,... | collective-permute-start | bytes 24584 | tf_op jit(solution)/shard_map/ppermute | solution.py:305
  96.8 28.8 %copy-start.7 = (s32[2,256]{1,0:T(2,128)S(1)}, s32[2,256]{1,0:T(2,128)}, u32[]{:S(2)}) copy-start(s32[2,256]{1,0:T(2,128)} %param.13) | copy-start | bytes 6148
  96.8 4.3 %collective-permute-start.3 = (f32[2,1024]{1,0:T(2,128)S(1)}, f32[2,1024]{1,0:T(2,128)S(1)}, u32[]{:S(2)}, u32[]{:S(2)}) collective-permute-start(f32[2,1024]{1,0:T(2,128)S(1)} %add.90.refs_0_), channel_id=1, source_target_pairs={{0,6},{2,4},{4,2},{6,0},{1,7},{3,5},{5,3},{7,1},{8,14},{10,12},{12... | collective-permute-start | bytes 24584 | tf_op jit(solution)/shard_map/ppermute | solution.py:305
  103.9 2.7 %collective-permute-start.4 = (f32[2,1024]{1,0:T(2,128)S(1)}, f32[2,1024]{1,0:T(2,128)S(1)}, u32[]{:S(2)}, u32[]{:S(2)}) collective-permute-start(f32[2,1024]{1,0:T(2,128)S(1)} %get-tuple-element.32), channel_id=1, source_target_pairs={{0,8},{8,0},{16,24},{24,16},{32,40},{40,32},{48,56},{56,48},{64,72... | collective-permute-start | bytes 24584 | tf_op jit(solution)/shard_map/ppermute | solution.py:305
  106.6 3.2 %collective-permute-start.5 = (f32[2,1024]{1,0:T(2,128)S(1)}, f32[2,1024]{1,0:T(2,128)S(1)}, u32[]{:S(2)}, u32[]{:S(2)}) collective-permute-start(f32[2,1024]{1,0:T(2,128)S(1)} %add.91), channel_id=1, source_target_pairs={{0,2},{2,0},{4,6},{6,4},{1,3},{3,1},{5,7},{7,5},{8,10},{10,8},{12,... | collective-permute-start | bytes 24584 | tf_op jit(solution)/shard_map/ppermute | solution.py:305
  109.9 4.4 %collective-permute-start.6 = (f32[2,1024]{1,0:T(2,128)S(1)}, f32[2,1024]{1,0:T(2,128)S(1)}, u32[]{:S(2)}, u32[]{:S(2)}) collective-permute-start(f32[2,1024]{1,0:T(2,128)S(1)} %add.92.refs_0_), channel_id=1, source_target_pairs={{0,6},{2,4},{4,2},{6,0},{1,7},{3,5},{5,3},{7,1},{8,14},{10,12},{12... | collective-permute-start | bytes 24584 | tf_op jit(solution)/shard_map/ppermute | solution.py:305
  117.0 2.8 %collective-permute-start.7 = (f32[2,1024]{1,0:T(2,128)S(1)}, f32[2,1024]{1,0:T(2,128)S(1)}, u32[]{:S(2)}, u32[]{:S(2)}) collective-permute-start(f32[2,1024]{1,0:T(2,128)S(1)} %get-tuple-element.34), channel_id=1, source_target_pairs={{0,8},{8,0},{16,24},{24,16},{32,40},{40,32},{48,56},{56,48},{64,72... | collective-permute-start | bytes 24584 | tf_op jit(solution)/shard_map/ppermute | solution.py:305
  119.9 3.2 %collective-permute-start.8 = (f32[2,1024]{1,0:T(2,128)S(1)}, f32[2,1024]{1,0:T(2,128)S(1)}, u32[]{:S(2)}, u32[]{:S(2)}) collective-permute-start(f32[2,1024]{1,0:T(2,128)S(1)} %add.93), channel_id=1, source_target_pairs={{0,2},{2,0},{4,6},{6,4},{1,3},{3,1},{5,7},{7,5},{8,10},{10,8},{12,... | collective-permute-start | bytes 24584 | tf_op jit(solution)/shard_map/ppermute | solution.py:305
  123.1 4.4 %collective-permute-start.9 = (f32[2,1024]{1,0:T(2,128)S(1)}, f32[2,1024]{1,0:T(2,128)S(1)}, u32[]{:S(2)}, u32[]{:S(2)}) collective-permute-start(f32[2,1024]{1,0:T(2,128)S(1)} %add.94.refs_0_), channel_id=1, source_target_pairs={{0,6},{2,4},{4,2},{6,0},{1,7},{3,5},{5,3},{7,1},{8,14},{10,12},{12... | collective-permute-start | bytes 24584 | tf_op jit(solution)/shard_map/ppermute | solution.py:305
  127.6 12.4 %copy-start.5 = (s32[512]{0:T(512)S(1)}, s32[512]{0:T(512)}, u32[]{:S(2)}) copy-start(s32[512]{0:T(512)} %map_hbm.3) | copy-start | bytes 6148
  127.6 12.4 %copy-start.6 = (f32[2,512]{1,0:T(2,128)S(1)}, f32[2,512]{1,0:T(2,128)}, u32[]{:S(2)}) copy-start(f32[2,512]{1,0:T(2,128)} %param.12) | copy-start | bytes 12292
  127.6 14.0 %copy-start.3 = (s32[32]{0:T(128)S(1)}, s32[32]{0:T(128)}, u32[]{:S(2)}) copy-start(s32[32]{0:T(128)} %beam_ref.3) | copy-start | bytes 388
  130.3 33.2 %copy-start.2 = (s32[32]{0:T(128)S(1)}, s32[32]{0:T(128)}, u32[]{:S(2)}) copy-start(s32[32]{0:T(128)} %corr_ref.3) | copy-start | bytes 388
  130.3 10.8 %collective-permute-start.10 = (f32[2,1024]{1,0:T(2,128)S(1)}, f32[2,1024]{1,0:T(2,128)S(1)}, u32[]{:S(2)}, u32[]{:S(2)}) collective-permute-start(f32[2,1024]{1,0:T(2,128)S(1)} %get-tuple-element.36), channel_id=1, source_target_pairs={{0,8},{8,0},{16,24},{24,16},{32,40},{40,32},{48,56},{56,48},{64,72... | collective-permute-start | bytes 24584 | tf_op jit(solution)/shard_map/ppermute | solution.py:305
  134.5 37.7 %collective-permute-start.16 = (bf16[2,512,256]{2,1,0:T(8,128)(2,1)}, bf16[2,512,256]{2,1,0:T(8,128)(2,1)}, u32[]{:S(2)}, u32[]{:S(2)}) collective-permute-start(bf16[2,512,256]{2,1,0:T(8,128)(2,1)} %get-tuple-element.60), channel_id=1, source_target_pairs={{0,0},{1,8},{8,1},{9,9},{16,16},{17,24},{24,17},{25,25},{32,32},{3... | collective-permute-start | bytes 1572872 | tf_op jit(solution)/shard_map/ppermute | solution.py:320
  137.6 34.5 %collective-permute-start.17 = (bf16[2,512,256]{2,1,0:T(8,128)(2,1)}, bf16[2,512,256]{2,1,0:T(8,128)(2,1)S(1)}, u32[]{:S(2)}, u32[]{:S(2)}) collective-permute-start(bf16[2,512,256]{2,1,0:T(8,128)(2,1)} %get-tuple-element.59), channel_id=1, source_target_pairs={{0,1},{1,9},{8,0},{9,8},{16,17},{17,25},{24,16},{25,24},{32,33},{3... | collective-permute-start | bytes 1572872 | tf_op jit(solution)/shard_map/ppermute | solution.py:320
  141.2 2.6 %collective-permute-start.11 = (f32[2,1024]{1,0:T(2,128)S(1)}, f32[2,1024]{1,0:T(2,128)S(1)}, u32[]{:S(2)}, u32[]{:S(2)}) collective-permute-start(f32[2,1024]{1,0:T(2,128)S(1)} %add.95), channel_id=1, source_target_pairs={{0,2},{2,0},{4,6},{6,4},{1,3},{3,1},{5,7},{7,5},{8,10},{10,8},{12,... | collective-permute-start | bytes 24584 | tf_op jit(solution)/shard_map/ppermute | solution.py:305
  143.8 5.2 %collective-permute-start.12 = (f32[2,1024]{1,0:T(2,128)S(1)}, f32[2,1024]{1,0:T(2,128)S(1)}, u32[]{:S(2)}, u32[]{:S(2)}) collective-permute-start(f32[2,1024]{1,0:T(2,128)S(1)} %add.96.near_ref), channel_id=1, source_target_pairs={{0,6},{2,4},{4,2},{6,0},{1,7},{3,5},{5,3},{7,1},{8,14},{10,12},{12... | collective-permute-start | bytes 24584 | tf_op jit(solution)/shard_map/ppermute | solution.py:305
  149.7 13.9 %all-to-all-start.2 = ((f32[8,2,1024]{2,1,0:T(2,128)}), f32[8,2,1024]{2,1,0:T(2,128)S(1)}, u32[]{:S(2)}, u32[]{:S(2)}) async-start(f32[8,2,1024]{2,1,0:T(2,128)} %get-tuple-element.39), calls=%async_computation.2 | async-start | bytes 131072 | tf_op jit(solution)/shard_map/all_to_all | solution.py:393
  156.3 12.2 %collective-permute-start.18 = (f32[2,1024]{1,0:T(2,128)S(1)}, f32[2,1024]{1,0:T(2,128)S(1)}, u32[]{:S(2)}, u32[]{:S(2)}) collective-permute-start(f32[2,1024]{1,0:T(2,128)S(1)} %get-tuple-element.44), channel_id=1, source_target_pairs={{0,0},{1,8},{8,1},{9,9},{16,16},{17,24},{24,17},{25,25},{32,32},{3... | collective-permute-start | bytes 24584 | tf_op jit(solution)/shard_map/ppermute | solution.py:320
  164.3 4.2 %collective-permute-start.13 = (f32[2,1024]{1,0:T(2,128)S(1)}, f32[2,1024]{1,0:T(2,128)S(1)}, u32[]{:S(2)}, u32[]{:S(2)}) collective-permute-start(f32[2,1024]{1,0:T(2,128)S(1)} %get-tuple-element.41), channel_id=1, source_target_pairs={{0,1},{1,0},{8,9},{9,8},{16,17},{17,16},{24,25},{25,24},{32,33},{3... | collective-permute-start | bytes 24584 | tf_op jit(solution)/shard_map/ppermute | solution.py:305
  165.9 4.0 %collective-permute-start.14 = (f32[2,1024]{1,0:T(2,128)S(1)}, f32[2,1024]{1,0:T(2,128)S(1)}, u32[]{:S(2)}, u32[]{:S(2)}) collective-permute-start(f32[2,1024]{1,0:T(2,128)S(1)} %get-tuple-element.42), channel_id=1, source_target_pairs={{0,128},{1,129},{8,136},{9,137},{16,144},{17,145},{24,152},{25,153... | collective-permute-start | bytes 24584 | tf_op jit(solution)/shard_map/ppermute | solution.py:305
  168.5 3.7 %collective-permute-start.15 = (f32[2,1024]{1,0:T(2,128)S(1)}, f32[2,1024]{1,0:T(2,128)S(1)}, u32[]{:S(2)}, u32[]{:S(2)}) collective-permute-start(f32[2,1024]{1,0:T(2,128)S(1)} %get-tuple-element.43), channel_id=1, source_target_pairs={{0,129},{1,128},{8,137},{9,136},{16,145},{17,144},{24,153},{25,152... | collective-permute-start | bytes 24584 | tf_op jit(solution)/shard_map/ppermute | solution.py:305
  173.0 1.0 copy-start
  174.0 1.0 copy-start.1
  177.2 8.9 %collective-permute-start.19 = (bf16[2,2,128,512]{3,2,1,0:T(8,128)(2,1)S(1)}, bf16[2,2,128,512]{3,2,1,0:T(8,128)(2,1)S(1)}, u32[]{:S(2)}, u32[]{:S(2)}) collective-permute-start(bf16[2,2,128,512]{3,2,1,0:T(8,128)(2,1)S(1)} %dynamic-slice_bitcast_fusion), channel_id=1, source_target_pairs={{0,1},{1,0},{2,3},{3,2},{4,5},{5,4},{6,7},{7,6},{8,9},{9,8},{10,11... | collective-permute-start | bytes 1572872 | tf_op jit(solution)/shard_map/ppermute | solution.py:305
  (1 other events, 0.8 us)
Sparse Core Ops, SparseCore 0:
  82.7 47.7 reduce-scatter.1

commit v3 on v2

--- a/solution.py
+++ b/solution.py
@@ -84,7 +84,7 @@
         store.wait()
 
 
-def ingest(voltages, channels, ingest_map, station_flags, base, groups, pick):
+def ingest(voltages, channels, ingest_map, station_flags, base, groups, pick, grant):
     slots, parts, rows, samples = voltages.shape
     stations = ingest_map.shape[0]
     half = samples // 2
@@ -94,7 +94,7 @@
         functools.partial(ingest_kernel, stations, pick),
         in_specs=[whole(SMEM)] + [whole(pltpu.HBM)] * 4,
         out_specs=whole(pltpu.HBM),
-        out_shape=jax.ShapeDtypeStruct(shape, BF16),
+        out_shape=pltpu.HBM(shape, BF16),
         scratch_shapes=[
             SMEM(channels.shape, jnp.int32),
             SMEM(ingest_map.shape, jnp.int32),
@@ -105,9 +105,15 @@
             pltpu.SemaphoreType.DMA,
             pltpu.SemaphoreType.DMA((steps,)),
         ],
-        compiler_params=params(62),
+        compiler_params=params(grant),
         name="ingest",
-    )(base, channels, ingest_map, station_flags, voltages)
+    )(
+        base,
+        *(
+            pltpu.with_memory_space_constraint(x, pltpu.HBM)
+            for x in (channels, ingest_map, station_flags, voltages)
+        ),
+    )
     return out.reshape(slots * groups, parts, rows, half)
 
 
@@ -120,40 +126,66 @@
     return lax.dot_general(a, b, (((1,), (1,)), ((), ())), preferred_element_type=F32)
 
 
-def correlate_kernel(scale, y_ref, out_ref, left_ref, turn_ref):
-    row, col = pl.program_id(0), pl.program_id(1)
+def correlate_kernel(
+    scale, side_ref, y_ref, near_hbm, far_hbm, left_ref, turn_ref, out_ref, sems
+):
     samples = y_ref.shape[3]
-
-    @pl.when((col == 0) & (row == 0))
-    def _():
-        real, imag = load_part(y_ref, 0), load_part(y_ref, 1)
-        left_ref[:, :samples] = real
-        left_ref[:, samples:] = imag
-        turn_ref[:, :samples] = imag
-        turn_ref[:, samples:] = -real
-
-    height, width = out_ref.shape[1], out_ref.shape[2]
-    rows = pl.ds(pl.multiple_of(row * height, height), height)
-    cols = pl.ds(pl.multiple_of(col * width, width), width)
-    right = left_ref[cols, :]
-    out_ref[0] = (nt_dot(left_ref[rows, :], right) * scale).astype(BF16)
-    out_ref[1] = (nt_dot(turn_ref[rows, :], right) * scale).astype(BF16)
-
-
-def correlate(y, scale):
+    inputs = left_ref.shape[0]
+    blocks = sems.shape[0]
+    tile = inputs // blocks
+    half = blocks // 2
+    real, imag = load_part(y_ref, 0), load_part(y_ref, 1)
+    left_ref[:, :samples] = real
+    left_ref[:, samples:] = imag
+    turn_ref[:, :samples] = imag
+    turn_ref[:, samples:] = -real
+
+    def store(b, target):
+        source = out_ref.at[:, pl.ds(b * tile, tile)]
+        return pltpu.make_async_copy(
+            source, target.at[:, pl.ds(b % half * tile, tile)], sems.at[b]
+        )
+
+    for b in reversed(range(blocks)):
+        height = (b + 1) * tile
+        cols = slice(b * tile, height)
+        right = left_ref[cols, :]
+        real = nt_dot(left_ref[:height, :], right) * scale
+        imag = nt_dot(turn_ref[:height, :], right) * scale
+        out_ref[0, :height, cols] = real.astype(BF16)
+        out_ref[1, :height, cols] = imag.astype(BF16)
+        for a in range(b):
+            rows = slice(a * tile, (a + 1) * tile)
+            out_ref[0, cols, rows] = real[rows].T.astype(BF16)
+            out_ref[1, cols, rows] = (-imag[rows].T).astype(BF16)
+
+        @pl.when(side_ref[0] == b // half)
+        def _():
+            store(b, near_hbm).start()
+
+        @pl.when(side_ref[0] != b // half)
+        def _():
+            store(b, far_hbm).start()
+
+    for b in reversed(range(blocks)):
+        store(b, near_hbm).wait()
+
+
+def correlate(y, side, scale):
     blocks, _, rows, samples = y.shape
     inputs = blocks * rows
-    height, width = inputs // 2, inputs // 4
+    tiles = 4
+    out = pltpu.HBM((2, inputs // 2, inputs), BF16)
     return pl.pallas_call(
         functools.partial(correlate_kernel, scale),
-        grid=(inputs // height, inputs // width),
-        in_specs=[whole(VMEM)],
-        out_specs=pl.BlockSpec((2, height, width), lambda i, j: (0, i, j)),
-        out_shape=jax.ShapeDtypeStruct((2, inputs, inputs), BF16),
-        scratch_shapes=[VMEM((inputs, 2 * samples), BF16)] * 2,
-        compiler_params=params(60),
+        in_specs=[whole(SMEM), whole(VMEM)],
+        out_specs=[whole(pltpu.HBM)] * 2,
+        out_shape=[out] * 2,
+        scratch_shapes=[VMEM((inputs, 2 * samples), BF16)] * 2
+        + [VMEM((2, inputs, inputs), BF16), pltpu.SemaphoreType.DMA((tiles,))],
+        compiler_params=params(28),
         name="correlate",
-    )(y)
+    )(side, y)
 
 
 def in_terms(x):
@@ -257,7 +289,7 @@
 def beam_kernel(
     reach, corr_ref, beam_ref, me_ref, *refs
 ):
-    gain_refs, (cos_ref, sin_ref, y_ref, out_ref) = refs[: len(reach)], refs[len(reach) :]
+    gain_refs, (cos_ref, sin_ref, y_ref, *out_refs) = refs[: len(reach)], refs[len(reach) :]
     slot = find_slot(corr_ref, beam_ref[me_ref[0]])
     half_ring = corr_ref.shape[0] // 2
     far = (slot // half_ring) ^ (me_ref[0] // half_ring)
@@ -268,7 +300,7 @@
         gains = jnp.where(jnp.full(gains.shape, hit) == 1, ref[...], gains)
     blocks, _, rows, samples = y_ref.shape
     stations = blocks // 2 * rows
-    beams = out_ref.shape[3]
+    beams = out_refs[0].shape[2]
     factor = 1.0 / math.sqrt(stations)
     for pol in range(2):
         gain_r = gains[0:1, pol * stations : (pol + 1) * stations]
@@ -277,14 +309,14 @@
         along_r, along_i = gain_r / denom, gain_i / denom
         y_r = y_ref[pol * blocks // 2 : (pol + 1) * blocks // 2, 0].reshape(stations, samples)
         y_i = y_ref[pol * blocks // 2 : (pol + 1) * blocks // 2, 1].reshape(stations, samples)
-        for g in range(out_ref.shape[0]):
-            cosine = cos_ref[g * beams : (g + 1) * beams]
-            sine = sin_ref[g * beams : (g + 1) * beams]
+        for turn, out_ref in enumerate(out_refs):
+            half = pl.ds(pl.multiple_of((me_ref[1] ^ turn) * beams, beams), beams)
+            cosine, sine = cos_ref[half, :], sin_ref[half, :]
             w_r = ((cosine * along_r - sine * along_i) * factor).astype(BF16)
             w_i = (-(cosine * along_i + sine * along_r) * factor).astype(BF16)
             dot = functools.partial(jnp.dot, preferred_element_type=F32)
-            out_ref[g, pol, 0] = (dot(w_r, y_r) - dot(w_i, y_i)).astype(BF16)
-            out_ref[g, pol, 1] = (dot(w_i, y_r) + dot(w_r, y_i)).astype(BF16)
+            out_ref[pol, 0] = (dot(w_r, y_r) - dot(w_i, y_i)).astype(BF16)
+            out_ref[pol, 1] = (dot(w_i, y_r) + dot(w_r, y_i)).astype(BF16)
 
 
 def beamform(reach, corr_channels, beam_channels, me, gains, cosine, sine, y, groups):
@@ -293,9 +325,9 @@
     return pl.pallas_call(
         functools.partial(beam_kernel, reach),
         in_specs=[whole(SMEM)] * 3 + [whole(VMEM)] * (3 + len(reach)),
-        out_specs=whole(VMEM),
-        out_shape=jax.ShapeDtypeStruct((groups, 2, 2, beams, samples), BF16),
-        compiler_params=params(24),
+        out_specs=[whole(VMEM)] * groups,
+        out_shape=[jax.ShapeDtypeStruct((2, 2, beams, samples), BF16)] * groups,
+        compiler_params=params(16),
         name="beamform",
     )(corr_channels, beam_channels, me, *gains, cosine, sine, y)
 
@@ -346,17 +378,13 @@
 
     corr_send = ingest(
         voltages, corr_channels, ingest_map, station_flags, base, n_group,
-        lambda slot, g: (slot // 2 * 2 + g, slot % 2),
+        lambda slot, g: (slot // 2 * 2 + g, slot % 2), 16,
     )
     corr_y = lax.all_to_all(corr_send, WIDE, split_axis=0, concat_axis=0, tiled=True)
     beam_send = ingest(
         voltages, beam_channels, ingest_map, station_flags, base, n_group,
-        lambda slot, g: (slot, g),
-    )
-    z = cross(prior_gains[0], 0)
-    beam_send, corr_y, z = lax.optimization_barrier((beam_send, corr_y, z))
-    beam_y = lax.all_to_all(beam_send, WIDE, split_axis=0, concat_axis=0, tiled=True)
-
+        lambda slot, g: (slot, g), 16,
+    )
     my_beam = lax.dynamic_slice_in_dim(beam_channels, freq_index, 1, 0)[0]
     ratio = 0.875 + 0.25 * (my_beam.astype(F32) + 0.5) / slots
     slot_coords = jnp.take(station_coords, ingest_map, axis=1, mode="clip")
@@ -367,12 +395,16 @@
     )
     cosine, sine = jnp.cos(phase), jnp.sin(phase)
 
-    parts = correlate(corr_y, 1.0 / total)
-    parts = lax.psum_scatter(parts, "tm", scatter_dimension=2, tiled=True)
-    height = inputs // n_group
-    near = lax.dynamic_slice_in_dim(parts, core * height, height, 1)
-    far = lax.dynamic_slice_in_dim(parts, (1 - core) * height, height, 1)
-    near, far = cross(near, 0), cross(far, 1)
+    z = cross(prior_gains[0], 0)
+    beam_send, corr_y, z, cosine, sine = lax.optimization_barrier(
+        (beam_send, corr_y, z, cosine, sine)
+    )
+    beam_y = lax.all_to_all(beam_send, WIDE, split_axis=0, concat_axis=0, tiled=True)
+
+    near, far = (
+        lax.psum_scatter(part, "tm", scatter_dimension=2, tiled=True)
+        for part in correlate(corr_y, core.astype(jnp.int32).reshape(1), 1.0 / total)
+    )
 
     scale = float(inputs) / total
     sums = None
@@ -384,7 +416,8 @@
         sums = exchange(part)
     depth = slots // 4
     z, copies = finish(z, sums, scale, depth)
-    copies, beam_y, cosine, sine = lax.optimization_barrier((copies, beam_y, cosine, sine))
+    copies, beam_y, near, far = lax.optimization_barrier((copies, beam_y, near, far))
+    near, far = cross(near, 0), cross(far, 1)
     line = [
         [high * 2 * depth + 2 * i + c for i in range(depth)]
         for high in range(2)
@@ -400,14 +433,12 @@
         for (high, low), pick in zip(reach[1:], picks[1:])
     ]
     solved = cross(z, 0)
-    gains, near, far, solved = lax.optimization_barrier((gains, near, far, solved))
+    gains, near, far = lax.optimization_barrier((gains, near, far))
     visibilities = (near.astype(F32) + far.astype(F32))[None]
 
-    beams = beamform(
+    own, away = beamform(
         reach, corr_channels, beam_channels, me, gains, cosine, sine, beam_y, n_group
     )
-    own = lax.dynamic_index_in_dim(beams, group_index, 0, keepdims=False)
-    away = lax.dynamic_index_in_dim(beams, 1 - group_index, 0, keepdims=False)
     other = swap(away, "grp", 1)
     first = jnp.where(group_index == 0, own, other)
     second = jnp.where(group_index == 0, other, own)

time: 198 us -> 200 us (1.010); the launches traced: 195 us -> 199 us
  waiting for transfers between devices: 72.9 us -> 93.8 us
  Pallas kernels: 29.5 us -> 19.2 us
  local copies, waits for them, and re-layouts: 7.87 us -> 3.52 us
    ppermute x4, waiting for transfers between devices: 0.01 us -> 8.31 us  [cross(): return lax.ppermute(x, WIDE, pairs)]
    reduce_scatter x1 -> x2, waiting for transfers between devices: 0.01 us -> 7.47 us  [body(): lax.psum_scatter(part, 'tm', scatter_dimension=2, tiled=True)]
    pallas_call x4, Pallas kernels: 10.8 us -> 4.36 us  [apply_visibilities(): pl.pallas_call(functools.partial(apply_kernel, scale, first), in_specs=[w...]
    all_to_all x1, waiting for transfers between devices: 0.01 us -> 5.9 us  [body(): lax.all_to_all(beam_send, WIDE, split_axis=0, concat_axis=0, tiled=True)]
    all_to_all x1, waiting for transfers between devices: 2.11 us -> 7.16 us  [body(): lax.all_to_all(copies, 'freq', split_axis=0, concat_axis=0, axis_index_gr...]
    pallas_call x1, Pallas kernels: 9.02 us -> 4.2 us  [correlate(): pl.pallas_call(functools.partial(correlate_kernel, scale), in_specs=[whol...]
    all_to_all x1, waiting for transfers between devices: 43.1 us -> 38.5 us  [body(): lax.all_to_all(corr_send, WIDE, split_axis=0, concat_axis=0, tiled=True)]
    dynamic_slice x1 -> x0, local copies, waits for them, and re-layouts: 2.23 us -> none  [body(): far = lax.dynamic_slice_in_dim(parts, (1 - core) * height, height, 1)]
  transfers between devices with their start and end apart: 24 -> 25, of which waited for: 15 -> 19; matrix products, arithmetic and copies ran while one was open for 5% -> 3% of each run, Pallas kernels for 8% -> 4%
where the time goes in v3:
time: 200 us; the launch traced here: 199 us
  waiting for transfers between devices  93.8 us (47%)
  starting transfers between devices  62 us (31%)
  Pallas kernels  19.2 us (10%)
  between operations  14.9 us (7%)
  other arithmetic  5.63 us (3%)
  local copies, waits for them, and re-layouts  3.52 us (2%)
    all_to_all x1, waiting for transfers between devices, body(): lax.all_to_all(corr_send, WIDE, split_axis=0, concat_axis=0, tiled=True)  38.5 us
    ppermute x16, waiting for transfers between devices, swap(): return lax.ppermute(x, axis, [(i, i ^ mask) for i in range(n)])  25.7 us
    ppermute x16, starting transfers between devices, swap(): return lax.ppermute(x, axis, [(i, i ^ mask) for i in range(n)])  21.6 us
    all_to_all x1, starting transfers between devices, body(): lax.all_to_all(corr_send, WIDE, split_axis=0, concat_axis=0, tiled=True)  13.3 us
    ppermute x4, starting transfers between devices, cross(): return lax.ppermute(x, WIDE, pairs)  12.9 us
    ppermute x4, waiting for transfers between devices, cross(): return lax.ppermute(x, WIDE, pairs)  8.31 us
    reduce_scatter x2, waiting for transfers between devices, body(): lax.psum_scatter(part, 'tm', scatter_dimension=2, tiled=True)  7.47 us
    all_to_all x1, starting transfers between devices, body(): lax.all_to_all(beam_send, WIDE, split_axis=0, concat_axis=0, tiled=True)  7.4 us
  transfers between devices with their start and end apart: 25, of which 19 were waited for; matrix products, arithmetic and copies ran while one was open for 3% of the time, Pallas kernels for 4%

profile of v3, /device:TPU:1, one launch (start us, length us, event | category | flops | bytes accessed | tf_op | source)
XLA Modules:
  0.0 199.1 jit_solution(6954450149618605457)
XLA Ops:
  7.2 3.1 %ingest.3 = bf16[32,2,2,16,512]{4,3,2,1,0:T(8,128)(2,1)} custom-call(s32[1]{0:T(128)} %bitcast.2.base_ref, s32[32]{0:T(128)} %corr_ref.3, s32[512]{0:T(512)} %map_hbm.3, s32[512]{0:T(512)} %flag_hbm.3, bf16[32,2,16,1024]{3,2,1,0:T(8,128)(2,1)} %volts_hbm.3), custom_call_target="tpu_custom_call" | custom-call | tf_op jit(solution)/shard_map/ingest/pallas_call | solution.py:93
  10.3 13.3 %all-to-all-start = ((bf16[64,2,16,512]{3,2,1,0:T(8,128)(2,1)}), bf16[64,2,16,512]{3,2,1,0:T(8,128)(2,1)S(1)}, u32[]{:S(2)}, u32[]{:S(2)}) async-start(bf16[64,2,16,512]{3,2,1,0:T(8,128)(2,1)} %bitcast.17), calls=%async_computation | async-start | bytes 4194304 | tf_op jit(solution)/shard_map/all_to_all | solution.py:383
  23.7 3.5 %collective-permute-start = (f32[2,1024]{1,0:T(2,128)S(1)}, f32[2,1024]{1,0:T(2,128)S(1)}, u32[]{:S(2)}, u32[]{:S(2)}) collective-permute-start(f32[2,1024]{1,0:T(2,128)S(1)} %bitcast.22), channel_id=1, source_target_pairs={{0,0},{1,8},{8,1},{9,9},{16,16},{17,24},{24,17},{25,25},{32,32},{3... | collective-permute-start | bytes 24584 | tf_op jit(solution)/shard_map/ppermute | solution.py:352
  30.0 2.0 fusion
  32.0 3.1 %ingest.2 = bf16[32,2,2,16,512]{4,3,2,1,0:T(8,128)(2,1)} custom-call(s32[1]{0:T(128)} %bitcast.2.base_ref, s32[32]{0:T(128)} %beam_ref.3, s32[512]{0:T(512)} %map_hbm.3, s32[512]{0:T(512)} %flag_hbm.3, bf16[32,2,16,1024]{3,2,1,0:T(8,128)(2,1)} %volts_hbm.3), custom_call_target="tpu_custom_call" | custom-call | tf_op jit(solution)/shard_map/ingest/pallas_call | solution.py:93
  35.0 38.5 %all-to-all-done.y_ref = bf16[64,2,16,512]{3,2,1,0:T(8,128)(2,1)S(1)} async-done(((bf16[64,2,16,512]{3,2,1,0:T(8,128)(2,1)}), bf16[64,2,16,512]{3,2,1,0:T(8,128)(2,1)S(1)}, u32[]{:S(2)}, u32[]{:S(2)}) %all-to-all-start) | async-done | bytes 2097184 | tf_op jit(solution)/shard_map/all_to_all | solution.py:383
  73.6 4.2 %correlate.1 = (bf16[2,512,1024]{2,1,0:T(8,128)(2,1)}, bf16[2,512,1024]{2,1,0:T(8,128)(2,1)}) custom-call(s32[1]{0:T(128)} %bitcast.10.side_ref, bf16[64,2,16,512]{3,2,1,0:T(8,128)(2,1)S(1)} %all-to-all-done.y_ref), custom_call_target="tpu_custom_call" | custom-call | tf_op jit(solution)/shard_map/correlate/pallas_call | solution.py:179
  78.6 7.4 %all-to-all-start.1 = ((bf16[64,2,16,512]{3,2,1,0:T(8,128)(2,1)}), bf16[64,2,16,512]{3,2,1,0:T(8,128)(2,1)}, u32[]{:S(2)}, u32[]{:S(2)}) async-start(bf16[64,2,16,512]{3,2,1,0:T(8,128)(2,1)} %bitcast.16), calls=%async_computation.1 | async-start | bytes 4194304 | tf_op jit(solution)/shard_map/all_to_all | solution.py:402
  89.6 1.8 collective-permute-done.2
  91.5 2.5 %collective-permute-start.3 = (f32[2,1024]{1,0:T(2,128)S(1)}, f32[2,1024]{1,0:T(2,128)S(1)}, u32[]{:S(2)}, u32[]{:S(2)}) collective-permute-start(f32[2,1024]{1,0:T(2,128)S(1)} %add.83.refs_0_), channel_id=1, source_target_pairs={{0,6},{2,4},{4,2},{6,0},{1,7},{3,5},{5,3},{7,1},{8,14},{10,12},{12... | collective-permute-start | bytes 24584 | tf_op jit(solution)/shard_map/ppermute | solution.py:337
  96.9 2.1 %collective-permute-start.4 = (f32[2,1024]{1,0:T(2,128)S(1)}, f32[2,1024]{1,0:T(2,128)S(1)}, u32[]{:S(2)}, u32[]{:S(2)}) collective-permute-start(f32[2,1024]{1,0:T(2,128)S(1)} %get-tuple-element.37), channel_id=1, source_target_pairs={{0,8},{8,0},{16,24},{24,16},{32,40},{40,32},{48,56},{56,48},{64,72... | collective-permute-start | bytes 24584 | tf_op jit(solution)/shard_map/ppermute | solution.py:337
  99.8 3.2 %collective-permute-done.5 = f32[2,1024]{1,0:T(2,128)S(1)} collective-permute-done((f32[2,1024]{1,0:T(2,128)S(1)}, f32[2,1024]{1,0:T(2,128)S(1)}, u32[]{:S(2)}, u32[]{:S(2)}) %collective-permute-start.5) | collective-permute-done | bytes 8224 | tf_op jit(solution)/shard_map/ppermute | solution.py:337
  103.1 2.2 %collective-permute-start.6 = (f32[2,1024]{1,0:T(2,128)S(1)}, f32[2,1024]{1,0:T(2,128)S(1)}, u32[]{:S(2)}, u32[]{:S(2)}) collective-permute-start(f32[2,1024]{1,0:T(2,128)S(1)} %add.85.refs_0_), channel_id=1, source_target_pairs={{0,6},{2,4},{4,2},{6,0},{1,7},{3,5},{5,3},{7,1},{8,14},{10,12},{12... | collective-permute-start | bytes 24584 | tf_op jit(solution)/shard_map/ppermute | solution.py:337
  105.3 2.1 %collective-permute-done.6.refs_1_ = f32[2,1024]{1,0:T(2,128)S(1)} collective-permute-done((f32[2,1024]{1,0:T(2,128)S(1)}, f32[2,1024]{1,0:T(2,128)S(1)}, u32[]{:S(2)}, u32[]{:S(2)}) %collective-permute-start.6) | collective-permute-done | bytes 8224 | tf_op jit(solution)/shard_map/ppermute | solution.py:337
  111.1 2.9 %collective-permute-done.8 = f32[2,1024]{1,0:T(2,128)S(1)} collective-permute-done((f32[2,1024]{1,0:T(2,128)S(1)}, f32[2,1024]{1,0:T(2,128)S(1)}, u32[]{:S(2)}, u32[]{:S(2)}) %collective-permute-start.8) | collective-permute-done | bytes 8224 | tf_op jit(solution)/shard_map/ppermute | solution.py:337
  114.0 2.2 %collective-permute-start.9 = (f32[2,1024]{1,0:T(2,128)S(1)}, f32[2,1024]{1,0:T(2,128)S(1)}, u32[]{:S(2)}, u32[]{:S(2)}) collective-permute-start(f32[2,1024]{1,0:T(2,128)S(1)} %add.87.refs_0_), channel_id=1, source_target_pairs={{0,6},{2,4},{4,2},{6,0},{1,7},{3,5},{5,3},{7,1},{8,14},{10,12},{12... | collective-permute-start | bytes 24584 | tf_op jit(solution)/shard_map/ppermute | solution.py:337
  116.2 1.9 collective-permute-done.9.refs_1_
  119.2 1.9 collective-permute-start.10
  122.0 2.9 %collective-permute-done.11 = f32[2,1024]{1,0:T(2,128)S(1)} collective-permute-done((f32[2,1024]{1,0:T(2,128)S(1)}, f32[2,1024]{1,0:T(2,128)S(1)}, u32[]{:S(2)}, u32[]{:S(2)}) %collective-permute-start.11) | collective-permute-done | bytes 8224 | tf_op jit(solution)/shard_map/ppermute | solution.py:337
  124.9 2.2 %collective-permute-start.12 = (f32[2,1024]{1,0:T(2,128)S(1)}, f32[2,1024]{1,0:T(2,128)S(1)}, u32[]{:S(2)}, u32[]{:S(2)}) collective-permute-start(f32[2,1024]{1,0:T(2,128)S(1)} %add.89.near_ref), channel_id=1, source_target_pairs={{0,6},{2,4},{4,2},{6,0},{1,7},{3,5},{5,3},{7,1},{8,14},{10,12},{12... | collective-permute-start | bytes 24584 | tf_op jit(solution)/shard_map/ppermute | solution.py:337
  127.2 2.0 %collective-permute-done.12.far_ref = f32[2,1024]{1,0:T(2,128)S(1)} collective-permute-done((f32[2,1024]{1,0:T(2,128)S(1)}, f32[2,1024]{1,0:T(2,128)S(1)}, u32[]{:S(2)}, u32[]{:S(2)}) %collective-permute-start.12) | collective-permute-done | bytes 8224 | tf_op jit(solution)/shard_map/ppermute | solution.py:337
  130.0 5.9 %all-to-all-done.1.refs_6_ = bf16[64,2,16,512]{3,2,1,0:T(8,128)(2,1)} async-done(((bf16[64,2,16,512]{3,2,1,0:T(8,128)(2,1)}), bf16[64,2,16,512]{3,2,1,0:T(8,128)(2,1)}, u32[]{:S(2)}, u32[]{:S(2)}) %all-to-all-start.1) | async-done | bytes 2097184 | tf_op jit(solution)/shard_map/all_to_all | solution.py:402
  135.9 7.5 %reduce-scatter.5.cloned.1.call-done = bf16[2,512,256]{2,1,0:T(8,128)(2,1)} async-done(((bf16[2,512,1024]{2,1,0:T(8,128)(2,1)}), bf16[2,512,256]{2,1,0:T(8,128)(2,1)}) %reduce-scatter.5.cloned.1.call-update) | async-done | bytes 524304 | tf_op jit(solution)/shard_map/reduce_scatter | solution.py:405
  143.3 3.6 %collective-permute-start.16 = (bf16[2,512,256]{2,1,0:T(8,128)(2,1)}, bf16[2,512,256]{2,1,0:T(8,128)(2,1)S(1)}, u32[]{:S(2)}, u32[]{:S(2)}) collective-permute-start(bf16[2,512,256]{2,1,0:T(8,128)(2,1)} %reduce-scatter.3.cloned.1.call-done), channel_id=1, source_target_pairs={{0,0},{1,8},{8,1},{9,9},{16,16},{17,24},{24,17},{25,25},{32,32},{3... | collective-permute-start | bytes 1572872 | tf_op jit(solution)/shard_map/ppermute | solution.py:352
  147.1 6.7 %all-to-all-start.2 = ((f32[8,2,1024]{2,1,0:T(2,128)}), f32[8,2,1024]{2,1,0:T(2,128)S(1)}, u32[]{:S(2)}, u32[]{:S(2)}) async-start(f32[8,2,1024]{2,1,0:T(2,128)} %get-tuple-element.46), calls=%async_computation.4 | async-start | bytes 131072 | tf_op jit(solution)/shard_map/all_to_all | solution.py:426
  153.9 7.2 %all-to-all-done.2.line_ref = f32[8,2,1024]{2,1,0:T(2,128)S(1)} async-done(((f32[8,2,1024]{2,1,0:T(2,128)}), f32[8,2,1024]{2,1,0:T(2,128)S(1)}, u32[]{:S(2)}, u32[]{:S(2)}) %all-to-all-start.2) | async-done | bytes 65568 | tf_op jit(solution)/shard_map/all_to_all | solution.py:426
  163.4 3.0 %collective-permute-start.14 = (f32[2,1024]{1,0:T(2,128)S(1)}, f32[2,1024]{1,0:T(2,128)S(1)}, u32[]{:S(2)}, u32[]{:S(2)}) collective-permute-start(f32[2,1024]{1,0:T(2,128)S(1)} %get-tuple-element.49), channel_id=1, source_target_pairs={{0,128},{1,129},{8,136},{9,137},{16,144},{17,145},{24,152},{25,153... | collective-permute-start | bytes 24584 | tf_op jit(solution)/shard_map/ppermute | solution.py:337
  167.5 2.6 %collective-permute-done.15.refs_3_ = f32[2,1024]{1,0:T(2,128)S(1)} collective-permute-done((f32[2,1024]{1,0:T(2,128)S(1)}, f32[2,1024]{1,0:T(2,128)S(1)}, u32[]{:S(2)}, u32[]{:S(2)}) %collective-permute-start.15) | collective-permute-done | bytes 8224 | tf_op jit(solution)/shard_map/ppermute | solution.py:337
  170.9 3.1 %beamform.1 = (bf16[2,2,128,512]{3,2,1,0:T(8,128)(2,1)S(1)}, bf16[2,2,128,512]{3,2,1,0:T(8,128)(2,1)S(1)}) custom-call(s32[32]{0:T(128)S(1)} %copy-done, s32[32]{0:T(128)S(1)} %copy-done.2, s32[2]{0:T(128)S(1)} %pad_add_fusion.me_ref, f32[2,1024]{1,0:T(2,128)S(1)} %get-tuple-element.56.refs_0_, f32[2,1024]{1,0:T(2,128)S(1)} %collective-permute-done.13.refs_1_, ...), custom_call_target="tpu_custom_call" | custom-call | tf_op jit(solution)/shard_map/beamform/pallas_call | solution.py:325
  174.2 5.6 %collective-permute-start.18 = (f32[2,1024]{1,0:T(2,128)S(1)}, f32[2,1024]{1,0:T(2,128)S(1)}, u32[]{:S(2)}, u32[]{:S(2)}) collective-permute-start(f32[2,1024]{1,0:T(2,128)S(1)} %get-tuple-element.55), channel_id=1, source_target_pairs={{0,0},{1,8},{8,1},{9,9},{16,16},{17,24},{24,17},{25,25},{32,32},{3... | collective-permute-start | bytes 24584 | tf_op jit(solution)/shard_map/ppermute | solution.py:352
  179.8 8.3 %collective-permute-done.18 = f32[2,1024]{1,0:T(2,128)S(1)} collective-permute-done((f32[2,1024]{1,0:T(2,128)S(1)}, f32[2,1024]{1,0:T(2,128)S(1)}, u32[]{:S(2)}, u32[]{:S(2)}) %collective-permute-start.18) | collective-permute-done | bytes 8224 | tf_op jit(solution)/shard_map/ppermute | solution.py:352
  188.1 2.3 %add_bitcast_fusion = f32[1,2,512,256]{3,2,1,0:T(8,128)} fusion(bf16[2,512,256]{2,1,0:T(8,128)(2,1)} %copy-done.4, bf16[2,512,256]{2,1,0:T(8,128)(2,1)} %copy-done.3), kind=kLoop, calls=%fused_computation.2 | loop fusion | flops 786432 | bytes 2097152 | tf_op jit(solution)/shard_map/broadcast_in_dim | solution.py:437
  (68 shorter events, 23.1 us)
Async XLA Ops:
  10.3 13.4 %copy-start.8 = (f32[1,2,1024]{2,1,0:T(2,128)S(1)}, f32[1,2,1024]{2,1,0:T(2,128)}, u32[]{:S(2)}) copy-start(f32[1,2,1024]{2,1,0:T(2,128)} %param.9) | copy-start | bytes 24580
  10.3 17.0 %copy-start.1 = (s32[32]{0:T(128)S(1)}, s32[32]{0:T(128)}, u32[]{:S(2)}) copy-start(s32[32]{0:T(128)} %beam_ref.3) | copy-start | bytes 388
  10.3 18.1 %copy-start.6 = (f32[2,512]{1,0:T(2,128)S(1)}, f32[2,512]{1,0:T(2,128)}, u32[]{:S(2)}) copy-start(f32[2,512]{1,0:T(2,128)} %param.12) | copy-start | bytes 12292
  10.3 18.3 %copy-start.5 = (s32[512]{0:T(512)S(1)}, s32[512]{0:T(512)}, u32[]{:S(2)}) copy-start(s32[512]{0:T(512)} %map_hbm.3) | copy-start | bytes 6148
  10.3 19.7 %copy-start.7 = (s32[2,256]{1,0:T(2,128)S(1)}, s32[2,256]{1,0:T(2,128)}, u32[]{:S(2)}) copy-start(s32[2,256]{1,0:T(2,128)} %param.13) | copy-start | bytes 6148
  10.3 63.3 %all-to-all-start = ((bf16[64,2,16,512]{3,2,1,0:T(8,128)(2,1)}), bf16[64,2,16,512]{3,2,1,0:T(8,128)(2,1)S(1)}, u32[]{:S(2)}, u32[]{:S(2)}) async-start(bf16[64,2,16,512]{3,2,1,0:T(8,128)(2,1)} %bitcast.17), calls=%async_computation | async-start | bytes 4194304 | tf_op jit(solution)/shard_map/all_to_all | solution.py:383
  23.6 112.2 %reduce-scatter.3.cloned.1.call-start = ((), (), s32[]{:S(2)}) async-start(), calls=%async_computation.5 | async-start | bytes 2621440 | tf_op jit(solution)/shard_map/reduce_scatter | solution.py:405
  23.7 11.4 %collective-permute-start = (f32[2,1024]{1,0:T(2,128)S(1)}, f32[2,1024]{1,0:T(2,128)S(1)}, u32[]{:S(2)}, u32[]{:S(2)}) collective-permute-start(f32[2,1024]{1,0:T(2,128)S(1)} %bitcast.22), channel_id=1, source_target_pairs={{0,0},{1,8},{8,1},{9,9},{16,16},{17,24},{24,17},{25,25},{32,32},{3... | collective-permute-start | bytes 24584 | tf_op jit(solution)/shard_map/ppermute | solution.py:352
  77.8 65.5 %reduce-scatter.5.cloned.1.call-start = ((), (), s32[]{:S(2)}) async-start(), calls=%async_computation.6 | async-start | bytes 2621440 | tf_op jit(solution)/shard_map/reduce_scatter | solution.py:405
  78.6 57.3 %all-to-all-start.1 = ((bf16[64,2,16,512]{3,2,1,0:T(8,128)(2,1)}), bf16[64,2,16,512]{3,2,1,0:T(8,128)(2,1)}, u32[]{:S(2)}, u32[]{:S(2)}) async-start(bf16[64,2,16,512]{3,2,1,0:T(8,128)(2,1)} %bitcast.16), calls=%async_computation.1 | async-start | bytes 4194304 | tf_op jit(solution)/shard_map/all_to_all | solution.py:402
  87.0 1.4 collective-permute-start.1
  88.4 3.0 %collective-permute-start.2 = (f32[2,1024]{1,0:T(2,128)S(1)}, f32[2,1024]{1,0:T(2,128)S(1)}, u32[]{:S(2)}, u32[]{:S(2)}) collective-permute-start(f32[2,1024]{1,0:T(2,128)S(1)} %add.82), channel_id=1, source_target_pairs={{0,2},{2,0},{4,6},{6,4},{1,3},{3,1},{5,7},{7,5},{8,10},{10,8},{12,... | collective-permute-start | bytes 24584 | tf_op jit(solution)/shard_map/ppermute | solution.py:337
  91.5 4.3 %collective-permute-start.3 = (f32[2,1024]{1,0:T(2,128)S(1)}, f32[2,1024]{1,0:T(2,128)S(1)}, u32[]{:S(2)}, u32[]{:S(2)}) collective-permute-start(f32[2,1024]{1,0:T(2,128)S(1)} %add.83.refs_0_), channel_id=1, source_target_pairs={{0,6},{2,4},{4,2},{6,0},{1,7},{3,5},{5,3},{7,1},{8,14},{10,12},{12... | collective-permute-start | bytes 24584 | tf_op jit(solution)/shard_map/ppermute | solution.py:337
  96.9 3.0 %collective-permute-start.4 = (f32[2,1024]{1,0:T(2,128)S(1)}, f32[2,1024]{1,0:T(2,128)S(1)}, u32[]{:S(2)}, u32[]{:S(2)}) collective-permute-start(f32[2,1024]{1,0:T(2,128)S(1)} %get-tuple-element.37), channel_id=1, source_target_pairs={{0,8},{8,0},{16,24},{24,16},{32,40},{40,32},{48,56},{56,48},{64,72... | collective-permute-start | bytes 24584 | tf_op jit(solution)/shard_map/ppermute | solution.py:337
  99.8 3.2 %collective-permute-start.5 = (f32[2,1024]{1,0:T(2,128)S(1)}, f32[2,1024]{1,0:T(2,128)S(1)}, u32[]{:S(2)}, u32[]{:S(2)}) collective-permute-start(f32[2,1024]{1,0:T(2,128)S(1)} %add.84), channel_id=1, source_target_pairs={{0,2},{2,0},{4,6},{6,4},{1,3},{3,1},{5,7},{7,5},{8,10},{10,8},{12,... | collective-permute-start | bytes 24584 | tf_op jit(solution)/shard_map/ppermute | solution.py:337
  103.1 4.4 %collective-permute-start.6 = (f32[2,1024]{1,0:T(2,128)S(1)}, f32[2,1024]{1,0:T(2,128)S(1)}, u32[]{:S(2)}, u32[]{:S(2)}) collective-permute-start(f32[2,1024]{1,0:T(2,128)S(1)} %add.85.refs_0_), channel_id=1, source_target_pairs={{0,6},{2,4},{4,2},{6,0},{1,7},{3,5},{5,3},{7,1},{8,14},{10,12},{12... | collective-permute-start | bytes 24584 | tf_op jit(solution)/shard_map/ppermute | solution.py:337
  107.4 53.6 %copy-start = (s32[32]{0:T(128)S(1)}, s32[32]{0:T(128)}, u32[]{:S(2)}) copy-start(s32[32]{0:T(128)} %corr_ref.3) | copy-start | bytes 388
  107.4 53.6 %copy-start.2 = (s32[32]{0:T(128)S(1)}, s32[32]{0:T(128)}, u32[]{:S(2)}) copy-start(s32[32]{0:T(128)} %beam_ref.3) | copy-start | bytes 388
  108.6 2.5 %collective-permute-start.7 = (f32[2,1024]{1,0:T(2,128)S(1)}, f32[2,1024]{1,0:T(2,128)S(1)}, u32[]{:S(2)}, u32[]{:S(2)}) collective-permute-start(f32[2,1024]{1,0:T(2,128)S(1)} %get-tuple-element.39), channel_id=1, source_target_pairs={{0,8},{8,0},{16,24},{24,16},{32,40},{40,32},{48,56},{56,48},{64,72... | collective-permute-start | bytes 24584 | tf_op jit(solution)/shard_map/ppermute | solution.py:337
  111.1 2.9 %collective-permute-start.8 = (f32[2,1024]{1,0:T(2,128)S(1)}, f32[2,1024]{1,0:T(2,128)S(1)}, u32[]{:S(2)}, u32[]{:S(2)}) collective-permute-start(f32[2,1024]{1,0:T(2,128)S(1)} %add.86), channel_id=1, source_target_pairs={{0,2},{2,0},{4,6},{6,4},{1,3},{3,1},{5,7},{7,5},{8,10},{10,8},{12,... | collective-permute-start | bytes 24584 | tf_op jit(solution)/shard_map/ppermute | solution.py:337
  114.0 4.1 %collective-permute-start.9 = (f32[2,1024]{1,0:T(2,128)S(1)}, f32[2,1024]{1,0:T(2,128)S(1)}, u32[]{:S(2)}, u32[]{:S(2)}) collective-permute-start(f32[2,1024]{1,0:T(2,128)S(1)} %add.87.refs_0_), channel_id=1, source_target_pairs={{0,6},{2,4},{4,2},{6,0},{1,7},{3,5},{5,3},{7,1},{8,14},{10,12},{12... | collective-permute-start | bytes 24584 | tf_op jit(solution)/shard_map/ppermute | solution.py:337
  119.2 2.8 %collective-permute-start.10 = (f32[2,1024]{1,0:T(2,128)S(1)}, f32[2,1024]{1,0:T(2,128)S(1)}, u32[]{:S(2)}, u32[]{:S(2)}) collective-permute-start(f32[2,1024]{1,0:T(2,128)S(1)} %get-tuple-element.41), channel_id=1, source_target_pairs={{0,8},{8,0},{16,24},{24,16},{32,40},{40,32},{48,56},{56,48},{64,72... | collective-permute-start | bytes 24584 | tf_op jit(solution)/shard_map/ppermute | solution.py:337
  122.0 2.9 %collective-permute-start.11 = (f32[2,1024]{1,0:T(2,128)S(1)}, f32[2,1024]{1,0:T(2,128)S(1)}, u32[]{:S(2)}, u32[]{:S(2)}) collective-permute-start(f32[2,1024]{1,0:T(2,128)S(1)} %add.88), channel_id=1, source_target_pairs={{0,2},{2,0},{4,6},{6,4},{1,3},{3,1},{5,7},{7,5},{8,10},{10,8},{12,... | collective-permute-start | bytes 24584 | tf_op jit(solution)/shard_map/ppermute | solution.py:337
  124.9 4.3 %collective-permute-start.12 = (f32[2,1024]{1,0:T(2,128)S(1)}, f32[2,1024]{1,0:T(2,128)S(1)}, u32[]{:S(2)}, u32[]{:S(2)}) collective-permute-start(f32[2,1024]{1,0:T(2,128)S(1)} %add.89.near_ref), channel_id=1, source_target_pairs={{0,6},{2,4},{4,2},{6,0},{1,7},{3,5},{5,3},{7,1},{8,14},{10,12},{12... | collective-permute-start | bytes 24584 | tf_op jit(solution)/shard_map/ppermute | solution.py:337
  143.3 26.8 %collective-permute-start.16 = (bf16[2,512,256]{2,1,0:T(8,128)(2,1)}, bf16[2,512,256]{2,1,0:T(8,128)(2,1)S(1)}, u32[]{:S(2)}, u32[]{:S(2)}) collective-permute-start(bf16[2,512,256]{2,1,0:T(8,128)(2,1)} %reduce-scatter.3.cloned.1.call-done), channel_id=1, source_target_pairs={{0,0},{1,8},{8,1},{9,9},{16,16},{17,24},{24,17},{25,25},{32,32},{3... | collective-permute-start | bytes 1572872 | tf_op jit(solution)/shard_map/ppermute | solution.py:352
  147.0 23.2 %collective-permute-start.17 = (bf16[2,512,256]{2,1,0:T(8,128)(2,1)}, bf16[2,512,256]{2,1,0:T(8,128)(2,1)S(1)}, u32[]{:S(2)}, u32[]{:S(2)}) collective-permute-start(bf16[2,512,256]{2,1,0:T(8,128)(2,1)} %reduce-scatter.5.cloned.1.call-done), channel_id=1, source_target_pairs={{0,1},{1,9},{8,0},{9,8},{16,17},{17,25},{24,16},{25,24},{32,33},{3... | collective-permute-start | bytes 1572872 | tf_op jit(solution)/shard_map/ppermute | solution.py:352
  147.1 14.0 %all-to-all-start.2 = ((f32[8,2,1024]{2,1,0:T(2,128)}), f32[8,2,1024]{2,1,0:T(2,128)S(1)}, u32[]{:S(2)}, u32[]{:S(2)}) async-start(f32[8,2,1024]{2,1,0:T(2,128)} %get-tuple-element.46), calls=%async_computation.4 | async-start | bytes 131072 | tf_op jit(solution)/shard_map/all_to_all | solution.py:426
  161.7 4.7 %collective-permute-start.13 = (f32[2,1024]{1,0:T(2,128)S(1)}, f32[2,1024]{1,0:T(2,128)S(1)}, u32[]{:S(2)}, u32[]{:S(2)}) collective-permute-start(f32[2,1024]{1,0:T(2,128)S(1)} %get-tuple-element.48), channel_id=1, source_target_pairs={{0,1},{1,0},{8,9},{9,8},{16,17},{17,16},{24,25},{25,24},{32,33},{3... | collective-permute-start | bytes 24584 | tf_op jit(solution)/shard_map/ppermute | solution.py:337
  163.4 4.1 %collective-permute-start.14 = (f32[2,1024]{1,0:T(2,128)S(1)}, f32[2,1024]{1,0:T(2,128)S(1)}, u32[]{:S(2)}, u32[]{:S(2)}) collective-permute-start(f32[2,1024]{1,0:T(2,128)S(1)} %get-tuple-element.49), channel_id=1, source_target_pairs={{0,128},{1,129},{8,136},{9,137},{16,144},{17,145},{24,152},{25,153... | collective-permute-start | bytes 24584 | tf_op jit(solution)/shard_map/ppermute | solution.py:337
  166.4 3.7 %collective-permute-start.15 = (f32[2,1024]{1,0:T(2,128)S(1)}, f32[2,1024]{1,0:T(2,128)S(1)}, u32[]{:S(2)}, u32[]{:S(2)}) collective-permute-start(f32[2,1024]{1,0:T(2,128)S(1)} %get-tuple-element.50), channel_id=1, source_target_pairs={{0,129},{1,128},{8,137},{9,136},{16,145},{17,144},{24,153},{25,152... | collective-permute-start | bytes 24584 | tf_op jit(solution)/shard_map/ppermute | solution.py:337
  174.0 16.3 %collective-permute-start.19 = (bf16[2,2,128,512]{3,2,1,0:T(8,128)(2,1)S(1)}, bf16[2,2,128,512]{3,2,1,0:T(8,128)(2,1)S(1)}, u32[]{:S(2)}, u32[]{:S(2)}) collective-permute-start(bf16[2,2,128,512]{3,2,1,0:T(8,128)(2,1)S(1)} %get-tuple-element.64), channel_id=1, source_target_pairs={{0,1},{1,0},{2,3},{3,2},{4,5},{5,4},{6,7},{7,6},{8,9},{9,8},{10,11... | collective-permute-start | bytes 1572872 | tf_op jit(solution)/shard_map/ppermute | solution.py:337
  174.2 13.9 %collective-permute-start.18 = (f32[2,1024]{1,0:T(2,128)S(1)}, f32[2,1024]{1,0:T(2,128)S(1)}, u32[]{:S(2)}, u32[]{:S(2)}) collective-permute-start(f32[2,1024]{1,0:T(2,128)S(1)} %get-tuple-element.55), channel_id=1, source_target_pairs={{0,0},{1,8},{8,1},{9,9},{16,16},{17,24},{24,17},{25,25},{32,32},{3... | collective-permute-start | bytes 24584 | tf_op jit(solution)/shard_map/ppermute | solution.py:352
  (2 other events, 3.9 us)
Sparse Core Ops, SparseCore 0:
  77.9 30.2 reduce-scatter.2
  111.0 32.3 reduce-scatter.4

commit v4 on v3

--- a/solution.py
+++ b/solution.py
@@ -127,7 +127,7 @@
 
 
 def correlate_kernel(
-    scale, side_ref, y_ref, near_hbm, far_hbm, left_ref, turn_ref, out_ref, sems
+    scale, side_ref, y_ref, out_hbm, left_ref, turn_ref, out_ref, sems
 ):
     samples = y_ref.shape[3]
     inputs = left_ref.shape[0]
@@ -140,11 +140,10 @@
     turn_ref[:, :samples] = imag
     turn_ref[:, samples:] = -real
 
-    def store(b, target):
+    def store(b, far):
         source = out_ref.at[:, pl.ds(b * tile, tile)]
-        return pltpu.make_async_copy(
-            source, target.at[:, pl.ds(b % half * tile, tile)], sems.at[b]
-        )
+        target = out_hbm.at[far, :, pl.ds(b % half * tile, tile)]
+        return pltpu.make_async_copy(source, target, sems.at[b])
 
     for b in reversed(range(blocks)):
         height = (b + 1) * tile
@@ -161,26 +160,26 @@
 
         @pl.when(side_ref[0] == b // half)
         def _():
-            store(b, near_hbm).start()
+            store(b, 0).start()
 
         @pl.when(side_ref[0] != b // half)
         def _():
-            store(b, far_hbm).start()
+            store(b, 1).start()
 
     for b in reversed(range(blocks)):
-        store(b, near_hbm).wait()
+        store(b, 0).wait()
 
 
 def correlate(y, side, scale):
     blocks, _, rows, samples = y.shape
     inputs = blocks * rows
     tiles = 4
-    out = pltpu.HBM((2, inputs // 2, inputs), BF16)
+    out = pltpu.HBM((2, 2, inputs // 2, inputs), BF16)
     return pl.pallas_call(
         functools.partial(correlate_kernel, scale),
         in_specs=[whole(SMEM), whole(VMEM)],
-        out_specs=[whole(pltpu.HBM)] * 2,
-        out_shape=[out] * 2,
+        out_specs=whole(pltpu.HBM),
+        out_shape=out,
         scratch_shapes=[VMEM((inputs, 2 * samples), BF16)] * 2
         + [VMEM((2, inputs, inputs), BF16), pltpu.SemaphoreType.DMA((tiles,))],
         compiler_params=params(28),
@@ -289,7 +288,9 @@
 def beam_kernel(
     reach, corr_ref, beam_ref, me_ref, *refs
 ):
-    gain_refs, (cos_ref, sin_ref, y_ref, *out_refs) = refs[: len(reach)], refs[len(reach) :]
+    gain_refs = refs[: len(reach)]
+    cos_ref, sin_ref, y_ref, own_hbm, away_ref, own_ref, sems = refs[len(reach) :]
+    out_refs = (own_ref, away_ref)
     slot = find_slot(corr_ref, beam_ref[me_ref[0]])
     half_ring = corr_ref.shape[0] // 2
     far = (slot // half_ring) ^ (me_ref[0] // half_ring)
@@ -300,8 +301,10 @@
         gains = jnp.where(jnp.full(gains.shape, hit) == 1, ref[...], gains)
     blocks, _, rows, samples = y_ref.shape
     stations = blocks // 2 * rows
-    beams = out_refs[0].shape[2]
+    beams = away_ref.shape[2]
     factor = 1.0 / math.sqrt(stations)
+    span = pl.ds(pl.multiple_of(me_ref[1] * samples, samples), samples)
+    stores = []
     for pol in range(2):
         gain_r = gains[0:1, pol * stations : (pol + 1) * stations]
         gain_i = gains[1:2, pol * stations : (pol + 1) * stations]
@@ -317,19 +320,78 @@
             dot = functools.partial(jnp.dot, preferred_element_type=F32)
             out_ref[pol, 0] = (dot(w_r, y_r) - dot(w_i, y_i)).astype(BF16)
             out_ref[pol, 1] = (dot(w_i, y_r) + dot(w_r, y_i)).astype(BF16)
+            if turn == 0:
+                store = pltpu.make_async_copy(
+                    own_ref.at[pol], own_hbm.at[pol, :, :, span], sems.at[pol]
+                )
+                store.start()
+                stores.append(store)
+    for store in stores:
+        store.wait()
 
 
 def beamform(reach, corr_channels, beam_channels, me, gains, cosine, sine, y, groups):
     samples = y.shape[3]
     beams = cosine.shape[0] // groups
+    shape = (2, 2, beams, samples)
     return pl.pallas_call(
         functools.partial(beam_kernel, reach),
         in_specs=[whole(SMEM)] * 3 + [whole(VMEM)] * (3 + len(reach)),
-        out_specs=[whole(VMEM)] * groups,
-        out_shape=[jax.ShapeDtypeStruct((2, 2, beams, samples), BF16)] * groups,
+        out_specs=[whole(pltpu.HBM), whole(VMEM)],
+        out_shape=[
+            pltpu.HBM((2, 2, beams, groups * samples), BF16),
+            jax.ShapeDtypeStruct(shape, BF16),
+        ],
+        scratch_shapes=[VMEM(shape, BF16), pltpu.SemaphoreType.DMA((2,))],
         compiler_params=params(16),
         name="beamform",
     )(corr_channels, beam_channels, me, *gains, cosine, sine, y)
+
+
+def place_kernel(me_ref, own_hbm, other_ref, out_hbm, sem):
+    samples = other_ref.shape[3]
+    span = pl.ds(pl.multiple_of((1 - me_ref[1]) * samples, samples), samples)
+    store = pltpu.make_async_copy(other_ref, out_hbm.at[:, :, :, span], sem)
+    store.start()
+    store.wait()
+
+
+def place(me, own, other):
+    return pl.pallas_call(
+        place_kernel,
+        in_specs=[whole(SMEM), whole(pltpu.HBM), whole(pl.ANY)],
+        out_specs=whole(pltpu.HBM),
+        out_shape=pltpu.HBM(own.shape, BF16),
+        scratch_shapes=[pltpu.SemaphoreType.DMA],
+        input_output_aliases={1: 0},
+        compiler_params=params(8),
+        name="place",
+    )(me, own, other)
+
+
+def join_kernel(near_ref, far_ref, z_ref, vis_ref, solved_ref):
+    vis_ref[...] = near_ref[...].astype(F32) + far_ref[...].astype(F32)
+
+    @pl.when(pl.program_id(0) == 0)
+    def _():
+        solved_ref[...] = z_ref[...]
+
+
+def join(near, far, z):
+    parts, rows, cols = near.shape
+    steps = 4
+    block = pl.BlockSpec((parts, rows // steps, cols), lambda i: (0, i, 0))
+    fixed = pl.BlockSpec(z.shape, lambda i: (0, 0))
+    near, far = (pltpu.with_memory_space_constraint(x, pltpu.HBM) for x in (near, far))
+    return pl.pallas_call(
+        join_kernel,
+        grid=(steps,),
+        in_specs=[block, block, fixed],
+        out_specs=[block, fixed],
+        out_shape=[pltpu.HBM(near.shape, F32), pltpu.HBM(z.shape, F32)],
+        compiler_params=params(8),
+        name="join",
+    )(near, far, z)
 
 
 def swap(x, axis, mask):
@@ -401,23 +463,21 @@
     )
     beam_y = lax.all_to_all(beam_send, WIDE, split_axis=0, concat_axis=0, tiled=True)
 
-    near, far = (
-        lax.psum_scatter(part, "tm", scatter_dimension=2, tiled=True)
-        for part in correlate(corr_y, core.astype(jnp.int32).reshape(1), 1.0 / total)
-    )
-
     scale = float(inputs) / total
-    sums = None
-    for _ in range(ITERS):
-        if sums is None:
-            part = apply_visibilities(corr_y, z, None, scale)
-        else:
-            part, z = apply_visibilities(corr_y, z, sums, scale)
+    part = apply_visibilities(corr_y, z, None, scale)
+
+    halves = correlate(corr_y, core.astype(jnp.int32).reshape(1), 1.0 / total)
+    halves = lax.psum_scatter(halves, "tm", scatter_dimension=3, tiled=True)
+
+    sums = exchange(part)
+    for _ in range(ITERS - 1):
+        part, z = apply_visibilities(corr_y, z, sums, scale)
         sums = exchange(part)
     depth = slots // 4
     z, copies = finish(z, sums, scale, depth)
-    copies, beam_y, near, far = lax.optimization_barrier((copies, beam_y, near, far))
-    near, far = cross(near, 0), cross(far, 1)
+    z, halves = lax.optimization_barrier((z, halves))
+    near, far, solved = cross(halves[0], 0), cross(halves[1], 1), cross(z, 0)
+    copies, beam_y = lax.optimization_barrier((copies, beam_y))
     line = [
         [high * 2 * depth + 2 * i + c for i in range(depth)]
         for high in range(2)
@@ -432,17 +492,14 @@
         swap(pick, WIDE, high * 8 * depth // 2 + low)
         for (high, low), pick in zip(reach[1:], picks[1:])
     ]
-    solved = cross(z, 0)
-    gains, near, far = lax.optimization_barrier((gains, near, far))
-    visibilities = (near.astype(F32) + far.astype(F32))[None]
+    gains, near, far, solved = lax.optimization_barrier((gains, near, far, solved))
+    visibilities, solved = join(near, far, solved)
 
     own, away = beamform(
         reach, corr_channels, beam_channels, me, gains, cosine, sine, beam_y, n_group
     )
-    other = swap(away, "grp", 1)
-    first = jnp.where(group_index == 0, own, other)
-    second = jnp.where(group_index == 0, other, own)
-    return visibilities, solved[None], jnp.concatenate([first, second], axis=3)[None]
+    beams = place(me, own, swap(away, "grp", 1))
+    return visibilities[None], solved[None], beams[None]
 
 
 def solution(mesh):

time: 200 us -> 187 us (0.935)
  waiting for transfers between devices: 93.8 us -> 76.9 us
  Pallas kernels: 19.2 us -> 24.7 us
  other arithmetic: 5.63 us -> 2.09 us
    reduce_scatter x2 -> x1, waiting for transfers between devices: 7.47 us -> 0.01 us  [body(): halves = lax.psum_scatter(halves, 'tm', scatter_dimension=3, tiled=True)]
    ppermute x4, waiting for transfers between devices: 8.31 us -> 1.31 us  [cross(): return lax.ppermute(x, WIDE, pairs)]
    all_to_all x1, waiting for transfers between devices: 5.9 us -> 0.01 us  [body(): lax.all_to_all(beam_send, WIDE, split_axis=0, concat_axis=0, tiled=True)]
    pallas_call x0 -> x2, Pallas kernels: none -> 4.79 us  [the longest x1 3.45 us: join(): pl.pallas_call(join_kernel, grid=(steps,), in_specs=[block, block, fixed]...]
    ppermute x16, waiting for transfers between devices: 25.7 us -> 30.1 us  [swap(): return lax.ppermute(x, axis, [(i, i ^ mask) for i in range(n)])]
    broadcast_in_dim x2 -> x0, other arithmetic: 3.4 us -> none  [the longest x1 2.28 us: body(): visibilities = (near.astype(F32) + far.astype(F32))[None]]
    squeeze x0 -> x1, local copies, waits for them, and re-layouts: none -> 2.23 us  [body(): near, far, solved = (cross(halves[0], 0), cross(halves[1], 1), cross(z, 0))]
  transfers between devices with their start and end apart: 25 -> 24, of which waited for: 19 -> 16; matrix products, arithmetic and copies ran while one was open for 3% -> 3% of each run, Pallas kernels for 4% -> 7%
where the time goes in v4:
time: 187 us; the launch traced here: 184 us
  waiting for transfers between devices  76.9 us (41%)
  starting transfers between devices  61.1 us (33%)
  Pallas kernels  24.7 us (13%)
  between operations  15.1 us (8%)
  local copies, waits for them, and re-layouts  4.35 us (2%)
  other arithmetic  2.09 us (1%)
    all_to_all x1, waiting for transfers between devices, body(): lax.all_to_all(corr_send, WIDE, split_axis=0, concat_axis=0, tiled=True)  38.4 us
    ppermute x16, waiting for transfers between devices, swap(): return lax.ppermute(x, axis, [(i, i ^ mask) for i in range(n)])  30.1 us
    ppermute x16, starting transfers between devices, swap(): return lax.ppermute(x, axis, [(i, i ^ mask) for i in range(n)])  21.8 us
    all_to_all x1, starting transfers between devices, body(): lax.all_to_all(corr_send, WIDE, split_axis=0, concat_axis=0, tiled=True)  13.3 us
    ppermute x4, starting transfers between devices, cross(): return lax.ppermute(x, WIDE, pairs)  12.3 us
    all_to_all x1, starting transfers between devices, body(): lax.all_to_all(beam_send, WIDE, split_axis=0, concat_axis=0, tiled=True)  7.42 us
    all_to_all x1, waiting for transfers between devices, body(): lax.all_to_all(copies, 'freq', split_axis=0, concat_axis=0, axis_index_gr...  7.07 us
    all_to_all x1, starting transfers between devices, body(): lax.all_to_all(copies, 'freq', split_axis=0, concat_axis=0, axis_index_gr...  6.31 us
  transfers between devices with their start and end apart: 24, of which 16 were waited for; matrix products, arithmetic and copies ran while one was open for 3% of the time, Pallas kernels for 7%

profile of v4, /device:TPU:1, one launch (start us, length us, event | category | flops | bytes accessed | tf_op | source)
XLA Modules:
  0.0 184.2 jit_solution(1426588617188859307)
XLA Ops:
  7.2 3.1 %ingest.3 = bf16[32,2,2,16,512]{4,3,2,1,0:T(8,128)(2,1)} custom-call(s32[1]{0:T(128)} %bitcast.2.base_ref, s32[32]{0:T(128)} %corr_ref.3, s32[512]{0:T(512)} %map_hbm.3, s32[512]{0:T(512)} %flag_hbm.3, bf16[32,2,16,1024]{3,2,1,0:T(8,128)(2,1)} %volts_hbm.3), custom_call_target="tpu_custom_call" | custom-call | tf_op jit(solution)/shard_map/ingest/pallas_call | solution.py:93
  10.3 13.3 %all-to-all-start = ((bf16[64,2,16,512]{3,2,1,0:T(8,128)(2,1)}), bf16[64,2,16,512]{3,2,1,0:T(8,128)(2,1)S(1)}, u32[]{:S(2)}, u32[]{:S(2)}) async-start(bf16[64,2,16,512]{3,2,1,0:T(8,128)(2,1)} %bitcast.19), calls=%async_computation | async-start | bytes 4194304 | tf_op jit(solution)/shard_map/all_to_all | solution.py:445
  23.7 3.5 %collective-permute-start = (f32[2,1024]{1,0:T(2,128)S(1)}, f32[2,1024]{1,0:T(2,128)S(1)}, u32[]{:S(2)}, u32[]{:S(2)}) collective-permute-start(f32[2,1024]{1,0:T(2,128)S(1)} %bitcast.25), channel_id=1, source_target_pairs={{0,0},{1,8},{8,1},{9,9},{16,16},{17,24},{24,17},{25,25},{32,32},{3... | collective-permute-start | bytes 24584 | tf_op jit(solution)/shard_map/ppermute | solution.py:414
  30.1 2.0 %fusion = (f32[256,512]{1,0:T(8,128)S(1)}, f32[256,512]{1,0:T(8,128)S(1)}) fusion(f32[512]{0:T(512)S(1)} %get-tuple-element.68, f32[256]{0:T(256)S(1)} %bitcast.23, f32[512]{0:T(512)S(1)} %get-tuple-element.67, f32[256]{0:T(256)S(1)} %bitcast.22, f32[]{:T(128)} %bitcast.6), kind=kLoop, calls=%fused_computation.4 | loop fusion | flops 524288 | bytes 1054724 | tf_op jit(solution)/shard_map/sin | solution.py:458
  32.0 3.1 %ingest.2 = bf16[32,2,2,16,512]{4,3,2,1,0:T(8,128)(2,1)} custom-call(s32[1]{0:T(128)} %bitcast.2.base_ref, s32[32]{0:T(128)} %beam_ref.3, s32[512]{0:T(512)} %map_hbm.3, s32[512]{0:T(512)} %flag_hbm.3, bf16[32,2,16,1024]{3,2,1,0:T(8,128)(2,1)} %volts_hbm.3), custom_call_target="tpu_custom_call" | custom-call | tf_op jit(solution)/shard_map/ingest/pallas_call | solution.py:93
  35.2 38.4 %all-to-all-done.y_ref = bf16[64,2,16,512]{3,2,1,0:T(8,128)(2,1)S(1)} async-done(((bf16[64,2,16,512]{3,2,1,0:T(8,128)(2,1)}), bf16[64,2,16,512]{3,2,1,0:T(8,128)(2,1)S(1)}, u32[]{:S(2)}, u32[]{:S(2)}) %all-to-all-start) | async-done | bytes 2097184 | tf_op jit(solution)/shard_map/all_to_all | solution.py:445
  73.6 4.1 %correlate.1 = bf16[2,2,512,1024]{3,2,1,0:T(8,128)(2,1)} custom-call(s32[1]{0:T(128)} %bitcast.10.side_ref, bf16[64,2,16,512]{3,2,1,0:T(8,128)(2,1)S(1)} %all-to-all-done.y_ref), custom_call_target="tpu_custom_call" | custom-call | tf_op jit(solution)/shard_map/correlate/pallas_call | solution.py:178
  77.8 7.4 %all-to-all-start.1 = ((bf16[64,2,16,512]{3,2,1,0:T(8,128)(2,1)}), bf16[64,2,16,512]{3,2,1,0:T(8,128)(2,1)}, u32[]{:S(2)}, u32[]{:S(2)}) async-start(bf16[64,2,16,512]{3,2,1,0:T(8,128)(2,1)} %bitcast.18), calls=%async_computation.1 | async-start | bytes 4194304 | tf_op jit(solution)/shard_map/all_to_all | solution.py:464
  88.9 1.7 collective-permute-done.2
  90.6 2.6 %collective-permute-start.3 = (f32[2,1024]{1,0:T(2,128)S(1)}, f32[2,1024]{1,0:T(2,128)S(1)}, u32[]{:S(2)}, u32[]{:S(2)}) collective-permute-start(f32[2,1024]{1,0:T(2,128)S(1)} %add.78.refs_0_), channel_id=1, source_target_pairs={{0,6},{2,4},{4,2},{6,0},{1,7},{3,5},{5,3},{7,1},{8,14},{10,12},{12... | collective-permute-start | bytes 24584 | tf_op jit(solution)/shard_map/ppermute | solution.py:399
  93.1 1.7 collective-permute-done.3.refs_1_
  95.9 2.1 %collective-permute-start.4 = (f32[2,1024]{1,0:T(2,128)S(1)}, f32[2,1024]{1,0:T(2,128)S(1)}, u32[]{:S(2)}, u32[]{:S(2)}) collective-permute-start(f32[2,1024]{1,0:T(2,128)S(1)} %get-tuple-element.38), channel_id=1, source_target_pairs={{0,8},{8,0},{16,24},{24,16},{32,40},{40,32},{48,56},{56,48},{64,72... | collective-permute-start | bytes 24584 | tf_op jit(solution)/shard_map/ppermute | solution.py:399
  98.9 3.2 %collective-permute-done.5 = f32[2,1024]{1,0:T(2,128)S(1)} collective-permute-done((f32[2,1024]{1,0:T(2,128)S(1)}, f32[2,1024]{1,0:T(2,128)S(1)}, u32[]{:S(2)}, u32[]{:S(2)}) %collective-permute-start.5) | collective-permute-done | bytes 8224 | tf_op jit(solution)/shard_map/ppermute | solution.py:399
  102.1 2.5 %collective-permute-start.6 = (f32[2,1024]{1,0:T(2,128)S(1)}, f32[2,1024]{1,0:T(2,128)S(1)}, u32[]{:S(2)}, u32[]{:S(2)}) collective-permute-start(f32[2,1024]{1,0:T(2,128)S(1)} %add.80.refs_0_), channel_id=1, source_target_pairs={{0,6},{2,4},{4,2},{6,0},{1,7},{3,5},{5,3},{7,1},{8,14},{10,12},{12... | collective-permute-start | bytes 24584 | tf_op jit(solution)/shard_map/ppermute | solution.py:399
  104.6 2.0 %collective-permute-done.6.refs_1_ = f32[2,1024]{1,0:T(2,128)S(1)} collective-permute-done((f32[2,1024]{1,0:T(2,128)S(1)}, f32[2,1024]{1,0:T(2,128)S(1)}, u32[]{:S(2)}, u32[]{:S(2)}) %collective-permute-start.6) | collective-permute-done | bytes 8224 | tf_op jit(solution)/shard_map/ppermute | solution.py:399
  107.7 1.9 %collective-permute-start.7 = (f32[2,1024]{1,0:T(2,128)S(1)}, f32[2,1024]{1,0:T(2,128)S(1)}, u32[]{:S(2)}, u32[]{:S(2)}) collective-permute-start(f32[2,1024]{1,0:T(2,128)S(1)} %get-tuple-element.40), channel_id=1, source_target_pairs={{0,8},{8,0},{16,24},{24,16},{32,40},{40,32},{48,56},{56,48},{64,72... | collective-permute-start | bytes 24584 | tf_op jit(solution)/shard_map/ppermute | solution.py:399
  110.5 3.2 %collective-permute-done.8 = f32[2,1024]{1,0:T(2,128)S(1)} collective-permute-done((f32[2,1024]{1,0:T(2,128)S(1)}, f32[2,1024]{1,0:T(2,128)S(1)}, u32[]{:S(2)}, u32[]{:S(2)}) %collective-permute-start.8) | collective-permute-done | bytes 8224 | tf_op jit(solution)/shard_map/ppermute | solution.py:399
  113.7 2.5 %collective-permute-start.9 = (f32[2,1024]{1,0:T(2,128)S(1)}, f32[2,1024]{1,0:T(2,128)S(1)}, u32[]{:S(2)}, u32[]{:S(2)}) collective-permute-start(f32[2,1024]{1,0:T(2,128)S(1)} %add.82.refs_0_), channel_id=1, source_target_pairs={{0,6},{2,4},{4,2},{6,0},{1,7},{3,5},{5,3},{7,1},{8,14},{10,12},{12... | collective-permute-start | bytes 24584 | tf_op jit(solution)/shard_map/ppermute | solution.py:399
  116.2 2.0 %collective-permute-done.9.refs_1_ = f32[2,1024]{1,0:T(2,128)S(1)} collective-permute-done((f32[2,1024]{1,0:T(2,128)S(1)}, f32[2,1024]{1,0:T(2,128)S(1)}, u32[]{:S(2)}, u32[]{:S(2)}) %collective-permute-start.9) | collective-permute-done | bytes 8224 | tf_op jit(solution)/shard_map/ppermute | solution.py:399
  119.3 1.9 %collective-permute-start.10 = (f32[2,1024]{1,0:T(2,128)S(1)}, f32[2,1024]{1,0:T(2,128)S(1)}, u32[]{:S(2)}, u32[]{:S(2)}) collective-permute-start(f32[2,1024]{1,0:T(2,128)S(1)} %get-tuple-element.42), channel_id=1, source_target_pairs={{0,8},{8,0},{16,24},{24,16},{32,40},{40,32},{48,56},{56,48},{64,72... | collective-permute-start | bytes 24584 | tf_op jit(solution)/shard_map/ppermute | solution.py:399
  122.1 2.9 %collective-permute-done.11 = f32[2,1024]{1,0:T(2,128)S(1)} collective-permute-done((f32[2,1024]{1,0:T(2,128)S(1)}, f32[2,1024]{1,0:T(2,128)S(1)}, u32[]{:S(2)}, u32[]{:S(2)}) %collective-permute-start.11) | collective-permute-done | bytes 8224 | tf_op jit(solution)/shard_map/ppermute | solution.py:399
  125.0 2.5 %collective-permute-start.12 = (f32[2,1024]{1,0:T(2,128)S(1)}, f32[2,1024]{1,0:T(2,128)S(1)}, u32[]{:S(2)}, u32[]{:S(2)}) collective-permute-start(f32[2,1024]{1,0:T(2,128)S(1)} %add.84.near_ref), channel_id=1, source_target_pairs={{0,6},{2,4},{4,2},{6,0},{1,7},{3,5},{5,3},{7,1},{8,14},{10,12},{12... | collective-permute-start | bytes 24584 | tf_op jit(solution)/shard_map/ppermute | solution.py:399
  129.8 2.2 %slice_bitcast_fusion = (bf16[2,512,256]{2,1,0:T(8,128)(2,1)}, bf16[2,512,256]{2,1,0:T(8,128)(2,1)}) fusion(bf16[2,2,512,256]{3,2,1,0:T(8,128)(2,1)} %reduce-scatter.2.cloned.1.call-done), kind=kLoop, calls=%fused_computation.1 | loop fusion | bytes 2097152 | tf_op jit(solution)/shard_map/squeeze | solution.py:479
  132.1 1.8 %collective-permute-start.17 = (bf16[2,512,256]{2,1,0:T(8,128)(2,1)}, bf16[2,512,256]{2,1,0:T(8,128)(2,1)S(1)}, u32[]{:S(2)}, u32[]{:S(2)}) collective-permute-start(bf16[2,512,256]{2,1,0:T(8,128)(2,1)} %get-tuple-element.69), channel_id=1, source_target_pairs={{0,1},{1,9},{8,0},{9,8},{16,17},{17,25},{24,16},{25,24},{32,33},{3... | collective-permute-start | bytes 1572872 | tf_op jit(solution)/shard_map/ppermute | solution.py:414
  133.9 3.0 %collective-permute-start.16 = (bf16[2,512,256]{2,1,0:T(8,128)(2,1)}, bf16[2,512,256]{2,1,0:T(8,128)(2,1)S(1)}, u32[]{:S(2)}, u32[]{:S(2)}) collective-permute-start(bf16[2,512,256]{2,1,0:T(8,128)(2,1)} %get-tuple-element.70), channel_id=1, source_target_pairs={{0,0},{1,8},{8,1},{9,9},{16,16},{17,24},{24,17},{25,25},{32,32},{3... | collective-permute-start | bytes 1572872 | tf_op jit(solution)/shard_map/ppermute | solution.py:414
  136.9 6.3 %all-to-all-start.2 = ((f32[8,2,1024]{2,1,0:T(2,128)}), f32[8,2,1024]{2,1,0:T(2,128)S(1)}, u32[]{:S(2)}, u32[]{:S(2)}) async-start(f32[8,2,1024]{2,1,0:T(2,128)} %get-tuple-element.45), calls=%async_computation.2 | async-start | bytes 131072 | tf_op jit(solution)/shard_map/all_to_all | solution.py:486
  143.3 7.1 %all-to-all-done.2.line_ref = f32[8,2,1024]{2,1,0:T(2,128)S(1)} async-done(((f32[8,2,1024]{2,1,0:T(2,128)}), f32[8,2,1024]{2,1,0:T(2,128)S(1)}, u32[]{:S(2)}, u32[]{:S(2)}) %all-to-all-start.2) | async-done | bytes 65568 | tf_op jit(solution)/shard_map/all_to_all | solution.py:486
  151.2 2.7 %collective-permute-start.14 = (f32[2,1024]{1,0:T(2,128)S(1)}, f32[2,1024]{1,0:T(2,128)S(1)}, u32[]{:S(2)}, u32[]{:S(2)}) collective-permute-start(f32[2,1024]{1,0:T(2,128)S(1)} %get-tuple-element.48), channel_id=1, source_target_pairs={{0,128},{1,129},{8,136},{9,137},{16,144},{17,145},{24,152},{25,153... | collective-permute-start | bytes 24584 | tf_op jit(solution)/shard_map/ppermute | solution.py:399
  155.0 3.9 %collective-permute-start.18 = (f32[2,1024]{1,0:T(2,128)S(1)}, f32[2,1024]{1,0:T(2,128)S(1)}, u32[]{:S(2)}, u32[]{:S(2)}) collective-permute-start(f32[2,1024]{1,0:T(2,128)S(1)} %get-tuple-element.52), channel_id=1, source_target_pairs={{0,0},{1,8},{8,1},{9,9},{16,16},{17,24},{24,17},{25,25},{32,32},{3... | collective-permute-start | bytes 24584 | tf_op jit(solution)/shard_map/ppermute | solution.py:414
  160.3 3.8 %beamform.1 = (bf16[2,2,128,1024]{3,2,1,0:T(8,128)(2,1)}, bf16[2,2,128,512]{3,2,1,0:T(8,128)(2,1)S(1)}) custom-call(s32[32]{0:T(128)S(1)} %copy-done, s32[32]{0:T(128)S(1)} %copy-done.2, s32[2]{0:T(128)S(1)} %pad_add_fusion.me_ref, f32[2,1024]{1,0:T(2,128)S(1)} %get-tuple-element.58.refs_0_, f32[2,1024]{1,0:T(2,128)S(1)} %collective-permute-done.13.refs_1_, ...), custom_call_target="tpu_custom_call" | custom-call | tf_op jit(solution)/shard_map/beamform/pallas_call | solution.py:337
  164.2 3.4 %join.1 = (f32[2,512,256]{2,1,0:T(8,128)}, f32[2,1024]{1,0:T(2,128)}) custom-call(bf16[2,512,256]{2,1,0:T(8,128)(2,1)} %copy-done.4, bf16[2,512,256]{2,1,0:T(8,128)(2,1)} %copy-done.3, f32[2,1024]{1,0:T(2,128)S(1)} %collective-permute-done.18.z_ref), custom_call_target="tpu_custom_call" | custom-call | tf_op jit(solution)/shard_map/join/pallas_call | solution.py:386
  167.6 8.4 %collective-permute-done.19.other_ref = bf16[2,2,128,512]{3,2,1,0:T(8,128)(2,1)S(1)} collective-permute-done((bf16[2,2,128,512]{3,2,1,0:T(8,128)(2,1)S(1)}, bf16[2,2,128,512]{3,2,1,0:T(8,128)(2,1)S(1)}, u32[]{:S(2)}, u32[]{:S(2)}) %collective-permute-start.19) | collective-permute-done | bytes 524320 | tf_op jit(solution)/shard_map/ppermute | solution.py:399
  (64 shorter events, 18.9 us)
Async XLA Ops:
  10.3 13.4 %copy-start.8 = (f32[1,2,1024]{2,1,0:T(2,128)S(1)}, f32[1,2,1024]{2,1,0:T(2,128)}, u32[]{:S(2)}) copy-start(f32[1,2,1024]{2,1,0:T(2,128)} %param.9) | copy-start | bytes 24580
  10.3 17.0 %copy-start.1 = (s32[32]{0:T(128)S(1)}, s32[32]{0:T(128)}, u32[]{:S(2)}) copy-start(s32[32]{0:T(128)} %beam_ref.3) | copy-start | bytes 388
  10.3 18.2 %copy-start.6 = (f32[2,512]{1,0:T(2,128)S(1)}, f32[2,512]{1,0:T(2,128)}, u32[]{:S(2)}) copy-start(f32[2,512]{1,0:T(2,128)} %param.12) | copy-start | bytes 12292
  10.3 18.4 %copy-start.5 = (s32[512]{0:T(512)S(1)}, s32[512]{0:T(512)}, u32[]{:S(2)}) copy-start(s32[512]{0:T(512)} %map_hbm.3) | copy-start | bytes 6148
  10.3 19.7 %copy-start.7 = (s32[2,256]{1,0:T(2,128)S(1)}, s32[2,256]{1,0:T(2,128)}, u32[]{:S(2)}) copy-start(s32[2,256]{1,0:T(2,128)} %param.13) | copy-start | bytes 6148
  10.3 63.3 %all-to-all-start = ((bf16[64,2,16,512]{3,2,1,0:T(8,128)(2,1)}), bf16[64,2,16,512]{3,2,1,0:T(8,128)(2,1)S(1)}, u32[]{:S(2)}, u32[]{:S(2)}) async-start(bf16[64,2,16,512]{3,2,1,0:T(8,128)(2,1)} %bitcast.19), calls=%async_computation | async-start | bytes 4194304 | tf_op jit(solution)/shard_map/all_to_all | solution.py:445
  23.6 106.2 %reduce-scatter.2.cloned.1.call-start = ((), (), s32[]{:S(2)}) async-start(), calls=%async_computation.4 | async-start | bytes 5242880 | tf_op jit(solution)/shard_map/reduce_scatter | solution.py:470
  23.7 11.5 %collective-permute-start = (f32[2,1024]{1,0:T(2,128)S(1)}, f32[2,1024]{1,0:T(2,128)S(1)}, u32[]{:S(2)}, u32[]{:S(2)}) collective-permute-start(f32[2,1024]{1,0:T(2,128)S(1)} %bitcast.25), channel_id=1, source_target_pairs={{0,0},{1,8},{8,1},{9,9},{16,16},{17,24},{24,17},{25,25},{32,32},{3... | collective-permute-start | bytes 24584 | tf_op jit(solution)/shard_map/ppermute | solution.py:414
  77.8 59.1 %all-to-all-start.1 = ((bf16[64,2,16,512]{3,2,1,0:T(8,128)(2,1)}), bf16[64,2,16,512]{3,2,1,0:T(8,128)(2,1)}, u32[]{:S(2)}, u32[]{:S(2)}) async-start(bf16[64,2,16,512]{3,2,1,0:T(8,128)(2,1)} %bitcast.18), calls=%async_computation.1 | async-start | bytes 4194304 | tf_op jit(solution)/shard_map/all_to_all | solution.py:464
  86.2 1.4 collective-permute-start.1
  87.6 2.9 %collective-permute-start.2 = (f32[2,1024]{1,0:T(2,128)S(1)}, f32[2,1024]{1,0:T(2,128)S(1)}, u32[]{:S(2)}, u32[]{:S(2)}) collective-permute-start(f32[2,1024]{1,0:T(2,128)S(1)} %add.77), channel_id=1, source_target_pairs={{0,2},{2,0},{4,6},{6,4},{1,3},{3,1},{5,7},{7,5},{8,10},{10,8},{12,... | collective-permute-start | bytes 24584 | tf_op jit(solution)/shard_map/ppermute | solution.py:399
  90.6 4.3 %collective-permute-start.3 = (f32[2,1024]{1,0:T(2,128)S(1)}, f32[2,1024]{1,0:T(2,128)S(1)}, u32[]{:S(2)}, u32[]{:S(2)}) collective-permute-start(f32[2,1024]{1,0:T(2,128)S(1)} %add.78.refs_0_), channel_id=1, source_target_pairs={{0,6},{2,4},{4,2},{6,0},{1,7},{3,5},{5,3},{7,1},{8,14},{10,12},{12... | collective-permute-start | bytes 24584 | tf_op jit(solution)/shard_map/ppermute | solution.py:399
  95.9 2.9 %collective-permute-start.4 = (f32[2,1024]{1,0:T(2,128)S(1)}, f32[2,1024]{1,0:T(2,128)S(1)}, u32[]{:S(2)}, u32[]{:S(2)}) collective-permute-start(f32[2,1024]{1,0:T(2,128)S(1)} %get-tuple-element.38), channel_id=1, source_target_pairs={{0,8},{8,0},{16,24},{24,16},{32,40},{40,32},{48,56},{56,48},{64,72... | collective-permute-start | bytes 24584 | tf_op jit(solution)/shard_map/ppermute | solution.py:399
  98.9 3.2 %collective-permute-start.5 = (f32[2,1024]{1,0:T(2,128)S(1)}, f32[2,1024]{1,0:T(2,128)S(1)}, u32[]{:S(2)}, u32[]{:S(2)}) collective-permute-start(f32[2,1024]{1,0:T(2,128)S(1)} %add.79), channel_id=1, source_target_pairs={{0,2},{2,0},{4,6},{6,4},{1,3},{3,1},{5,7},{7,5},{8,10},{10,8},{12,... | collective-permute-start | bytes 24584 | tf_op jit(solution)/shard_map/ppermute | solution.py:399
  102.1 4.5 %collective-permute-start.6 = (f32[2,1024]{1,0:T(2,128)S(1)}, f32[2,1024]{1,0:T(2,128)S(1)}, u32[]{:S(2)}, u32[]{:S(2)}) collective-permute-start(f32[2,1024]{1,0:T(2,128)S(1)} %add.80.refs_0_), channel_id=1, source_target_pairs={{0,6},{2,4},{4,2},{6,0},{1,7},{3,5},{5,3},{7,1},{8,14},{10,12},{12... | collective-permute-start | bytes 24584 | tf_op jit(solution)/shard_map/ppermute | solution.py:399
  107.7 2.8 %collective-permute-start.7 = (f32[2,1024]{1,0:T(2,128)S(1)}, f32[2,1024]{1,0:T(2,128)S(1)}, u32[]{:S(2)}, u32[]{:S(2)}) collective-permute-start(f32[2,1024]{1,0:T(2,128)S(1)} %get-tuple-element.40), channel_id=1, source_target_pairs={{0,8},{8,0},{16,24},{24,16},{32,40},{40,32},{48,56},{56,48},{64,72... | collective-permute-start | bytes 24584 | tf_op jit(solution)/shard_map/ppermute | solution.py:399
  110.5 3.2 %collective-permute-start.8 = (f32[2,1024]{1,0:T(2,128)S(1)}, f32[2,1024]{1,0:T(2,128)S(1)}, u32[]{:S(2)}, u32[]{:S(2)}) collective-permute-start(f32[2,1024]{1,0:T(2,128)S(1)} %add.81), channel_id=1, source_target_pairs={{0,2},{2,0},{4,6},{6,4},{1,3},{3,1},{5,7},{7,5},{8,10},{10,8},{12,... | collective-permute-start | bytes 24584 | tf_op jit(solution)/shard_map/ppermute | solution.py:399
  113.7 4.5 %collective-permute-start.9 = (f32[2,1024]{1,0:T(2,128)S(1)}, f32[2,1024]{1,0:T(2,128)S(1)}, u32[]{:S(2)}, u32[]{:S(2)}) collective-permute-start(f32[2,1024]{1,0:T(2,128)S(1)} %add.82.refs_0_), channel_id=1, source_target_pairs={{0,6},{2,4},{4,2},{6,0},{1,7},{3,5},{5,3},{7,1},{8,14},{10,12},{12... | collective-permute-start | bytes 24584 | tf_op jit(solution)/shard_map/ppermute | solution.py:399
  118.2 32.2 %copy-start = (s32[32]{0:T(128)S(1)}, s32[32]{0:T(128)}, u32[]{:S(2)}) copy-start(s32[32]{0:T(128)} %corr_ref.3) | copy-start | bytes 388
  118.2 32.2 %copy-start.2 = (s32[32]{0:T(128)S(1)}, s32[32]{0:T(128)}, u32[]{:S(2)}) copy-start(s32[32]{0:T(128)} %beam_ref.3) | copy-start | bytes 388
  119.3 2.8 %collective-permute-start.10 = (f32[2,1024]{1,0:T(2,128)S(1)}, f32[2,1024]{1,0:T(2,128)S(1)}, u32[]{:S(2)}, u32[]{:S(2)}) collective-permute-start(f32[2,1024]{1,0:T(2,128)S(1)} %get-tuple-element.42), channel_id=1, source_target_pairs={{0,8},{8,0},{16,24},{24,16},{32,40},{40,32},{48,56},{56,48},{64,72... | collective-permute-start | bytes 24584 | tf_op jit(solution)/shard_map/ppermute | solution.py:399
  122.1 2.9 %collective-permute-start.11 = (f32[2,1024]{1,0:T(2,128)S(1)}, f32[2,1024]{1,0:T(2,128)S(1)}, u32[]{:S(2)}, u32[]{:S(2)}) collective-permute-start(f32[2,1024]{1,0:T(2,128)S(1)} %add.83), channel_id=1, source_target_pairs={{0,2},{2,0},{4,6},{6,4},{1,3},{3,1},{5,7},{7,5},{8,10},{10,8},{12,... | collective-permute-start | bytes 24584 | tf_op jit(solution)/shard_map/ppermute | solution.py:399
  125.0 4.1 %collective-permute-start.12 = (f32[2,1024]{1,0:T(2,128)S(1)}, f32[2,1024]{1,0:T(2,128)S(1)}, u32[]{:S(2)}, u32[]{:S(2)}) collective-permute-start(f32[2,1024]{1,0:T(2,128)S(1)} %add.84.near_ref), channel_id=1, source_target_pairs={{0,6},{2,4},{4,2},{6,0},{1,7},{3,5},{5,3},{7,1},{8,14},{10,12},{12... | collective-permute-start | bytes 24584 | tf_op jit(solution)/shard_map/ppermute | solution.py:399
  132.1 28.2 %collective-permute-start.17 = (bf16[2,512,256]{2,1,0:T(8,128)(2,1)}, bf16[2,512,256]{2,1,0:T(8,128)(2,1)S(1)}, u32[]{:S(2)}, u32[]{:S(2)}) collective-permute-start(bf16[2,512,256]{2,1,0:T(8,128)(2,1)} %get-tuple-element.69), channel_id=1, source_target_pairs={{0,1},{1,9},{8,0},{9,8},{16,17},{17,25},{24,16},{25,24},{32,33},{3... | collective-permute-start | bytes 1572872 | tf_op jit(solution)/shard_map/ppermute | solution.py:414
  133.9 26.4 %collective-permute-start.16 = (bf16[2,512,256]{2,1,0:T(8,128)(2,1)}, bf16[2,512,256]{2,1,0:T(8,128)(2,1)S(1)}, u32[]{:S(2)}, u32[]{:S(2)}) collective-permute-start(bf16[2,512,256]{2,1,0:T(8,128)(2,1)} %get-tuple-element.70), channel_id=1, source_target_pairs={{0,0},{1,8},{8,1},{9,9},{16,16},{17,24},{24,17},{25,25},{32,32},{3... | collective-permute-start | bytes 1572872 | tf_op jit(solution)/shard_map/ppermute | solution.py:414
  136.9 13.5 %all-to-all-start.2 = ((f32[8,2,1024]{2,1,0:T(2,128)}), f32[8,2,1024]{2,1,0:T(2,128)S(1)}, u32[]{:S(2)}, u32[]{:S(2)}) async-start(f32[8,2,1024]{2,1,0:T(2,128)} %get-tuple-element.45), calls=%async_computation.2 | async-start | bytes 131072 | tf_op jit(solution)/shard_map/all_to_all | solution.py:486
  151.1 3.9 %collective-permute-start.13 = (f32[2,1024]{1,0:T(2,128)S(1)}, f32[2,1024]{1,0:T(2,128)S(1)}, u32[]{:S(2)}, u32[]{:S(2)}) collective-permute-start(f32[2,1024]{1,0:T(2,128)S(1)} %get-tuple-element.47), channel_id=1, source_target_pairs={{0,1},{1,0},{8,9},{9,8},{16,17},{17,16},{24,25},{25,24},{32,33},{3... | collective-permute-start | bytes 24584 | tf_op jit(solution)/shard_map/ppermute | solution.py:399
  151.2 7.8 %collective-permute-start.14 = (f32[2,1024]{1,0:T(2,128)S(1)}, f32[2,1024]{1,0:T(2,128)S(1)}, u32[]{:S(2)}, u32[]{:S(2)}) collective-permute-start(f32[2,1024]{1,0:T(2,128)S(1)} %get-tuple-element.48), channel_id=1, source_target_pairs={{0,128},{1,129},{8,136},{9,137},{16,144},{17,145},{24,152},{25,153... | collective-permute-start | bytes 24584 | tf_op jit(solution)/shard_map/ppermute | solution.py:399
  153.9 5.1 %collective-permute-start.15 = (f32[2,1024]{1,0:T(2,128)S(1)}, f32[2,1024]{1,0:T(2,128)S(1)}, u32[]{:S(2)}, u32[]{:S(2)}) collective-permute-start(f32[2,1024]{1,0:T(2,128)S(1)} %get-tuple-element.49), channel_id=1, source_target_pairs={{0,129},{1,128},{8,137},{9,136},{16,145},{17,144},{24,153},{25,152... | collective-permute-start | bytes 24584 | tf_op jit(solution)/shard_map/ppermute | solution.py:399
  155.0 5.3 %collective-permute-start.18 = (f32[2,1024]{1,0:T(2,128)S(1)}, f32[2,1024]{1,0:T(2,128)S(1)}, u32[]{:S(2)}, u32[]{:S(2)}) collective-permute-start(f32[2,1024]{1,0:T(2,128)S(1)} %get-tuple-element.52), channel_id=1, source_target_pairs={{0,0},{1,8},{8,1},{9,9},{16,16},{17,24},{24,17},{25,25},{32,32},{3... | collective-permute-start | bytes 24584 | tf_op jit(solution)/shard_map/ppermute | solution.py:414
  160.3 3.9 %copy-start.4 = (bf16[2,512,256]{2,1,0:T(8,128)(2,1)}, bf16[2,512,256]{2,1,0:T(8,128)(2,1)S(1)}, u32[]{:S(2)}) copy-start(bf16[2,512,256]{2,1,0:T(8,128)(2,1)S(1)} %collective-permute-done.16.near_ref) | copy-start | bytes 1572868
  164.1 12.0 %collective-permute-start.19 = (bf16[2,2,128,512]{3,2,1,0:T(8,128)(2,1)S(1)}, bf16[2,2,128,512]{3,2,1,0:T(8,128)(2,1)S(1)}, u32[]{:S(2)}, u32[]{:S(2)}) collective-permute-start(bf16[2,2,128,512]{3,2,1,0:T(8,128)(2,1)S(1)} %get-tuple-element.66), channel_id=1, source_target_pairs={{0,1},{1,0},{2,3},{3,2},{4,5},{5,4},{6,7},{7,6},{8,9},{9,8},{10,11... | collective-permute-start | bytes 1572872 | tf_op jit(solution)/shard_map/ppermute | solution.py:399
  (1 other events, 3.9 us)
Sparse Core Ops, SparseCore 0:
  77.9 47.6 reduce-scatter.1

commit v5 on v4

--- a/solution.py
+++ b/solution.py
@@ -126,24 +126,22 @@
     return lax.dot_general(a, b, (((1,), (1,)), ((), ())), preferred_element_type=F32)
 
 
-def correlate_kernel(
-    scale, side_ref, y_ref, out_hbm, left_ref, turn_ref, out_ref, sems
-):
+def correlate_kernel(scale, me_ref, y_ref, *refs):
     samples = y_ref.shape[3]
+    *out_hbms, left_ref, turn_ref, out_ref, sems = refs
     inputs = left_ref.shape[0]
     blocks = sems.shape[0]
-    tile = inputs // blocks
-    half = blocks // 2
+    tile, half = inputs // blocks, inputs // 2
+    core, time = me_ref[0] % 2, me_ref[2]
     real, imag = load_part(y_ref, 0), load_part(y_ref, 1)
     left_ref[:, :samples] = real
     left_ref[:, samples:] = imag
     turn_ref[:, :samples] = imag
     turn_ref[:, samples:] = -real
 
-    def store(b, far):
-        source = out_ref.at[:, pl.ds(b * tile, tile)]
-        target = out_hbm.at[far, :, pl.ds(b % half * tile, tile)]
-        return pltpu.make_async_copy(source, target, sems.at[b])
+    def store(b, side, target):
+        source = out_ref.at[:, side * half : (side + 1) * half, b * tile : (b + 1) * tile]
+        return pltpu.make_async_copy(source, target.at[core ^ side], sems.at[b, side])
 
     for b in reversed(range(blocks)):
         height = (b + 1) * tile
@@ -157,34 +155,54 @@
             rows = slice(a * tile, (a + 1) * tile)
             out_ref[0, cols, rows] = real[rows].T.astype(BF16)
             out_ref[1, cols, rows] = (-imag[rows].T).astype(BF16)
-
-        @pl.when(side_ref[0] == b // half)
-        def _():
-            store(b, 0).start()
-
-        @pl.when(side_ref[0] != b // half)
-        def _():
-            store(b, 1).start()
+        for mask, target in enumerate(out_hbms):
+
+            @pl.when((time ^ mask) == b)
+            def _(b=b, target=target):
+                store(b, 0, target).start()
+                store(b, 1, target).start()
 
     for b in reversed(range(blocks)):
-        store(b, 0).wait()
-
-
-def correlate(y, side, scale):
+        for side in range(2):
+            store(b, side, out_hbms[0]).wait()
+
+
+def correlate(y, me, scale, n_time):
     blocks, _, rows, samples = y.shape
     inputs = blocks * rows
-    tiles = 4
-    out = pltpu.HBM((2, 2, inputs // 2, inputs), BF16)
+    out = pltpu.HBM((2, 2, inputs // 2, inputs // n_time), BF16)
     return pl.pallas_call(
         functools.partial(correlate_kernel, scale),
         in_specs=[whole(SMEM), whole(VMEM)],
-        out_specs=whole(pltpu.HBM),
-        out_shape=out,
+        out_specs=[whole(pltpu.HBM)] * n_time,
+        out_shape=[out] * n_time,
         scratch_shapes=[VMEM((inputs, 2 * samples), BF16)] * 2
-        + [VMEM((2, inputs, inputs), BF16), pltpu.SemaphoreType.DMA((tiles,))],
+        + [VMEM((2, inputs, inputs), BF16), pltpu.SemaphoreType.DMA((n_time, 2))],
         compiler_params=params(28),
         name="correlate",
-    )(side, y)
+    )(me, y)
+
+
+def gather_kernel(*refs):
+    *part_refs, near_ref, far_ref = refs
+    for side, out_ref in enumerate((near_ref, far_ref)):
+        pieces = [ref[side].astype(F32) for ref in part_refs]
+        out_ref[...] = ((pieces[0] + pieces[1]) + (pieces[2] + pieces[3])).astype(BF16)
+
+
+def gather(pieces):
+    _, parts, rows, cols = pieces[0].shape
+    steps = 4
+    return pl.pallas_call(
+        gather_kernel,
+        grid=(steps,),
+        in_specs=[pl.BlockSpec((2, parts, rows // steps, cols), lambda i: (0, 0, i, 0))]
+        * len(pieces),
+        out_specs=[pl.BlockSpec((parts, rows // steps, cols), lambda i: (0, i, 0))] * 2,
+        out_shape=[pltpu.HBM((parts, rows, cols), BF16)] * 2,
+        compiler_params=params(16),
+        name="gather",
+    )(*pieces)
 
 
 def in_terms(x):
@@ -237,73 +255,66 @@
     )(y, z, *(sums or ()))
 
 
-def finish_kernel(scale, z_ref, near_ref, far_ref, fresh_ref, copies_ref):
-    z = advance(scale, z_ref[...], near_ref[...] + far_ref[...])
-    fresh_ref[...] = z
-    for i in range(copies_ref.shape[0]):
-        copies_ref[i] = z
-
-
-def finish(z, sums, scale, copies):
+def finish_kernel(scale, z_ref, near_ref, far_ref, fresh_ref):
+    fresh_ref[...] = advance(scale, z_ref[...], near_ref[...] + far_ref[...])
+
+
+def finish(z, sums, scale):
     return pl.pallas_call(
         functools.partial(finish_kernel, scale),
         in_specs=[whole(VMEM)] * 3,
-        out_specs=[whole(VMEM)] * 2,
-        out_shape=[
-            jax.ShapeDtypeStruct(z.shape, F32),
-            jax.ShapeDtypeStruct((copies,) + z.shape, F32),
-        ],
+        out_specs=whole(VMEM),
+        out_shape=jax.ShapeDtypeStruct(z.shape, F32),
         compiler_params=params(8),
         name="finish",
     )(z, *sums)
 
 
-def find_slot(corr_ref, channel):
-    slot = jnp.int32(0)
-    for k in range(corr_ref.shape[0]):
-        slot = jnp.where(corr_ref[k] == channel, k, slot)
-    return slot
-
-
-def choose_kernel(reach, corr_ref, beam_ref, me_ref, line_ref, *out_refs):
-    column, chip = me_ref[0] // 2, me_ref[0]
-    for (high, _), out_ref in zip(reach, out_refs):
-        peer = chip ^ (high * 2 * line_ref.shape[0])
-        slot = find_slot(corr_ref, beam_ref[peer])
-        out_ref[...] = line_ref[(slot // 2) % line_ref.shape[0]]
-
-
-def choose(corr_channels, beam_channels, me, line, reach):
-    vector = jax.ShapeDtypeStruct(line.shape[1:], F32)
+def choose_kernel(reach, source_ref, me_ref, *refs):
+    z_refs, (copies_ref, solved_ref) = refs[: len(reach)], refs[len(reach) :]
+    depth = copies_ref.shape[0]
+    chip, grp = me_ref[0], me_ref[1]
+    core, high_half = chip % 2, chip // (2 * depth)
+    vectors = [ref[...] for ref in z_refs]
+    own = jnp.full(vectors[0].shape, (core == grp).astype(jnp.int32)) == 1
+    solved_ref[...] = jnp.where(own, vectors[0], vectors[1])
+    for i in range(depth):
+        slot = source_ref[high_half * 2 * depth + 2 * i + core]
+        far, side = (slot // (2 * depth)) ^ high_half, (slot % 2) ^ grp
+        which = jnp.full(vectors[0].shape, 2 * far + side)
+        chosen = vectors[0]
+        for (high, low), vector in zip(reach[1:], vectors[1:]):
+            chosen = jnp.where(which == 2 * high + low, vector, chosen)
+        copies_ref[i] = chosen
+
+
+def choose(source, me, vectors, reach, depth):
+    shape = vectors[0].shape
     return pl.pallas_call(
         functools.partial(choose_kernel, reach),
-        in_specs=[whole(SMEM)] * 3 + [whole(VMEM)],
-        out_specs=[whole(VMEM)] * len(reach),
-        out_shape=[vector] * len(reach),
+        in_specs=[whole(SMEM)] * 2 + [whole(VMEM)] * len(reach),
+        out_specs=[whole(VMEM)] * 2,
+        out_shape=[
+            jax.ShapeDtypeStruct((depth,) + shape, F32),
+            jax.ShapeDtypeStruct(shape, F32),
+        ],
         compiler_params=params(8),
         name="choose",
-    )(corr_channels, beam_channels, me, line)
-
-
-def beam_kernel(
-    reach, corr_ref, beam_ref, me_ref, *refs
-):
-    gain_refs = refs[: len(reach)]
-    cos_ref, sin_ref, y_ref, own_hbm, away_ref, own_ref, sems = refs[len(reach) :]
-    out_refs = (own_ref, away_ref)
-    slot = find_slot(corr_ref, beam_ref[me_ref[0]])
-    half_ring = corr_ref.shape[0] // 2
-    far = (slot // half_ring) ^ (me_ref[0] // half_ring)
-    side = (slot % 2) ^ me_ref[1]
-    gains = gain_refs[0][...]
-    for (high, low), ref in zip(reach[1:], gain_refs[1:]):
-        hit = ((far == high) & (side == low)).astype(jnp.int32)
-        gains = jnp.where(jnp.full(gains.shape, hit) == 1, ref[...], gains)
+    )(source, me, *vectors)
+
+
+def beam_kernel(turn, source_ref, me_ref, line_ref, cos_ref, sin_ref, y_ref, *refs):
+    out_ref = refs[0] if turn else refs[1]
+    slot = source_ref[me_ref[0]]
+    gains = line_ref[(slot // 2) % line_ref.shape[0]]
     blocks, _, rows, samples = y_ref.shape
     stations = blocks // 2 * rows
-    beams = away_ref.shape[2]
+    beams = out_ref.shape[2]
     factor = 1.0 / math.sqrt(stations)
+    half = pl.ds(pl.multiple_of((me_ref[1] ^ turn) * beams, beams), beams)
+    cosine, sine = cos_ref[half, :], sin_ref[half, :]
     span = pl.ds(pl.multiple_of(me_ref[1] * samples, samples), samples)
+    dot = functools.partial(jnp.dot, preferred_element_type=F32)
     stores = []
     for pol in range(2):
         gain_r = gains[0:1, pol * stations : (pol + 1) * stations]
@@ -312,40 +323,39 @@
         along_r, along_i = gain_r / denom, gain_i / denom
         y_r = y_ref[pol * blocks // 2 : (pol + 1) * blocks // 2, 0].reshape(stations, samples)
         y_i = y_ref[pol * blocks // 2 : (pol + 1) * blocks // 2, 1].reshape(stations, samples)
-        for turn, out_ref in enumerate(out_refs):
-            half = pl.ds(pl.multiple_of((me_ref[1] ^ turn) * beams, beams), beams)
-            cosine, sine = cos_ref[half, :], sin_ref[half, :]
-            w_r = ((cosine * along_r - sine * along_i) * factor).astype(BF16)
-            w_i = (-(cosine * along_i + sine * along_r) * factor).astype(BF16)
-            dot = functools.partial(jnp.dot, preferred_element_type=F32)
-            out_ref[pol, 0] = (dot(w_r, y_r) - dot(w_i, y_i)).astype(BF16)
-            out_ref[pol, 1] = (dot(w_i, y_r) + dot(w_r, y_i)).astype(BF16)
-            if turn == 0:
-                store = pltpu.make_async_copy(
-                    own_ref.at[pol], own_hbm.at[pol, :, :, span], sems.at[pol]
-                )
-                store.start()
-                stores.append(store)
+        w_r = ((cosine * along_r - sine * along_i) * factor).astype(BF16)
+        w_i = (-(cosine * along_i + sine * along_r) * factor).astype(BF16)
+        out_ref[pol, 0] = (dot(w_r, y_r) - dot(w_i, y_i)).astype(BF16)
+        out_ref[pol, 1] = (dot(w_i, y_r) + dot(w_r, y_i)).astype(BF16)
+        if not turn:
+            store = pltpu.make_async_copy(
+                out_ref.at[pol], refs[0].at[pol, :, :, span], refs[2].at[pol]
+            )
+            store.start()
+            stores.append(store)
     for store in stores:
         store.wait()
 
 
-def beamform(reach, corr_channels, beam_channels, me, gains, cosine, sine, y, groups):
+def beamform(turn, source, me, line, cosine, sine, y, groups):
     samples = y.shape[3]
     beams = cosine.shape[0] // groups
     shape = (2, 2, beams, samples)
-    return pl.pallas_call(
-        functools.partial(beam_kernel, reach),
-        in_specs=[whole(SMEM)] * 3 + [whole(VMEM)] * (3 + len(reach)),
-        out_specs=[whole(pltpu.HBM), whole(VMEM)],
-        out_shape=[
-            pltpu.HBM((2, 2, beams, groups * samples), BF16),
-            jax.ShapeDtypeStruct(shape, BF16),
-        ],
-        scratch_shapes=[VMEM(shape, BF16), pltpu.SemaphoreType.DMA((2,))],
+    if turn:
+        out_spec, out_shape, scratch = whole(VMEM), jax.ShapeDtypeStruct(shape, BF16), []
+    else:
+        out_spec = whole(pltpu.HBM)
+        out_shape = pltpu.HBM((2, 2, beams, groups * samples), BF16)
+        scratch = [VMEM(shape, BF16), pltpu.SemaphoreType.DMA((2,))]
+    return pl.pallas_call(
+        functools.partial(beam_kernel, turn),
+        in_specs=[whole(SMEM)] * 2 + [whole(VMEM)] * 4,
+        out_specs=out_spec,
+        out_shape=out_shape,
+        scratch_shapes=scratch,
         compiler_params=params(16),
         name="beamform",
-    )(corr_channels, beam_channels, me, *gains, cosine, sine, y)
+    )(source, me, line, cosine, sine, y)
 
 
 def place_kernel(me_ref, own_hbm, other_ref, out_hbm, sem):
@@ -369,29 +379,23 @@
     )(me, own, other)
 
 
-def join_kernel(near_ref, far_ref, z_ref, vis_ref, solved_ref):
+def join_kernel(near_ref, far_ref, vis_ref):
     vis_ref[...] = near_ref[...].astype(F32) + far_ref[...].astype(F32)
 
-    @pl.when(pl.program_id(0) == 0)
-    def _():
-        solved_ref[...] = z_ref[...]
-
-
-def join(near, far, z):
+
+def join(near, far):
     parts, rows, cols = near.shape
     steps = 4
     block = pl.BlockSpec((parts, rows // steps, cols), lambda i: (0, i, 0))
-    fixed = pl.BlockSpec(z.shape, lambda i: (0, 0))
-    near, far = (pltpu.with_memory_space_constraint(x, pltpu.HBM) for x in (near, far))
     return pl.pallas_call(
         join_kernel,
         grid=(steps,),
-        in_specs=[block, block, fixed],
-        out_specs=[block, fixed],
-        out_shape=[pltpu.HBM(near.shape, F32), pltpu.HBM(z.shape, F32)],
+        in_specs=[block, block],
+        out_specs=block,
+        out_shape=pltpu.HBM(near.shape, F32),
         compiler_params=params(8),
         name="join",
-    )(near, far, z)
+    )(near, far)
 
 
 def swap(x, axis, mask):
@@ -435,7 +439,7 @@
     total = samples * n_time
     core = freq_index % 2
 
-    me = jnp.stack([freq_index, group_index]).astype(jnp.int32)
+    me = jnp.stack([freq_index, group_index, lax.axis_index("tm")]).astype(jnp.int32)
     base = ((freq_index * n_group + group_index) * rows).astype(jnp.int32).reshape(1)
 
     corr_send = ingest(
@@ -458,47 +462,48 @@
     cosine, sine = jnp.cos(phase), jnp.sin(phase)
 
     z = cross(prior_gains[0], 0)
-    beam_send, corr_y, z, cosine, sine = lax.optimization_barrier(
-        (beam_send, corr_y, z, cosine, sine)
+    slot = lax.broadcasted_iota(jnp.int32, (slots, slots), 1)
+    same = corr_channels[None, :] == beam_channels[:, None]
+    source = jnp.sum(jnp.where(same, slot, 0), axis=1)
+    beam_send, corr_y, z, cosine, sine, source, me = lax.optimization_barrier(
+        (beam_send, corr_y, z, cosine, sine, source, me)
     )
     beam_y = lax.all_to_all(beam_send, WIDE, split_axis=0, concat_axis=0, tiled=True)
 
     scale = float(inputs) / total
     part = apply_visibilities(corr_y, z, None, scale)
 
-    halves = correlate(corr_y, core.astype(jnp.int32).reshape(1), 1.0 / total)
-    halves = lax.psum_scatter(halves, "tm", scatter_dimension=3, tiled=True)
+    pieces = correlate(corr_y, me, 1.0 / total, n_time)
+    pieces = [pieces[0]] + [swap(x, "tm", m + 1) for m, x in enumerate(pieces[1:])]
 
     sums = exchange(part)
     for _ in range(ITERS - 1):
         part, z = apply_visibilities(corr_y, z, sums, scale)
         sums = exchange(part)
     depth = slots // 4
-    z, copies = finish(z, sums, scale, depth)
-    z, halves = lax.optimization_barrier((z, halves))
-    near, far, solved = cross(halves[0], 0), cross(halves[1], 1), cross(z, 0)
+    z = finish(z, sums, scale)
+    reach = [(0, 0), (0, 1), (1, 0), (1, 1)]
+    half_ring = slots // 2 * n_group
+    vectors = [z] + [swap(z, WIDE, high * half_ring + low) for high, low in reach[1:]]
+    copies, solved = choose(source, me, vectors, reach, depth)
+    copies, near, far = lax.optimization_barrier((copies, *gather(pieces)))
+    near, far = cross(near, 0), cross(far, 1)
     copies, beam_y = lax.optimization_barrier((copies, beam_y))
-    line = [
+    groups = [
         [high * 2 * depth + 2 * i + c for i in range(depth)]
         for high in range(2)
         for c in range(2)
     ]
     line = lax.all_to_all(
-        copies, "freq", split_axis=0, concat_axis=0, axis_index_groups=line, tiled=True
-    )
-    reach = [(0, 0), (0, 1), (1, 0), (1, 1)]
-    picks = choose(corr_channels, beam_channels, me, line, reach)
-    gains = [picks[0]] + [
-        swap(pick, WIDE, high * 8 * depth // 2 + low)
-        for (high, low), pick in zip(reach[1:], picks[1:])
-    ]
-    gains, near, far, solved = lax.optimization_barrier((gains, near, far, solved))
-    visibilities, solved = join(near, far, solved)
-
-    own, away = beamform(
-        reach, corr_channels, beam_channels, me, gains, cosine, sine, beam_y, n_group
-    )
-    beams = place(me, own, swap(away, "grp", 1))
+        copies, "freq", split_axis=0, concat_axis=0, axis_index_groups=groups, tiled=True
+    )
+
+    line, near, far = lax.optimization_barrier((line, near, far))
+    away = beamform(1, source, me, line, cosine, sine, beam_y, n_group)
+    other = swap(away, "grp", 1)
+    own = beamform(0, source, me, line, cosine, sine, beam_y, n_group)
+    visibilities = join(near, far)
+    beams = place(me, own, other)
     return visibilities[None], solved[None], beams[None]
 
 

time: 187 us -> 213 us (1.14)
  waiting for transfers between devices: 76.9 us -> 112 us
  between operations: 15.1 us -> 1.69 us
  starting transfers between devices: 61.1 us -> 65.1 us
  Pallas kernels: 24.7 us -> 27.9 us
  local copies, waits for them, and re-layouts: 4.35 us -> 2.11 us
    ppermute x16 -> x19, waiting for transfers between devices: 30.1 us -> 66.1 us  [swap(): return lax.ppermute(x, axis, [(i, i ^ mask) for i in range(n)])]
    all_to_all x1, waiting for transfers between devices: 7.07 us -> 0.77 us  [body(): lax.all_to_all(copies, 'freq', split_axis=0, concat_axis=0, axis_index_gr...]
    ppermute x16 -> x19, starting transfers between devices: 21.8 us -> 28 us  [swap(): return lax.ppermute(x, axis, [(i, i ^ mask) for i in range(n)])]
    ppermute x4 -> x3, waiting for transfers between devices: 1.31 us -> 6.47 us  [cross(): return lax.ppermute(x, WIDE, pairs)]
    ppermute x4 -> x3, starting transfers between devices: 12.3 us -> 10 us  [cross(): return lax.ppermute(x, WIDE, pairs)]
    squeeze x1 -> x0, local copies, waits for them, and re-layouts: 2.23 us -> none  [body(): near, far, solved = (cross(halves[0], 0), cross(halves[1], 1), cross(z, 0))]
    pallas_call x2 -> x4, Pallas kernels: 7.2 us -> 9.28 us  [the longest x2 5.56 us: beamform(): pl.pallas_call(functools.partial(beam_kernel, turn), in_specs=[whole(SMEM...]
  transfers between devices with their start and end apart: 24 -> 25, of which waited for: 16 -> 19; matrix products, arithmetic and copies ran while one was open for 3% -> 2% of each run, Pallas kernels for 7% -> 10%
where the time goes in v5:
time: 213 us; the launch traced here: 211 us
  waiting for transfers between devices  112 us (53%)
  starting transfers between devices  65.1 us (31%)
  Pallas kernels  27.9 us (13%)
  other arithmetic  2.28 us (1%)
    ppermute x19, waiting for transfers between devices, swap(): return lax.ppermute(x, axis, [(i, i ^ mask) for i in range(n)])  66.1 us
    all_to_all x1, waiting for transfers between devices, body(): lax.all_to_all(corr_send, WIDE, split_axis=0, concat_axis=0, tiled=True)  38.4 us
    ppermute x19, starting transfers between devices, swap(): return lax.ppermute(x, axis, [(i, i ^ mask) for i in range(n)])  28 us
    all_to_all x1, starting transfers between devices, body(): lax.all_to_all(corr_send, WIDE, split_axis=0, concat_axis=0, tiled=True)  13.3 us
    ppermute x3, starting transfers between devices, cross(): return lax.ppermute(x, WIDE, pairs)  10 us
    all_to_all x1, starting transfers between devices, body(): lax.all_to_all(beam_send, WIDE, split_axis=0, concat_axis=0, tiled=True)  7.35 us
    ppermute x3, waiting for transfers between devices, cross(): return lax.ppermute(x, WIDE, pairs)  6.47 us
    all_to_all x1, starting transfers between devices, body(): lax.all_to_all(copies, 'freq', split_axis=0, concat_axis=0, axis_index_gr...  6.39 us
  transfers between devices with their start and end apart: 25, of which 19 were waited for; matrix products, arithmetic and copies ran while one was open for 2% of the time, Pallas kernels for 10%

profile of v5, /device:TPU:1, one launch (start us, length us, event | category | flops | bytes accessed | tf_op | source)
XLA Modules:
  0.0 210.7 jit_solution(5366928223698871946)
XLA Ops:
  0.6 3.1 %ingest.3 = bf16[32,2,2,16,512]{4,3,2,1,0:T(8,128)(2,1)} custom-call(s32[1]{0:T(128)} %bitcast.base_ref, s32[32]{0:T(128)} %chan_hbm.3, s32[512]{0:T(512)} %map_hbm.3, s32[512]{0:T(512)} %flag_hbm.3, bf16[32,2,16,1024]{3,2,1,0:T(8,128)(2,1)} %volts_hbm.3), custom_call_target="tpu_custom_call" | custom-call | tf_op jit(solution)/shard_map/ingest/pallas_call | solution.py:93
  3.8 13.3 %all-to-all-start = ((bf16[64,2,16,512]{3,2,1,0:T(8,128)(2,1)}), bf16[64,2,16,512]{3,2,1,0:T(8,128)(2,1)S(1)}, u32[]{:S(2)}, u32[]{:S(2)}) async-start(bf16[64,2,16,512]{3,2,1,0:T(8,128)(2,1)} %bitcast.15), calls=%async_computation | async-start | bytes 4194304 | tf_op jit(solution)/shard_map/all_to_all | solution.py:449
  17.1 3.5 %collective-permute-start = (f32[2,1024]{1,0:T(2,128)S(1)}, f32[2,1024]{1,0:T(2,128)S(1)}, u32[]{:S(2)}, u32[]{:S(2)}) collective-permute-start(f32[2,1024]{1,0:T(2,128)S(1)} %bitcast.21), channel_id=1, source_target_pairs={{0,0},{1,8},{8,1},{9,9},{16,16},{17,24},{24,17},{25,25},{32,32},{3... | collective-permute-start | bytes 24584 | tf_op jit(solution)/shard_map/ppermute | solution.py:418
  23.6 2.0 fusion
  25.6 3.1 %ingest.2 = bf16[32,2,2,16,512]{4,3,2,1,0:T(8,128)(2,1)} custom-call(s32[1]{0:T(128)} %bitcast.base_ref, s32[32]{0:T(128)} %chan_hbm.2, s32[512]{0:T(512)} %map_hbm.3, s32[512]{0:T(512)} %flag_hbm.3, bf16[32,2,16,1024]{3,2,1,0:T(8,128)(2,1)} %volts_hbm.3), custom_call_target="tpu_custom_call" | custom-call | tf_op jit(solution)/shard_map/ingest/pallas_call | solution.py:93
  28.7 38.4 %all-to-all-done.y_ref = bf16[64,2,16,512]{3,2,1,0:T(8,128)(2,1)S(1)} async-done(((bf16[64,2,16,512]{3,2,1,0:T(8,128)(2,1)}), bf16[64,2,16,512]{3,2,1,0:T(8,128)(2,1)S(1)}, u32[]{:S(2)}, u32[]{:S(2)}) %all-to-all-start) | async-done | bytes 2097184 | tf_op jit(solution)/shard_map/all_to_all | solution.py:449
  67.0 7.3 %all-to-all-start.1 = ((bf16[64,2,16,512]{3,2,1,0:T(8,128)(2,1)}), bf16[64,2,16,512]{3,2,1,0:T(8,128)(2,1)}, u32[]{:S(2)}, u32[]{:S(2)}) async-start(bf16[64,2,16,512]{3,2,1,0:T(8,128)(2,1)} %bitcast.14), calls=%async_computation.1 | async-start | bytes 4194304 | tf_op jit(solution)/shard_map/all_to_all | solution.py:471
  74.4 5.4 %correlate.1 = (bf16[2,2,512,256]{3,2,1,0:T(8,128)(2,1)}, bf16[2,2,512,256]{3,2,1,0:T(8,128)(2,1)}, bf16[2,2,512,256]{3,2,1,0:T(8,128)(2,1)}, bf16[2,2,512,256]{3,2,1,0:T(8,128)(2,1)}) custom-call(s32[3]{0:T(128)S(1)} %pad_add_fusion.me_ref, bf16[64,2,16,512]{3,2,1,0:T(8,128)(2,1)S(1)} %all-to-all-done.y_ref), custom_call_target="tpu_custom_call" | custom-call | tf_op jit(solution)/shard_map/correlate/pallas_call | solution.py:174
  81.1 2.4 %collective-permute-start.17 = (bf16[2,2,512,256]{3,2,1,0:T(8,128)(2,1)}, bf16[2,2,512,256]{3,2,1,0:T(8,128)(2,1)S(1)}, u32[]{:S(2)}, u32[]{:S(2)}) collective-permute-start(bf16[2,2,512,256]{3,2,1,0:T(8,128)(2,1)} %get-tuple-element.45), channel_id=1, source_target_pairs={{0,4},{2,6},{4,0},{6,2},{1,5},{3,7},{5,1},{7,3},{8,12},{10,14},{12... | collective-permute-start | bytes 3145736 | tf_op jit(solution)/shard_map/ppermute | solution.py:403
  87.1 39.9 %collective-permute-done.2 = f32[2,1024]{1,0:T(2,128)S(1)} collective-permute-done((f32[2,1024]{1,0:T(2,128)S(1)}, f32[2,1024]{1,0:T(2,128)S(1)}, u32[]{:S(2)}, u32[]{:S(2)}) %collective-permute-start.2) | collective-permute-done | bytes 8224 | tf_op jit(solution)/shard_map/ppermute | solution.py:403
  127.0 2.4 %collective-permute-start.3 = (f32[2,1024]{1,0:T(2,128)S(1)}, f32[2,1024]{1,0:T(2,128)S(1)}, u32[]{:S(2)}, u32[]{:S(2)}) collective-permute-start(f32[2,1024]{1,0:T(2,128)S(1)} %add.72.refs_0_), channel_id=1, source_target_pairs={{0,6},{2,4},{4,2},{6,0},{1,7},{3,5},{5,3},{7,1},{8,14},{10,12},{12... | collective-permute-start | bytes 24584 | tf_op jit(solution)/shard_map/ppermute | solution.py:403
  129.5 1.7 collective-permute-done.3.refs_1_
  132.3 2.2 %collective-permute-start.4 = (f32[2,1024]{1,0:T(2,128)S(1)}, f32[2,1024]{1,0:T(2,128)S(1)}, u32[]{:S(2)}, u32[]{:S(2)}) collective-permute-start(f32[2,1024]{1,0:T(2,128)S(1)} %get-tuple-element.37), channel_id=1, source_target_pairs={{0,8},{8,0},{16,24},{24,16},{32,40},{40,32},{48,56},{56,48},{64,72... | collective-permute-start | bytes 24584 | tf_op jit(solution)/shard_map/ppermute | solution.py:403
  135.3 2.5 %collective-permute-done.5 = f32[2,1024]{1,0:T(2,128)S(1)} collective-permute-done((f32[2,1024]{1,0:T(2,128)S(1)}, f32[2,1024]{1,0:T(2,128)S(1)}, u32[]{:S(2)}, u32[]{:S(2)}) %collective-permute-start.5) | collective-permute-done | bytes 8224 | tf_op jit(solution)/shard_map/ppermute | solution.py:403
  137.8 2.5 %collective-permute-start.6 = (f32[2,1024]{1,0:T(2,128)S(1)}, f32[2,1024]{1,0:T(2,128)S(1)}, u32[]{:S(2)}, u32[]{:S(2)}) collective-permute-start(f32[2,1024]{1,0:T(2,128)S(1)} %add.74.refs_0_), channel_id=1, source_target_pairs={{0,6},{2,4},{4,2},{6,0},{1,7},{3,5},{5,3},{7,1},{8,14},{10,12},{12... | collective-permute-start | bytes 24584 | tf_op jit(solution)/shard_map/ppermute | solution.py:403
  142.7 2.7 %collective-permute-start.7 = (f32[2,1024]{1,0:T(2,128)S(1)}, f32[2,1024]{1,0:T(2,128)S(1)}, u32[]{:S(2)}, u32[]{:S(2)}) collective-permute-start(f32[2,1024]{1,0:T(2,128)S(1)} %get-tuple-element.39), channel_id=1, source_target_pairs={{0,8},{8,0},{16,24},{24,16},{32,40},{40,32},{48,56},{56,48},{64,72... | collective-permute-start | bytes 24584 | tf_op jit(solution)/shard_map/ppermute | solution.py:403
  146.2 2.5 %collective-permute-done.8 = f32[2,1024]{1,0:T(2,128)S(1)} collective-permute-done((f32[2,1024]{1,0:T(2,128)S(1)}, f32[2,1024]{1,0:T(2,128)S(1)}, u32[]{:S(2)}, u32[]{:S(2)}) %collective-permute-start.8) | collective-permute-done | bytes 8224 | tf_op jit(solution)/shard_map/ppermute | solution.py:403
  148.7 2.5 %collective-permute-start.9 = (f32[2,1024]{1,0:T(2,128)S(1)}, f32[2,1024]{1,0:T(2,128)S(1)}, u32[]{:S(2)}, u32[]{:S(2)}) collective-permute-start(f32[2,1024]{1,0:T(2,128)S(1)} %add.76.refs_0_), channel_id=1, source_target_pairs={{0,6},{2,4},{4,2},{6,0},{1,7},{3,5},{5,3},{7,1},{8,14},{10,12},{12... | collective-permute-start | bytes 24584 | tf_op jit(solution)/shard_map/ppermute | solution.py:403
  153.6 2.7 %collective-permute-start.10 = (f32[2,1024]{1,0:T(2,128)S(1)}, f32[2,1024]{1,0:T(2,128)S(1)}, u32[]{:S(2)}, u32[]{:S(2)}) collective-permute-start(f32[2,1024]{1,0:T(2,128)S(1)} %get-tuple-element.41), channel_id=1, source_target_pairs={{0,8},{8,0},{16,24},{24,16},{32,40},{40,32},{48,56},{56,48},{64,72... | collective-permute-start | bytes 24584 | tf_op jit(solution)/shard_map/ppermute | solution.py:403
  157.1 2.5 %collective-permute-done.11 = f32[2,1024]{1,0:T(2,128)S(1)} collective-permute-done((f32[2,1024]{1,0:T(2,128)S(1)}, f32[2,1024]{1,0:T(2,128)S(1)}, u32[]{:S(2)}, u32[]{:S(2)}) %collective-permute-start.11) | collective-permute-done | bytes 8224 | tf_op jit(solution)/shard_map/ppermute | solution.py:403
  159.6 2.5 %collective-permute-start.12 = (f32[2,1024]{1,0:T(2,128)S(1)}, f32[2,1024]{1,0:T(2,128)S(1)}, u32[]{:S(2)}, u32[]{:S(2)}) collective-permute-start(f32[2,1024]{1,0:T(2,128)S(1)} %add.78.near_ref), channel_id=1, source_target_pairs={{0,6},{2,4},{4,2},{6,0},{1,7},{3,5},{5,3},{7,1},{8,14},{10,12},{12... | collective-permute-start | bytes 24584 | tf_op jit(solution)/shard_map/ppermute | solution.py:403
  163.5 2.8 %collective-permute-start.15 = (f32[2,1024]{1,0:T(2,128)S(1)}, f32[2,1024]{1,0:T(2,128)S(1)}, u32[]{:S(2)}, u32[]{:S(2)}) collective-permute-start(f32[2,1024]{1,0:T(2,128)S(1)} %finish.1.refs_0_), channel_id=1, source_target_pairs={{0,129},{1,128},{8,137},{9,136},{16,145},{17,144},{24,153},{25,152... | collective-permute-start | bytes 24584 | tf_op jit(solution)/shard_map/ppermute | solution.py:403
  167.5 2.8 %collective-permute-done.14.refs_2_ = f32[2,1024]{1,0:T(2,128)S(1)} collective-permute-done((f32[2,1024]{1,0:T(2,128)S(1)}, f32[2,1024]{1,0:T(2,128)S(1)}, u32[]{:S(2)}, u32[]{:S(2)}) %collective-permute-start.14) | collective-permute-done | bytes 8224 | tf_op jit(solution)/shard_map/ppermute | solution.py:403
  171.6 2.1 gather.8
  173.6 6.4 %collective-permute-start.19 = (bf16[2,512,256]{2,1,0:T(8,128)(2,1)}, bf16[2,512,256]{2,1,0:T(8,128)(2,1)S(1)}, u32[]{:S(2)}, u32[]{:S(2)}) collective-permute-start(bf16[2,512,256]{2,1,0:T(8,128)(2,1)} %get-tuple-element.52), channel_id=1, source_target_pairs={{0,0},{1,8},{8,1},{9,9},{16,16},{17,24},{24,17},{25,25},{32,32},{3... | collective-permute-start | bytes 1572872 | tf_op jit(solution)/shard_map/ppermute | solution.py:418
  180.2 6.4 %all-to-all-start.2 = ((f32[8,2,1024]{2,1,0:T(2,128)}), f32[8,2,1024]{2,1,0:T(2,128)S(1)}, u32[]{:S(2)}, u32[]{:S(2)}) async-start(f32[8,2,1024]{2,1,0:T(2,128)} %get-tuple-element.51), calls=%async_computation.2 | async-start | bytes 131072 | tf_op jit(solution)/shard_map/all_to_all | solution.py:497
  186.5 5.2 %collective-permute-done.19.near_ref = bf16[2,512,256]{2,1,0:T(8,128)(2,1)S(1)} collective-permute-done((bf16[2,512,256]{2,1,0:T(8,128)(2,1)}, bf16[2,512,256]{2,1,0:T(8,128)(2,1)S(1)}, u32[]{:S(2)}, u32[]{:S(2)}) %collective-permute-start.19) | collective-permute-done | bytes 524320 | tf_op jit(solution)/shard_map/ppermute | solution.py:418
  193.8 2.4 %beamform.3 = bf16[2,2,128,512]{3,2,1,0:T(8,128)(2,1)S(1)} custom-call(s32[32]{0:T(128)S(1)} %select_reduce_fusion.source_ref, s32[3]{0:T(128)S(1)} %pad_add_fusion.me_ref, f32[8,2,1024]{2,1,0:T(2,128)S(1)} %all-to-all-done.2.line_ref, f32[256,512]{1,0:T(8,128)S(1)} %get-tuple-element.58.cos_ref, f32[256,512]{1,0:T(8,128)S(1)} %get-tuple-element.59.sin_ref, ...), custom_call_target="tpu_custom_call" | custom-call | tf_op jit(solution)/shard_map/beamform/pallas_call | solution.py:350
  196.2 1.6 collective-permute-start.21
  197.9 3.1 %beamform.2.own_hbm = bf16[2,2,128,1024]{3,2,1,0:T(8,128)(2,1)} custom-call(s32[32]{0:T(128)S(1)} %select_reduce_fusion.source_ref, s32[3]{0:T(128)S(1)} %pad_add_fusion.me_ref, f32[8,2,1024]{2,1,0:T(2,128)S(1)} %all-to-all-done.2.line_ref, f32[256,512]{1,0:T(8,128)S(1)} %get-tuple-element.58.cos_ref, f32[256,512]{1,0:T(8,128)S(1)} %get-tuple-element.59.sin_ref, ...), custom_call_target="tpu_custom_call" | custom-call | tf_op jit(solution)/shard_map/beamform/pallas_call | solution.py:350
  201.0 1.6 join.1
  202.7 6.6 %collective-permute-done.21.other_ref = bf16[2,2,128,512]{3,2,1,0:T(8,128)(2,1)S(1)} collective-permute-done((bf16[2,2,128,512]{3,2,1,0:T(8,128)(2,1)S(1)}, bf16[2,2,128,512]{3,2,1,0:T(8,128)(2,1)S(1)}, u32[]{:S(2)}, u32[]{:S(2)}) %collective-permute-start.21) | collective-permute-done | bytes 524320 | tf_op jit(solution)/shard_map/ppermute | solution.py:403
  (63 shorter events, 22.9 us)
Async XLA Ops:
  3.7 13.4 %copy-start.6 = (f32[1,2,1024]{2,1,0:T(2,128)S(1)}, f32[1,2,1024]{2,1,0:T(2,128)}, u32[]{:S(2)}) copy-start(f32[1,2,1024]{2,1,0:T(2,128)} %param.9) | copy-start | bytes 24580
  3.7 16.9 %copy-start.5 = (s32[32]{0:T(128)S(1)}, s32[32]{0:T(128)}, u32[]{:S(2)}) copy-start(s32[32]{0:T(128)} %chan_hbm.2) | copy-start | bytes 388
  3.7 18.1 %copy-start.2 = (f32[2,512]{1,0:T(2,128)S(1)}, f32[2,512]{1,0:T(2,128)}, u32[]{:S(2)}) copy-start(f32[2,512]{1,0:T(2,128)} %param.12) | copy-start | bytes 12292
  3.7 18.2 %copy-start.1 = (s32[512]{0:T(512)S(1)}, s32[512]{0:T(512)}, u32[]{:S(2)}) copy-start(s32[512]{0:T(512)} %map_hbm.3) | copy-start | bytes 6148
  3.7 19.3 %copy-start.4 = (s32[32]{0:T(128)S(1)}, s32[32]{0:T(128)}, u32[]{:S(2)}) copy-start(s32[32]{0:T(128)} %chan_hbm.3) | copy-start | bytes 388
  3.8 19.8 %copy-start.3 = (s32[2,256]{1,0:T(2,128)S(1)}, s32[2,256]{1,0:T(2,128)}, u32[]{:S(2)}) copy-start(s32[2,256]{1,0:T(2,128)} %param.13) | copy-start | bytes 6148
  3.8 63.3 %all-to-all-start = ((bf16[64,2,16,512]{3,2,1,0:T(8,128)(2,1)}), bf16[64,2,16,512]{3,2,1,0:T(8,128)(2,1)S(1)}, u32[]{:S(2)}, u32[]{:S(2)}) async-start(bf16[64,2,16,512]{3,2,1,0:T(8,128)(2,1)} %bitcast.15), calls=%async_computation | async-start | bytes 4194304 | tf_op jit(solution)/shard_map/all_to_all | solution.py:449
  17.1 11.6 %collective-permute-start = (f32[2,1024]{1,0:T(2,128)S(1)}, f32[2,1024]{1,0:T(2,128)S(1)}, u32[]{:S(2)}, u32[]{:S(2)}) collective-permute-start(f32[2,1024]{1,0:T(2,128)S(1)} %bitcast.21), channel_id=1, source_target_pairs={{0,0},{1,8},{8,1},{9,9},{16,16},{17,24},{24,17},{25,25},{32,32},{3... | collective-permute-start | bytes 24584 | tf_op jit(solution)/shard_map/ppermute | solution.py:418
  67.0 113.1 %all-to-all-start.1 = ((bf16[64,2,16,512]{3,2,1,0:T(8,128)(2,1)}), bf16[64,2,16,512]{3,2,1,0:T(8,128)(2,1)}, u32[]{:S(2)}, u32[]{:S(2)}) async-start(bf16[64,2,16,512]{3,2,1,0:T(8,128)(2,1)} %bitcast.14), calls=%async_computation.1 | async-start | bytes 4194304 | tf_op jit(solution)/shard_map/all_to_all | solution.py:471
  79.8 91.7 %collective-permute-start.16 = (bf16[2,2,512,256]{3,2,1,0:T(8,128)(2,1)}, bf16[2,2,512,256]{3,2,1,0:T(8,128)(2,1)S(1)}, u32[]{:S(2)}, u32[]{:S(2)}) collective-permute-start(bf16[2,2,512,256]{3,2,1,0:T(8,128)(2,1)} %get-tuple-element.44), channel_id=1, source_target_pairs={{0,2},{2,0},{4,6},{6,4},{1,3},{3,1},{5,7},{7,5},{8,10},{10,8},{12,... | collective-permute-start | bytes 3145736 | tf_op jit(solution)/shard_map/ppermute | solution.py:403
  81.1 90.4 %collective-permute-start.17 = (bf16[2,2,512,256]{3,2,1,0:T(8,128)(2,1)}, bf16[2,2,512,256]{3,2,1,0:T(8,128)(2,1)S(1)}, u32[]{:S(2)}, u32[]{:S(2)}) collective-permute-start(bf16[2,2,512,256]{3,2,1,0:T(8,128)(2,1)} %get-tuple-element.45), channel_id=1, source_target_pairs={{0,4},{2,6},{4,0},{6,2},{1,5},{3,7},{5,1},{7,3},{8,12},{10,14},{12... | collective-permute-start | bytes 3145736 | tf_op jit(solution)/shard_map/ppermute | solution.py:403
  83.6 88.0 %collective-permute-start.18 = (bf16[2,2,512,256]{3,2,1,0:T(8,128)(2,1)}, bf16[2,2,512,256]{3,2,1,0:T(8,128)(2,1)S(1)}, u32[]{:S(2)}, u32[]{:S(2)}) collective-permute-start(bf16[2,2,512,256]{3,2,1,0:T(8,128)(2,1)} %get-tuple-element.46), channel_id=1, source_target_pairs={{0,6},{2,4},{4,2},{6,0},{1,7},{3,5},{5,3},{7,1},{8,14},{10,12},{12... | collective-permute-start | bytes 3145736 | tf_op jit(solution)/shard_map/ppermute | solution.py:403
  84.8 2.3 %collective-permute-start.1 = (f32[2,1024]{1,0:T(2,128)S(1)}, f32[2,1024]{1,0:T(2,128)S(1)}, u32[]{:S(2)}, u32[]{:S(2)}) collective-permute-start(f32[2,1024]{1,0:T(2,128)S(1)} %apply.4), channel_id=1, source_target_pairs={{0,8},{8,0},{16,24},{24,16},{32,40},{40,32},{48,56},{56,48},{64,72... | collective-permute-start | bytes 24584 | tf_op jit(solution)/shard_map/ppermute | solution.py:403
  87.1 39.9 %collective-permute-start.2 = (f32[2,1024]{1,0:T(2,128)S(1)}, f32[2,1024]{1,0:T(2,128)S(1)}, u32[]{:S(2)}, u32[]{:S(2)}) collective-permute-start(f32[2,1024]{1,0:T(2,128)S(1)} %add.71), channel_id=1, source_target_pairs={{0,2},{2,0},{4,6},{6,4},{1,3},{3,1},{5,7},{7,5},{8,10},{10,8},{12,... | collective-permute-start | bytes 24584 | tf_op jit(solution)/shard_map/ppermute | solution.py:403
  127.0 4.2 %collective-permute-start.3 = (f32[2,1024]{1,0:T(2,128)S(1)}, f32[2,1024]{1,0:T(2,128)S(1)}, u32[]{:S(2)}, u32[]{:S(2)}) collective-permute-start(f32[2,1024]{1,0:T(2,128)S(1)} %add.72.refs_0_), channel_id=1, source_target_pairs={{0,6},{2,4},{4,2},{6,0},{1,7},{3,5},{5,3},{7,1},{8,14},{10,12},{12... | collective-permute-start | bytes 24584 | tf_op jit(solution)/shard_map/ppermute | solution.py:403
  132.3 3.0 %collective-permute-start.4 = (f32[2,1024]{1,0:T(2,128)S(1)}, f32[2,1024]{1,0:T(2,128)S(1)}, u32[]{:S(2)}, u32[]{:S(2)}) collective-permute-start(f32[2,1024]{1,0:T(2,128)S(1)} %get-tuple-element.37), channel_id=1, source_target_pairs={{0,8},{8,0},{16,24},{24,16},{32,40},{40,32},{48,56},{56,48},{64,72... | collective-permute-start | bytes 24584 | tf_op jit(solution)/shard_map/ppermute | solution.py:403
  135.3 2.5 %collective-permute-start.5 = (f32[2,1024]{1,0:T(2,128)S(1)}, f32[2,1024]{1,0:T(2,128)S(1)}, u32[]{:S(2)}, u32[]{:S(2)}) collective-permute-start(f32[2,1024]{1,0:T(2,128)S(1)} %add.73), channel_id=1, source_target_pairs={{0,2},{2,0},{4,6},{6,4},{1,3},{3,1},{5,7},{7,5},{8,10},{10,8},{12,... | collective-permute-start | bytes 24584 | tf_op jit(solution)/shard_map/ppermute | solution.py:403
  137.8 3.7 %collective-permute-start.6 = (f32[2,1024]{1,0:T(2,128)S(1)}, f32[2,1024]{1,0:T(2,128)S(1)}, u32[]{:S(2)}, u32[]{:S(2)}) collective-permute-start(f32[2,1024]{1,0:T(2,128)S(1)} %add.74.refs_0_), channel_id=1, source_target_pairs={{0,6},{2,4},{4,2},{6,0},{1,7},{3,5},{5,3},{7,1},{8,14},{10,12},{12... | collective-permute-start | bytes 24584 | tf_op jit(solution)/shard_map/ppermute | solution.py:403
  141.5 30.0 %copy-start = (bf16[2,2,512,256]{3,2,1,0:T(8,128)(2,1)S(1)}, bf16[2,2,512,256]{3,2,1,0:T(8,128)(2,1)}, u32[]{:S(2)}) copy-start(bf16[2,2,512,256]{3,2,1,0:T(8,128)(2,1)} %get-tuple-element.43.refs_0_) | copy-start | bytes 3145732
  142.7 3.6 %collective-permute-start.7 = (f32[2,1024]{1,0:T(2,128)S(1)}, f32[2,1024]{1,0:T(2,128)S(1)}, u32[]{:S(2)}, u32[]{:S(2)}) collective-permute-start(f32[2,1024]{1,0:T(2,128)S(1)} %get-tuple-element.39), channel_id=1, source_target_pairs={{0,8},{8,0},{16,24},{24,16},{32,40},{40,32},{48,56},{56,48},{64,72... | collective-permute-start | bytes 24584 | tf_op jit(solution)/shard_map/ppermute | solution.py:403
  146.2 2.5 %collective-permute-start.8 = (f32[2,1024]{1,0:T(2,128)S(1)}, f32[2,1024]{1,0:T(2,128)S(1)}, u32[]{:S(2)}, u32[]{:S(2)}) collective-permute-start(f32[2,1024]{1,0:T(2,128)S(1)} %add.75), channel_id=1, source_target_pairs={{0,2},{2,0},{4,6},{6,4},{1,3},{3,1},{5,7},{7,5},{8,10},{10,8},{12,... | collective-permute-start | bytes 24584 | tf_op jit(solution)/shard_map/ppermute | solution.py:403
  148.7 3.7 %collective-permute-start.9 = (f32[2,1024]{1,0:T(2,128)S(1)}, f32[2,1024]{1,0:T(2,128)S(1)}, u32[]{:S(2)}, u32[]{:S(2)}) collective-permute-start(f32[2,1024]{1,0:T(2,128)S(1)} %add.76.refs_0_), channel_id=1, source_target_pairs={{0,6},{2,4},{4,2},{6,0},{1,7},{3,5},{5,3},{7,1},{8,14},{10,12},{12... | collective-permute-start | bytes 24584 | tf_op jit(solution)/shard_map/ppermute | solution.py:403
  153.6 3.6 %collective-permute-start.10 = (f32[2,1024]{1,0:T(2,128)S(1)}, f32[2,1024]{1,0:T(2,128)S(1)}, u32[]{:S(2)}, u32[]{:S(2)}) collective-permute-start(f32[2,1024]{1,0:T(2,128)S(1)} %get-tuple-element.41), channel_id=1, source_target_pairs={{0,8},{8,0},{16,24},{24,16},{32,40},{40,32},{48,56},{56,48},{64,72... | collective-permute-start | bytes 24584 | tf_op jit(solution)/shard_map/ppermute | solution.py:403
  157.1 2.5 %collective-permute-start.11 = (f32[2,1024]{1,0:T(2,128)S(1)}, f32[2,1024]{1,0:T(2,128)S(1)}, u32[]{:S(2)}, u32[]{:S(2)}) collective-permute-start(f32[2,1024]{1,0:T(2,128)S(1)} %add.77), channel_id=1, source_target_pairs={{0,2},{2,0},{4,6},{6,4},{1,3},{3,1},{5,7},{7,5},{8,10},{10,8},{12,... | collective-permute-start | bytes 24584 | tf_op jit(solution)/shard_map/ppermute | solution.py:403
  159.6 3.7 %collective-permute-start.12 = (f32[2,1024]{1,0:T(2,128)S(1)}, f32[2,1024]{1,0:T(2,128)S(1)}, u32[]{:S(2)}, u32[]{:S(2)}) collective-permute-start(f32[2,1024]{1,0:T(2,128)S(1)} %add.78.near_ref), channel_id=1, source_target_pairs={{0,6},{2,4},{4,2},{6,0},{1,7},{3,5},{5,3},{7,1},{8,14},{10,12},{12... | collective-permute-start | bytes 24584 | tf_op jit(solution)/shard_map/ppermute | solution.py:403
  163.5 3.8 %collective-permute-start.15 = (f32[2,1024]{1,0:T(2,128)S(1)}, f32[2,1024]{1,0:T(2,128)S(1)}, u32[]{:S(2)}, u32[]{:S(2)}) collective-permute-start(f32[2,1024]{1,0:T(2,128)S(1)} %finish.1.refs_0_), channel_id=1, source_target_pairs={{0,129},{1,128},{8,137},{9,136},{16,145},{17,144},{24,153},{25,152... | collective-permute-start | bytes 24584 | tf_op jit(solution)/shard_map/ppermute | solution.py:403
  166.3 4.0 %collective-permute-start.14 = (f32[2,1024]{1,0:T(2,128)S(1)}, f32[2,1024]{1,0:T(2,128)S(1)}, u32[]{:S(2)}, u32[]{:S(2)}) collective-permute-start(f32[2,1024]{1,0:T(2,128)S(1)} %finish.1.refs_0_), channel_id=1, source_target_pairs={{0,128},{1,129},{8,136},{9,137},{16,144},{17,145},{24,152},{25,153... | collective-permute-start | bytes 24584 | tf_op jit(solution)/shard_map/ppermute | solution.py:403
  167.3 3.0 %collective-permute-start.13 = (f32[2,1024]{1,0:T(2,128)S(1)}, f32[2,1024]{1,0:T(2,128)S(1)}, u32[]{:S(2)}, u32[]{:S(2)}) collective-permute-start(f32[2,1024]{1,0:T(2,128)S(1)} %finish.1.refs_0_), channel_id=1, source_target_pairs={{0,1},{1,0},{8,9},{9,8},{16,17},{17,16},{24,25},{25,24},{32,33},{3... | collective-permute-start | bytes 24584 | tf_op jit(solution)/shard_map/ppermute | solution.py:403
  173.6 18.1 %collective-permute-start.19 = (bf16[2,512,256]{2,1,0:T(8,128)(2,1)}, bf16[2,512,256]{2,1,0:T(8,128)(2,1)S(1)}, u32[]{:S(2)}, u32[]{:S(2)}) collective-permute-start(bf16[2,512,256]{2,1,0:T(8,128)(2,1)} %get-tuple-element.52), channel_id=1, source_target_pairs={{0,0},{1,8},{8,1},{9,9},{16,16},{17,24},{24,17},{25,25},{32,32},{3... | collective-permute-start | bytes 1572872 | tf_op jit(solution)/shard_map/ppermute | solution.py:418
  180.0 13.0 %collective-permute-start.20 = (bf16[2,512,256]{2,1,0:T(8,128)(2,1)}, bf16[2,512,256]{2,1,0:T(8,128)(2,1)S(1)}, u32[]{:S(2)}, u32[]{:S(2)}) collective-permute-start(bf16[2,512,256]{2,1,0:T(8,128)(2,1)} %get-tuple-element.53), channel_id=1, source_target_pairs={{0,1},{1,9},{8,0},{9,8},{16,17},{17,25},{24,16},{25,24},{32,33},{3... | collective-permute-start | bytes 1572872 | tf_op jit(solution)/shard_map/ppermute | solution.py:418
  180.2 13.6 %all-to-all-start.2 = ((f32[8,2,1024]{2,1,0:T(2,128)}), f32[8,2,1024]{2,1,0:T(2,128)S(1)}, u32[]{:S(2)}, u32[]{:S(2)}) async-start(f32[8,2,1024]{2,1,0:T(2,128)} %get-tuple-element.51), calls=%async_computation.2 | async-start | bytes 131072 | tf_op jit(solution)/shard_map/all_to_all | solution.py:497
  196.2 13.0 %collective-permute-start.21 = (bf16[2,2,128,512]{3,2,1,0:T(8,128)(2,1)S(1)}, bf16[2,2,128,512]{3,2,1,0:T(8,128)(2,1)S(1)}, u32[]{:S(2)}, u32[]{:S(2)}) collective-permute-start(bf16[2,2,128,512]{3,2,1,0:T(8,128)(2,1)S(1)} %beamform.3), channel_id=1, source_target_pairs={{0,1},{1,0},{2,3},{3,2},{4,5},{5,4},{6,7},{7,6},{8,9},{9,8},{10,11... | collective-permute-start | bytes 1572872 | tf_op jit(solution)/shard_map/ppermute | solution.py:403

commit v6 on v5

--- a/solution.py
+++ b/solution.py
@@ -126,80 +126,56 @@
     return lax.dot_general(a, b, (((1,), (1,)), ((), ())), preferred_element_type=F32)
 
 
-def correlate_kernel(scale, me_ref, y_ref, *refs):
-    samples = y_ref.shape[3]
-    *out_hbms, left_ref, turn_ref, out_ref, sems = refs
-    inputs = left_ref.shape[0]
-    blocks = sems.shape[0]
-    tile, half = inputs // blocks, inputs // 2
-    core, time = me_ref[0] % 2, me_ref[2]
-    real, imag = load_part(y_ref, 0), load_part(y_ref, 1)
-    left_ref[:, :samples] = real
-    left_ref[:, samples:] = imag
-    turn_ref[:, :samples] = imag
-    turn_ref[:, samples:] = -real
-
-    def store(b, side, target):
-        source = out_ref.at[:, side * half : (side + 1) * half, b * tile : (b + 1) * tile]
-        return pltpu.make_async_copy(source, target.at[core ^ side], sems.at[b, side])
-
-    for b in reversed(range(blocks)):
-        height = (b + 1) * tile
-        cols = slice(b * tile, height)
-        right = left_ref[cols, :]
-        real = nt_dot(left_ref[:height, :], right) * scale
-        imag = nt_dot(turn_ref[:height, :], right) * scale
-        out_ref[0, :height, cols] = real.astype(BF16)
-        out_ref[1, :height, cols] = imag.astype(BF16)
-        for a in range(b):
-            rows = slice(a * tile, (a + 1) * tile)
-            out_ref[0, cols, rows] = real[rows].T.astype(BF16)
-            out_ref[1, cols, rows] = (-imag[rows].T).astype(BF16)
-        for mask, target in enumerate(out_hbms):
-
-            @pl.when((time ^ mask) == b)
-            def _(b=b, target=target):
-                store(b, 0, target).start()
-                store(b, 1, target).start()
-
-    for b in reversed(range(blocks)):
-        for side in range(2):
-            store(b, side, out_hbms[0]).wait()
-
-
-def correlate(y, me, scale, n_time):
-    blocks, _, rows, samples = y.shape
+def correlate_kernel(scale, mask, me_ref, *refs):
+    *y_refs, out_ref = refs
+    blocks = y_refs[0].shape[0]
+    _, height, width = out_ref.shape
+    rows = blocks * height // (height * 2)
+    cols = blocks * width // (height * 2)
+    high = pl.ds(pl.multiple_of((me_ref[0] % 2) * rows, rows), rows)
+    wide = pl.ds(pl.multiple_of((me_ref[2] ^ mask) * cols, cols), cols)
+    samples = y_refs[0].shape[3]
+    real, imag = 0.0, 0.0
+    for y_ref in y_refs:
+        left_r = y_ref[high, 0].reshape(height, samples)
+        left_i = y_ref[high, 1].reshape(height, samples)
+        right_r = y_ref[wide, 0].reshape(width, samples)
+        right_i = y_ref[wide, 1].reshape(width, samples)
+        real = real + nt_dot(left_r, right_r) + nt_dot(left_i, right_i)
+        imag = imag + nt_dot(left_i, right_r) + nt_dot(-left_r, right_i)
+    out_ref[0] = (real * scale).astype(BF16)
+    out_ref[1] = (imag * scale).astype(BF16)
+
+
+def correlate(ys, me, scale, mask, n_time):
+    blocks, _, rows, samples = ys[0].shape
     inputs = blocks * rows
-    out = pltpu.HBM((2, 2, inputs // 2, inputs // n_time), BF16)
-    return pl.pallas_call(
-        functools.partial(correlate_kernel, scale),
-        in_specs=[whole(SMEM), whole(VMEM)],
-        out_specs=[whole(pltpu.HBM)] * n_time,
-        out_shape=[out] * n_time,
-        scratch_shapes=[VMEM((inputs, 2 * samples), BF16)] * 2
-        + [VMEM((2, inputs, inputs), BF16), pltpu.SemaphoreType.DMA((n_time, 2))],
-        compiler_params=params(28),
+    return pl.pallas_call(
+        functools.partial(correlate_kernel, scale, mask),
+        in_specs=[whole(SMEM)] + [whole(VMEM)] * len(ys),
+        out_specs=whole(VMEM),
+        out_shape=jax.ShapeDtypeStruct((2, inputs // 2, inputs // n_time), BF16),
+        compiler_params=params(16),
         name="correlate",
-    )(me, y)
+    )(me, *ys)
 
 
 def gather_kernel(*refs):
-    *part_refs, near_ref, far_ref = refs
-    for side, out_ref in enumerate((near_ref, far_ref)):
-        pieces = [ref[side].astype(F32) for ref in part_refs]
-        out_ref[...] = ((pieces[0] + pieces[1]) + (pieces[2] + pieces[3])).astype(BF16)
+    *part_refs, out_ref = refs
+    pieces = [ref[...].astype(F32) for ref in part_refs]
+    out_ref[...] = ((pieces[0] + pieces[1]) + (pieces[2] + pieces[3])).astype(BF16)
 
 
 def gather(pieces):
-    _, parts, rows, cols = pieces[0].shape
-    steps = 4
+    parts, rows, cols = pieces[0].shape
+    steps = 2
+    block = pl.BlockSpec((parts, rows // steps, cols), lambda i: (0, i, 0))
     return pl.pallas_call(
         gather_kernel,
         grid=(steps,),
-        in_specs=[pl.BlockSpec((2, parts, rows // steps, cols), lambda i: (0, 0, i, 0))]
-        * len(pieces),
-        out_specs=[pl.BlockSpec((parts, rows // steps, cols), lambda i: (0, i, 0))] * 2,
-        out_shape=[pltpu.HBM((parts, rows, cols), BF16)] * 2,
+        in_specs=[block] * len(pieces),
+        out_specs=block,
+        out_shape=jax.ShapeDtypeStruct((parts, rows, cols), BF16),
         compiler_params=params(16),
         name="gather",
     )(*pieces)
@@ -223,7 +199,18 @@
     return 0.5 * (z + scale * update / power)
 
 
-def apply_kernel(scale, first, y_ref, z_ref, *refs):
+def apply_half(terms, y_ref):
+    real, imag = load_part(y_ref, 0), load_part(y_ref, 1)
+    a = add_terms(jnp.dot(terms, real, preferred_element_type=F32))
+    b = add_terms(jnp.dot(terms, imag, preferred_element_type=F32))
+    w = jnp.concatenate([a[0:1] + b[1:2], a[1:2] - b[0:1]], axis=0)
+    terms = in_terms(w)
+    c = add_terms(nt_dot(terms, real))
+    d = add_terms(nt_dot(terms, imag))
+    return jnp.concatenate([c[0:1] - d[1:2], c[1:2] + d[0:1]], axis=0)
+
+
+def apply_kernel(scale, first, mine_ref, other_ref, z_ref, *refs):
     z = z_ref[...]
     if first:
         (out_ref,) = refs
@@ -231,28 +218,21 @@
         near_ref, far_ref, out_ref, fresh_ref = refs
         z = advance(scale, z, near_ref[...] + far_ref[...])
         fresh_ref[...] = z
-    real, imag = load_part(y_ref, 0), load_part(y_ref, 1)
     terms = in_terms(z)
-    a = add_terms(jnp.dot(terms, real, preferred_element_type=F32))
-    b = add_terms(jnp.dot(terms, imag, preferred_element_type=F32))
-    w = jnp.concatenate([a[0:1] + b[1:2], a[1:2] - b[0:1]], axis=0)
-    terms = in_terms(w)
-    c = add_terms(nt_dot(terms, real))
-    d = add_terms(nt_dot(terms, imag))
-    out_ref[...] = jnp.concatenate([c[0:1] - d[1:2], c[1:2] + d[0:1]], axis=0)
-
-
-def apply_visibilities(y, z, sums, scale):
+    out_ref[...] = apply_half(terms, mine_ref) + apply_half(terms, other_ref)
+
+
+def apply_visibilities(ys, z, sums, scale):
     first = sums is None
     vector = jax.ShapeDtypeStruct(z.shape, F32)
     return pl.pallas_call(
         functools.partial(apply_kernel, scale, first),
-        in_specs=[whole(VMEM)] * (2 if first else 4),
+        in_specs=[whole(VMEM)] * (3 if first else 5),
         out_specs=whole(VMEM) if first else [whole(VMEM)] * 2,
         out_shape=vector if first else [vector] * 2,
         compiler_params=params(16),
         name="apply",
-    )(y, z, *(sums or ()))
+    )(*ys, z, *(sums or ()))
 
 
 def finish_kernel(scale, z_ref, near_ref, far_ref, fresh_ref):
@@ -379,23 +359,23 @@
     )(me, own, other)
 
 
-def join_kernel(near_ref, far_ref, vis_ref):
-    vis_ref[...] = near_ref[...].astype(F32) + far_ref[...].astype(F32)
-
-
-def join(near, far):
-    parts, rows, cols = near.shape
-    steps = 4
+def widen_kernel(in_ref, out_ref):
+    out_ref[...] = in_ref[...].astype(F32)
+
+
+def widen(x):
+    parts, rows, cols = x.shape
+    steps = 2
     block = pl.BlockSpec((parts, rows // steps, cols), lambda i: (0, i, 0))
     return pl.pallas_call(
-        join_kernel,
+        widen_kernel,
         grid=(steps,),
-        in_specs=[block, block],
+        in_specs=[block],
         out_specs=block,
-        out_shape=pltpu.HBM(near.shape, F32),
+        out_shape=pltpu.HBM(x.shape, F32),
         compiler_params=params(8),
-        name="join",
-    )(near, far)
+        name="widen",
+    )(x)
 
 
 def swap(x, axis, mask):
@@ -403,18 +383,12 @@
     return lax.ppermute(x, axis, [(i, i ^ mask) for i in range(n)])
 
 
-def exchange(part):
-    part = part + swap(part, "freq", 1)
-    part = part + swap(part, "tm", 1)
-    return part, swap(part, "tm", 3)
-
-
-def cross(x, turn):
+def cross(x):
     pairs = []
     for i in range(lax.axis_size("freq") // 2):
         for core in range(2):
             for g in range(2):
-                pairs.append(((2 * i + core) * 2 + g, (2 * i + g) * 2 + (core ^ turn)))
+                pairs.append(((2 * i + core) * 2 + g, (2 * i + g) * 2 + core))
     return lax.ppermute(x, WIDE, pairs)
 
 
@@ -437,7 +411,6 @@
     stations = ingest_map.shape[0]
     inputs = 2 * stations
     total = samples * n_time
-    core = freq_index % 2
 
     me = jnp.stack([freq_index, group_index, lax.axis_index("tm")]).astype(jnp.int32)
     base = ((freq_index * n_group + group_index) * rows).astype(jnp.int32).reshape(1)
@@ -461,7 +434,7 @@
     )
     cosine, sine = jnp.cos(phase), jnp.sin(phase)
 
-    z = cross(prior_gains[0], 0)
+    z = cross(prior_gains[0])
     slot = lax.broadcasted_iota(jnp.int32, (slots, slots), 1)
     same = corr_channels[None, :] == beam_channels[:, None]
     source = jnp.sum(jnp.where(same, slot, 0), axis=1)
@@ -470,24 +443,28 @@
     )
     beam_y = lax.all_to_all(beam_send, WIDE, split_axis=0, concat_axis=0, tiled=True)
 
+    ys = [corr_y, swap(corr_y, "freq", 1)]
     scale = float(inputs) / total
-    part = apply_visibilities(corr_y, z, None, scale)
-
-    pieces = correlate(corr_y, me, 1.0 / total, n_time)
+    part = apply_visibilities(ys, z, None, scale)
+    pieces = []
+    for step in range(ITERS):
+        if step:
+            part, z = apply_visibilities(ys, z, sums, scale)
+        part = part + swap(part, "tm", 1)
+        far = swap(part, "tm", 3)
+        part, *late = lax.optimization_barrier((part, *ys))
+        piece = correlate(late, me, 1.0 / total, step, n_time)
+        far, piece = lax.optimization_barrier((far, piece))
+        pieces.append(piece)
+        sums = (part, far)
+    depth = slots // 4
+    part, far, *pieces = lax.optimization_barrier((*sums, *pieces))
     pieces = [pieces[0]] + [swap(x, "tm", m + 1) for m, x in enumerate(pieces[1:])]
-
-    sums = exchange(part)
-    for _ in range(ITERS - 1):
-        part, z = apply_visibilities(corr_y, z, sums, scale)
-        sums = exchange(part)
-    depth = slots // 4
-    z = finish(z, sums, scale)
+    z = finish(z, (part, far), scale)
     reach = [(0, 0), (0, 1), (1, 0), (1, 1)]
     half_ring = slots // 2 * n_group
     vectors = [z] + [swap(z, WIDE, high * half_ring + low) for high, low in reach[1:]]
     copies, solved = choose(source, me, vectors, reach, depth)
-    copies, near, far = lax.optimization_barrier((copies, *gather(pieces)))
-    near, far = cross(near, 0), cross(far, 1)
     copies, beam_y = lax.optimization_barrier((copies, beam_y))
     groups = [
         [high * 2 * depth + 2 * i + c for i in range(depth)]
@@ -498,11 +475,11 @@
         copies, "freq", split_axis=0, concat_axis=0, axis_index_groups=groups, tiled=True
     )
 
-    line, near, far = lax.optimization_barrier((line, near, far))
+    block = cross(gather(pieces))
     away = beamform(1, source, me, line, cosine, sine, beam_y, n_group)
     other = swap(away, "grp", 1)
     own = beamform(0, source, me, line, cosine, sine, beam_y, n_group)
-    visibilities = join(near, far)
+    visibilities = widen(block)
     beams = place(me, own, other)
     return visibilities[None], solved[None], beams[None]
 

time: 213 us -> 171 us (0.80)
  waiting for transfers between devices: 112 us -> 65.5 us
  Pallas kernels: 27.9 us -> 34.2 us
    ppermute x19 -> x16, waiting for transfers between devices: 66.1 us -> 20.6 us  [swap(): return lax.ppermute(x, axis, [(i, i ^ mask) for i in range(n)])]
    ppermute x19 -> x16, starting transfers between devices: 28 us -> 19.2 us  [swap(): return lax.ppermute(x, axis, [(i, i ^ mask) for i in range(n)])]
    ppermute x3 -> x2, starting transfers between devices: 10 us -> 16.7 us  [cross(): return lax.ppermute(x, WIDE, pairs)]
    pallas_call x4, Pallas kernels: 4.36 us -> 7.89 us  [apply_visibilities(): pl.pallas_call(functools.partial(apply_kernel, scale, first), in_specs=[w...]
    pallas_call x3 -> x6, Pallas kernels: 9.13 us -> 11.9 us  [the longest x4 9.71 us: correlate(): pl.pallas_call(functools.partial(correlate_kernel, scale, mask), in_specs...]
    ppermute x3 -> x2, waiting for transfers between devices: 6.47 us -> 6.55 us  [cross(): return lax.ppermute(x, WIDE, pairs)]
  transfers between devices with their start and end apart: 25 -> 21, of which waited for: 19 -> 10; matrix products, arithmetic and copies ran while one was open for 2% -> 3% of each run, Pallas kernels for 10% -> 18%
where the time goes in v6:
time: 171 us; the launch traced here: 170 us
  waiting for transfers between devices  65.5 us (38%)
  starting transfers between devices  63.2 us (37%)
  Pallas kernels  34.2 us (20%)
  local copies, waits for them, and re-layouts  3.16 us (2%)
  other arithmetic  2.25 us (1%)
  between operations  1.8 us (1%)
    all_to_all x1, waiting for transfers between devices, body(): lax.all_to_all(corr_send, WIDE, split_axis=0, concat_axis=0, tiled=True)  38.3 us
    ppermute x16, waiting for transfers between devices, swap(): return lax.ppermute(x, axis, [(i, i ^ mask) for i in range(n)])  20.6 us
    ppermute x16, starting transfers between devices, swap(): return lax.ppermute(x, axis, [(i, i ^ mask) for i in range(n)])  19.2 us
    ppermute x2, starting transfers between devices, cross(): return lax.ppermute(x, WIDE, pairs)  16.7 us
    all_to_all x1, starting transfers between devices, body(): lax.all_to_all(corr_send, WIDE, split_axis=0, concat_axis=0, tiled=True)  13.3 us
    pallas_call x4, Pallas kernels, correlate(): pl.pallas_call(functools.partial(correlate_kernel, scale, mask), in_specs...  9.71 us
    pallas_call x4, Pallas kernels, apply_visibilities(): pl.pallas_call(functools.partial(apply_kernel, scale, first), in_specs=[w...  7.89 us
    all_to_all x1, starting transfers between devices, body(): lax.all_to_all(beam_send, WIDE, split_axis=0, concat_axis=0, tiled=True)  7.35 us
  transfers between devices with their start and end apart: 21, of which 10 were waited for; matrix products, arithmetic and copies ran while one was open for 3% of the time, Pallas kernels for 18%

profile of v6, /device:TPU:1, one launch (start us, length us, event | category | flops | bytes accessed | tf_op | source)
XLA Modules:
  0.0 170.1 jit_solution(11042671114207474249)
XLA Ops:
  0.6 3.1 %ingest.3 = bf16[32,2,2,16,512]{4,3,2,1,0:T(8,128)(2,1)} custom-call(s32[1]{0:T(128)} %bitcast.base_ref, s32[32]{0:T(128)} %chan_hbm.3, s32[512]{0:T(512)} %map_hbm.3, s32[512]{0:T(512)} %flag_hbm.3, bf16[32,2,16,1024]{3,2,1,0:T(8,128)(2,1)} %volts_hbm.3), custom_call_target="tpu_custom_call" | custom-call | tf_op jit(solution)/shard_map/ingest/pallas_call | solution.py:93
  3.8 13.3 %all-to-all-start = ((bf16[64,2,16,512]{3,2,1,0:T(8,128)(2,1)}), bf16[64,2,16,512]{3,2,1,0:T(8,128)(2,1)S(1)}, u32[]{:S(2)}, u32[]{:S(2)}) async-start(bf16[64,2,16,512]{3,2,1,0:T(8,128)(2,1)} %bitcast.15), calls=%async_computation | async-start | bytes 4194304 | tf_op jit(solution)/shard_map/all_to_all | solution.py:422
  17.1 3.5 %collective-permute-start = (f32[2,1024]{1,0:T(2,128)S(1)}, f32[2,1024]{1,0:T(2,128)S(1)}, u32[]{:S(2)}, u32[]{:S(2)}) collective-permute-start(f32[2,1024]{1,0:T(2,128)S(1)} %bitcast.21), channel_id=1, source_target_pairs={{0,0},{1,8},{8,1},{9,9},{16,16},{17,24},{24,17},{25,25},{32,32},{3... | collective-permute-start | bytes 24584 | tf_op jit(solution)/shard_map/ppermute | solution.py:392
  23.7 2.0 %fusion = (f32[256,512]{1,0:T(8,128)S(1)}, f32[256,512]{1,0:T(8,128)S(1)}) fusion(f32[512]{0:T(512)S(1)} %get-tuple-element.90, f32[256]{0:T(256)S(1)} %bitcast.20, f32[512]{0:T(512)S(1)} %get-tuple-element.89, f32[256]{0:T(256)S(1)} %bitcast.19, f32[]{:T(128)} %bitcast.4), kind=kLoop, calls=%fused_computation.2 | loop fusion | flops 524288 | bytes 1054724 | tf_op jit(solution)/shard_map/sin | solution.py:435
  25.7 3.0 %ingest.2 = bf16[32,2,2,16,512]{4,3,2,1,0:T(8,128)(2,1)} custom-call(s32[1]{0:T(128)} %bitcast.base_ref, s32[32]{0:T(128)} %chan_hbm.2, s32[512]{0:T(512)} %map_hbm.3, s32[512]{0:T(512)} %flag_hbm.3, bf16[32,2,16,1024]{3,2,1,0:T(8,128)(2,1)} %volts_hbm.3), custom_call_target="tpu_custom_call" | custom-call | tf_op jit(solution)/shard_map/ingest/pallas_call | solution.py:93
  28.8 38.3 %all-to-all-done.mine_ref.refs_0_ = bf16[64,2,16,512]{3,2,1,0:T(8,128)(2,1)S(1)} async-done(((bf16[64,2,16,512]{3,2,1,0:T(8,128)(2,1)}), bf16[64,2,16,512]{3,2,1,0:T(8,128)(2,1)S(1)}, u32[]{:S(2)}, u32[]{:S(2)}) %all-to-all-start) | async-done | bytes 2097184 | tf_op jit(solution)/shard_map/all_to_all | solution.py:422
  67.1 7.3 %all-to-all-start.1 = ((bf16[64,2,16,512]{3,2,1,0:T(8,128)(2,1)}), bf16[64,2,16,512]{3,2,1,0:T(8,128)(2,1)}, u32[]{:S(2)}, u32[]{:S(2)}) async-start(bf16[64,2,16,512]{3,2,1,0:T(8,128)(2,1)} %bitcast.14), calls=%async_computation.1 | async-start | bytes 4194304 | tf_op jit(solution)/shard_map/all_to_all | solution.py:444
  75.0 3.8 %collective-permute-done.1.other_ref.refs_1_ = bf16[64,2,16,512]{3,2,1,0:T(8,128)(2,1)S(1)} collective-permute-done((bf16[64,2,16,512]{3,2,1,0:T(8,128)(2,1)S(1)}, bf16[64,2,16,512]{3,2,1,0:T(8,128)(2,1)S(1)}, u32[]{:S(2)}, u32[]{:S(2)}) %collective-permute-start.1) | collective-permute-done | bytes 2097184 | tf_op jit(solution)/shard_map/ppermute | solution.py:383
  78.8 1.9 %apply.4 = f32[2,1024]{1,0:T(2,128)S(1)} custom-call(bf16[64,2,16,512]{3,2,1,0:T(8,128)(2,1)S(1)} %all-to-all-done.mine_ref.refs_0_, bf16[64,2,16,512]{3,2,1,0:T(8,128)(2,1)S(1)} %collective-permute-done.1.other_ref.refs_1_, f32[2,1024]{1,0:T(2,128)S(1)} %collective-permute-done.z_ref), custom_call_target="tpu_custom_call" | custom-call | tf_op jit(solution)/shard_map/apply/pallas_call | solution.py:228
  82.0 1.7 collective-permute-done.2
  83.7 2.5 %collective-permute-start.3 = (f32[2,1024]{1,0:T(2,128)S(1)}, f32[2,1024]{1,0:T(2,128)S(1)}, u32[]{:S(2)}, u32[]{:S(2)}) collective-permute-start(f32[2,1024]{1,0:T(2,128)S(1)} %add.59.refs_0_), channel_id=1, source_target_pairs={{0,6},{2,4},{4,2},{6,0},{1,7},{3,5},{5,3},{7,1},{8,14},{10,12},{12... | collective-permute-start | bytes 24584 | tf_op jit(solution)/shard_map/ppermute | solution.py:383
  86.2 1.8 %correlate.4.refs_0_ = bf16[2,512,256]{2,1,0:T(8,128)(2,1)S(1)} custom-call(s32[3]{0:T(128)S(1)} %pad_add_fusion.me_ref, bf16[64,2,16,512]{3,2,1,0:T(8,128)(2,1)S(1)} %all-to-all-done.mine_ref.refs_0_, bf16[64,2,16,512]{3,2,1,0:T(8,128)(2,1)S(1)} %collective-permute-done.1.other_ref.refs_1_), custom_call_target="tpu_custom_call" | custom-call | tf_op jit(solution)/shard_map/correlate/pallas_call | solution.py:153
  88.0 2.0 %apply.5 = (f32[2,1024]{1,0:T(2,128)S(1)}, f32[2,1024]{1,0:T(2,128)S(1)}) custom-call(bf16[64,2,16,512]{3,2,1,0:T(8,128)(2,1)S(1)} %all-to-all-done.mine_ref.refs_0_, bf16[64,2,16,512]{3,2,1,0:T(8,128)(2,1)S(1)} %collective-permute-done.1.other_ref.refs_1_, f32[2,1024]{1,0:T(2,128)S(1)} %collective-permute-done.z_ref, f32[2,1024]{1,0:T(2,128)S(1)} %add.59.refs_0_, ...), custom_call_target="tpu_custom_call" | custom-call | tf_op jit(solution)/shard_map/apply/pallas_call | solution.py:228
  90.2 2.9 %collective-permute-done.4 = f32[2,1024]{1,0:T(2,128)S(1)} collective-permute-done((f32[2,1024]{1,0:T(2,128)S(1)}, f32[2,1024]{1,0:T(2,128)S(1)}, u32[]{:S(2)}, u32[]{:S(2)}) %collective-permute-start.4) | collective-permute-done | bytes 8224 | tf_op jit(solution)/shard_map/ppermute | solution.py:383
  93.0 2.3 %collective-permute-start.5 = (f32[2,1024]{1,0:T(2,128)S(1)}, f32[2,1024]{1,0:T(2,128)S(1)}, u32[]{:S(2)}, u32[]{:S(2)}) collective-permute-start(f32[2,1024]{1,0:T(2,128)S(1)} %add.60.refs_0_), channel_id=1, source_target_pairs={{0,6},{2,4},{4,2},{6,0},{1,7},{3,5},{5,3},{7,1},{8,14},{10,12},{12... | collective-permute-start | bytes 24584 | tf_op jit(solution)/shard_map/ppermute | solution.py:383
  95.3 2.6 %correlate.5 = bf16[2,512,256]{2,1,0:T(8,128)(2,1)} custom-call(s32[3]{0:T(128)S(1)} %pad_add_fusion.me_ref, bf16[64,2,16,512]{3,2,1,0:T(8,128)(2,1)S(1)} %all-to-all-done.mine_ref.refs_0_, bf16[64,2,16,512]{3,2,1,0:T(8,128)(2,1)S(1)} %collective-permute-done.1.other_ref.refs_1_), custom_call_target="tpu_custom_call" | custom-call | tf_op jit(solution)/shard_map/correlate/pallas_call | solution.py:153
  97.9 2.0 %apply.6 = (f32[2,1024]{1,0:T(2,128)S(1)}, f32[2,1024]{1,0:T(2,128)S(1)}) custom-call(bf16[64,2,16,512]{3,2,1,0:T(8,128)(2,1)S(1)} %all-to-all-done.mine_ref.refs_0_, bf16[64,2,16,512]{3,2,1,0:T(8,128)(2,1)S(1)} %collective-permute-done.1.other_ref.refs_1_, f32[2,1024]{1,0:T(2,128)S(1)} %get-tuple-element.53.z_ref, f32[2,1024]{1,0:T(2,128)S(1)} %add.60.refs_0_, ...), custom_call_target="tpu_custom_call" | custom-call | tf_op jit(solution)/shard_map/apply/pallas_call | solution.py:228
  100.0 2.9 %collective-permute-done.6 = f32[2,1024]{1,0:T(2,128)S(1)} collective-permute-done((f32[2,1024]{1,0:T(2,128)S(1)}, f32[2,1024]{1,0:T(2,128)S(1)}, u32[]{:S(2)}, u32[]{:S(2)}) %collective-permute-start.6) | collective-permute-done | bytes 8224 | tf_op jit(solution)/shard_map/ppermute | solution.py:383
  104.4 2.6 %correlate.6 = bf16[2,512,256]{2,1,0:T(8,128)(2,1)} custom-call(s32[3]{0:T(128)S(1)} %pad_add_fusion.me_ref, bf16[64,2,16,512]{3,2,1,0:T(8,128)(2,1)S(1)} %all-to-all-done.mine_ref.refs_0_, bf16[64,2,16,512]{3,2,1,0:T(8,128)(2,1)S(1)} %collective-permute-done.1.other_ref.refs_1_), custom_call_target="tpu_custom_call" | custom-call | tf_op jit(solution)/shard_map/correlate/pallas_call | solution.py:153
  107.1 2.0 %apply.7 = (f32[2,1024]{1,0:T(2,128)S(1)}, f32[2,1024]{1,0:T(2,128)S(1)}) custom-call(bf16[64,2,16,512]{3,2,1,0:T(8,128)(2,1)S(1)} %all-to-all-done.mine_ref.refs_0_, bf16[64,2,16,512]{3,2,1,0:T(8,128)(2,1)S(1)} %collective-permute-done.1.other_ref.refs_1_, f32[2,1024]{1,0:T(2,128)S(1)} %get-tuple-element.59.z_ref, f32[2,1024]{1,0:T(2,128)S(1)} %add.61.refs_0_, ...), custom_call_target="tpu_custom_call" | custom-call | tf_op jit(solution)/shard_map/apply/pallas_call | solution.py:228
  109.2 2.9 %collective-permute-done.8 = f32[2,1024]{1,0:T(2,128)S(1)} collective-permute-done((f32[2,1024]{1,0:T(2,128)S(1)}, f32[2,1024]{1,0:T(2,128)S(1)}, u32[]{:S(2)}, u32[]{:S(2)}) %collective-permute-start.8) | collective-permute-done | bytes 8224 | tf_op jit(solution)/shard_map/ppermute | solution.py:383
  113.6 2.6 %correlate.7 = bf16[2,512,256]{2,1,0:T(8,128)(2,1)} custom-call(s32[3]{0:T(128)S(1)} %pad_add_fusion.me_ref, bf16[64,2,16,512]{3,2,1,0:T(8,128)(2,1)S(1)} %all-to-all-done.mine_ref.refs_0_, bf16[64,2,16,512]{3,2,1,0:T(8,128)(2,1)S(1)} %collective-permute-done.1.other_ref.refs_1_), custom_call_target="tpu_custom_call" | custom-call | tf_op jit(solution)/shard_map/correlate/pallas_call | solution.py:153
  116.2 2.6 %collective-permute-start.11 = (bf16[2,512,256]{2,1,0:T(8,128)(2,1)}, bf16[2,512,256]{2,1,0:T(8,128)(2,1)S(1)}, u32[]{:S(2)}, u32[]{:S(2)}) collective-permute-start(bf16[2,512,256]{2,1,0:T(8,128)(2,1)} %correlate.6), channel_id=1, source_target_pairs={{0,4},{2,6},{4,0},{6,2},{1,5},{3,7},{5,1},{7,3},{8,12},{10,14},{12... | collective-permute-start | bytes 1572872 | tf_op jit(solution)/shard_map/ppermute | solution.py:383
  121.5 2.3 %collective-permute-start.15 = (f32[2,1024]{1,0:T(2,128)S(1)}, f32[2,1024]{1,0:T(2,128)S(1)}, u32[]{:S(2)}, u32[]{:S(2)}) collective-permute-start(f32[2,1024]{1,0:T(2,128)S(1)} %finish.1.refs_0_), channel_id=1, source_target_pairs={{0,128},{1,129},{8,136},{9,137},{16,144},{17,145},{24,152},{25,153... | collective-permute-start | bytes 24584 | tf_op jit(solution)/shard_map/ppermute | solution.py:383
  123.9 1.7 %collective-permute-start.16 = (f32[2,1024]{1,0:T(2,128)S(1)}, f32[2,1024]{1,0:T(2,128)S(1)}, u32[]{:S(2)}, u32[]{:S(2)}) collective-permute-start(f32[2,1024]{1,0:T(2,128)S(1)} %finish.1.refs_0_), channel_id=1, source_target_pairs={{0,129},{1,128},{8,137},{9,136},{16,145},{17,144},{24,153},{25,152... | collective-permute-start | bytes 24584 | tf_op jit(solution)/shard_map/ppermute | solution.py:383
  125.6 2.0 %collective-permute-done.16.refs_3_ = f32[2,1024]{1,0:T(2,128)S(1)} collective-permute-done((f32[2,1024]{1,0:T(2,128)S(1)}, f32[2,1024]{1,0:T(2,128)S(1)}, u32[]{:S(2)}, u32[]{:S(2)}) %collective-permute-start.16) | collective-permute-done | bytes 8224 | tf_op jit(solution)/shard_map/ppermute | solution.py:383
  128.8 6.6 %all-to-all-start.2 = ((f32[8,2,1024]{2,1,0:T(2,128)}), f32[8,2,1024]{2,1,0:T(2,128)S(1)}, u32[]{:S(2)}, u32[]{:S(2)}) async-start(f32[8,2,1024]{2,1,0:T(2,128)} %get-tuple-element.85), calls=%async_computation.2 | async-start | bytes 131072 | tf_op jit(solution)/shard_map/all_to_all | solution.py:474
  137.9 13.2 %collective-permute-start.13 = (bf16[2,512,256]{2,1,0:T(8,128)(2,1)}, bf16[2,512,256]{2,1,0:T(8,128)(2,1)S(1)}, u32[]{:S(2)}, u32[]{:S(2)}) collective-permute-start(bf16[2,512,256]{2,1,0:T(8,128)(2,1)} %gather.8), channel_id=1, source_target_pairs={{0,0},{1,8},{8,1},{9,9},{16,16},{17,24},{24,17},{25,25},{32,32},{3... | collective-permute-start | bytes 1572872 | tf_op jit(solution)/shard_map/ppermute | solution.py:392
  151.1 2.4 %beamform.3 = bf16[2,2,128,512]{3,2,1,0:T(8,128)(2,1)S(1)} custom-call(s32[32]{0:T(128)S(1)} %select_reduce_fusion.source_ref, s32[3]{0:T(128)S(1)} %pad_add_fusion.me_ref, f32[8,2,1024]{2,1,0:T(2,128)S(1)} %all-to-all-done.2.line_ref, f32[256,512]{1,0:T(8,128)S(1)} %get-tuple-element.86.cos_ref, f32[256,512]{1,0:T(8,128)S(1)} %get-tuple-element.87.sin_ref, ...), custom_call_target="tpu_custom_call" | custom-call | tf_op jit(solution)/shard_map/beamform/pallas_call | solution.py:330
  153.6 6.6 %collective-permute-done.13.in_ref = bf16[2,512,256]{2,1,0:T(8,128)(2,1)S(1)} collective-permute-done((bf16[2,512,256]{2,1,0:T(8,128)(2,1)}, bf16[2,512,256]{2,1,0:T(8,128)(2,1)S(1)}, u32[]{:S(2)}, u32[]{:S(2)}) %collective-permute-start.13) | collective-permute-done | bytes 524320 | tf_op jit(solution)/shard_map/ppermute | solution.py:392
  161.2 3.1 %beamform.2.own_hbm = bf16[2,2,128,1024]{3,2,1,0:T(8,128)(2,1)} custom-call(s32[32]{0:T(128)S(1)} %select_reduce_fusion.source_ref, s32[3]{0:T(128)S(1)} %pad_add_fusion.me_ref, f32[8,2,1024]{2,1,0:T(2,128)S(1)} %all-to-all-done.2.line_ref, f32[256,512]{1,0:T(8,128)S(1)} %get-tuple-element.86.cos_ref, f32[256,512]{1,0:T(8,128)S(1)} %get-tuple-element.87.sin_ref, ...), custom_call_target="tpu_custom_call" | custom-call | tf_op jit(solution)/shard_map/beamform/pallas_call | solution.py:330
  164.4 4.2 %collective-permute-done.17.other_ref = bf16[2,2,128,512]{3,2,1,0:T(8,128)(2,1)S(1)} collective-permute-done((bf16[2,2,128,512]{3,2,1,0:T(8,128)(2,1)S(1)}, bf16[2,2,128,512]{3,2,1,0:T(8,128)(2,1)S(1)}, u32[]{:S(2)}, u32[]{:S(2)}) %collective-permute-start.17) | collective-permute-done | bytes 524320 | tf_op jit(solution)/shard_map/ppermute | solution.py:383
  (56 shorter events, 16.4 us)
Async XLA Ops:
  3.7 13.4 %copy-start.7 = (f32[1,2,1024]{2,1,0:T(2,128)S(1)}, f32[1,2,1024]{2,1,0:T(2,128)}, u32[]{:S(2)}) copy-start(f32[1,2,1024]{2,1,0:T(2,128)} %param.9) | copy-start | bytes 24580
  3.7 16.9 %copy-start.6 = (s32[32]{0:T(128)S(1)}, s32[32]{0:T(128)}, u32[]{:S(2)}) copy-start(s32[32]{0:T(128)} %chan_hbm.2) | copy-start | bytes 388
  3.7 18.2 %copy-start.3 = (f32[2,512]{1,0:T(2,128)S(1)}, f32[2,512]{1,0:T(2,128)}, u32[]{:S(2)}) copy-start(f32[2,512]{1,0:T(2,128)} %param.12) | copy-start | bytes 12292
  3.8 18.3 %copy-start.2 = (s32[512]{0:T(512)S(1)}, s32[512]{0:T(512)}, u32[]{:S(2)}) copy-start(s32[512]{0:T(512)} %map_hbm.3) | copy-start | bytes 6148
  3.8 19.4 %copy-start.5 = (s32[32]{0:T(128)S(1)}, s32[32]{0:T(128)}, u32[]{:S(2)}) copy-start(s32[32]{0:T(128)} %chan_hbm.3) | copy-start | bytes 388
  3.8 19.9 %copy-start.4 = (s32[2,256]{1,0:T(2,128)S(1)}, s32[2,256]{1,0:T(2,128)}, u32[]{:S(2)}) copy-start(s32[2,256]{1,0:T(2,128)} %param.13) | copy-start | bytes 6148
  3.8 63.3 %all-to-all-start = ((bf16[64,2,16,512]{3,2,1,0:T(8,128)(2,1)}), bf16[64,2,16,512]{3,2,1,0:T(8,128)(2,1)S(1)}, u32[]{:S(2)}, u32[]{:S(2)}) async-start(bf16[64,2,16,512]{3,2,1,0:T(8,128)(2,1)} %bitcast.15), calls=%async_computation | async-start | bytes 4194304 | tf_op jit(solution)/shard_map/all_to_all | solution.py:422
  17.1 11.6 %collective-permute-start = (f32[2,1024]{1,0:T(2,128)S(1)}, f32[2,1024]{1,0:T(2,128)S(1)}, u32[]{:S(2)}, u32[]{:S(2)}) collective-permute-start(f32[2,1024]{1,0:T(2,128)S(1)} %bitcast.21), channel_id=1, source_target_pairs={{0,0},{1,8},{8,1},{9,9},{16,16},{17,24},{24,17},{25,25},{32,32},{3... | collective-permute-start | bytes 24584 | tf_op jit(solution)/shard_map/ppermute | solution.py:392
  67.1 61.8 %all-to-all-start.1 = ((bf16[64,2,16,512]{3,2,1,0:T(8,128)(2,1)}), bf16[64,2,16,512]{3,2,1,0:T(8,128)(2,1)}, u32[]{:S(2)}, u32[]{:S(2)}) async-start(bf16[64,2,16,512]{3,2,1,0:T(8,128)(2,1)} %bitcast.14), calls=%async_computation.1 | async-start | bytes 4194304 | tf_op jit(solution)/shard_map/all_to_all | solution.py:444
  74.4 4.4 %collective-permute-start.1 = (bf16[64,2,16,512]{3,2,1,0:T(8,128)(2,1)S(1)}, bf16[64,2,16,512]{3,2,1,0:T(8,128)(2,1)S(1)}, u32[]{:S(2)}, u32[]{:S(2)}) collective-permute-start(bf16[64,2,16,512]{3,2,1,0:T(8,128)(2,1)S(1)} %all-to-all-done.mine_ref.refs_0_), channel_id=1, source_target_pairs={{0,8},{8,0},{16,24},{24,16},{32,40},{40,32},{48,56},{56,48},{64,72... | collective-permute-start | bytes 6291464 | tf_op jit(solution)/shard_map/ppermute | solution.py:383
  80.7 3.0 %collective-permute-start.2 = (f32[2,1024]{1,0:T(2,128)S(1)}, f32[2,1024]{1,0:T(2,128)S(1)}, u32[]{:S(2)}, u32[]{:S(2)}) collective-permute-start(f32[2,1024]{1,0:T(2,128)S(1)} %apply.4), channel_id=1, source_target_pairs={{0,2},{2,0},{4,6},{6,4},{1,3},{3,1},{5,7},{7,5},{8,10},{10,8},{12,... | collective-permute-start | bytes 24584 | tf_op jit(solution)/shard_map/ppermute | solution.py:383
  83.7 4.3 %collective-permute-start.3 = (f32[2,1024]{1,0:T(2,128)S(1)}, f32[2,1024]{1,0:T(2,128)S(1)}, u32[]{:S(2)}, u32[]{:S(2)}) collective-permute-start(f32[2,1024]{1,0:T(2,128)S(1)} %add.59.refs_0_), channel_id=1, source_target_pairs={{0,6},{2,4},{4,2},{6,0},{1,7},{3,5},{5,3},{7,1},{8,14},{10,12},{12... | collective-permute-start | bytes 24584 | tf_op jit(solution)/shard_map/ppermute | solution.py:383
  88.0 2.0 %copy-start = (bf16[2,512,256]{2,1,0:T(8,128)(2,1)}, bf16[2,512,256]{2,1,0:T(8,128)(2,1)S(1)}, u32[]{:S(2)}) copy-start(bf16[2,512,256]{2,1,0:T(8,128)(2,1)S(1)} %correlate.4.refs_0_) | copy-start | bytes 1572868
  90.0 3.0 %collective-permute-start.4 = (f32[2,1024]{1,0:T(2,128)S(1)}, f32[2,1024]{1,0:T(2,128)S(1)}, u32[]{:S(2)}, u32[]{:S(2)}) collective-permute-start(f32[2,1024]{1,0:T(2,128)S(1)} %get-tuple-element.54), channel_id=1, source_target_pairs={{0,2},{2,0},{4,6},{6,4},{1,3},{3,1},{5,7},{7,5},{8,10},{10,8},{12,... | collective-permute-start | bytes 24584 | tf_op jit(solution)/shard_map/ppermute | solution.py:383
  93.0 4.9 %collective-permute-start.5 = (f32[2,1024]{1,0:T(2,128)S(1)}, f32[2,1024]{1,0:T(2,128)S(1)}, u32[]{:S(2)}, u32[]{:S(2)}) collective-permute-start(f32[2,1024]{1,0:T(2,128)S(1)} %add.60.refs_0_), channel_id=1, source_target_pairs={{0,6},{2,4},{4,2},{6,0},{1,7},{3,5},{5,3},{7,1},{8,14},{10,12},{12... | collective-permute-start | bytes 24584 | tf_op jit(solution)/shard_map/ppermute | solution.py:383
  99.9 3.0 %collective-permute-start.6 = (f32[2,1024]{1,0:T(2,128)S(1)}, f32[2,1024]{1,0:T(2,128)S(1)}, u32[]{:S(2)}, u32[]{:S(2)}) collective-permute-start(f32[2,1024]{1,0:T(2,128)S(1)} %get-tuple-element.60), channel_id=1, source_target_pairs={{0,2},{2,0},{4,6},{6,4},{1,3},{3,1},{5,7},{7,5},{8,10},{10,8},{12,... | collective-permute-start | bytes 24584 | tf_op jit(solution)/shard_map/ppermute | solution.py:383
  102.9 4.1 %collective-permute-start.7 = (f32[2,1024]{1,0:T(2,128)S(1)}, f32[2,1024]{1,0:T(2,128)S(1)}, u32[]{:S(2)}, u32[]{:S(2)}) collective-permute-start(f32[2,1024]{1,0:T(2,128)S(1)} %add.61.refs_0_), channel_id=1, source_target_pairs={{0,6},{2,4},{4,2},{6,0},{1,7},{3,5},{5,3},{7,1},{8,14},{10,12},{12... | collective-permute-start | bytes 24584 | tf_op jit(solution)/shard_map/ppermute | solution.py:383
  109.1 3.0 %collective-permute-start.8 = (f32[2,1024]{1,0:T(2,128)S(1)}, f32[2,1024]{1,0:T(2,128)S(1)}, u32[]{:S(2)}, u32[]{:S(2)}) collective-permute-start(f32[2,1024]{1,0:T(2,128)S(1)} %get-tuple-element.65), channel_id=1, source_target_pairs={{0,2},{2,0},{4,6},{6,4},{1,3},{3,1},{5,7},{7,5},{8,10},{10,8},{12,... | collective-permute-start | bytes 24584 | tf_op jit(solution)/shard_map/ppermute | solution.py:383
  112.1 4.1 %collective-permute-start.9 = (f32[2,1024]{1,0:T(2,128)S(1)}, f32[2,1024]{1,0:T(2,128)S(1)}, u32[]{:S(2)}, u32[]{:S(2)}) collective-permute-start(f32[2,1024]{1,0:T(2,128)S(1)} %add.62.near_ref), channel_id=1, source_target_pairs={{0,6},{2,4},{4,2},{6,0},{1,7},{3,5},{5,3},{7,1},{8,14},{10,12},{12... | collective-permute-start | bytes 24584 | tf_op jit(solution)/shard_map/ppermute | solution.py:383
  116.2 19.3 %collective-permute-start.10 = (bf16[2,512,256]{2,1,0:T(8,128)(2,1)}, bf16[2,512,256]{2,1,0:T(8,128)(2,1)S(1)}, u32[]{:S(2)}, u32[]{:S(2)}) collective-permute-start(bf16[2,512,256]{2,1,0:T(8,128)(2,1)} %correlate.5), channel_id=1, source_target_pairs={{0,2},{2,0},{4,6},{6,4},{1,3},{3,1},{5,7},{7,5},{8,10},{10,8},{12,... | collective-permute-start | bytes 1572872 | tf_op jit(solution)/shard_map/ppermute | solution.py:383
  116.2 19.5 %collective-permute-start.11 = (bf16[2,512,256]{2,1,0:T(8,128)(2,1)}, bf16[2,512,256]{2,1,0:T(8,128)(2,1)S(1)}, u32[]{:S(2)}, u32[]{:S(2)}) collective-permute-start(bf16[2,512,256]{2,1,0:T(8,128)(2,1)} %correlate.6), channel_id=1, source_target_pairs={{0,4},{2,6},{4,0},{6,2},{1,5},{3,7},{5,1},{7,3},{8,12},{10,14},{12... | collective-permute-start | bytes 1572872 | tf_op jit(solution)/shard_map/ppermute | solution.py:383
  118.8 16.8 %collective-permute-start.12 = (bf16[2,512,256]{2,1,0:T(8,128)(2,1)}, bf16[2,512,256]{2,1,0:T(8,128)(2,1)S(1)}, u32[]{:S(2)}, u32[]{:S(2)}) collective-permute-start(bf16[2,512,256]{2,1,0:T(8,128)(2,1)} %correlate.7), channel_id=1, source_target_pairs={{0,6},{2,4},{4,2},{6,0},{1,7},{3,5},{5,3},{7,1},{8,14},{10,12},{12... | collective-permute-start | bytes 1572872 | tf_op jit(solution)/shard_map/ppermute | solution.py:383
  120.2 3.7 %collective-permute-start.14 = (f32[2,1024]{1,0:T(2,128)S(1)}, f32[2,1024]{1,0:T(2,128)S(1)}, u32[]{:S(2)}, u32[]{:S(2)}) collective-permute-start(f32[2,1024]{1,0:T(2,128)S(1)} %finish.1.refs_0_), channel_id=1, source_target_pairs={{0,1},{1,0},{8,9},{9,8},{16,17},{17,16},{24,25},{25,24},{32,33},{3... | collective-permute-start | bytes 24584 | tf_op jit(solution)/shard_map/ppermute | solution.py:383
  121.5 4.1 %collective-permute-start.15 = (f32[2,1024]{1,0:T(2,128)S(1)}, f32[2,1024]{1,0:T(2,128)S(1)}, u32[]{:S(2)}, u32[]{:S(2)}) collective-permute-start(f32[2,1024]{1,0:T(2,128)S(1)} %finish.1.refs_0_), channel_id=1, source_target_pairs={{0,128},{1,129},{8,136},{9,137},{16,144},{17,145},{24,152},{25,153... | collective-permute-start | bytes 24584 | tf_op jit(solution)/shard_map/ppermute | solution.py:383
  123.9 3.7 %collective-permute-start.16 = (f32[2,1024]{1,0:T(2,128)S(1)}, f32[2,1024]{1,0:T(2,128)S(1)}, u32[]{:S(2)}, u32[]{:S(2)}) collective-permute-start(f32[2,1024]{1,0:T(2,128)S(1)} %finish.1.refs_0_), channel_id=1, source_target_pairs={{0,129},{1,128},{8,137},{9,136},{16,145},{17,144},{24,153},{25,152... | collective-permute-start | bytes 24584 | tf_op jit(solution)/shard_map/ppermute | solution.py:383
  128.8 22.2 %all-to-all-start.2 = ((f32[8,2,1024]{2,1,0:T(2,128)}), f32[8,2,1024]{2,1,0:T(2,128)S(1)}, u32[]{:S(2)}, u32[]{:S(2)}) async-start(f32[8,2,1024]{2,1,0:T(2,128)} %get-tuple-element.85), calls=%async_computation.2 | async-start | bytes 131072 | tf_op jit(solution)/shard_map/all_to_all | solution.py:474
  135.7 1.0 copy-start.1
  137.9 22.3 %collective-permute-start.13 = (bf16[2,512,256]{2,1,0:T(8,128)(2,1)}, bf16[2,512,256]{2,1,0:T(8,128)(2,1)S(1)}, u32[]{:S(2)}, u32[]{:S(2)}) collective-permute-start(bf16[2,512,256]{2,1,0:T(8,128)(2,1)} %gather.8), channel_id=1, source_target_pairs={{0,0},{1,8},{8,1},{9,9},{16,16},{17,24},{24,17},{25,25},{32,32},{3... | collective-permute-start | bytes 1572872 | tf_op jit(solution)/shard_map/ppermute | solution.py:392
  153.5 15.1 %collective-permute-start.17 = (bf16[2,2,128,512]{3,2,1,0:T(8,128)(2,1)S(1)}, bf16[2,2,128,512]{3,2,1,0:T(8,128)(2,1)S(1)}, u32[]{:S(2)}, u32[]{:S(2)}) collective-permute-start(bf16[2,2,128,512]{3,2,1,0:T(8,128)(2,1)S(1)} %beamform.3), channel_id=1, source_target_pairs={{0,1},{1,0},{2,3},{3,2},{4,5},{5,4},{6,7},{7,6},{8,9},{9,8},{10,11... | collective-permute-start | bytes 1572872 | tf_op jit(solution)/shard_map/ppermute | solution.py:383

commit v7 on v6

--- a/solution.py
+++ b/solution.py
@@ -154,7 +154,7 @@
         functools.partial(correlate_kernel, scale, mask),
         in_specs=[whole(SMEM)] + [whole(VMEM)] * len(ys),
         out_specs=whole(VMEM),
-        out_shape=jax.ShapeDtypeStruct((2, inputs // 2, inputs // n_time), BF16),
+        out_shape=pltpu.HBM((2, inputs // 2, inputs // n_time), BF16),
         compiler_params=params(16),
         name="correlate",
     )(me, *ys)
@@ -170,6 +170,7 @@
     parts, rows, cols = pieces[0].shape
     steps = 2
     block = pl.BlockSpec((parts, rows // steps, cols), lambda i: (0, i, 0))
+    pieces = [pltpu.with_memory_space_constraint(pieces[0], pltpu.HBM), *pieces[1:]]
     return pl.pallas_call(
         gather_kernel,
         grid=(steps,),
@@ -210,29 +211,37 @@
     return jnp.concatenate([c[0:1] - d[1:2], c[1:2] + d[0:1]], axis=0)
 
 
-def apply_kernel(scale, first, mine_ref, other_ref, z_ref, *refs):
-    z = z_ref[...]
-    if first:
-        (out_ref,) = refs
-    else:
-        near_ref, far_ref, out_ref, fresh_ref = refs
-        z = advance(scale, z, near_ref[...] + far_ref[...])
-        fresh_ref[...] = z
+def apply_kernel(scale, mine_ref, other_ref, z_ref, near_ref, far_ref, out_ref, fresh_ref):
+    z = advance(scale, z_ref[...], near_ref[...] + far_ref[...])
+    fresh_ref[...] = z
     terms = in_terms(z)
     out_ref[...] = apply_half(terms, mine_ref) + apply_half(terms, other_ref)
 
 
 def apply_visibilities(ys, z, sums, scale):
-    first = sums is None
-    vector = jax.ShapeDtypeStruct(z.shape, F32)
-    return pl.pallas_call(
-        functools.partial(apply_kernel, scale, first),
-        in_specs=[whole(VMEM)] * (3 if first else 5),
-        out_specs=whole(VMEM) if first else [whole(VMEM)] * 2,
-        out_shape=vector if first else [vector] * 2,
+    return pl.pallas_call(
+        functools.partial(apply_kernel, scale),
+        in_specs=[whole(VMEM)] * 5,
+        out_specs=[whole(VMEM)] * 2,
+        out_shape=[jax.ShapeDtypeStruct(z.shape, F32)] * 2,
         compiler_params=params(16),
         name="apply",
-    )(*ys, z, *(sums or ()))
+    )(*ys, z, *sums)
+
+
+def begin_kernel(y_ref, z_ref, out_ref):
+    out_ref[...] = apply_half(in_terms(z_ref[...]), y_ref)
+
+
+def begin(y, z):
+    return pl.pallas_call(
+        begin_kernel,
+        in_specs=[whole(VMEM)] * 2,
+        out_specs=whole(VMEM),
+        out_shape=jax.ShapeDtypeStruct(z.shape, F32),
+        compiler_params=params(16),
+        name="begin",
+    )(y, z)
 
 
 def finish_kernel(scale, z_ref, near_ref, far_ref, fresh_ref):
@@ -251,21 +260,17 @@
 
 
 def choose_kernel(reach, source_ref, me_ref, *refs):
-    z_refs, (copies_ref, solved_ref) = refs[: len(reach)], refs[len(reach) :]
+    *z_refs, copies_ref, solved_ref, table_ref = refs
     depth = copies_ref.shape[0]
     chip, grp = me_ref[0], me_ref[1]
     core, high_half = chip % 2, chip // (2 * depth)
-    vectors = [ref[...] for ref in z_refs]
-    own = jnp.full(vectors[0].shape, (core == grp).astype(jnp.int32)) == 1
-    solved_ref[...] = jnp.where(own, vectors[0], vectors[1])
+    for (high, low), z_ref in zip(reach, z_refs):
+        table_ref[2 * high + low] = z_ref[...]
+    solved_ref[...] = table_ref[core ^ grp]
     for i in range(depth):
         slot = source_ref[high_half * 2 * depth + 2 * i + core]
         far, side = (slot // (2 * depth)) ^ high_half, (slot % 2) ^ grp
-        which = jnp.full(vectors[0].shape, 2 * far + side)
-        chosen = vectors[0]
-        for (high, low), vector in zip(reach[1:], vectors[1:]):
-            chosen = jnp.where(which == 2 * high + low, vector, chosen)
-        copies_ref[i] = chosen
+        copies_ref[i] = table_ref[2 * far + side]
 
 
 def choose(source, me, vectors, reach, depth):
@@ -278,6 +283,7 @@
             jax.ShapeDtypeStruct((depth,) + shape, F32),
             jax.ShapeDtypeStruct(shape, F32),
         ],
+        scratch_shapes=[VMEM((len(reach),) + shape, F32)],
         compiler_params=params(8),
         name="choose",
     )(source, me, *vectors)
@@ -441,25 +447,36 @@
     beam_send, corr_y, z, cosine, sine, source, me = lax.optimization_barrier(
         (beam_send, corr_y, z, cosine, sine, source, me)
     )
+    part = begin(corr_y, z)
     beam_y = lax.all_to_all(beam_send, WIDE, split_axis=0, concat_axis=0, tiled=True)
 
-    ys = [corr_y, swap(corr_y, "freq", 1)]
     scale = float(inputs) / total
-    part = apply_visibilities(ys, z, None, scale)
-    pieces = []
+    part = part + swap(part, "freq", 1)
+    part, late = lax.optimization_barrier((part, corr_y))
+    ys = [corr_y, swap(late, "freq", 1)]
+    pieces = {}
     for step in range(ITERS):
         if step:
             part, z = apply_visibilities(ys, z, sums, scale)
-        part = part + swap(part, "tm", 1)
+        near = swap(part, "tm", 1)
+        if step == 2:
+            part, *late = lax.optimization_barrier((part, *ys))
+            near, pieces[0] = lax.optimization_barrier(
+                (near, correlate(late, me, 1.0 / total, 0, n_time))
+            )
+        part = part + near
         far = swap(part, "tm", 3)
-        part, *late = lax.optimization_barrier((part, *ys))
-        piece = correlate(late, me, 1.0 / total, step, n_time)
-        far, piece = lax.optimization_barrier((far, piece))
-        pieces.append(piece)
+        if step:
+            part, *late = lax.optimization_barrier((part, *ys))
+            far, pieces[step] = lax.optimization_barrier(
+                (far, correlate(late, me, 1.0 / total, step, n_time))
+            )
         sums = (part, far)
     depth = slots // 4
-    part, far, *pieces = lax.optimization_barrier((*sums, *pieces))
-    pieces = [pieces[0]] + [swap(x, "tm", m + 1) for m, x in enumerate(pieces[1:])]
+    part, far, *bulk = lax.optimization_barrier(
+        (*sums, *(pieces[m] for m in range(1, n_time)))
+    )
+    pieces = [pieces[0]] + [swap(x, "tm", m + 1) for m, x in enumerate(bulk)]
     z = finish(z, (part, far), scale)
     reach = [(0, 0), (0, 1), (1, 0), (1, 1)]
     half_ring = slots // 2 * n_group

time: 171 us -> 167 us (0.977)
  waiting for transfers between devices: 65.5 us -> 61.1 us
    ppermute x16 -> x17, waiting for transfers between devices: 20.6 us -> 16.2 us  [swap(): return lax.ppermute(x, axis, [(i, i ^ mask) for i in range(n)])]
    ppermute x16 -> x17, starting transfers between devices: 19.2 us -> 20.7 us  [swap(): return lax.ppermute(x, axis, [(i, i ^ mask) for i in range(n)])]
  transfers between devices with their start and end apart: 21 -> 22, of which waited for: 10 -> 12; matrix products, arithmetic and copies ran while one was open for 3% -> 3% of each run, Pallas kernels for 18% -> 18%
where the time goes in v7:
time: 167 us; the launch traced here: 166 us
  starting transfers between devices  64.3 us (39%)
  waiting for transfers between devices  61.1 us (37%)
  Pallas kernels  34.9 us (21%)
  other arithmetic  2.26 us (1%)
  local copies, waits for them, and re-layouts  2.12 us (1%)
  between operations  1.76 us (1%)
    all_to_all x1, waiting for transfers between devices, body(): lax.all_to_all(corr_send, WIDE, split_axis=0, concat_axis=0, tiled=True)  38.3 us
    ppermute x17, starting transfers between devices, swap(): return lax.ppermute(x, axis, [(i, i ^ mask) for i in range(n)])  20.7 us
    ppermute x2, starting transfers between devices, cross(): return lax.ppermute(x, WIDE, pairs)  16.5 us
    ppermute x17, waiting for transfers between devices, swap(): return lax.ppermute(x, axis, [(i, i ^ mask) for i in range(n)])  16.2 us
    all_to_all x1, starting transfers between devices, body(): lax.all_to_all(corr_send, WIDE, split_axis=0, concat_axis=0, tiled=True)  13.3 us
    pallas_call x4, Pallas kernels, correlate(): pl.pallas_call(functools.partial(correlate_kernel, scale, mask), in_specs...  10.5 us
    all_to_all x1, starting transfers between devices, body(): lax.all_to_all(beam_send, WIDE, split_axis=0, concat_axis=0, tiled=True)  7.35 us
    ppermute x2, waiting for transfers between devices, cross(): return lax.ppermute(x, WIDE, pairs)  6.56 us
  transfers between devices with their start and end apart: 22, of which 12 were waited for; matrix products, arithmetic and copies ran while one was open for 3% of the time, Pallas kernels for 18%

profile of v7, /device:TPU:1, one launch (start us, length us, event | category | flops | bytes accessed | tf_op | source)
XLA Modules:
  0.0 166.4 jit_solution(16498664974215307272)
XLA Ops:
  0.6 3.1 %ingest.3 = bf16[32,2,2,16,512]{4,3,2,1,0:T(8,128)(2,1)} custom-call(s32[1]{0:T(128)} %bitcast.base_ref, s32[32]{0:T(128)} %chan_hbm.3, s32[512]{0:T(512)} %map_hbm.3, s32[512]{0:T(512)} %flag_hbm.3, bf16[32,2,16,1024]{3,2,1,0:T(8,128)(2,1)} %volts_hbm.3), custom_call_target="tpu_custom_call" | custom-call | tf_op jit(solution)/shard_map/ingest/pallas_call | solution.py:93
  3.8 13.3 %all-to-all-start = ((bf16[64,2,16,512]{3,2,1,0:T(8,128)(2,1)}), bf16[64,2,16,512]{3,2,1,0:T(8,128)(2,1)S(1)}, u32[]{:S(2)}, u32[]{:S(2)}) async-start(bf16[64,2,16,512]{3,2,1,0:T(8,128)(2,1)} %bitcast.15), calls=%async_computation | async-start | bytes 4194304 | tf_op jit(solution)/shard_map/all_to_all | solution.py:428
  17.1 3.5 %collective-permute-start = (f32[2,1024]{1,0:T(2,128)S(1)}, f32[2,1024]{1,0:T(2,128)S(1)}, u32[]{:S(2)}, u32[]{:S(2)}) collective-permute-start(f32[2,1024]{1,0:T(2,128)S(1)} %bitcast.21), channel_id=1, source_target_pairs={{0,0},{1,8},{8,1},{9,9},{16,16},{17,24},{24,17},{25,25},{32,32},{3... | collective-permute-start | bytes 24584 | tf_op jit(solution)/shard_map/ppermute | solution.py:398
  23.7 2.0 %fusion = (f32[256,512]{1,0:T(8,128)S(1)}, f32[256,512]{1,0:T(8,128)S(1)}) fusion(f32[512]{0:T(512)S(1)} %get-tuple-element.92, f32[256]{0:T(256)S(1)} %bitcast.20, f32[512]{0:T(512)S(1)} %get-tuple-element.91, f32[256]{0:T(256)S(1)} %bitcast.19, f32[]{:T(128)} %bitcast.4), kind=kLoop, calls=%fused_computation.2 | loop fusion | flops 524288 | bytes 1054724 | tf_op jit(solution)/shard_map/sin | solution.py:441
  25.7 3.0 %ingest.2 = bf16[32,2,2,16,512]{4,3,2,1,0:T(8,128)(2,1)} custom-call(s32[1]{0:T(128)} %bitcast.base_ref, s32[32]{0:T(128)} %chan_hbm.2, s32[512]{0:T(512)} %map_hbm.3, s32[512]{0:T(512)} %flag_hbm.3, bf16[32,2,16,1024]{3,2,1,0:T(8,128)(2,1)} %volts_hbm.3), custom_call_target="tpu_custom_call" | custom-call | tf_op jit(solution)/shard_map/ingest/pallas_call | solution.py:93
  28.7 38.3 %all-to-all-done.y_ref.mine_ref.refs_0_ = bf16[64,2,16,512]{3,2,1,0:T(8,128)(2,1)S(1)} async-done(((bf16[64,2,16,512]{3,2,1,0:T(8,128)(2,1)}), bf16[64,2,16,512]{3,2,1,0:T(8,128)(2,1)S(1)}, u32[]{:S(2)}, u32[]{:S(2)}) %all-to-all-start) | async-done | bytes 2097184 | tf_op jit(solution)/shard_map/all_to_all | solution.py:428
  67.1 7.3 %all-to-all-start.1 = ((bf16[64,2,16,512]{3,2,1,0:T(8,128)(2,1)}), bf16[64,2,16,512]{3,2,1,0:T(8,128)(2,1)}, u32[]{:S(2)}, u32[]{:S(2)}) async-start(bf16[64,2,16,512]{3,2,1,0:T(8,128)(2,1)} %bitcast.14), calls=%async_computation.1 | async-start | bytes 4194304 | tf_op jit(solution)/shard_map/all_to_all | solution.py:451
  78.4 1.7 %collective-permute-done.3 = f32[2,1024]{1,0:T(2,128)S(1)} collective-permute-done((f32[2,1024]{1,0:T(2,128)S(1)}, f32[2,1024]{1,0:T(2,128)S(1)}, u32[]{:S(2)}, u32[]{:S(2)}) %collective-permute-start.3) | collective-permute-done | bytes 8224 | tf_op jit(solution)/shard_map/ppermute | solution.py:389
  80.1 2.5 %collective-permute-start.4 = (f32[2,1024]{1,0:T(2,128)S(1)}, f32[2,1024]{1,0:T(2,128)S(1)}, u32[]{:S(2)}, u32[]{:S(2)}) collective-permute-start(f32[2,1024]{1,0:T(2,128)S(1)} %add.63.near_ref), channel_id=1, source_target_pairs={{0,6},{2,4},{4,2},{6,0},{1,7},{3,5},{5,3},{7,1},{8,14},{10,12},{12... | collective-permute-start | bytes 24584 | tf_op jit(solution)/shard_map/ppermute | solution.py:389
  82.6 1.6 collective-permute-done.4.far_ref
  84.2 2.0 %apply.3 = (f32[2,1024]{1,0:T(2,128)S(1)}, f32[2,1024]{1,0:T(2,128)S(1)}) custom-call(bf16[64,2,16,512]{3,2,1,0:T(8,128)(2,1)S(1)} %all-to-all-done.y_ref.mine_ref.refs_0_, bf16[64,2,16,512]{3,2,1,0:T(8,128)(2,1)S(1)} %collective-permute-done.2.other_ref.refs_1_, f32[2,1024]{1,0:T(2,128)S(1)} %collective-permute-done.z_ref, f32[2,1024]{1,0:T(2,128)S(1)} %add.63.near_ref, ...), custom_call_target="tpu_custom_call" | custom-call | tf_op jit(solution)/shard_map/apply/pallas_call | solution.py:222
  86.3 2.9 %collective-permute-done.5 = f32[2,1024]{1,0:T(2,128)S(1)} collective-permute-done((f32[2,1024]{1,0:T(2,128)S(1)}, f32[2,1024]{1,0:T(2,128)S(1)}, u32[]{:S(2)}, u32[]{:S(2)}) %collective-permute-start.5) | collective-permute-done | bytes 8224 | tf_op jit(solution)/shard_map/ppermute | solution.py:389
  89.2 2.5 %collective-permute-start.6 = (f32[2,1024]{1,0:T(2,128)S(1)}, f32[2,1024]{1,0:T(2,128)S(1)}, u32[]{:S(2)}, u32[]{:S(2)}) collective-permute-start(f32[2,1024]{1,0:T(2,128)S(1)} %add.64.near_ref), channel_id=1, source_target_pairs={{0,6},{2,4},{4,2},{6,0},{1,7},{3,5},{5,3},{7,1},{8,14},{10,12},{12... | collective-permute-start | bytes 24584 | tf_op jit(solution)/shard_map/ppermute | solution.py:389
  91.7 2.6 %correlate.4 = bf16[2,512,256]{2,1,0:T(8,128)(2,1)} custom-call(s32[3]{0:T(128)S(1)} %pad_add_fusion.me_ref, bf16[64,2,16,512]{3,2,1,0:T(8,128)(2,1)S(1)} %all-to-all-done.y_ref.mine_ref.refs_0_, bf16[64,2,16,512]{3,2,1,0:T(8,128)(2,1)S(1)} %collective-permute-done.2.other_ref.refs_1_), custom_call_target="tpu_custom_call" | custom-call | tf_op jit(solution)/shard_map/correlate/pallas_call | solution.py:153
  94.3 2.0 %apply.4 = (f32[2,1024]{1,0:T(2,128)S(1)}, f32[2,1024]{1,0:T(2,128)S(1)}) custom-call(bf16[64,2,16,512]{3,2,1,0:T(8,128)(2,1)S(1)} %all-to-all-done.y_ref.mine_ref.refs_0_, bf16[64,2,16,512]{3,2,1,0:T(8,128)(2,1)S(1)} %collective-permute-done.2.other_ref.refs_1_, f32[2,1024]{1,0:T(2,128)S(1)} %get-tuple-element.51.z_ref, f32[2,1024]{1,0:T(2,128)S(1)} %add.64.near_ref, ...), custom_call_target="tpu_custom_call" | custom-call | tf_op jit(solution)/shard_map/apply/pallas_call | solution.py:222
  96.6 2.6 %correlate.5.refs_0_ = bf16[2,512,256]{2,1,0:T(8,128)(2,1)} custom-call(s32[3]{0:T(128)S(1)} %pad_add_fusion.me_ref, bf16[64,2,16,512]{3,2,1,0:T(8,128)(2,1)S(1)} %all-to-all-done.y_ref.mine_ref.refs_0_, bf16[64,2,16,512]{3,2,1,0:T(8,128)(2,1)S(1)} %collective-permute-done.2.other_ref.refs_1_), custom_call_target="tpu_custom_call" | custom-call | tf_op jit(solution)/shard_map/correlate/pallas_call | solution.py:153
  99.5 1.5 collective-permute-start.8
  101.0 2.6 %correlate.6 = bf16[2,512,256]{2,1,0:T(8,128)(2,1)} custom-call(s32[3]{0:T(128)S(1)} %pad_add_fusion.me_ref, bf16[64,2,16,512]{3,2,1,0:T(8,128)(2,1)S(1)} %all-to-all-done.y_ref.mine_ref.refs_0_, bf16[64,2,16,512]{3,2,1,0:T(8,128)(2,1)S(1)} %collective-permute-done.2.other_ref.refs_1_), custom_call_target="tpu_custom_call" | custom-call | tf_op jit(solution)/shard_map/correlate/pallas_call | solution.py:153
  103.7 2.0 %apply.5 = (f32[2,1024]{1,0:T(2,128)S(1)}, f32[2,1024]{1,0:T(2,128)S(1)}) custom-call(bf16[64,2,16,512]{3,2,1,0:T(8,128)(2,1)S(1)} %all-to-all-done.y_ref.mine_ref.refs_0_, bf16[64,2,16,512]{3,2,1,0:T(8,128)(2,1)S(1)} %collective-permute-done.2.other_ref.refs_1_, f32[2,1024]{1,0:T(2,128)S(1)} %get-tuple-element.62.z_ref, f32[2,1024]{1,0:T(2,128)S(1)} %add.65.near_ref, ...), custom_call_target="tpu_custom_call" | custom-call | tf_op jit(solution)/shard_map/apply/pallas_call | solution.py:222
  106.4 2.2 %collective-permute-done.9 = f32[2,1024]{1,0:T(2,128)S(1)} collective-permute-done((f32[2,1024]{1,0:T(2,128)S(1)}, f32[2,1024]{1,0:T(2,128)S(1)}, u32[]{:S(2)}, u32[]{:S(2)}) %collective-permute-start.9) | collective-permute-done | bytes 8224 | tf_op jit(solution)/shard_map/ppermute | solution.py:389
  108.7 1.5 collective-permute-start.10
  110.1 2.6 %correlate.7 = bf16[2,512,256]{2,1,0:T(8,128)(2,1)} custom-call(s32[3]{0:T(128)S(1)} %pad_add_fusion.me_ref, bf16[64,2,16,512]{3,2,1,0:T(8,128)(2,1)S(1)} %all-to-all-done.y_ref.mine_ref.refs_0_, bf16[64,2,16,512]{3,2,1,0:T(8,128)(2,1)S(1)} %collective-permute-done.2.other_ref.refs_1_), custom_call_target="tpu_custom_call" | custom-call | tf_op jit(solution)/shard_map/correlate/pallas_call | solution.py:153
  112.8 2.7 %collective-permute-start.12 = (bf16[2,512,256]{2,1,0:T(8,128)(2,1)}, bf16[2,512,256]{2,1,0:T(8,128)(2,1)S(1)}, u32[]{:S(2)}, u32[]{:S(2)}) collective-permute-start(bf16[2,512,256]{2,1,0:T(8,128)(2,1)} %correlate.6), channel_id=1, source_target_pairs={{0,4},{2,6},{4,0},{6,2},{1,5},{3,7},{5,1},{7,3},{8,12},{10,14},{12... | collective-permute-start | bytes 1572872 | tf_op jit(solution)/shard_map/ppermute | solution.py:389
  118.1 2.5 %collective-permute-start.16 = (f32[2,1024]{1,0:T(2,128)S(1)}, f32[2,1024]{1,0:T(2,128)S(1)}, u32[]{:S(2)}, u32[]{:S(2)}) collective-permute-start(f32[2,1024]{1,0:T(2,128)S(1)} %finish.1.refs_0_), channel_id=1, source_target_pairs={{0,128},{1,129},{8,136},{9,137},{16,144},{17,145},{24,152},{25,153... | collective-permute-start | bytes 24584 | tf_op jit(solution)/shard_map/ppermute | solution.py:389
  120.6 1.8 %collective-permute-start.17 = (f32[2,1024]{1,0:T(2,128)S(1)}, f32[2,1024]{1,0:T(2,128)S(1)}, u32[]{:S(2)}, u32[]{:S(2)}) collective-permute-start(f32[2,1024]{1,0:T(2,128)S(1)} %finish.1.refs_0_), channel_id=1, source_target_pairs={{0,129},{1,128},{8,137},{9,136},{16,145},{17,144},{24,153},{25,152... | collective-permute-start | bytes 24584 | tf_op jit(solution)/shard_map/ppermute | solution.py:389
  125.5 6.5 %all-to-all-start.2 = ((f32[8,2,1024]{2,1,0:T(2,128)}), f32[8,2,1024]{2,1,0:T(2,128)S(1)}, u32[]{:S(2)}, u32[]{:S(2)}) async-start(f32[8,2,1024]{2,1,0:T(2,128)} %get-tuple-element.87), calls=%async_computation.2 | async-start | bytes 131072 | tf_op jit(solution)/shard_map/all_to_all | solution.py:491
  132.5 1.9 %gather.8 = bf16[2,512,256]{2,1,0:T(8,128)(2,1)} custom-call(bf16[2,512,256]{2,1,0:T(8,128)(2,1)} %correlate.5.refs_0_, bf16[2,512,256]{2,1,0:T(8,128)(2,1)S(1)} %collective-permute-done.11.refs_1_, bf16[2,512,256]{2,1,0:T(8,128)(2,1)S(1)} %collective-permute-done.12.refs_2_, bf16[2,512,256]{2,1,0:T(8,128)(2,1)S(1)} %collective-permute-done.13.refs_3_), custom_call_target="tpu_custom_call" | custom-call | tf_op jit(solution)/shard_map/gather/pallas_call | solution.py:174
  134.4 13.0 %collective-permute-start.14 = (bf16[2,512,256]{2,1,0:T(8,128)(2,1)}, bf16[2,512,256]{2,1,0:T(8,128)(2,1)S(1)}, u32[]{:S(2)}, u32[]{:S(2)}) collective-permute-start(bf16[2,512,256]{2,1,0:T(8,128)(2,1)} %gather.8), channel_id=1, source_target_pairs={{0,0},{1,8},{8,1},{9,9},{16,16},{17,24},{24,17},{25,25},{32,32},{3... | collective-permute-start | bytes 1572872 | tf_op jit(solution)/shard_map/ppermute | solution.py:398
  147.4 2.4 %beamform.3 = bf16[2,2,128,512]{3,2,1,0:T(8,128)(2,1)S(1)} custom-call(s32[32]{0:T(128)S(1)} %select_reduce_fusion.source_ref, s32[3]{0:T(128)S(1)} %pad_add_fusion.me_ref, f32[8,2,1024]{2,1,0:T(2,128)S(1)} %all-to-all-done.2.line_ref, f32[256,512]{1,0:T(8,128)S(1)} %get-tuple-element.88.cos_ref, f32[256,512]{1,0:T(8,128)S(1)} %get-tuple-element.89.sin_ref, ...), custom_call_target="tpu_custom_call" | custom-call | tf_op jit(solution)/shard_map/beamform/pallas_call | solution.py:336
  149.9 6.6 %collective-permute-done.14.in_ref = bf16[2,512,256]{2,1,0:T(8,128)(2,1)S(1)} collective-permute-done((bf16[2,512,256]{2,1,0:T(8,128)(2,1)}, bf16[2,512,256]{2,1,0:T(8,128)(2,1)S(1)}, u32[]{:S(2)}, u32[]{:S(2)}) %collective-permute-start.14) | collective-permute-done | bytes 524320 | tf_op jit(solution)/shard_map/ppermute | solution.py:398
  157.5 3.1 %beamform.2.own_hbm = bf16[2,2,128,1024]{3,2,1,0:T(8,128)(2,1)} custom-call(s32[32]{0:T(128)S(1)} %select_reduce_fusion.source_ref, s32[3]{0:T(128)S(1)} %pad_add_fusion.me_ref, f32[8,2,1024]{2,1,0:T(2,128)S(1)} %all-to-all-done.2.line_ref, f32[256,512]{1,0:T(8,128)S(1)} %get-tuple-element.88.cos_ref, f32[256,512]{1,0:T(8,128)S(1)} %get-tuple-element.89.sin_ref, ...), custom_call_target="tpu_custom_call" | custom-call | tf_op jit(solution)/shard_map/beamform/pallas_call | solution.py:336
  160.7 4.2 %collective-permute-done.18.other_ref = bf16[2,2,128,512]{3,2,1,0:T(8,128)(2,1)S(1)} collective-permute-done((bf16[2,2,128,512]{3,2,1,0:T(8,128)(2,1)S(1)}, bf16[2,2,128,512]{3,2,1,0:T(8,128)(2,1)S(1)}, u32[]{:S(2)}, u32[]{:S(2)}) %collective-permute-start.18) | collective-permute-done | bytes 524320 | tf_op jit(solution)/shard_map/ppermute | solution.py:389
  (55 shorter events, 16.6 us)
Async XLA Ops:
  3.7 13.4 %copy-start.5 = (f32[1,2,1024]{2,1,0:T(2,128)S(1)}, f32[1,2,1024]{2,1,0:T(2,128)}, u32[]{:S(2)}) copy-start(f32[1,2,1024]{2,1,0:T(2,128)} %param.9) | copy-start | bytes 24580
  3.7 16.9 %copy-start.4 = (s32[32]{0:T(128)S(1)}, s32[32]{0:T(128)}, u32[]{:S(2)}) copy-start(s32[32]{0:T(128)} %chan_hbm.2) | copy-start | bytes 388
  3.7 18.2 %copy-start.1 = (f32[2,512]{1,0:T(2,128)S(1)}, f32[2,512]{1,0:T(2,128)}, u32[]{:S(2)}) copy-start(f32[2,512]{1,0:T(2,128)} %param.12) | copy-start | bytes 12292
  3.7 18.3 %copy-start = (s32[512]{0:T(512)S(1)}, s32[512]{0:T(512)}, u32[]{:S(2)}) copy-start(s32[512]{0:T(512)} %map_hbm.3) | copy-start | bytes 6148
  3.8 19.4 %copy-start.3 = (s32[32]{0:T(128)S(1)}, s32[32]{0:T(128)}, u32[]{:S(2)}) copy-start(s32[32]{0:T(128)} %chan_hbm.3) | copy-start | bytes 388
  3.8 19.9 %copy-start.2 = (s32[2,256]{1,0:T(2,128)S(1)}, s32[2,256]{1,0:T(2,128)}, u32[]{:S(2)}) copy-start(s32[2,256]{1,0:T(2,128)} %param.13) | copy-start | bytes 6148
  3.8 63.3 %all-to-all-start = ((bf16[64,2,16,512]{3,2,1,0:T(8,128)(2,1)}), bf16[64,2,16,512]{3,2,1,0:T(8,128)(2,1)S(1)}, u32[]{:S(2)}, u32[]{:S(2)}) async-start(bf16[64,2,16,512]{3,2,1,0:T(8,128)(2,1)} %bitcast.15), calls=%async_computation | async-start | bytes 4194304 | tf_op jit(solution)/shard_map/all_to_all | solution.py:428
  17.1 11.6 %collective-permute-start = (f32[2,1024]{1,0:T(2,128)S(1)}, f32[2,1024]{1,0:T(2,128)S(1)}, u32[]{:S(2)}, u32[]{:S(2)}) collective-permute-start(f32[2,1024]{1,0:T(2,128)S(1)} %bitcast.21), channel_id=1, source_target_pairs={{0,0},{1,8},{8,1},{9,9},{16,16},{17,24},{24,17},{25,25},{32,32},{3... | collective-permute-start | bytes 24584 | tf_op jit(solution)/shard_map/ppermute | solution.py:398
  67.1 58.5 %all-to-all-start.1 = ((bf16[64,2,16,512]{3,2,1,0:T(8,128)(2,1)}), bf16[64,2,16,512]{3,2,1,0:T(8,128)(2,1)}, u32[]{:S(2)}, u32[]{:S(2)}) async-start(bf16[64,2,16,512]{3,2,1,0:T(8,128)(2,1)} %bitcast.14), calls=%async_computation.1 | async-start | bytes 4194304 | tf_op jit(solution)/shard_map/all_to_all | solution.py:451
  75.4 1.4 collective-permute-start.1
  76.9 7.4 %collective-permute-start.2 = (bf16[64,2,16,512]{3,2,1,0:T(8,128)(2,1)S(1)}, bf16[64,2,16,512]{3,2,1,0:T(8,128)(2,1)S(1)}, u32[]{:S(2)}, u32[]{:S(2)}) collective-permute-start(bf16[64,2,16,512]{3,2,1,0:T(8,128)(2,1)S(1)} %all-to-all-done.y_ref.mine_ref.refs_0_), channel_id=1, source_target_pairs={{0,8},{8,0},{16,24},{24,16},{32,40},{40,32},{48,56},{56,48},{64,72... | collective-permute-start | bytes 6291464 | tf_op jit(solution)/shard_map/ppermute | solution.py:389
  77.2 2.9 %collective-permute-start.3 = (f32[2,1024]{1,0:T(2,128)S(1)}, f32[2,1024]{1,0:T(2,128)S(1)}, u32[]{:S(2)}, u32[]{:S(2)}) collective-permute-start(f32[2,1024]{1,0:T(2,128)S(1)} %add.62), channel_id=1, source_target_pairs={{0,2},{2,0},{4,6},{6,4},{1,3},{3,1},{5,7},{7,5},{8,10},{10,8},{12,... | collective-permute-start | bytes 24584 | tf_op jit(solution)/shard_map/ppermute | solution.py:389
  80.1 4.1 %collective-permute-start.4 = (f32[2,1024]{1,0:T(2,128)S(1)}, f32[2,1024]{1,0:T(2,128)S(1)}, u32[]{:S(2)}, u32[]{:S(2)}) collective-permute-start(f32[2,1024]{1,0:T(2,128)S(1)} %add.63.near_ref), channel_id=1, source_target_pairs={{0,6},{2,4},{4,2},{6,0},{1,7},{3,5},{5,3},{7,1},{8,14},{10,12},{12... | collective-permute-start | bytes 24584 | tf_op jit(solution)/shard_map/ppermute | solution.py:389
  86.2 3.0 %collective-permute-start.5 = (f32[2,1024]{1,0:T(2,128)S(1)}, f32[2,1024]{1,0:T(2,128)S(1)}, u32[]{:S(2)}, u32[]{:S(2)}) collective-permute-start(f32[2,1024]{1,0:T(2,128)S(1)} %get-tuple-element.52), channel_id=1, source_target_pairs={{0,2},{2,0},{4,6},{6,4},{1,3},{3,1},{5,7},{7,5},{8,10},{10,8},{12,... | collective-permute-start | bytes 24584 | tf_op jit(solution)/shard_map/ppermute | solution.py:389
  89.2 5.1 %collective-permute-start.6 = (f32[2,1024]{1,0:T(2,128)S(1)}, f32[2,1024]{1,0:T(2,128)S(1)}, u32[]{:S(2)}, u32[]{:S(2)}) collective-permute-start(f32[2,1024]{1,0:T(2,128)S(1)} %add.64.near_ref), channel_id=1, source_target_pairs={{0,6},{2,4},{4,2},{6,0},{1,7},{3,5},{5,3},{7,1},{8,14},{10,12},{12... | collective-permute-start | bytes 24584 | tf_op jit(solution)/shard_map/ppermute | solution.py:389
  96.4 3.2 %collective-permute-start.7 = (f32[2,1024]{1,0:T(2,128)S(1)}, f32[2,1024]{1,0:T(2,128)S(1)}, u32[]{:S(2)}, u32[]{:S(2)}) collective-permute-start(f32[2,1024]{1,0:T(2,128)S(1)} %get-tuple-element.63), channel_id=1, source_target_pairs={{0,2},{2,0},{4,6},{6,4},{1,3},{3,1},{5,7},{7,5},{8,10},{10,8},{12,... | collective-permute-start | bytes 24584 | tf_op jit(solution)/shard_map/ppermute | solution.py:389
  99.5 4.1 %collective-permute-start.8 = (f32[2,1024]{1,0:T(2,128)S(1)}, f32[2,1024]{1,0:T(2,128)S(1)}, u32[]{:S(2)}, u32[]{:S(2)}) collective-permute-start(f32[2,1024]{1,0:T(2,128)S(1)} %add.65.near_ref), channel_id=1, source_target_pairs={{0,6},{2,4},{4,2},{6,0},{1,7},{3,5},{5,3},{7,1},{8,14},{10,12},{12... | collective-permute-start | bytes 24584 | tf_op jit(solution)/shard_map/ppermute | solution.py:389
  105.7 3.0 %collective-permute-start.9 = (f32[2,1024]{1,0:T(2,128)S(1)}, f32[2,1024]{1,0:T(2,128)S(1)}, u32[]{:S(2)}, u32[]{:S(2)}) collective-permute-start(f32[2,1024]{1,0:T(2,128)S(1)} %get-tuple-element.69), channel_id=1, source_target_pairs={{0,2},{2,0},{4,6},{6,4},{1,3},{3,1},{5,7},{7,5},{8,10},{10,8},{12,... | collective-permute-start | bytes 24584 | tf_op jit(solution)/shard_map/ppermute | solution.py:389
  108.7 4.1 %collective-permute-start.10 = (f32[2,1024]{1,0:T(2,128)S(1)}, f32[2,1024]{1,0:T(2,128)S(1)}, u32[]{:S(2)}, u32[]{:S(2)}) collective-permute-start(f32[2,1024]{1,0:T(2,128)S(1)} %add.66.near_ref), channel_id=1, source_target_pairs={{0,6},{2,4},{4,2},{6,0},{1,7},{3,5},{5,3},{7,1},{8,14},{10,12},{12... | collective-permute-start | bytes 24584 | tf_op jit(solution)/shard_map/ppermute | solution.py:389
  112.8 19.2 %collective-permute-start.11 = (bf16[2,512,256]{2,1,0:T(8,128)(2,1)}, bf16[2,512,256]{2,1,0:T(8,128)(2,1)S(1)}, u32[]{:S(2)}, u32[]{:S(2)}) collective-permute-start(bf16[2,512,256]{2,1,0:T(8,128)(2,1)} %correlate.4), channel_id=1, source_target_pairs={{0,2},{2,0},{4,6},{6,4},{1,3},{3,1},{5,7},{7,5},{8,10},{10,8},{12,... | collective-permute-start | bytes 1572872 | tf_op jit(solution)/shard_map/ppermute | solution.py:389
  112.8 19.7 %collective-permute-start.12 = (bf16[2,512,256]{2,1,0:T(8,128)(2,1)}, bf16[2,512,256]{2,1,0:T(8,128)(2,1)S(1)}, u32[]{:S(2)}, u32[]{:S(2)}) collective-permute-start(bf16[2,512,256]{2,1,0:T(8,128)(2,1)} %correlate.6), channel_id=1, source_target_pairs={{0,4},{2,6},{4,0},{6,2},{1,5},{3,7},{5,1},{7,3},{8,12},{10,14},{12... | collective-permute-start | bytes 1572872 | tf_op jit(solution)/shard_map/ppermute | solution.py:389
  115.4 17.0 %collective-permute-start.13 = (bf16[2,512,256]{2,1,0:T(8,128)(2,1)}, bf16[2,512,256]{2,1,0:T(8,128)(2,1)S(1)}, u32[]{:S(2)}, u32[]{:S(2)}) collective-permute-start(bf16[2,512,256]{2,1,0:T(8,128)(2,1)} %correlate.7), channel_id=1, source_target_pairs={{0,6},{2,4},{4,2},{6,0},{1,7},{3,5},{5,3},{7,1},{8,14},{10,12},{12... | collective-permute-start | bytes 1572872 | tf_op jit(solution)/shard_map/ppermute | solution.py:389
  116.8 3.8 %collective-permute-start.15 = (f32[2,1024]{1,0:T(2,128)S(1)}, f32[2,1024]{1,0:T(2,128)S(1)}, u32[]{:S(2)}, u32[]{:S(2)}) collective-permute-start(f32[2,1024]{1,0:T(2,128)S(1)} %finish.1.refs_0_), channel_id=1, source_target_pairs={{0,1},{1,0},{8,9},{9,8},{16,17},{17,16},{24,25},{25,24},{32,33},{3... | collective-permute-start | bytes 24584 | tf_op jit(solution)/shard_map/ppermute | solution.py:389
  118.1 5.0 %collective-permute-start.16 = (f32[2,1024]{1,0:T(2,128)S(1)}, f32[2,1024]{1,0:T(2,128)S(1)}, u32[]{:S(2)}, u32[]{:S(2)}) collective-permute-start(f32[2,1024]{1,0:T(2,128)S(1)} %finish.1.refs_0_), channel_id=1, source_target_pairs={{0,128},{1,129},{8,136},{9,137},{16,144},{17,145},{24,152},{25,153... | collective-permute-start | bytes 24584 | tf_op jit(solution)/shard_map/ppermute | solution.py:389
  120.6 3.7 %collective-permute-start.17 = (f32[2,1024]{1,0:T(2,128)S(1)}, f32[2,1024]{1,0:T(2,128)S(1)}, u32[]{:S(2)}, u32[]{:S(2)}) collective-permute-start(f32[2,1024]{1,0:T(2,128)S(1)} %finish.1.refs_0_), channel_id=1, source_target_pairs={{0,129},{1,128},{8,137},{9,136},{16,145},{17,144},{24,153},{25,152... | collective-permute-start | bytes 24584 | tf_op jit(solution)/shard_map/ppermute | solution.py:389
  125.5 21.8 %all-to-all-start.2 = ((f32[8,2,1024]{2,1,0:T(2,128)}), f32[8,2,1024]{2,1,0:T(2,128)S(1)}, u32[]{:S(2)}, u32[]{:S(2)}) async-start(f32[8,2,1024]{2,1,0:T(2,128)} %get-tuple-element.87), calls=%async_computation.2 | async-start | bytes 131072 | tf_op jit(solution)/shard_map/all_to_all | solution.py:491
  134.4 22.1 %collective-permute-start.14 = (bf16[2,512,256]{2,1,0:T(8,128)(2,1)}, bf16[2,512,256]{2,1,0:T(8,128)(2,1)S(1)}, u32[]{:S(2)}, u32[]{:S(2)}) collective-permute-start(bf16[2,512,256]{2,1,0:T(8,128)(2,1)} %gather.8), channel_id=1, source_target_pairs={{0,0},{1,8},{8,1},{9,9},{16,16},{17,24},{24,17},{25,25},{32,32},{3... | collective-permute-start | bytes 1572872 | tf_op jit(solution)/shard_map/ppermute | solution.py:398
  149.8 15.1 %collective-permute-start.18 = (bf16[2,2,128,512]{3,2,1,0:T(8,128)(2,1)S(1)}, bf16[2,2,128,512]{3,2,1,0:T(8,128)(2,1)S(1)}, u32[]{:S(2)}, u32[]{:S(2)}) collective-permute-start(bf16[2,2,128,512]{3,2,1,0:T(8,128)(2,1)S(1)} %beamform.3), channel_id=1, source_target_pairs={{0,1},{1,0},{2,3},{3,2},{4,5},{5,4},{6,7},{7,6},{8,9},{9,8},{10,11... | collective-permute-start | bytes 1572872 | tf_op jit(solution)/shard_map/ppermute | solution.py:389

commit v8 on v7

--- a/solution.py
+++ b/solution.py
@@ -260,17 +260,16 @@
 
 
 def choose_kernel(reach, source_ref, me_ref, *refs):
-    *z_refs, copies_ref, solved_ref, table_ref = refs
+    *z_refs, copies_ref, table_ref = refs
     depth = copies_ref.shape[0]
-    chip, grp = me_ref[0], me_ref[1]
-    core, high_half = chip % 2, chip // (2 * depth)
+    high_half, grp = me_ref[0] // (2 * depth), me_ref[1]
     for (high, low), z_ref in zip(reach, z_refs):
         table_ref[2 * high + low] = z_ref[...]
-    solved_ref[...] = table_ref[core ^ grp]
     for i in range(depth):
-        slot = source_ref[high_half * 2 * depth + 2 * i + core]
-        far, side = (slot // (2 * depth)) ^ high_half, (slot % 2) ^ grp
-        copies_ref[i] = table_ref[2 * far + side]
+        for core in range(2):
+            slot = source_ref[high_half * 2 * depth + 2 * i + core]
+            far, side = (slot // (2 * depth)) ^ high_half, (slot % 2) ^ grp
+            copies_ref[i, core] = table_ref[2 * far + side]
 
 
 def choose(source, me, vectors, reach, depth):
@@ -278,21 +277,56 @@
     return pl.pallas_call(
         functools.partial(choose_kernel, reach),
         in_specs=[whole(SMEM)] * 2 + [whole(VMEM)] * len(reach),
-        out_specs=[whole(VMEM)] * 2,
-        out_shape=[
-            jax.ShapeDtypeStruct((depth,) + shape, F32),
-            jax.ShapeDtypeStruct(shape, F32),
-        ],
+        out_specs=whole(VMEM),
+        out_shape=jax.ShapeDtypeStruct((depth, 2) + shape, F32),
         scratch_shapes=[VMEM((len(reach),) + shape, F32)],
         compiler_params=params(8),
         name="choose",
     )(source, me, *vectors)
 
 
-def beam_kernel(turn, source_ref, me_ref, line_ref, cos_ref, sin_ref, y_ref, *refs):
+def hand_kernel(source_ref, me_ref, line_ref, vector_ref, hand_ref):
+    slot = source_ref[me_ref[0] // 2 * 2]
+    hand_ref[0] = line_ref[(slot // 2) % line_ref.shape[0], 0]
+    hand_ref[1] = vector_ref[...]
+
+
+def hand(source, me, line, vector):
+    return pl.pallas_call(
+        hand_kernel,
+        in_specs=[whole(SMEM)] * 2 + [whole(VMEM)] * 2,
+        out_specs=whole(VMEM),
+        out_shape=jax.ShapeDtypeStruct((2,) + vector.shape, F32),
+        compiler_params=params(8),
+        name="hand",
+    )(source, me, line, vector)
+
+
+def settle_kernel(me_ref, z_ref, vector_ref, handed_ref, solved_ref):
+    core, grp = me_ref[0] % 2, me_ref[1]
+    shape = z_ref.shape
+    first = jnp.full(shape, core) == 0
+    away = jnp.where(first, handed_ref[1], vector_ref[...])
+    solved_ref[...] = jnp.where(jnp.full(shape, core ^ grp) == 0, z_ref[...], away)
+
+
+def settle(me, z, vector, handed):
+    return pl.pallas_call(
+        settle_kernel,
+        in_specs=[whole(SMEM)] + [whole(VMEM)] * 3,
+        out_specs=pl.BlockSpec(z.shape, lambda: (0, 0)),
+        out_shape=pltpu.HBM(z.shape, F32),
+        compiler_params=params(8),
+        name="settle",
+    )(me, z, vector, handed)
+
+
+def beam_kernel(turn, source_ref, me_ref, line_ref, handed_ref, cos_ref, sin_ref, y_ref, *refs):
     out_ref = refs[0] if turn else refs[1]
     slot = source_ref[me_ref[0]]
-    gains = line_ref[(slot // 2) % line_ref.shape[0]]
+    gains = line_ref[(slot // 2) % line_ref.shape[0], 1]
+    first = jnp.full(gains.shape, me_ref[0] % 2) == 0
+    gains = jnp.where(first, handed_ref[0], gains)
     blocks, _, rows, samples = y_ref.shape
     stations = blocks // 2 * rows
     beams = out_ref.shape[2]
@@ -323,7 +357,7 @@
         store.wait()
 
 
-def beamform(turn, source, me, line, cosine, sine, y, groups):
+def beamform(turn, source, me, line, handed, cosine, sine, y, groups):
     samples = y.shape[3]
     beams = cosine.shape[0] // groups
     shape = (2, 2, beams, samples)
@@ -335,13 +369,13 @@
         scratch = [VMEM(shape, BF16), pltpu.SemaphoreType.DMA((2,))]
     return pl.pallas_call(
         functools.partial(beam_kernel, turn),
-        in_specs=[whole(SMEM)] * 2 + [whole(VMEM)] * 4,
+        in_specs=[whole(SMEM)] * 2 + [whole(VMEM)] * 5,
         out_specs=out_spec,
         out_shape=out_shape,
         scratch_shapes=scratch,
         compiler_params=params(16),
         name="beamform",
-    )(source, me, line, cosine, sine, y)
+    )(source, me, line, handed, cosine, sine, y)
 
 
 def place_kernel(me_ref, own_hbm, other_ref, out_hbm, sem):
@@ -387,6 +421,11 @@
 def swap(x, axis, mask):
     n = lax.axis_size(axis)
     return lax.ppermute(x, axis, [(i, i ^ mask) for i in range(n)])
+
+
+def swap_odd(x, mask):
+    n = lax.axis_size("freq") * lax.axis_size("grp")
+    return lax.ppermute(x, WIDE, [(i, i ^ mask) for i in range(n) if i // 2 % 2])
 
 
 def cross(x):
@@ -480,8 +519,8 @@
     z = finish(z, (part, far), scale)
     reach = [(0, 0), (0, 1), (1, 0), (1, 1)]
     half_ring = slots // 2 * n_group
-    vectors = [z] + [swap(z, WIDE, high * half_ring + low) for high, low in reach[1:]]
-    copies, solved = choose(source, me, vectors, reach, depth)
+    vectors = [z] + [swap_odd(z, high * half_ring + low) for high, low in reach[1:]]
+    copies = choose(source, me, vectors, reach, depth)
     copies, beam_y = lax.optimization_barrier((copies, beam_y))
     groups = [
         [high * 2 * depth + 2 * i + c for i in range(depth)]
@@ -492,11 +531,18 @@
         copies, "freq", split_axis=0, concat_axis=0, axis_index_groups=groups, tiled=True
     )
 
-    block = cross(gather(pieces))
-    away = beamform(1, source, me, line, cosine, sine, beam_y, n_group)
+    line, block = lax.optimization_barrier((line, gather(pieces)))
+    block = cross(block)
+    handed = lax.ppermute(
+        hand(source, me, line, vectors[1]),
+        "freq",
+        [(i + 1, i) for i in range(0, slots, 2)],
+    )
+    away = beamform(1, source, me, line, handed, cosine, sine, beam_y, n_group)
     other = swap(away, "grp", 1)
-    own = beamform(0, source, me, line, cosine, sine, beam_y, n_group)
+    own = beamform(0, source, me, line, handed, cosine, sine, beam_y, n_group)
     visibilities = widen(block)
+    solved = settle(me, z, vectors[1], handed)
     beams = place(me, own, other)
     return visibilities[None], solved[None], beams[None]
 

time: 167 us -> 170 us (1.018)
  waiting for transfers between devices: 61.1 us -> 67.3 us
  starting transfers between devices: 64.3 us -> 58.7 us
    ppermute x2, starting transfers between devices: 16.5 us -> 5.46 us  [cross(): return lax.ppermute(x, WIDE, pairs)]
    ppermute x0 -> x4, starting transfers between devices: none -> 10.9 us  [the longest x3 9.58 us: swap_odd(): lax.ppermute(x, WIDE, [(i, i ^ mask) for i in range(n) if i // 2 % 2])]
    all_to_all x1, waiting for transfers between devices: 0.01 us -> 5.82 us  [body(): lax.all_to_all(copies, 'freq', split_axis=0, concat_axis=0, axis_index_gr...]
    ppermute x17 -> x14, starting transfers between devices: 20.7 us -> 15.2 us  [swap(): return lax.ppermute(x, axis, [(i, i ^ mask) for i in range(n)])]
    ppermute x0 -> x4, waiting for transfers between devices: none -> 3.84 us  [the longest x3 3.84 us: swap_odd(): lax.ppermute(x, WIDE, [(i, i ^ mask) for i in range(n) if i // 2 % 2])]
    ppermute x17 -> x14, waiting for transfers between devices: 16.2 us -> 13.4 us  [swap(): return lax.ppermute(x, axis, [(i, i ^ mask) for i in range(n)])]
    pallas_call x0 -> x2, Pallas kernels: none -> 1.72 us  [the longest x1 1.15 us: settle(): pl.pallas_call(settle_kernel, in_specs=[whole(SMEM)] + [whole(VMEM)] * 3,...]
  transfers between devices with their start and end apart: 22 -> 23, of which waited for: 12 -> 11; matrix products, arithmetic and copies ran while one was open for 3% -> 3% of each run, Pallas kernels for 18% -> 18%
where the time goes in v8:
time: 170 us; the launch traced here: 169 us
  waiting for transfers between devices  67.3 us (40%)
  starting transfers between devices  58.7 us (35%)
  Pallas kernels  35.9 us (21%)
  local copies, waits for them, and re-layouts  2.9 us (2%)
  other arithmetic  2.26 us (1%)
  between operations  1.84 us (1%)
    all_to_all x1, waiting for transfers between devices, body(): lax.all_to_all(corr_send, WIDE, split_axis=0, concat_axis=0, tiled=True)  38.3 us
    ppermute x14, starting transfers between devices, swap(): return lax.ppermute(x, axis, [(i, i ^ mask) for i in range(n)])  15.2 us
    ppermute x14, waiting for transfers between devices, swap(): return lax.ppermute(x, axis, [(i, i ^ mask) for i in range(n)])  13.4 us
    all_to_all x1, starting transfers between devices, body(): lax.all_to_all(corr_send, WIDE, split_axis=0, concat_axis=0, tiled=True)  13.3 us
    pallas_call x4, Pallas kernels, correlate(): pl.pallas_call(functools.partial(correlate_kernel, scale, mask), in_specs...  10.5 us
    ppermute x3, starting transfers between devices, swap_odd(): lax.ppermute(x, WIDE, [(i, i ^ mask) for i in range(n) if i // 2 % 2])  9.58 us
    all_to_all x1, starting transfers between devices, body(): lax.all_to_all(beam_send, WIDE, split_axis=0, concat_axis=0, tiled=True)  7.35 us
    all_to_all x1, starting transfers between devices, body(): lax.all_to_all(copies, 'freq', split_axis=0, concat_axis=0, axis_index_gr...  6.48 us
  transfers between devices with their start and end apart: 23, of which 11 were waited for; matrix products, arithmetic and copies ran while one was open for 3% of the time, Pallas kernels for 18%

profile of v8, /device:TPU:1, one launch (start us, length us, event | category | flops | bytes accessed | tf_op | source)
XLA Modules:
  0.0 168.9 jit_solution(3814091420299588843)
XLA Ops:
  0.6 3.1 %ingest.3 = bf16[32,2,2,16,512]{4,3,2,1,0:T(8,128)(2,1)} custom-call(s32[1]{0:T(128)} %bitcast.base_ref, s32[32]{0:T(128)} %chan_hbm.3, s32[512]{0:T(512)} %map_hbm.3, s32[512]{0:T(512)} %flag_hbm.3, bf16[32,2,16,1024]{3,2,1,0:T(8,128)(2,1)} %volts_hbm.3), custom_call_target="tpu_custom_call" | custom-call | tf_op jit(solution)/shard_map/ingest/pallas_call | solution.py:93
  3.8 13.3 %all-to-all-start = ((bf16[64,2,16,512]{3,2,1,0:T(8,128)(2,1)}), bf16[64,2,16,512]{3,2,1,0:T(8,128)(2,1)S(1)}, u32[]{:S(2)}, u32[]{:S(2)}) async-start(bf16[64,2,16,512]{3,2,1,0:T(8,128)(2,1)} %bitcast.15), calls=%async_computation | async-start | bytes 4194304 | tf_op jit(solution)/shard_map/all_to_all | solution.py:467
  17.1 3.5 %collective-permute-start = (f32[2,1024]{1,0:T(2,128)S(1)}, f32[2,1024]{1,0:T(2,128)S(1)}, u32[]{:S(2)}, u32[]{:S(2)}) collective-permute-start(f32[2,1024]{1,0:T(2,128)S(1)} %bitcast.22), channel_id=1, source_target_pairs={{0,0},{1,8},{8,1},{9,9},{16,16},{17,24},{24,17},{25,25},{32,32},{3... | collective-permute-start | bytes 24584 | tf_op jit(solution)/shard_map/ppermute | solution.py:437
  23.7 2.0 %fusion = (f32[256,512]{1,0:T(8,128)S(1)}, f32[256,512]{1,0:T(8,128)S(1)}) fusion(f32[512]{0:T(512)S(1)} %get-tuple-element.92, f32[256]{0:T(256)S(1)} %bitcast.21, f32[512]{0:T(512)S(1)} %get-tuple-element.91, f32[256]{0:T(256)S(1)} %bitcast.20, f32[]{:T(128)} %bitcast.4), kind=kLoop, calls=%fused_computation.2 | loop fusion | flops 524288 | bytes 1054724 | tf_op jit(solution)/shard_map/sin | solution.py:480
  25.7 3.0 %ingest.2 = bf16[32,2,2,16,512]{4,3,2,1,0:T(8,128)(2,1)} custom-call(s32[1]{0:T(128)} %bitcast.base_ref, s32[32]{0:T(128)} %chan_hbm.2, s32[512]{0:T(512)} %map_hbm.3, s32[512]{0:T(512)} %flag_hbm.3, bf16[32,2,16,1024]{3,2,1,0:T(8,128)(2,1)} %volts_hbm.3), custom_call_target="tpu_custom_call" | custom-call | tf_op jit(solution)/shard_map/ingest/pallas_call | solution.py:93
  28.8 38.3 %all-to-all-done.y_ref.mine_ref.refs_0_ = bf16[64,2,16,512]{3,2,1,0:T(8,128)(2,1)S(1)} async-done(((bf16[64,2,16,512]{3,2,1,0:T(8,128)(2,1)}), bf16[64,2,16,512]{3,2,1,0:T(8,128)(2,1)S(1)}, u32[]{:S(2)}, u32[]{:S(2)}) %all-to-all-start) | async-done | bytes 2097184 | tf_op jit(solution)/shard_map/all_to_all | solution.py:467
  67.1 7.3 %all-to-all-start.1 = ((bf16[64,2,16,512]{3,2,1,0:T(8,128)(2,1)}), bf16[64,2,16,512]{3,2,1,0:T(8,128)(2,1)}, u32[]{:S(2)}, u32[]{:S(2)}) async-start(bf16[64,2,16,512]{3,2,1,0:T(8,128)(2,1)} %bitcast.14), calls=%async_computation.1 | async-start | bytes 4194304 | tf_op jit(solution)/shard_map/all_to_all | solution.py:490
  78.4 1.7 %collective-permute-done.3 = f32[2,1024]{1,0:T(2,128)S(1)} collective-permute-done((f32[2,1024]{1,0:T(2,128)S(1)}, f32[2,1024]{1,0:T(2,128)S(1)}, u32[]{:S(2)}, u32[]{:S(2)}) %collective-permute-start.3) | collective-permute-done | bytes 8224 | tf_op jit(solution)/shard_map/ppermute | solution.py:423
  80.1 2.5 %collective-permute-start.4 = (f32[2,1024]{1,0:T(2,128)S(1)}, f32[2,1024]{1,0:T(2,128)S(1)}, u32[]{:S(2)}, u32[]{:S(2)}) collective-permute-start(f32[2,1024]{1,0:T(2,128)S(1)} %add.63.near_ref), channel_id=1, source_target_pairs={{0,6},{2,4},{4,2},{6,0},{1,7},{3,5},{5,3},{7,1},{8,14},{10,12},{12... | collective-permute-start | bytes 24584 | tf_op jit(solution)/shard_map/ppermute | solution.py:423
  82.6 1.6 collective-permute-done.4.far_ref
  84.2 2.0 %apply.3 = (f32[2,1024]{1,0:T(2,128)S(1)}, f32[2,1024]{1,0:T(2,128)S(1)}) custom-call(bf16[64,2,16,512]{3,2,1,0:T(8,128)(2,1)S(1)} %all-to-all-done.y_ref.mine_ref.refs_0_, bf16[64,2,16,512]{3,2,1,0:T(8,128)(2,1)S(1)} %collective-permute-done.2.other_ref.refs_1_, f32[2,1024]{1,0:T(2,128)S(1)} %collective-permute-done.z_ref, f32[2,1024]{1,0:T(2,128)S(1)} %add.63.near_ref, ...), custom_call_target="tpu_custom_call" | custom-call | tf_op jit(solution)/shard_map/apply/pallas_call | solution.py:222
  86.4 2.9 %collective-permute-done.5 = f32[2,1024]{1,0:T(2,128)S(1)} collective-permute-done((f32[2,1024]{1,0:T(2,128)S(1)}, f32[2,1024]{1,0:T(2,128)S(1)}, u32[]{:S(2)}, u32[]{:S(2)}) %collective-permute-start.5) | collective-permute-done | bytes 8224 | tf_op jit(solution)/shard_map/ppermute | solution.py:423
  89.3 2.5 %collective-permute-start.6 = (f32[2,1024]{1,0:T(2,128)S(1)}, f32[2,1024]{1,0:T(2,128)S(1)}, u32[]{:S(2)}, u32[]{:S(2)}) collective-permute-start(f32[2,1024]{1,0:T(2,128)S(1)} %add.64.near_ref), channel_id=1, source_target_pairs={{0,6},{2,4},{4,2},{6,0},{1,7},{3,5},{5,3},{7,1},{8,14},{10,12},{12... | collective-permute-start | bytes 24584 | tf_op jit(solution)/shard_map/ppermute | solution.py:423
  91.7 2.6 %correlate.4 = bf16[2,512,256]{2,1,0:T(8,128)(2,1)} custom-call(s32[3]{0:T(128)S(1)} %pad_add_fusion.me_ref, bf16[64,2,16,512]{3,2,1,0:T(8,128)(2,1)S(1)} %all-to-all-done.y_ref.mine_ref.refs_0_, bf16[64,2,16,512]{3,2,1,0:T(8,128)(2,1)S(1)} %collective-permute-done.2.other_ref.refs_1_), custom_call_target="tpu_custom_call" | custom-call | tf_op jit(solution)/shard_map/correlate/pallas_call | solution.py:153
  94.4 2.0 %apply.4 = (f32[2,1024]{1,0:T(2,128)S(1)}, f32[2,1024]{1,0:T(2,128)S(1)}) custom-call(bf16[64,2,16,512]{3,2,1,0:T(8,128)(2,1)S(1)} %all-to-all-done.y_ref.mine_ref.refs_0_, bf16[64,2,16,512]{3,2,1,0:T(8,128)(2,1)S(1)} %collective-permute-done.2.other_ref.refs_1_, f32[2,1024]{1,0:T(2,128)S(1)} %get-tuple-element.53.z_ref, f32[2,1024]{1,0:T(2,128)S(1)} %add.64.near_ref, ...), custom_call_target="tpu_custom_call" | custom-call | tf_op jit(solution)/shard_map/apply/pallas_call | solution.py:222
  96.6 2.6 %correlate.5.refs_0_ = bf16[2,512,256]{2,1,0:T(8,128)(2,1)} custom-call(s32[3]{0:T(128)S(1)} %pad_add_fusion.me_ref, bf16[64,2,16,512]{3,2,1,0:T(8,128)(2,1)S(1)} %all-to-all-done.y_ref.mine_ref.refs_0_, bf16[64,2,16,512]{3,2,1,0:T(8,128)(2,1)S(1)} %collective-permute-done.2.other_ref.refs_1_), custom_call_target="tpu_custom_call" | custom-call | tf_op jit(solution)/shard_map/correlate/pallas_call | solution.py:153
  101.0 2.6 %correlate.6 = bf16[2,512,256]{2,1,0:T(8,128)(2,1)} custom-call(s32[3]{0:T(128)S(1)} %pad_add_fusion.me_ref, bf16[64,2,16,512]{3,2,1,0:T(8,128)(2,1)S(1)} %all-to-all-done.y_ref.mine_ref.refs_0_, bf16[64,2,16,512]{3,2,1,0:T(8,128)(2,1)S(1)} %collective-permute-done.2.other_ref.refs_1_), custom_call_target="tpu_custom_call" | custom-call | tf_op jit(solution)/shard_map/correlate/pallas_call | solution.py:153
  103.7 2.0 %apply.5 = (f32[2,1024]{1,0:T(2,128)S(1)}, f32[2,1024]{1,0:T(2,128)S(1)}) custom-call(bf16[64,2,16,512]{3,2,1,0:T(8,128)(2,1)S(1)} %all-to-all-done.y_ref.mine_ref.refs_0_, bf16[64,2,16,512]{3,2,1,0:T(8,128)(2,1)S(1)} %collective-permute-done.2.other_ref.refs_1_, f32[2,1024]{1,0:T(2,128)S(1)} %get-tuple-element.59.z_ref, f32[2,1024]{1,0:T(2,128)S(1)} %add.65.near_ref, ...), custom_call_target="tpu_custom_call" | custom-call | tf_op jit(solution)/shard_map/apply/pallas_call | solution.py:222
  106.4 2.2 %collective-permute-done.9 = f32[2,1024]{1,0:T(2,128)S(1)} collective-permute-done((f32[2,1024]{1,0:T(2,128)S(1)}, f32[2,1024]{1,0:T(2,128)S(1)}, u32[]{:S(2)}, u32[]{:S(2)}) %collective-permute-start.9) | collective-permute-done | bytes 8224 | tf_op jit(solution)/shard_map/ppermute | solution.py:423
  110.1 2.6 %correlate.7 = bf16[2,512,256]{2,1,0:T(8,128)(2,1)} custom-call(s32[3]{0:T(128)S(1)} %pad_add_fusion.me_ref, bf16[64,2,16,512]{3,2,1,0:T(8,128)(2,1)S(1)} %all-to-all-done.y_ref.mine_ref.refs_0_, bf16[64,2,16,512]{3,2,1,0:T(8,128)(2,1)S(1)} %collective-permute-done.2.other_ref.refs_1_), custom_call_target="tpu_custom_call" | custom-call | tf_op jit(solution)/shard_map/correlate/pallas_call | solution.py:153
  112.8 2.6 %collective-permute-start.15 = (bf16[2,512,256]{2,1,0:T(8,128)(2,1)}, bf16[2,512,256]{2,1,0:T(8,128)(2,1)S(1)}, u32[]{:S(2)}, u32[]{:S(2)}) collective-permute-start(bf16[2,512,256]{2,1,0:T(8,128)(2,1)} %correlate.6), channel_id=1, source_target_pairs={{0,4},{2,6},{4,0},{6,2},{1,5},{3,7},{5,1},{7,3},{8,12},{10,14},{12... | collective-permute-start | bytes 1572872 | tf_op jit(solution)/shard_map/ppermute | solution.py:423
  116.8 3.1 %collective-permute-start.11 = (f32[2,1024]{1,0:T(2,128)S(1)}, f32[2,1024]{1,0:T(2,128)S(1)}, u32[]{:S(2)}, u32[]{:S(2)}) collective-permute-start(f32[2,1024]{1,0:T(2,128)S(1)} %finish.1.refs_0_.z_ref), channel_id=1, source_target_pairs={{8,9},{9,8},{24,25},{25,24},{40,41},{41,40},{56,57},{57,56},{72,73... | collective-permute-start | bytes 24584 | tf_op jit(solution)/shard_map/ppermute | solution.py:428
  119.9 4.4 %collective-permute-start.12 = (f32[2,1024]{1,0:T(2,128)S(1)}, f32[2,1024]{1,0:T(2,128)S(1)}, u32[]{:S(2)}, u32[]{:S(2)}) collective-permute-start(f32[2,1024]{1,0:T(2,128)S(1)} %finish.1.refs_0_.z_ref), channel_id=1, source_target_pairs={{8,136},{9,137},{24,152},{25,153},{40,168},{41,169},{56,184},{57,1... | collective-permute-start | bytes 24584 | tf_op jit(solution)/shard_map/ppermute | solution.py:428
  124.4 2.0 %collective-permute-start.13 = (f32[2,1024]{1,0:T(2,128)S(1)}, f32[2,1024]{1,0:T(2,128)S(1)}, u32[]{:S(2)}, u32[]{:S(2)}) collective-permute-start(f32[2,1024]{1,0:T(2,128)S(1)} %finish.1.refs_0_.z_ref), channel_id=1, source_target_pairs={{8,137},{9,136},{24,153},{25,152},{40,169},{41,168},{56,185},{57,1... | collective-permute-start | bytes 24584 | tf_op jit(solution)/shard_map/ppermute | solution.py:428
  126.4 3.8 %collective-permute-done.13.refs_3_ = f32[2,1024]{1,0:T(2,128)S(1)} collective-permute-done((f32[2,1024]{1,0:T(2,128)S(1)}, f32[2,1024]{1,0:T(2,128)S(1)}, u32[]{:S(2)}, u32[]{:S(2)}) %collective-permute-start.13) | collective-permute-done | bytes 8224 | tf_op jit(solution)/shard_map/ppermute | solution.py:428
  131.6 6.5 %all-to-all-start.2 = ((f32[8,2,2,1024]{3,2,1,0:T(2,128)}), f32[8,2,2,1024]{3,2,1,0:T(2,128)S(1)}, u32[]{:S(2)}, u32[]{:S(2)}) async-start(f32[8,2,2,1024]{3,2,1,0:T(2,128)} %choose.1), calls=%async_computation.2 | async-start | bytes 262144 | tf_op jit(solution)/shard_map/all_to_all | solution.py:530
  140.2 5.8 %all-to-all-done.2.line_ref = f32[8,2,2,1024]{3,2,1,0:T(2,128)S(1)} async-done(((f32[8,2,2,1024]{3,2,1,0:T(2,128)}), f32[8,2,2,1024]{3,2,1,0:T(2,128)S(1)}, u32[]{:S(2)}, u32[]{:S(2)}) %all-to-all-start.2) | async-done | bytes 131104 | tf_op jit(solution)/shard_map/all_to_all | solution.py:530
  147.9 1.9 %collective-permute-start.17 = (bf16[2,512,256]{2,1,0:T(8,128)(2,1)}, bf16[2,512,256]{2,1,0:T(8,128)(2,1)S(1)}, u32[]{:S(2)}, u32[]{:S(2)}) collective-permute-start(bf16[2,512,256]{2,1,0:T(8,128)(2,1)} %copy-done), channel_id=1, source_target_pairs={{0,0},{1,8},{8,1},{9,9},{16,16},{17,24},{24,17},{25,25},{32,32},{3... | collective-permute-start | bytes 1572872 | tf_op jit(solution)/shard_map/ppermute | solution.py:437
  149.8 2.3 %beamform.3 = bf16[2,2,128,512]{3,2,1,0:T(8,128)(2,1)S(1)} custom-call(s32[32]{0:T(128)S(1)} %select_reduce_fusion.source_ref, s32[3]{0:T(128)S(1)} %pad_add_fusion.me_ref, f32[8,2,2,1024]{3,2,1,0:T(2,128)S(1)} %all-to-all-done.2.line_ref, f32[2,2,1024]{2,1,0:T(2,128)S(1)} %collective-permute-done.18.handed_ref, f32[256,512]{1,0:T(8,128)S(1)} %get-tuple-element.88.cos_ref, ...), custom_call_target="tpu_custom_call" | custom-call | tf_op jit(solution)/shard_map/beamform/pallas_call | solution.py:370
  152.3 3.1 %beamform.2.own_hbm = bf16[2,2,128,1024]{3,2,1,0:T(8,128)(2,1)} custom-call(s32[32]{0:T(128)S(1)} %select_reduce_fusion.source_ref, s32[3]{0:T(128)S(1)} %pad_add_fusion.me_ref, f32[8,2,2,1024]{3,2,1,0:T(2,128)S(1)} %all-to-all-done.2.line_ref, f32[2,2,1024]{2,1,0:T(2,128)S(1)} %collective-permute-done.18.handed_ref, ...), custom_call_target="tpu_custom_call" | custom-call | tf_op jit(solution)/shard_map/beamform/pallas_call | solution.py:370
  156.6 5.9 %collective-permute-done.17.in_ref = bf16[2,512,256]{2,1,0:T(8,128)(2,1)S(1)} collective-permute-done((bf16[2,512,256]{2,1,0:T(8,128)(2,1)}, bf16[2,512,256]{2,1,0:T(8,128)(2,1)S(1)}, u32[]{:S(2)}, u32[]{:S(2)}) %collective-permute-start.17) | collective-permute-done | bytes 524320 | tf_op jit(solution)/shard_map/ppermute | solution.py:437
  163.5 3.9 %collective-permute-done.19.other_ref = bf16[2,2,128,512]{3,2,1,0:T(8,128)(2,1)S(1)} collective-permute-done((bf16[2,2,128,512]{3,2,1,0:T(8,128)(2,1)S(1)}, bf16[2,2,128,512]{3,2,1,0:T(8,128)(2,1)S(1)}, u32[]{:S(2)}, u32[]{:S(2)}) %collective-permute-start.19) | collective-permute-done | bytes 524320 | tf_op jit(solution)/shard_map/ppermute | solution.py:423
  (61 shorter events, 21.1 us)
Async XLA Ops:
  3.7 13.4 %copy-start.6 = (f32[1,2,1024]{2,1,0:T(2,128)S(1)}, f32[1,2,1024]{2,1,0:T(2,128)}, u32[]{:S(2)}) copy-start(f32[1,2,1024]{2,1,0:T(2,128)} %param.9) | copy-start | bytes 24580
  3.7 16.9 %copy-start.5 = (s32[32]{0:T(128)S(1)}, s32[32]{0:T(128)}, u32[]{:S(2)}) copy-start(s32[32]{0:T(128)} %chan_hbm.2) | copy-start | bytes 388
  3.7 18.2 %copy-start.2 = (f32[2,512]{1,0:T(2,128)S(1)}, f32[2,512]{1,0:T(2,128)}, u32[]{:S(2)}) copy-start(f32[2,512]{1,0:T(2,128)} %param.12) | copy-start | bytes 12292
  3.8 18.3 %copy-start.1 = (s32[512]{0:T(512)S(1)}, s32[512]{0:T(512)}, u32[]{:S(2)}) copy-start(s32[512]{0:T(512)} %map_hbm.3) | copy-start | bytes 6148
  3.8 19.4 %copy-start.4 = (s32[32]{0:T(128)S(1)}, s32[32]{0:T(128)}, u32[]{:S(2)}) copy-start(s32[32]{0:T(128)} %chan_hbm.3) | copy-start | bytes 388
  3.8 19.9 %copy-start.3 = (s32[2,256]{1,0:T(2,128)S(1)}, s32[2,256]{1,0:T(2,128)}, u32[]{:S(2)}) copy-start(s32[2,256]{1,0:T(2,128)} %param.13) | copy-start | bytes 6148
  3.8 63.3 %all-to-all-start = ((bf16[64,2,16,512]{3,2,1,0:T(8,128)(2,1)}), bf16[64,2,16,512]{3,2,1,0:T(8,128)(2,1)S(1)}, u32[]{:S(2)}, u32[]{:S(2)}) async-start(bf16[64,2,16,512]{3,2,1,0:T(8,128)(2,1)} %bitcast.15), calls=%async_computation | async-start | bytes 4194304 | tf_op jit(solution)/shard_map/all_to_all | solution.py:467
  17.1 11.6 %collective-permute-start = (f32[2,1024]{1,0:T(2,128)S(1)}, f32[2,1024]{1,0:T(2,128)S(1)}, u32[]{:S(2)}, u32[]{:S(2)}) collective-permute-start(f32[2,1024]{1,0:T(2,128)S(1)} %bitcast.22), channel_id=1, source_target_pairs={{0,0},{1,8},{8,1},{9,9},{16,16},{17,24},{24,17},{25,25},{32,32},{3... | collective-permute-start | bytes 24584 | tf_op jit(solution)/shard_map/ppermute | solution.py:437
  67.1 64.5 %all-to-all-start.1 = ((bf16[64,2,16,512]{3,2,1,0:T(8,128)(2,1)}), bf16[64,2,16,512]{3,2,1,0:T(8,128)(2,1)}, u32[]{:S(2)}, u32[]{:S(2)}) async-start(bf16[64,2,16,512]{3,2,1,0:T(8,128)(2,1)} %bitcast.14), calls=%async_computation.1 | async-start | bytes 4194304 | tf_op jit(solution)/shard_map/all_to_all | solution.py:490
  75.4 1.4 collective-permute-start.1
  76.9 7.4 %collective-permute-start.2 = (bf16[64,2,16,512]{3,2,1,0:T(8,128)(2,1)S(1)}, bf16[64,2,16,512]{3,2,1,0:T(8,128)(2,1)S(1)}, u32[]{:S(2)}, u32[]{:S(2)}) collective-permute-start(bf16[64,2,16,512]{3,2,1,0:T(8,128)(2,1)S(1)} %all-to-all-done.y_ref.mine_ref.refs_0_), channel_id=1, source_target_pairs={{0,8},{8,0},{16,24},{24,16},{32,40},{40,32},{48,56},{56,48},{64,72... | collective-permute-start | bytes 6291464 | tf_op jit(solution)/shard_map/ppermute | solution.py:423
  77.2 2.9 %collective-permute-start.3 = (f32[2,1024]{1,0:T(2,128)S(1)}, f32[2,1024]{1,0:T(2,128)S(1)}, u32[]{:S(2)}, u32[]{:S(2)}) collective-permute-start(f32[2,1024]{1,0:T(2,128)S(1)} %add.62), channel_id=1, source_target_pairs={{0,2},{2,0},{4,6},{6,4},{1,3},{3,1},{5,7},{7,5},{8,10},{10,8},{12,... | collective-permute-start | bytes 24584 | tf_op jit(solution)/shard_map/ppermute | solution.py:423
  80.1 4.1 %collective-permute-start.4 = (f32[2,1024]{1,0:T(2,128)S(1)}, f32[2,1024]{1,0:T(2,128)S(1)}, u32[]{:S(2)}, u32[]{:S(2)}) collective-permute-start(f32[2,1024]{1,0:T(2,128)S(1)} %add.63.near_ref), channel_id=1, source_target_pairs={{0,6},{2,4},{4,2},{6,0},{1,7},{3,5},{5,3},{7,1},{8,14},{10,12},{12... | collective-permute-start | bytes 24584 | tf_op jit(solution)/shard_map/ppermute | solution.py:423
  86.3 3.0 %collective-permute-start.5 = (f32[2,1024]{1,0:T(2,128)S(1)}, f32[2,1024]{1,0:T(2,128)S(1)}, u32[]{:S(2)}, u32[]{:S(2)}) collective-permute-start(f32[2,1024]{1,0:T(2,128)S(1)} %get-tuple-element.54), channel_id=1, source_target_pairs={{0,2},{2,0},{4,6},{6,4},{1,3},{3,1},{5,7},{7,5},{8,10},{10,8},{12,... | collective-permute-start | bytes 24584 | tf_op jit(solution)/shard_map/ppermute | solution.py:423
  89.3 5.1 %collective-permute-start.6 = (f32[2,1024]{1,0:T(2,128)S(1)}, f32[2,1024]{1,0:T(2,128)S(1)}, u32[]{:S(2)}, u32[]{:S(2)}) collective-permute-start(f32[2,1024]{1,0:T(2,128)S(1)} %add.64.near_ref), channel_id=1, source_target_pairs={{0,6},{2,4},{4,2},{6,0},{1,7},{3,5},{5,3},{7,1},{8,14},{10,12},{12... | collective-permute-start | bytes 24584 | tf_op jit(solution)/shard_map/ppermute | solution.py:423
  96.4 3.2 %collective-permute-start.7 = (f32[2,1024]{1,0:T(2,128)S(1)}, f32[2,1024]{1,0:T(2,128)S(1)}, u32[]{:S(2)}, u32[]{:S(2)}) collective-permute-start(f32[2,1024]{1,0:T(2,128)S(1)} %get-tuple-element.61), channel_id=1, source_target_pairs={{0,2},{2,0},{4,6},{6,4},{1,3},{3,1},{5,7},{7,5},{8,10},{10,8},{12,... | collective-permute-start | bytes 24584 | tf_op jit(solution)/shard_map/ppermute | solution.py:423
  99.5 4.1 %collective-permute-start.8 = (f32[2,1024]{1,0:T(2,128)S(1)}, f32[2,1024]{1,0:T(2,128)S(1)}, u32[]{:S(2)}, u32[]{:S(2)}) collective-permute-start(f32[2,1024]{1,0:T(2,128)S(1)} %add.65.near_ref), channel_id=1, source_target_pairs={{0,6},{2,4},{4,2},{6,0},{1,7},{3,5},{5,3},{7,1},{8,14},{10,12},{12... | collective-permute-start | bytes 24584 | tf_op jit(solution)/shard_map/ppermute | solution.py:423
  105.7 3.0 %collective-permute-start.9 = (f32[2,1024]{1,0:T(2,128)S(1)}, f32[2,1024]{1,0:T(2,128)S(1)}, u32[]{:S(2)}, u32[]{:S(2)}) collective-permute-start(f32[2,1024]{1,0:T(2,128)S(1)} %get-tuple-element.70), channel_id=1, source_target_pairs={{0,2},{2,0},{4,6},{6,4},{1,3},{3,1},{5,7},{7,5},{8,10},{10,8},{12,... | collective-permute-start | bytes 24584 | tf_op jit(solution)/shard_map/ppermute | solution.py:423
  108.7 4.1 %collective-permute-start.10 = (f32[2,1024]{1,0:T(2,128)S(1)}, f32[2,1024]{1,0:T(2,128)S(1)}, u32[]{:S(2)}, u32[]{:S(2)}) collective-permute-start(f32[2,1024]{1,0:T(2,128)S(1)} %add.66.near_ref), channel_id=1, source_target_pairs={{0,6},{2,4},{4,2},{6,0},{1,7},{3,5},{5,3},{7,1},{8,14},{10,12},{12... | collective-permute-start | bytes 24584 | tf_op jit(solution)/shard_map/ppermute | solution.py:423
  112.8 25.3 %collective-permute-start.14 = (bf16[2,512,256]{2,1,0:T(8,128)(2,1)}, bf16[2,512,256]{2,1,0:T(8,128)(2,1)S(1)}, u32[]{:S(2)}, u32[]{:S(2)}) collective-permute-start(bf16[2,512,256]{2,1,0:T(8,128)(2,1)} %correlate.4), channel_id=1, source_target_pairs={{0,2},{2,0},{4,6},{6,4},{1,3},{3,1},{5,7},{7,5},{8,10},{10,8},{12,... | collective-permute-start | bytes 1572872 | tf_op jit(solution)/shard_map/ppermute | solution.py:423
  112.8 25.3 %collective-permute-start.15 = (bf16[2,512,256]{2,1,0:T(8,128)(2,1)}, bf16[2,512,256]{2,1,0:T(8,128)(2,1)S(1)}, u32[]{:S(2)}, u32[]{:S(2)}) collective-permute-start(bf16[2,512,256]{2,1,0:T(8,128)(2,1)} %correlate.6), channel_id=1, source_target_pairs={{0,4},{2,6},{4,0},{6,2},{1,5},{3,7},{5,1},{7,3},{8,12},{10,14},{12... | collective-permute-start | bytes 1572872 | tf_op jit(solution)/shard_map/ppermute | solution.py:423
  115.4 22.7 %collective-permute-start.16 = (bf16[2,512,256]{2,1,0:T(8,128)(2,1)}, bf16[2,512,256]{2,1,0:T(8,128)(2,1)S(1)}, u32[]{:S(2)}, u32[]{:S(2)}) collective-permute-start(bf16[2,512,256]{2,1,0:T(8,128)(2,1)} %correlate.7), channel_id=1, source_target_pairs={{0,6},{2,4},{4,2},{6,0},{1,7},{3,5},{5,3},{7,1},{8,14},{10,12},{12... | collective-permute-start | bytes 1572872 | tf_op jit(solution)/shard_map/ppermute | solution.py:423
  116.8 7.6 %collective-permute-start.11 = (f32[2,1024]{1,0:T(2,128)S(1)}, f32[2,1024]{1,0:T(2,128)S(1)}, u32[]{:S(2)}, u32[]{:S(2)}) collective-permute-start(f32[2,1024]{1,0:T(2,128)S(1)} %finish.1.refs_0_.z_ref), channel_id=1, source_target_pairs={{8,9},{9,8},{24,25},{25,24},{40,41},{41,40},{56,57},{57,56},{72,73... | collective-permute-start | bytes 24584 | tf_op jit(solution)/shard_map/ppermute | solution.py:428
  119.9 6.5 %collective-permute-start.12 = (f32[2,1024]{1,0:T(2,128)S(1)}, f32[2,1024]{1,0:T(2,128)S(1)}, u32[]{:S(2)}, u32[]{:S(2)}) collective-permute-start(f32[2,1024]{1,0:T(2,128)S(1)} %finish.1.refs_0_.z_ref), channel_id=1, source_target_pairs={{8,136},{9,137},{24,152},{25,153},{40,168},{41,169},{56,184},{57,1... | collective-permute-start | bytes 24584 | tf_op jit(solution)/shard_map/ppermute | solution.py:428
  124.4 5.9 %collective-permute-start.13 = (f32[2,1024]{1,0:T(2,128)S(1)}, f32[2,1024]{1,0:T(2,128)S(1)}, u32[]{:S(2)}, u32[]{:S(2)}) collective-permute-start(f32[2,1024]{1,0:T(2,128)S(1)} %finish.1.refs_0_.z_ref), channel_id=1, source_target_pairs={{8,137},{9,136},{24,153},{25,152},{40,169},{41,168},{56,185},{57,1... | collective-permute-start | bytes 24584 | tf_op jit(solution)/shard_map/ppermute | solution.py:428
  131.6 14.4 %all-to-all-start.2 = ((f32[8,2,2,1024]{3,2,1,0:T(2,128)}), f32[8,2,2,1024]{3,2,1,0:T(2,128)S(1)}, u32[]{:S(2)}, u32[]{:S(2)}) async-start(f32[8,2,2,1024]{3,2,1,0:T(2,128)} %choose.1), calls=%async_computation.2 | async-start | bytes 262144 | tf_op jit(solution)/shard_map/all_to_all | solution.py:530
  139.4 0.8 copy-start
  146.6 3.2 %collective-permute-start.18 = (f32[2,2,1024]{2,1,0:T(2,128)S(1)}, f32[2,2,1024]{2,1,0:T(2,128)S(1)}, u32[]{:S(2)}, u32[]{:S(2)}) collective-permute-start(f32[2,2,1024]{2,1,0:T(2,128)S(1)} %hand.1), channel_id=1, source_target_pairs={{8,0},{24,16},{40,32},{56,48},{72,64},{88,80},{104,96},{120,112},{... | collective-permute-start | bytes 49160 | tf_op jit(solution)/shard_map/ppermute | solution.py:536
  147.9 14.6 %collective-permute-start.17 = (bf16[2,512,256]{2,1,0:T(8,128)(2,1)}, bf16[2,512,256]{2,1,0:T(8,128)(2,1)S(1)}, u32[]{:S(2)}, u32[]{:S(2)}) collective-permute-start(bf16[2,512,256]{2,1,0:T(8,128)(2,1)} %copy-done), channel_id=1, source_target_pairs={{0,0},{1,8},{8,1},{9,9},{16,16},{17,24},{24,17},{25,25},{32,32},{3... | collective-permute-start | bytes 1572872 | tf_op jit(solution)/shard_map/ppermute | solution.py:437
  152.2 15.2 %collective-permute-start.19 = (bf16[2,2,128,512]{3,2,1,0:T(8,128)(2,1)S(1)}, bf16[2,2,128,512]{3,2,1,0:T(8,128)(2,1)S(1)}, u32[]{:S(2)}, u32[]{:S(2)}) collective-permute-start(bf16[2,2,128,512]{3,2,1,0:T(8,128)(2,1)S(1)} %beamform.3), channel_id=1, source_target_pairs={{0,1},{1,0},{2,3},{3,2},{4,5},{5,4},{6,7},{7,6},{8,9},{9,8},{10,11... | collective-permute-start | bytes 1572872 | tf_op jit(solution)/shard_map/ppermute | solution.py:423

commit v9 on v7

--- a/solution.py
+++ b/solution.py
@@ -16,6 +16,7 @@
 TEAM = ("tm", "grp")
 VMEM = pltpu.VMEM
 SMEM = pltpu.SMEM
+LONG = pl.CostEstimate(flops=40 << 30, bytes_accessed=64 << 20, transcendentals=0)
 
 
 def whole(space=VMEM):
@@ -340,6 +341,7 @@
         out_shape=out_shape,
         scratch_shapes=scratch,
         compiler_params=params(16),
+        cost_estimate=LONG,
         name="beamform",
     )(source, me, line, cosine, sine, y)
 
@@ -473,15 +475,18 @@
             )
         sums = (part, far)
     depth = slots // 4
-    part, far, *bulk = lax.optimization_barrier(
-        (*sums, *(pieces[m] for m in range(1, n_time)))
-    )
-    pieces = [pieces[0]] + [swap(x, "tm", m + 1) for m, x in enumerate(bulk)]
+    part, far, piece = lax.optimization_barrier((*sums, pieces[2]))
+    pieces[2] = swap(piece, "tm", 2)
     z = finish(z, (part, far), scale)
     reach = [(0, 0), (0, 1), (1, 0), (1, 1)]
     half_ring = slots // 2 * n_group
     vectors = [z] + [swap(z, WIDE, high * half_ring + low) for high, low in reach[1:]]
     copies, solved = choose(source, me, vectors, reach, depth)
+    copies, beam_y, *bulk = lax.optimization_barrier(
+        (copies, beam_y, pieces[1], pieces[3])
+    )
+    pieces[1], pieces[3] = swap(bulk[0], "tm", 1), swap(bulk[1], "tm", 3)
+    pieces = [pieces[m] for m in range(n_time)]
     copies, beam_y = lax.optimization_barrier((copies, beam_y))
     groups = [
         [high * 2 * depth + 2 * i + c for i in range(depth)]
@@ -492,11 +497,11 @@
         copies, "freq", split_axis=0, concat_axis=0, axis_index_groups=groups, tiled=True
     )
 
-    block = cross(gather(pieces))
     away = beamform(1, source, me, line, cosine, sine, beam_y, n_group)
     other = swap(away, "grp", 1)
     own = beamform(0, source, me, line, cosine, sine, beam_y, n_group)
-    visibilities = widen(block)
+    own, *pieces = lax.optimization_barrier((own, *pieces))
+    visibilities = widen(cross(gather(pieces)))
     beams = place(me, own, other)
     return visibilities[None], solved[None], beams[None]
 

time: 167 us -> 170 us (1.018)
  waiting for transfers between devices: 61.1 us -> 73.3 us
  starting transfers between devices: 64.3 us -> 56.1 us
    ppermute x17, waiting for transfers between devices: 16.2 us -> 23.8 us  [swap(): return lax.ppermute(x, axis, [(i, i ^ mask) for i in range(n)])]
    ppermute x2, starting transfers between devices: 16.5 us -> 10 us  [cross(): return lax.ppermute(x, WIDE, pairs)]
    all_to_all x1, waiting for transfers between devices: 0.01 us -> 3.62 us  [body(): lax.all_to_all(copies, 'freq', split_axis=0, concat_axis=0, axis_index_gr...]
    all_to_all x1, waiting for transfers between devices: 0.01 us -> 2.09 us  [body(): lax.all_to_all(beam_send, WIDE, split_axis=0, concat_axis=0, tiled=True)]
  transfers between devices with their start and end apart: 22 -> 22, of which waited for: 12 -> 14; matrix products, arithmetic and copies ran while one was open for 3% -> 3% of each run, Pallas kernels for 18% -> 18%
where the time goes in v9:
time: 170 us; the launch traced here: 169 us
  waiting for transfers between devices  73.3 us (43%)
  starting transfers between devices  56.1 us (33%)
  Pallas kernels  34 us (20%)
  other arithmetic  2.26 us (1%)
  local copies, waits for them, and re-layouts  2.12 us (1%)
    all_to_all x1, waiting for transfers between devices, body(): lax.all_to_all(corr_send, WIDE, split_axis=0, concat_axis=0, tiled=True)  38.3 us
    ppermute x17, waiting for transfers between devices, swap(): return lax.ppermute(x, axis, [(i, i ^ mask) for i in range(n)])  23.8 us
    ppermute x17, starting transfers between devices, swap(): return lax.ppermute(x, axis, [(i, i ^ mask) for i in range(n)])  20.4 us
    all_to_all x1, starting transfers between devices, body(): lax.all_to_all(corr_send, WIDE, split_axis=0, concat_axis=0, tiled=True)  13.3 us
    pallas_call x4, Pallas kernels, correlate(): pl.pallas_call(functools.partial(correlate_kernel, scale, mask), in_specs...  10.5 us
    ppermute x2, starting transfers between devices, cross(): return lax.ppermute(x, WIDE, pairs)  10 us
    all_to_all x1, starting transfers between devices, body(): lax.all_to_all(beam_send, WIDE, split_axis=0, concat_axis=0, tiled=True)  7.35 us
    pallas_call x2, Pallas kernels, ingest(): pl.pallas_call(functools.partial(ingest_kernel, stations, pick), in_specs...  6.09 us
  transfers between devices with their start and end apart: 22, of which 14 were waited for; matrix products, arithmetic and copies ran while one was open for 3% of the time, Pallas kernels for 18%

profile of v9, /device:TPU:1, one launch (start us, length us, event | category | flops | bytes accessed | tf_op | source)
XLA Modules:
  0.0 169.5 jit_solution(14292290602197665014)
XLA Ops:
  0.6 3.0 %ingest.3 = bf16[32,2,2,16,512]{4,3,2,1,0:T(8,128)(2,1)} custom-call(s32[1]{0:T(128)} %bitcast.base_ref, s32[32]{0:T(128)} %chan_hbm.3, s32[512]{0:T(512)} %map_hbm.3, s32[512]{0:T(512)} %flag_hbm.3, bf16[32,2,16,1024]{3,2,1,0:T(8,128)(2,1)} %volts_hbm.3), custom_call_target="tpu_custom_call" | custom-call | tf_op jit(solution)/shard_map/ingest/pallas_call | solution.py:94
  3.7 13.3 %all-to-all-start = ((bf16[64,2,16,512]{3,2,1,0:T(8,128)(2,1)}), bf16[64,2,16,512]{3,2,1,0:T(8,128)(2,1)S(1)}, u32[]{:S(2)}, u32[]{:S(2)}) async-start(bf16[64,2,16,512]{3,2,1,0:T(8,128)(2,1)} %bitcast.15), calls=%async_computation | async-start | bytes 4194304 | tf_op jit(solution)/shard_map/all_to_all | solution.py:430
  17.1 3.5 %collective-permute-start = (f32[2,1024]{1,0:T(2,128)S(1)}, f32[2,1024]{1,0:T(2,128)S(1)}, u32[]{:S(2)}, u32[]{:S(2)}) collective-permute-start(f32[2,1024]{1,0:T(2,128)S(1)} %bitcast.21), channel_id=1, source_target_pairs={{0,0},{1,8},{8,1},{9,9},{16,16},{17,24},{24,17},{25,25},{32,32},{3... | collective-permute-start | bytes 24584 | tf_op jit(solution)/shard_map/ppermute | solution.py:400
  23.6 2.0 %fusion = (f32[256,512]{1,0:T(8,128)S(1)}, f32[256,512]{1,0:T(8,128)S(1)}) fusion(f32[512]{0:T(512)S(1)} %get-tuple-element.106, f32[256]{0:T(256)S(1)} %bitcast.20, f32[512]{0:T(512)S(1)} %get-tuple-element.105, f32[256]{0:T(256)S(1)} %bitcast.19, f32[]{:T(128)} %bitcast.4), kind=kLoop, calls=%fused_computation.2 | loop fusion | flops 524288 | bytes 1054724 | tf_op jit(solution)/shard_map/sin | solution.py:443
  25.7 3.1 %ingest.2 = bf16[32,2,2,16,512]{4,3,2,1,0:T(8,128)(2,1)} custom-call(s32[1]{0:T(128)} %bitcast.base_ref, s32[32]{0:T(128)} %chan_hbm.2, s32[512]{0:T(512)} %map_hbm.3, s32[512]{0:T(512)} %flag_hbm.3, bf16[32,2,16,1024]{3,2,1,0:T(8,128)(2,1)} %volts_hbm.3), custom_call_target="tpu_custom_call" | custom-call | tf_op jit(solution)/shard_map/ingest/pallas_call | solution.py:94
  28.7 38.3 %all-to-all-done.y_ref.mine_ref.refs_0_ = bf16[64,2,16,512]{3,2,1,0:T(8,128)(2,1)S(1)} async-done(((bf16[64,2,16,512]{3,2,1,0:T(8,128)(2,1)}), bf16[64,2,16,512]{3,2,1,0:T(8,128)(2,1)S(1)}, u32[]{:S(2)}, u32[]{:S(2)}) %all-to-all-start) | async-done | bytes 2097184 | tf_op jit(solution)/shard_map/all_to_all | solution.py:430
  67.0 7.3 %all-to-all-start.1 = ((bf16[64,2,16,512]{3,2,1,0:T(8,128)(2,1)}), bf16[64,2,16,512]{3,2,1,0:T(8,128)(2,1)}, u32[]{:S(2)}, u32[]{:S(2)}) async-start(bf16[64,2,16,512]{3,2,1,0:T(8,128)(2,1)} %bitcast.14), calls=%async_computation.1 | async-start | bytes 4194304 | tf_op jit(solution)/shard_map/all_to_all | solution.py:453
  78.4 1.7 collective-permute-done.3
  80.1 2.5 %collective-permute-start.4 = (f32[2,1024]{1,0:T(2,128)S(1)}, f32[2,1024]{1,0:T(2,128)S(1)}, u32[]{:S(2)}, u32[]{:S(2)}) collective-permute-start(f32[2,1024]{1,0:T(2,128)S(1)} %add.63.near_ref), channel_id=1, source_target_pairs={{0,6},{2,4},{4,2},{6,0},{1,7},{3,5},{5,3},{7,1},{8,14},{10,12},{12... | collective-permute-start | bytes 24584 | tf_op jit(solution)/shard_map/ppermute | solution.py:391
  84.2 2.0 %apply.3 = (f32[2,1024]{1,0:T(2,128)S(1)}, f32[2,1024]{1,0:T(2,128)S(1)}) custom-call(bf16[64,2,16,512]{3,2,1,0:T(8,128)(2,1)S(1)} %all-to-all-done.y_ref.mine_ref.refs_0_, bf16[64,2,16,512]{3,2,1,0:T(8,128)(2,1)S(1)} %collective-permute-done.2.other_ref.refs_1_, f32[2,1024]{1,0:T(2,128)S(1)} %collective-permute-done.z_ref, f32[2,1024]{1,0:T(2,128)S(1)} %add.63.near_ref, ...), custom_call_target="tpu_custom_call" | custom-call | tf_op jit(solution)/shard_map/apply/pallas_call | solution.py:223
  86.3 2.9 %collective-permute-done.5 = f32[2,1024]{1,0:T(2,128)S(1)} collective-permute-done((f32[2,1024]{1,0:T(2,128)S(1)}, f32[2,1024]{1,0:T(2,128)S(1)}, u32[]{:S(2)}, u32[]{:S(2)}) %collective-permute-start.5) | collective-permute-done | bytes 8224 | tf_op jit(solution)/shard_map/ppermute | solution.py:391
  89.2 2.5 %collective-permute-start.6 = (f32[2,1024]{1,0:T(2,128)S(1)}, f32[2,1024]{1,0:T(2,128)S(1)}, u32[]{:S(2)}, u32[]{:S(2)}) collective-permute-start(f32[2,1024]{1,0:T(2,128)S(1)} %add.64.near_ref), channel_id=1, source_target_pairs={{0,6},{2,4},{4,2},{6,0},{1,7},{3,5},{5,3},{7,1},{8,14},{10,12},{12... | collective-permute-start | bytes 24584 | tf_op jit(solution)/shard_map/ppermute | solution.py:391
  91.7 2.6 %correlate.4 = bf16[2,512,256]{2,1,0:T(8,128)(2,1)} custom-call(s32[3]{0:T(128)S(1)} %pad_add_fusion.me_ref, bf16[64,2,16,512]{3,2,1,0:T(8,128)(2,1)S(1)} %all-to-all-done.y_ref.mine_ref.refs_0_, bf16[64,2,16,512]{3,2,1,0:T(8,128)(2,1)S(1)} %collective-permute-done.2.other_ref.refs_1_), custom_call_target="tpu_custom_call" | custom-call | tf_op jit(solution)/shard_map/correlate/pallas_call | solution.py:154
  94.3 2.0 %apply.4 = (f32[2,1024]{1,0:T(2,128)S(1)}, f32[2,1024]{1,0:T(2,128)S(1)}) custom-call(bf16[64,2,16,512]{3,2,1,0:T(8,128)(2,1)S(1)} %all-to-all-done.y_ref.mine_ref.refs_0_, bf16[64,2,16,512]{3,2,1,0:T(8,128)(2,1)S(1)} %collective-permute-done.2.other_ref.refs_1_, f32[2,1024]{1,0:T(2,128)S(1)} %get-tuple-element.60.z_ref, f32[2,1024]{1,0:T(2,128)S(1)} %add.64.near_ref, ...), custom_call_target="tpu_custom_call" | custom-call | tf_op jit(solution)/shard_map/apply/pallas_call | solution.py:223
  96.6 2.6 %correlate.5.refs_0_ = bf16[2,512,256]{2,1,0:T(8,128)(2,1)} custom-call(s32[3]{0:T(128)S(1)} %pad_add_fusion.me_ref, bf16[64,2,16,512]{3,2,1,0:T(8,128)(2,1)S(1)} %all-to-all-done.y_ref.mine_ref.refs_0_, bf16[64,2,16,512]{3,2,1,0:T(8,128)(2,1)S(1)} %collective-permute-done.2.other_ref.refs_1_), custom_call_target="tpu_custom_call" | custom-call | tf_op jit(solution)/shard_map/correlate/pallas_call | solution.py:154
  101.0 2.6 %correlate.6 = bf16[2,512,256]{2,1,0:T(8,128)(2,1)} custom-call(s32[3]{0:T(128)S(1)} %pad_add_fusion.me_ref, bf16[64,2,16,512]{3,2,1,0:T(8,128)(2,1)S(1)} %all-to-all-done.y_ref.mine_ref.refs_0_, bf16[64,2,16,512]{3,2,1,0:T(8,128)(2,1)S(1)} %collective-permute-done.2.other_ref.refs_1_), custom_call_target="tpu_custom_call" | custom-call | tf_op jit(solution)/shard_map/correlate/pallas_call | solution.py:154
  103.6 2.0 %apply.5 = (f32[2,1024]{1,0:T(2,128)S(1)}, f32[2,1024]{1,0:T(2,128)S(1)}) custom-call(bf16[64,2,16,512]{3,2,1,0:T(8,128)(2,1)S(1)} %all-to-all-done.y_ref.mine_ref.refs_0_, bf16[64,2,16,512]{3,2,1,0:T(8,128)(2,1)S(1)} %collective-permute-done.2.other_ref.refs_1_, f32[2,1024]{1,0:T(2,128)S(1)} %get-tuple-element.66.z_ref, f32[2,1024]{1,0:T(2,128)S(1)} %add.65.near_ref, ...), custom_call_target="tpu_custom_call" | custom-call | tf_op jit(solution)/shard_map/apply/pallas_call | solution.py:223
  106.4 2.2 %collective-permute-done.9 = f32[2,1024]{1,0:T(2,128)S(1)} collective-permute-done((f32[2,1024]{1,0:T(2,128)S(1)}, f32[2,1024]{1,0:T(2,128)S(1)}, u32[]{:S(2)}, u32[]{:S(2)}) %collective-permute-start.9) | collective-permute-done | bytes 8224 | tf_op jit(solution)/shard_map/ppermute | solution.py:391
  110.1 2.6 %correlate.7 = bf16[2,512,256]{2,1,0:T(8,128)(2,1)} custom-call(s32[3]{0:T(128)S(1)} %pad_add_fusion.me_ref, bf16[64,2,16,512]{3,2,1,0:T(8,128)(2,1)S(1)} %all-to-all-done.y_ref.mine_ref.refs_0_, bf16[64,2,16,512]{3,2,1,0:T(8,128)(2,1)S(1)} %collective-permute-done.2.other_ref.refs_1_), custom_call_target="tpu_custom_call" | custom-call | tf_op jit(solution)/shard_map/correlate/pallas_call | solution.py:154
  114.2 2.5 %collective-permute-start.12 = (f32[2,1024]{1,0:T(2,128)S(1)}, f32[2,1024]{1,0:T(2,128)S(1)}, u32[]{:S(2)}, u32[]{:S(2)}) collective-permute-start(f32[2,1024]{1,0:T(2,128)S(1)} %finish.1.refs_0_), channel_id=1, source_target_pairs={{0,128},{1,129},{8,136},{9,137},{16,144},{17,145},{24,152},{25,153... | collective-permute-start | bytes 24584 | tf_op jit(solution)/shard_map/ppermute | solution.py:391
  116.8 1.8 %collective-permute-done.12.refs_2_ = f32[2,1024]{1,0:T(2,128)S(1)} collective-permute-done((f32[2,1024]{1,0:T(2,128)S(1)}, f32[2,1024]{1,0:T(2,128)S(1)}, u32[]{:S(2)}, u32[]{:S(2)}) %collective-permute-start.12) | collective-permute-done | bytes 8224 | tf_op jit(solution)/shard_map/ppermute | solution.py:391
  118.6 2.3 %collective-permute-done.13.refs_3_ = f32[2,1024]{1,0:T(2,128)S(1)} collective-permute-done((f32[2,1024]{1,0:T(2,128)S(1)}, f32[2,1024]{1,0:T(2,128)S(1)}, u32[]{:S(2)}, u32[]{:S(2)}) %collective-permute-start.13) | collective-permute-done | bytes 8224 | tf_op jit(solution)/shard_map/ppermute | solution.py:391
  122.2 2.1 %all-to-all-done.1.y_ref = bf16[64,2,16,512]{3,2,1,0:T(8,128)(2,1)} async-done(((bf16[64,2,16,512]{3,2,1,0:T(8,128)(2,1)}), bf16[64,2,16,512]{3,2,1,0:T(8,128)(2,1)}, u32[]{:S(2)}, u32[]{:S(2)}) %all-to-all-start.1) | async-done | bytes 2097184 | tf_op jit(solution)/shard_map/all_to_all | solution.py:453
  124.3 5.1 %all-to-all-start.2 = ((f32[8,2,1024]{2,1,0:T(2,128)}), f32[8,2,1024]{2,1,0:T(2,128)S(1)}, u32[]{:S(2)}, u32[]{:S(2)}) async-start(f32[8,2,1024]{2,1,0:T(2,128)} %get-tuple-element.91), calls=%async_computation.2 | async-start | bytes 131072 | tf_op jit(solution)/shard_map/all_to_all | solution.py:496
  129.4 2.7 %collective-permute-start.15 = (bf16[2,512,256]{2,1,0:T(8,128)(2,1)}, bf16[2,512,256]{2,1,0:T(8,128)(2,1)S(1)}, u32[]{:S(2)}, u32[]{:S(2)}) collective-permute-start(bf16[2,512,256]{2,1,0:T(8,128)(2,1)} %correlate.6), channel_id=1, source_target_pairs={{0,4},{2,6},{4,0},{6,2},{1,5},{3,7},{5,1},{7,3},{8,12},{10,14},{12... | collective-permute-start | bytes 1572872 | tf_op jit(solution)/shard_map/ppermute | solution.py:391
  133.0 3.6 %all-to-all-done.2.line_ref = f32[8,2,1024]{2,1,0:T(2,128)S(1)} async-done(((f32[8,2,1024]{2,1,0:T(2,128)}), f32[8,2,1024]{2,1,0:T(2,128)S(1)}, u32[]{:S(2)}, u32[]{:S(2)}) %all-to-all-start.2) | async-done | bytes 65568 | tf_op jit(solution)/shard_map/all_to_all | solution.py:496
  136.6 2.3 %beamform.3 = bf16[2,2,128,512]{3,2,1,0:T(8,128)(2,1)S(1)} custom-call(s32[32]{0:T(128)S(1)} %select_reduce_fusion.source_ref, s32[3]{0:T(128)S(1)} %pad_add_fusion.me_ref, f32[8,2,1024]{2,1,0:T(2,128)S(1)} %all-to-all-done.2.line_ref, f32[256,512]{1,0:T(8,128)S(1)} %get-tuple-element.92.cos_ref, f32[256,512]{1,0:T(8,128)S(1)} %get-tuple-element.93.sin_ref, ...), custom_call_target="tpu_custom_call" | custom-call | flops 42949672960 | bytes 67108864 | tf_op jit(solution)/shard_map/beamform/pallas_call | solution.py:337
  140.5 3.1 %beamform.2.own_hbm = bf16[2,2,128,1024]{3,2,1,0:T(8,128)(2,1)} custom-call(s32[32]{0:T(128)S(1)} %select_reduce_fusion.source_ref, s32[3]{0:T(128)S(1)} %pad_add_fusion.me_ref, f32[8,2,1024]{2,1,0:T(2,128)S(1)} %all-to-all-done.2.line_ref, f32[256,512]{1,0:T(8,128)S(1)} %get-tuple-element.92.cos_ref, f32[256,512]{1,0:T(8,128)S(1)} %get-tuple-element.93.sin_ref, ...), custom_call_target="tpu_custom_call" | custom-call | flops 42949672960 | bytes 67108864 | tf_op jit(solution)/shard_map/beamform/pallas_call | solution.py:337
  143.6 7.5 %collective-permute-done.14.refs_1_ = bf16[2,512,256]{2,1,0:T(8,128)(2,1)S(1)} collective-permute-done((bf16[2,512,256]{2,1,0:T(8,128)(2,1)}, bf16[2,512,256]{2,1,0:T(8,128)(2,1)S(1)}, u32[]{:S(2)}, u32[]{:S(2)}) %collective-permute-start.14) | collective-permute-done | bytes 524320 | tf_op jit(solution)/shard_map/ppermute | solution.py:391
  151.1 2.7 %collective-permute-done.16.refs_3_ = bf16[2,512,256]{2,1,0:T(8,128)(2,1)S(1)} collective-permute-done((bf16[2,512,256]{2,1,0:T(8,128)(2,1)}, bf16[2,512,256]{2,1,0:T(8,128)(2,1)S(1)}, u32[]{:S(2)}, u32[]{:S(2)}) %collective-permute-start.16) | collective-permute-done | bytes 524320 | tf_op jit(solution)/shard_map/ppermute | solution.py:391
  155.0 6.5 %collective-permute-start.17 = (bf16[2,512,256]{2,1,0:T(8,128)(2,1)S(1)}, bf16[2,512,256]{2,1,0:T(8,128)(2,1)S(1)}, u32[]{:S(2)}, u32[]{:S(2)}) collective-permute-start(bf16[2,512,256]{2,1,0:T(8,128)(2,1)S(1)} %gather.8), channel_id=1, source_target_pairs={{0,0},{1,8},{8,1},{9,9},{16,16},{17,24},{24,17},{25,25},{32,32},{3... | collective-permute-start | bytes 1572872 | tf_op jit(solution)/shard_map/ppermute | solution.py:400
  162.9 5.5 %collective-permute-done.17.in_ref = bf16[2,512,256]{2,1,0:T(8,128)(2,1)S(1)} collective-permute-done((bf16[2,512,256]{2,1,0:T(8,128)(2,1)S(1)}, bf16[2,512,256]{2,1,0:T(8,128)(2,1)S(1)}, u32[]{:S(2)}, u32[]{:S(2)}) %collective-permute-start.17) | collective-permute-done | bytes 524320 | tf_op jit(solution)/shard_map/ppermute | solution.py:400
  (55 shorter events, 21.4 us)
Async XLA Ops:
  3.7 13.4 %copy-start.5 = (f32[1,2,1024]{2,1,0:T(2,128)S(1)}, f32[1,2,1024]{2,1,0:T(2,128)}, u32[]{:S(2)}) copy-start(f32[1,2,1024]{2,1,0:T(2,128)} %param.9) | copy-start | bytes 24580
  3.7 16.9 %copy-start.4 = (s32[32]{0:T(128)S(1)}, s32[32]{0:T(128)}, u32[]{:S(2)}) copy-start(s32[32]{0:T(128)} %chan_hbm.2) | copy-start | bytes 388
  3.7 18.2 %copy-start.1 = (f32[2,512]{1,0:T(2,128)S(1)}, f32[2,512]{1,0:T(2,128)}, u32[]{:S(2)}) copy-start(f32[2,512]{1,0:T(2,128)} %param.12) | copy-start | bytes 12292
  3.7 18.3 %copy-start = (s32[512]{0:T(512)S(1)}, s32[512]{0:T(512)}, u32[]{:S(2)}) copy-start(s32[512]{0:T(512)} %map_hbm.3) | copy-start | bytes 6148
  3.7 19.4 %copy-start.3 = (s32[32]{0:T(128)S(1)}, s32[32]{0:T(128)}, u32[]{:S(2)}) copy-start(s32[32]{0:T(128)} %chan_hbm.3) | copy-start | bytes 388
  3.7 19.9 %copy-start.2 = (s32[2,256]{1,0:T(2,128)S(1)}, s32[2,256]{1,0:T(2,128)}, u32[]{:S(2)}) copy-start(s32[2,256]{1,0:T(2,128)} %param.13) | copy-start | bytes 6148
  3.7 63.3 %all-to-all-start = ((bf16[64,2,16,512]{3,2,1,0:T(8,128)(2,1)}), bf16[64,2,16,512]{3,2,1,0:T(8,128)(2,1)S(1)}, u32[]{:S(2)}, u32[]{:S(2)}) async-start(bf16[64,2,16,512]{3,2,1,0:T(8,128)(2,1)} %bitcast.15), calls=%async_computation | async-start | bytes 4194304 | tf_op jit(solution)/shard_map/all_to_all | solution.py:430
  17.1 11.7 %collective-permute-start = (f32[2,1024]{1,0:T(2,128)S(1)}, f32[2,1024]{1,0:T(2,128)S(1)}, u32[]{:S(2)}, u32[]{:S(2)}) collective-permute-start(f32[2,1024]{1,0:T(2,128)S(1)} %bitcast.21), channel_id=1, source_target_pairs={{0,0},{1,8},{8,1},{9,9},{16,16},{17,24},{24,17},{25,25},{32,32},{3... | collective-permute-start | bytes 24584 | tf_op jit(solution)/shard_map/ppermute | solution.py:400
  67.0 57.2 %all-to-all-start.1 = ((bf16[64,2,16,512]{3,2,1,0:T(8,128)(2,1)}), bf16[64,2,16,512]{3,2,1,0:T(8,128)(2,1)}, u32[]{:S(2)}, u32[]{:S(2)}) async-start(bf16[64,2,16,512]{3,2,1,0:T(8,128)(2,1)} %bitcast.14), calls=%async_computation.1 | async-start | bytes 4194304 | tf_op jit(solution)/shard_map/all_to_all | solution.py:453
  75.4 1.4 collective-permute-start.1
  76.8 7.4 %collective-permute-start.2 = (bf16[64,2,16,512]{3,2,1,0:T(8,128)(2,1)S(1)}, bf16[64,2,16,512]{3,2,1,0:T(8,128)(2,1)S(1)}, u32[]{:S(2)}, u32[]{:S(2)}) collective-permute-start(bf16[64,2,16,512]{3,2,1,0:T(8,128)(2,1)S(1)} %all-to-all-done.y_ref.mine_ref.refs_0_), channel_id=1, source_target_pairs={{0,8},{8,0},{16,24},{24,16},{32,40},{40,32},{48,56},{56,48},{64,72... | collective-permute-start | bytes 6291464 | tf_op jit(solution)/shard_map/ppermute | solution.py:391
  77.2 2.9 %collective-permute-start.3 = (f32[2,1024]{1,0:T(2,128)S(1)}, f32[2,1024]{1,0:T(2,128)S(1)}, u32[]{:S(2)}, u32[]{:S(2)}) collective-permute-start(f32[2,1024]{1,0:T(2,128)S(1)} %add.62), channel_id=1, source_target_pairs={{0,2},{2,0},{4,6},{6,4},{1,3},{3,1},{5,7},{7,5},{8,10},{10,8},{12,... | collective-permute-start | bytes 24584 | tf_op jit(solution)/shard_map/ppermute | solution.py:391
  80.1 4.1 %collective-permute-start.4 = (f32[2,1024]{1,0:T(2,128)S(1)}, f32[2,1024]{1,0:T(2,128)S(1)}, u32[]{:S(2)}, u32[]{:S(2)}) collective-permute-start(f32[2,1024]{1,0:T(2,128)S(1)} %add.63.near_ref), channel_id=1, source_target_pairs={{0,6},{2,4},{4,2},{6,0},{1,7},{3,5},{5,3},{7,1},{8,14},{10,12},{12... | collective-permute-start | bytes 24584 | tf_op jit(solution)/shard_map/ppermute | solution.py:391
  86.2 3.0 %collective-permute-start.5 = (f32[2,1024]{1,0:T(2,128)S(1)}, f32[2,1024]{1,0:T(2,128)S(1)}, u32[]{:S(2)}, u32[]{:S(2)}) collective-permute-start(f32[2,1024]{1,0:T(2,128)S(1)} %get-tuple-element.61), channel_id=1, source_target_pairs={{0,2},{2,0},{4,6},{6,4},{1,3},{3,1},{5,7},{7,5},{8,10},{10,8},{12,... | collective-permute-start | bytes 24584 | tf_op jit(solution)/shard_map/ppermute | solution.py:391
  89.2 5.1 %collective-permute-start.6 = (f32[2,1024]{1,0:T(2,128)S(1)}, f32[2,1024]{1,0:T(2,128)S(1)}, u32[]{:S(2)}, u32[]{:S(2)}) collective-permute-start(f32[2,1024]{1,0:T(2,128)S(1)} %add.64.near_ref), channel_id=1, source_target_pairs={{0,6},{2,4},{4,2},{6,0},{1,7},{3,5},{5,3},{7,1},{8,14},{10,12},{12... | collective-permute-start | bytes 24584 | tf_op jit(solution)/shard_map/ppermute | solution.py:391
  96.3 3.2 %collective-permute-start.7 = (f32[2,1024]{1,0:T(2,128)S(1)}, f32[2,1024]{1,0:T(2,128)S(1)}, u32[]{:S(2)}, u32[]{:S(2)}) collective-permute-start(f32[2,1024]{1,0:T(2,128)S(1)} %get-tuple-element.68), channel_id=1, source_target_pairs={{0,2},{2,0},{4,6},{6,4},{1,3},{3,1},{5,7},{7,5},{8,10},{10,8},{12,... | collective-permute-start | bytes 24584 | tf_op jit(solution)/shard_map/ppermute | solution.py:391
  99.5 4.1 %collective-permute-start.8 = (f32[2,1024]{1,0:T(2,128)S(1)}, f32[2,1024]{1,0:T(2,128)S(1)}, u32[]{:S(2)}, u32[]{:S(2)}) collective-permute-start(f32[2,1024]{1,0:T(2,128)S(1)} %add.65.near_ref), channel_id=1, source_target_pairs={{0,6},{2,4},{4,2},{6,0},{1,7},{3,5},{5,3},{7,1},{8,14},{10,12},{12... | collective-permute-start | bytes 24584 | tf_op jit(solution)/shard_map/ppermute | solution.py:391
  105.6 3.0 %collective-permute-start.9 = (f32[2,1024]{1,0:T(2,128)S(1)}, f32[2,1024]{1,0:T(2,128)S(1)}, u32[]{:S(2)}, u32[]{:S(2)}) collective-permute-start(f32[2,1024]{1,0:T(2,128)S(1)} %get-tuple-element.77), channel_id=1, source_target_pairs={{0,2},{2,0},{4,6},{6,4},{1,3},{3,1},{5,7},{7,5},{8,10},{10,8},{12,... | collective-permute-start | bytes 24584 | tf_op jit(solution)/shard_map/ppermute | solution.py:391
  108.6 4.1 %collective-permute-start.10 = (f32[2,1024]{1,0:T(2,128)S(1)}, f32[2,1024]{1,0:T(2,128)S(1)}, u32[]{:S(2)}, u32[]{:S(2)}) collective-permute-start(f32[2,1024]{1,0:T(2,128)S(1)} %add.66.near_ref), channel_id=1, source_target_pairs={{0,6},{2,4},{4,2},{6,0},{1,7},{3,5},{5,3},{7,1},{8,14},{10,12},{12... | collective-permute-start | bytes 24584 | tf_op jit(solution)/shard_map/ppermute | solution.py:391
  112.9 3.9 %collective-permute-start.11 = (f32[2,1024]{1,0:T(2,128)S(1)}, f32[2,1024]{1,0:T(2,128)S(1)}, u32[]{:S(2)}, u32[]{:S(2)}) collective-permute-start(f32[2,1024]{1,0:T(2,128)S(1)} %finish.1.refs_0_), channel_id=1, source_target_pairs={{0,1},{1,0},{8,9},{9,8},{16,17},{17,16},{24,25},{25,24},{32,33},{3... | collective-permute-start | bytes 24584 | tf_op jit(solution)/shard_map/ppermute | solution.py:391
  114.2 4.5 %collective-permute-start.12 = (f32[2,1024]{1,0:T(2,128)S(1)}, f32[2,1024]{1,0:T(2,128)S(1)}, u32[]{:S(2)}, u32[]{:S(2)}) collective-permute-start(f32[2,1024]{1,0:T(2,128)S(1)} %finish.1.refs_0_), channel_id=1, source_target_pairs={{0,128},{1,129},{8,136},{9,137},{16,144},{17,145},{24,152},{25,153... | collective-permute-start | bytes 24584 | tf_op jit(solution)/shard_map/ppermute | solution.py:391
  116.7 4.2 %collective-permute-start.13 = (f32[2,1024]{1,0:T(2,128)S(1)}, f32[2,1024]{1,0:T(2,128)S(1)}, u32[]{:S(2)}, u32[]{:S(2)}) collective-permute-start(f32[2,1024]{1,0:T(2,128)S(1)} %finish.1.refs_0_), channel_id=1, source_target_pairs={{0,129},{1,128},{8,137},{9,136},{16,145},{17,144},{24,153},{25,152... | collective-permute-start | bytes 24584 | tf_op jit(solution)/shard_map/ppermute | solution.py:391
  124.3 12.3 %all-to-all-start.2 = ((f32[8,2,1024]{2,1,0:T(2,128)}), f32[8,2,1024]{2,1,0:T(2,128)S(1)}, u32[]{:S(2)}, u32[]{:S(2)}) async-start(f32[8,2,1024]{2,1,0:T(2,128)} %get-tuple-element.91), calls=%async_computation.2 | async-start | bytes 131072 | tf_op jit(solution)/shard_map/all_to_all | solution.py:496
  129.4 14.2 %collective-permute-start.15 = (bf16[2,512,256]{2,1,0:T(8,128)(2,1)}, bf16[2,512,256]{2,1,0:T(8,128)(2,1)S(1)}, u32[]{:S(2)}, u32[]{:S(2)}) collective-permute-start(bf16[2,512,256]{2,1,0:T(8,128)(2,1)} %correlate.6), channel_id=1, source_target_pairs={{0,4},{2,6},{4,0},{6,2},{1,5},{3,7},{5,1},{7,3},{8,12},{10,14},{12... | collective-permute-start | bytes 1572872 | tf_op jit(solution)/shard_map/ppermute | solution.py:391
  132.1 19.0 %collective-permute-start.14 = (bf16[2,512,256]{2,1,0:T(8,128)(2,1)}, bf16[2,512,256]{2,1,0:T(8,128)(2,1)S(1)}, u32[]{:S(2)}, u32[]{:S(2)}) collective-permute-start(bf16[2,512,256]{2,1,0:T(8,128)(2,1)} %correlate.4), channel_id=1, source_target_pairs={{0,2},{2,0},{4,6},{6,4},{1,3},{3,1},{5,7},{7,5},{8,10},{10,8},{12,... | collective-permute-start | bytes 1572872 | tf_op jit(solution)/shard_map/ppermute | solution.py:391
  132.4 21.3 %collective-permute-start.16 = (bf16[2,512,256]{2,1,0:T(8,128)(2,1)}, bf16[2,512,256]{2,1,0:T(8,128)(2,1)S(1)}, u32[]{:S(2)}, u32[]{:S(2)}) collective-permute-start(bf16[2,512,256]{2,1,0:T(8,128)(2,1)} %correlate.7), channel_id=1, source_target_pairs={{0,6},{2,4},{4,2},{6,0},{1,7},{3,5},{5,3},{7,1},{8,14},{10,12},{12... | collective-permute-start | bytes 1572872 | tf_op jit(solution)/shard_map/ppermute | solution.py:391
  138.9 22.6 %collective-permute-start.18 = (bf16[2,2,128,512]{3,2,1,0:T(8,128)(2,1)S(1)}, bf16[2,2,128,512]{3,2,1,0:T(8,128)(2,1)S(1)}, u32[]{:S(2)}, u32[]{:S(2)}) collective-permute-start(bf16[2,2,128,512]{3,2,1,0:T(8,128)(2,1)S(1)} %beamform.3), channel_id=1, source_target_pairs={{0,1},{1,0},{2,3},{3,2},{4,5},{5,4},{6,7},{7,6},{8,9},{9,8},{10,11... | collective-permute-start | bytes 1572872 | tf_op jit(solution)/shard_map/ppermute | solution.py:391
  155.0 13.4 %collective-permute-start.17 = (bf16[2,512,256]{2,1,0:T(8,128)(2,1)S(1)}, bf16[2,512,256]{2,1,0:T(8,128)(2,1)S(1)}, u32[]{:S(2)}, u32[]{:S(2)}) collective-permute-start(bf16[2,512,256]{2,1,0:T(8,128)(2,1)S(1)} %gather.8), channel_id=1, source_target_pairs={{0,0},{1,8},{8,1},{9,9},{16,16},{17,24},{24,17},{25,25},{32,32},{3... | collective-permute-start | bytes 1572872 | tf_op jit(solution)/shard_map/ppermute | solution.py:400

commit v10 on v9

--- a/solution.py
+++ b/solution.py
@@ -497,11 +497,12 @@
         copies, "freq", split_axis=0, concat_axis=0, axis_index_groups=groups, tiled=True
     )
 
+    line, pieces[2] = lax.optimization_barrier((line, pieces[2]))
     away = beamform(1, source, me, line, cosine, sine, beam_y, n_group)
     other = swap(away, "grp", 1)
-    own = beamform(0, source, me, line, cosine, sine, beam_y, n_group)
-    own, *pieces = lax.optimization_barrier((own, *pieces))
+    late, *pieces = lax.optimization_barrier((line, *pieces))
     visibilities = widen(cross(gather(pieces)))
+    own = beamform(0, source, me, late, cosine, sine, beam_y, n_group)
     beams = place(me, own, other)
     return visibilities[None], solved[None], beams[None]
 

time: 170 us -> 164 us (0.965)
  waiting for transfers between devices: 73.3 us -> 62.3 us
  starting transfers between devices: 56.1 us -> 60.2 us
    ppermute x17, waiting for transfers between devices: 23.8 us -> 13.6 us  [swap(): return lax.ppermute(x, axis, [(i, i ^ mask) for i in range(n)])]
    ppermute x2, starting transfers between devices: 10 us -> 14 us  [cross(): return lax.ppermute(x, WIDE, pairs)]
  transfers between devices with their start and end apart: 22 -> 22, of which waited for: 14 -> 12; matrix products, arithmetic and copies ran while one was open for 3% -> 3% of each run, Pallas kernels for 18% -> 18%
where the time goes in v10:
time: 164 us; the launch traced here: 163 us
  waiting for transfers between devices  62.3 us (38%)
  starting transfers between devices  60.2 us (37%)
  Pallas kernels  34.2 us (21%)
  other arithmetic  2.26 us (1%)
  local copies, waits for them, and re-layouts  2.12 us (1%)
    all_to_all x1, waiting for transfers between devices, body(): lax.all_to_all(corr_send, WIDE, split_axis=0, concat_axis=0, tiled=True)  38.3 us
    ppermute x17, starting transfers between devices, swap(): return lax.ppermute(x, axis, [(i, i ^ mask) for i in range(n)])  20.2 us
    ppermute x2, starting transfers between devices, cross(): return lax.ppermute(x, WIDE, pairs)  14 us
    ppermute x17, waiting for transfers between devices, swap(): return lax.ppermute(x, axis, [(i, i ^ mask) for i in range(n)])  13.6 us
    all_to_all x1, starting transfers between devices, body(): lax.all_to_all(corr_send, WIDE, split_axis=0, concat_axis=0, tiled=True)  13.3 us
    pallas_call x4, Pallas kernels, correlate(): pl.pallas_call(functools.partial(correlate_kernel, scale, mask), in_specs...  10.5 us
    all_to_all x1, starting transfers between devices, body(): lax.all_to_all(beam_send, WIDE, split_axis=0, concat_axis=0, tiled=True)  7.35 us
    pallas_call x2, Pallas kernels, ingest(): pl.pallas_call(functools.partial(ingest_kernel, stations, pick), in_specs...  6.09 us
  transfers between devices with their start and end apart: 22, of which 12 were waited for; matrix products, arithmetic and copies ran while one was open for 3% of the time, Pallas kernels for 18%

profile of v10, /device:TPU:1, one launch (start us, length us, event | category | flops | bytes accessed | tf_op | source)
XLA Modules:
  0.0 162.7 jit_solution(5492210903685418989)
XLA Ops:
  0.6 3.1 %ingest.3 = bf16[32,2,2,16,512]{4,3,2,1,0:T(8,128)(2,1)} custom-call(s32[1]{0:T(128)} %bitcast.base_ref, s32[32]{0:T(128)} %chan_hbm.3, s32[512]{0:T(512)} %map_hbm.3, s32[512]{0:T(512)} %flag_hbm.3, bf16[32,2,16,1024]{3,2,1,0:T(8,128)(2,1)} %volts_hbm.3), custom_call_target="tpu_custom_call" | custom-call | tf_op jit(solution)/shard_map/ingest/pallas_call | solution.py:94
  3.8 13.3 %all-to-all-start = ((bf16[64,2,16,512]{3,2,1,0:T(8,128)(2,1)}), bf16[64,2,16,512]{3,2,1,0:T(8,128)(2,1)S(1)}, u32[]{:S(2)}, u32[]{:S(2)}) async-start(bf16[64,2,16,512]{3,2,1,0:T(8,128)(2,1)} %bitcast.15), calls=%async_computation | async-start | bytes 4194304 | tf_op jit(solution)/shard_map/all_to_all | solution.py:430
  17.1 3.5 %collective-permute-start = (f32[2,1024]{1,0:T(2,128)S(1)}, f32[2,1024]{1,0:T(2,128)S(1)}, u32[]{:S(2)}, u32[]{:S(2)}) collective-permute-start(f32[2,1024]{1,0:T(2,128)S(1)} %bitcast.21), channel_id=1, source_target_pairs={{0,0},{1,8},{8,1},{9,9},{16,16},{17,24},{24,17},{25,25},{32,32},{3... | collective-permute-start | bytes 24584 | tf_op jit(solution)/shard_map/ppermute | solution.py:400
  23.7 2.0 %fusion = (f32[256,512]{1,0:T(8,128)S(1)}, f32[256,512]{1,0:T(8,128)S(1)}) fusion(f32[512]{0:T(512)S(1)} %get-tuple-element.110, f32[256]{0:T(256)S(1)} %bitcast.20, f32[512]{0:T(512)S(1)} %get-tuple-element.109, f32[256]{0:T(256)S(1)} %bitcast.19, f32[]{:T(128)} %bitcast.4), kind=kLoop, calls=%fused_computation.2 | loop fusion | flops 524288 | bytes 1054724 | tf_op jit(solution)/shard_map/sin | solution.py:443
  25.7 3.0 %ingest.2 = bf16[32,2,2,16,512]{4,3,2,1,0:T(8,128)(2,1)} custom-call(s32[1]{0:T(128)} %bitcast.base_ref, s32[32]{0:T(128)} %chan_hbm.2, s32[512]{0:T(512)} %map_hbm.3, s32[512]{0:T(512)} %flag_hbm.3, bf16[32,2,16,1024]{3,2,1,0:T(8,128)(2,1)} %volts_hbm.3), custom_call_target="tpu_custom_call" | custom-call | tf_op jit(solution)/shard_map/ingest/pallas_call | solution.py:94
  28.7 38.3 %all-to-all-done.y_ref.mine_ref.refs_0_ = bf16[64,2,16,512]{3,2,1,0:T(8,128)(2,1)S(1)} async-done(((bf16[64,2,16,512]{3,2,1,0:T(8,128)(2,1)}), bf16[64,2,16,512]{3,2,1,0:T(8,128)(2,1)S(1)}, u32[]{:S(2)}, u32[]{:S(2)}) %all-to-all-start) | async-done | bytes 2097184 | tf_op jit(solution)/shard_map/all_to_all | solution.py:430
  67.1 7.3 %all-to-all-start.1 = ((bf16[64,2,16,512]{3,2,1,0:T(8,128)(2,1)}), bf16[64,2,16,512]{3,2,1,0:T(8,128)(2,1)}, u32[]{:S(2)}, u32[]{:S(2)}) async-start(bf16[64,2,16,512]{3,2,1,0:T(8,128)(2,1)} %bitcast.14), calls=%async_computation.1 | async-start | bytes 4194304 | tf_op jit(solution)/shard_map/all_to_all | solution.py:453
  78.4 1.7 %collective-permute-done.3 = f32[2,1024]{1,0:T(2,128)S(1)} collective-permute-done((f32[2,1024]{1,0:T(2,128)S(1)}, f32[2,1024]{1,0:T(2,128)S(1)}, u32[]{:S(2)}, u32[]{:S(2)}) %collective-permute-start.3) | collective-permute-done | bytes 8224 | tf_op jit(solution)/shard_map/ppermute | solution.py:391
  80.1 2.5 %collective-permute-start.4 = (f32[2,1024]{1,0:T(2,128)S(1)}, f32[2,1024]{1,0:T(2,128)S(1)}, u32[]{:S(2)}, u32[]{:S(2)}) collective-permute-start(f32[2,1024]{1,0:T(2,128)S(1)} %add.63.near_ref), channel_id=1, source_target_pairs={{0,6},{2,4},{4,2},{6,0},{1,7},{3,5},{5,3},{7,1},{8,14},{10,12},{12... | collective-permute-start | bytes 24584 | tf_op jit(solution)/shard_map/ppermute | solution.py:391
  82.6 1.6 %collective-permute-done.4.far_ref = f32[2,1024]{1,0:T(2,128)S(1)} collective-permute-done((f32[2,1024]{1,0:T(2,128)S(1)}, f32[2,1024]{1,0:T(2,128)S(1)}, u32[]{:S(2)}, u32[]{:S(2)}) %collective-permute-start.4) | collective-permute-done | bytes 8224 | tf_op jit(solution)/shard_map/ppermute | solution.py:391
  84.2 2.0 %apply.3 = (f32[2,1024]{1,0:T(2,128)S(1)}, f32[2,1024]{1,0:T(2,128)S(1)}) custom-call(bf16[64,2,16,512]{3,2,1,0:T(8,128)(2,1)S(1)} %all-to-all-done.y_ref.mine_ref.refs_0_, bf16[64,2,16,512]{3,2,1,0:T(8,128)(2,1)S(1)} %collective-permute-done.2.other_ref.refs_1_, f32[2,1024]{1,0:T(2,128)S(1)} %collective-permute-done.z_ref, f32[2,1024]{1,0:T(2,128)S(1)} %add.63.near_ref, ...), custom_call_target="tpu_custom_call" | custom-call | tf_op jit(solution)/shard_map/apply/pallas_call | solution.py:223
  86.3 2.9 %collective-permute-done.5 = f32[2,1024]{1,0:T(2,128)S(1)} collective-permute-done((f32[2,1024]{1,0:T(2,128)S(1)}, f32[2,1024]{1,0:T(2,128)S(1)}, u32[]{:S(2)}, u32[]{:S(2)}) %collective-permute-start.5) | collective-permute-done | bytes 8224 | tf_op jit(solution)/shard_map/ppermute | solution.py:391
  89.2 2.5 %collective-permute-start.6 = (f32[2,1024]{1,0:T(2,128)S(1)}, f32[2,1024]{1,0:T(2,128)S(1)}, u32[]{:S(2)}, u32[]{:S(2)}) collective-permute-start(f32[2,1024]{1,0:T(2,128)S(1)} %add.64.near_ref), channel_id=1, source_target_pairs={{0,6},{2,4},{4,2},{6,0},{1,7},{3,5},{5,3},{7,1},{8,14},{10,12},{12... | collective-permute-start | bytes 24584 | tf_op jit(solution)/shard_map/ppermute | solution.py:391
  91.7 2.6 %correlate.4 = bf16[2,512,256]{2,1,0:T(8,128)(2,1)} custom-call(s32[3]{0:T(128)S(1)} %pad_add_fusion.me_ref, bf16[64,2,16,512]{3,2,1,0:T(8,128)(2,1)S(1)} %all-to-all-done.y_ref.mine_ref.refs_0_, bf16[64,2,16,512]{3,2,1,0:T(8,128)(2,1)S(1)} %collective-permute-done.2.other_ref.refs_1_), custom_call_target="tpu_custom_call" | custom-call | tf_op jit(solution)/shard_map/correlate/pallas_call | solution.py:154
  94.3 2.0 %apply.4 = (f32[2,1024]{1,0:T(2,128)S(1)}, f32[2,1024]{1,0:T(2,128)S(1)}) custom-call(bf16[64,2,16,512]{3,2,1,0:T(8,128)(2,1)S(1)} %all-to-all-done.y_ref.mine_ref.refs_0_, bf16[64,2,16,512]{3,2,1,0:T(8,128)(2,1)S(1)} %collective-permute-done.2.other_ref.refs_1_, f32[2,1024]{1,0:T(2,128)S(1)} %get-tuple-element.62.z_ref, f32[2,1024]{1,0:T(2,128)S(1)} %add.64.near_ref, ...), custom_call_target="tpu_custom_call" | custom-call | tf_op jit(solution)/shard_map/apply/pallas_call | solution.py:223
  96.6 2.6 %correlate.5.refs_0_ = bf16[2,512,256]{2,1,0:T(8,128)(2,1)} custom-call(s32[3]{0:T(128)S(1)} %pad_add_fusion.me_ref, bf16[64,2,16,512]{3,2,1,0:T(8,128)(2,1)S(1)} %all-to-all-done.y_ref.mine_ref.refs_0_, bf16[64,2,16,512]{3,2,1,0:T(8,128)(2,1)S(1)} %collective-permute-done.2.other_ref.refs_1_), custom_call_target="tpu_custom_call" | custom-call | tf_op jit(solution)/shard_map/correlate/pallas_call | solution.py:154
  99.5 1.5 collective-permute-start.8
  101.0 2.6 %correlate.6 = bf16[2,512,256]{2,1,0:T(8,128)(2,1)} custom-call(s32[3]{0:T(128)S(1)} %pad_add_fusion.me_ref, bf16[64,2,16,512]{3,2,1,0:T(8,128)(2,1)S(1)} %all-to-all-done.y_ref.mine_ref.refs_0_, bf16[64,2,16,512]{3,2,1,0:T(8,128)(2,1)S(1)} %collective-permute-done.2.other_ref.refs_1_), custom_call_target="tpu_custom_call" | custom-call | tf_op jit(solution)/shard_map/correlate/pallas_call | solution.py:154
  103.7 2.0 %apply.5 = (f32[2,1024]{1,0:T(2,128)S(1)}, f32[2,1024]{1,0:T(2,128)S(1)}) custom-call(bf16[64,2,16,512]{3,2,1,0:T(8,128)(2,1)S(1)} %all-to-all-done.y_ref.mine_ref.refs_0_, bf16[64,2,16,512]{3,2,1,0:T(8,128)(2,1)S(1)} %collective-permute-done.2.other_ref.refs_1_, f32[2,1024]{1,0:T(2,128)S(1)} %get-tuple-element.68.z_ref, f32[2,1024]{1,0:T(2,128)S(1)} %add.65.near_ref, ...), custom_call_target="tpu_custom_call" | custom-call | tf_op jit(solution)/shard_map/apply/pallas_call | solution.py:223
  106.4 2.2 %collective-permute-done.9 = f32[2,1024]{1,0:T(2,128)S(1)} collective-permute-done((f32[2,1024]{1,0:T(2,128)S(1)}, f32[2,1024]{1,0:T(2,128)S(1)}, u32[]{:S(2)}, u32[]{:S(2)}) %collective-permute-start.9) | collective-permute-done | bytes 8224 | tf_op jit(solution)/shard_map/ppermute | solution.py:391
  108.7 1.5 collective-permute-start.10
  110.1 2.6 %correlate.7 = bf16[2,512,256]{2,1,0:T(8,128)(2,1)} custom-call(s32[3]{0:T(128)S(1)} %pad_add_fusion.me_ref, bf16[64,2,16,512]{3,2,1,0:T(8,128)(2,1)S(1)} %all-to-all-done.y_ref.mine_ref.refs_0_, bf16[64,2,16,512]{3,2,1,0:T(8,128)(2,1)S(1)} %collective-permute-done.2.other_ref.refs_1_), custom_call_target="tpu_custom_call" | custom-call | tf_op jit(solution)/shard_map/correlate/pallas_call | solution.py:154
  115.2 2.5 %collective-permute-start.12 = (f32[2,1024]{1,0:T(2,128)S(1)}, f32[2,1024]{1,0:T(2,128)S(1)}, u32[]{:S(2)}, u32[]{:S(2)}) collective-permute-start(f32[2,1024]{1,0:T(2,128)S(1)} %finish.1.refs_0_), channel_id=1, source_target_pairs={{0,128},{1,129},{8,136},{9,137},{16,144},{17,145},{24,152},{25,153... | collective-permute-start | bytes 24584 | tf_op jit(solution)/shard_map/ppermute | solution.py:391
  117.8 1.8 %collective-permute-done.12.refs_2_ = f32[2,1024]{1,0:T(2,128)S(1)} collective-permute-done((f32[2,1024]{1,0:T(2,128)S(1)}, f32[2,1024]{1,0:T(2,128)S(1)}, u32[]{:S(2)}, u32[]{:S(2)}) %collective-permute-start.12) | collective-permute-done | bytes 8224 | tf_op jit(solution)/shard_map/ppermute | solution.py:391
  119.6 2.3 %collective-permute-done.13.refs_3_ = f32[2,1024]{1,0:T(2,128)S(1)} collective-permute-done((f32[2,1024]{1,0:T(2,128)S(1)}, f32[2,1024]{1,0:T(2,128)S(1)}, u32[]{:S(2)}, u32[]{:S(2)}) %collective-permute-start.13) | collective-permute-done | bytes 8224 | tf_op jit(solution)/shard_map/ppermute | solution.py:391
  124.3 5.4 %all-to-all-start.2 = ((f32[8,2,1024]{2,1,0:T(2,128)}), f32[8,2,1024]{2,1,0:T(2,128)S(1)}, u32[]{:S(2)}, u32[]{:S(2)}) async-start(f32[8,2,1024]{2,1,0:T(2,128)} %get-tuple-element.93), calls=%async_computation.2 | async-start | bytes 131072 | tf_op jit(solution)/shard_map/all_to_all | solution.py:496
  130.7 1.7 %collective-permute-start.16 = (bf16[2,512,256]{2,1,0:T(8,128)(2,1)}, bf16[2,512,256]{2,1,0:T(8,128)(2,1)S(1)}, u32[]{:S(2)}, u32[]{:S(2)}) collective-permute-start(bf16[2,512,256]{2,1,0:T(8,128)(2,1)} %correlate.7), channel_id=1, source_target_pairs={{0,6},{2,4},{4,2},{6,0},{1,7},{3,5},{5,3},{7,1},{8,14},{10,12},{12... | collective-permute-start | bytes 1572872 | tf_op jit(solution)/shard_map/ppermute | solution.py:391
  132.4 4.5 %all-to-all-done.2.line_ref = f32[8,2,1024]{2,1,0:T(2,128)S(1)} async-done(((f32[8,2,1024]{2,1,0:T(2,128)}), f32[8,2,1024]{2,1,0:T(2,128)S(1)}, u32[]{:S(2)}, u32[]{:S(2)}) %all-to-all-start.2) | async-done | bytes 65568 | tf_op jit(solution)/shard_map/all_to_all | solution.py:496
  136.9 2.4 %beamform.3 = bf16[2,2,128,512]{3,2,1,0:T(8,128)(2,1)S(1)} custom-call(s32[32]{0:T(128)S(1)} %select_reduce_fusion.source_ref, s32[3]{0:T(128)S(1)} %pad_add_fusion.me_ref, f32[8,2,1024]{2,1,0:T(2,128)S(1)} %all-to-all-done.2.line_ref, f32[256,512]{1,0:T(8,128)S(1)} %get-tuple-element.106.cos_ref, f32[256,512]{1,0:T(8,128)S(1)} %get-tuple-element.107.sin_ref, ...), custom_call_target="tpu_custom_call" | custom-call | flops 42949672960 | bytes 67108864 | tf_op jit(solution)/shard_map/beamform/pallas_call | solution.py:337
  141.9 10.4 %collective-permute-start.17 = (bf16[2,512,256]{2,1,0:T(8,128)(2,1)S(1)}, bf16[2,512,256]{2,1,0:T(8,128)(2,1)S(1)}, u32[]{:S(2)}, u32[]{:S(2)}) collective-permute-start(bf16[2,512,256]{2,1,0:T(8,128)(2,1)S(1)} %gather.8), channel_id=1, source_target_pairs={{0,0},{1,8},{8,1},{9,9},{16,16},{17,24},{24,17},{25,25},{32,32},{3... | collective-permute-start | bytes 1572872 | tf_op jit(solution)/shard_map/ppermute | solution.py:400
  152.4 3.1 %beamform.2.own_hbm = bf16[2,2,128,1024]{3,2,1,0:T(8,128)(2,1)} custom-call(s32[32]{0:T(128)S(1)} %select_reduce_fusion.source_ref, s32[3]{0:T(128)S(1)} %pad_add_fusion.me_ref, f32[8,2,1024]{2,1,0:T(2,128)S(1)} %all-to-all-done.2.line_ref, f32[256,512]{1,0:T(8,128)S(1)} %get-tuple-element.106.cos_ref, f32[256,512]{1,0:T(8,128)S(1)} %get-tuple-element.107.sin_ref, ...), custom_call_target="tpu_custom_call" | custom-call | flops 42949672960 | bytes 67108864 | tf_op jit(solution)/shard_map/beamform/pallas_call | solution.py:337
  156.9 4.8 %collective-permute-done.17.in_ref = bf16[2,512,256]{2,1,0:T(8,128)(2,1)S(1)} collective-permute-done((bf16[2,512,256]{2,1,0:T(8,128)(2,1)S(1)}, bf16[2,512,256]{2,1,0:T(8,128)(2,1)S(1)}, u32[]{:S(2)}, u32[]{:S(2)}) %collective-permute-start.17) | collective-permute-done | bytes 524320 | tf_op jit(solution)/shard_map/ppermute | solution.py:400
  (55 shorter events, 18.8 us)
Async XLA Ops:
  3.7 13.4 %copy-start.5 = (f32[1,2,1024]{2,1,0:T(2,128)S(1)}, f32[1,2,1024]{2,1,0:T(2,128)}, u32[]{:S(2)}) copy-start(f32[1,2,1024]{2,1,0:T(2,128)} %param.9) | copy-start | bytes 24580
  3.7 16.9 %copy-start.4 = (s32[32]{0:T(128)S(1)}, s32[32]{0:T(128)}, u32[]{:S(2)}) copy-start(s32[32]{0:T(128)} %chan_hbm.2) | copy-start | bytes 388
  3.7 18.2 %copy-start.1 = (f32[2,512]{1,0:T(2,128)S(1)}, f32[2,512]{1,0:T(2,128)}, u32[]{:S(2)}) copy-start(f32[2,512]{1,0:T(2,128)} %param.12) | copy-start | bytes 12292
  3.7 18.3 %copy-start = (s32[512]{0:T(512)S(1)}, s32[512]{0:T(512)}, u32[]{:S(2)}) copy-start(s32[512]{0:T(512)} %map_hbm.3) | copy-start | bytes 6148
  3.8 19.4 %copy-start.3 = (s32[32]{0:T(128)S(1)}, s32[32]{0:T(128)}, u32[]{:S(2)}) copy-start(s32[32]{0:T(128)} %chan_hbm.3) | copy-start | bytes 388
  3.8 19.9 %copy-start.2 = (s32[2,256]{1,0:T(2,128)S(1)}, s32[2,256]{1,0:T(2,128)}, u32[]{:S(2)}) copy-start(s32[2,256]{1,0:T(2,128)} %param.13) | copy-start | bytes 6148
  3.8 63.3 %all-to-all-start = ((bf16[64,2,16,512]{3,2,1,0:T(8,128)(2,1)}), bf16[64,2,16,512]{3,2,1,0:T(8,128)(2,1)S(1)}, u32[]{:S(2)}, u32[]{:S(2)}) async-start(bf16[64,2,16,512]{3,2,1,0:T(8,128)(2,1)} %bitcast.15), calls=%async_computation | async-start | bytes 4194304 | tf_op jit(solution)/shard_map/all_to_all | solution.py:430
  17.1 11.6 %collective-permute-start = (f32[2,1024]{1,0:T(2,128)S(1)}, f32[2,1024]{1,0:T(2,128)S(1)}, u32[]{:S(2)}, u32[]{:S(2)}) collective-permute-start(f32[2,1024]{1,0:T(2,128)S(1)} %bitcast.21), channel_id=1, source_target_pairs={{0,0},{1,8},{8,1},{9,9},{16,16},{17,24},{24,17},{25,25},{32,32},{3... | collective-permute-start | bytes 24584 | tf_op jit(solution)/shard_map/ppermute | solution.py:400
  67.1 57.2 %all-to-all-start.1 = ((bf16[64,2,16,512]{3,2,1,0:T(8,128)(2,1)}), bf16[64,2,16,512]{3,2,1,0:T(8,128)(2,1)}, u32[]{:S(2)}, u32[]{:S(2)}) async-start(bf16[64,2,16,512]{3,2,1,0:T(8,128)(2,1)} %bitcast.14), calls=%async_computation.1 | async-start | bytes 4194304 | tf_op jit(solution)/shard_map/all_to_all | solution.py:453
  75.4 1.4 collective-permute-start.1
  76.9 7.4 %collective-permute-start.2 = (bf16[64,2,16,512]{3,2,1,0:T(8,128)(2,1)S(1)}, bf16[64,2,16,512]{3,2,1,0:T(8,128)(2,1)S(1)}, u32[]{:S(2)}, u32[]{:S(2)}) collective-permute-start(bf16[64,2,16,512]{3,2,1,0:T(8,128)(2,1)S(1)} %all-to-all-done.y_ref.mine_ref.refs_0_), channel_id=1, source_target_pairs={{0,8},{8,0},{16,24},{24,16},{32,40},{40,32},{48,56},{56,48},{64,72... | collective-permute-start | bytes 6291464 | tf_op jit(solution)/shard_map/ppermute | solution.py:391
  77.2 2.9 %collective-permute-start.3 = (f32[2,1024]{1,0:T(2,128)S(1)}, f32[2,1024]{1,0:T(2,128)S(1)}, u32[]{:S(2)}, u32[]{:S(2)}) collective-permute-start(f32[2,1024]{1,0:T(2,128)S(1)} %add.62), channel_id=1, source_target_pairs={{0,2},{2,0},{4,6},{6,4},{1,3},{3,1},{5,7},{7,5},{8,10},{10,8},{12,... | collective-permute-start | bytes 24584 | tf_op jit(solution)/shard_map/ppermute | solution.py:391
  80.1 4.1 %collective-permute-start.4 = (f32[2,1024]{1,0:T(2,128)S(1)}, f32[2,1024]{1,0:T(2,128)S(1)}, u32[]{:S(2)}, u32[]{:S(2)}) collective-permute-start(f32[2,1024]{1,0:T(2,128)S(1)} %add.63.near_ref), channel_id=1, source_target_pairs={{0,6},{2,4},{4,2},{6,0},{1,7},{3,5},{5,3},{7,1},{8,14},{10,12},{12... | collective-permute-start | bytes 24584 | tf_op jit(solution)/shard_map/ppermute | solution.py:391
  86.2 3.0 %collective-permute-start.5 = (f32[2,1024]{1,0:T(2,128)S(1)}, f32[2,1024]{1,0:T(2,128)S(1)}, u32[]{:S(2)}, u32[]{:S(2)}) collective-permute-start(f32[2,1024]{1,0:T(2,128)S(1)} %get-tuple-element.63), channel_id=1, source_target_pairs={{0,2},{2,0},{4,6},{6,4},{1,3},{3,1},{5,7},{7,5},{8,10},{10,8},{12,... | collective-permute-start | bytes 24584 | tf_op jit(solution)/shard_map/ppermute | solution.py:391
  89.2 5.1 %collective-permute-start.6 = (f32[2,1024]{1,0:T(2,128)S(1)}, f32[2,1024]{1,0:T(2,128)S(1)}, u32[]{:S(2)}, u32[]{:S(2)}) collective-permute-start(f32[2,1024]{1,0:T(2,128)S(1)} %add.64.near_ref), channel_id=1, source_target_pairs={{0,6},{2,4},{4,2},{6,0},{1,7},{3,5},{5,3},{7,1},{8,14},{10,12},{12... | collective-permute-start | bytes 24584 | tf_op jit(solution)/shard_map/ppermute | solution.py:391
  96.4 3.2 %collective-permute-start.7 = (f32[2,1024]{1,0:T(2,128)S(1)}, f32[2,1024]{1,0:T(2,128)S(1)}, u32[]{:S(2)}, u32[]{:S(2)}) collective-permute-start(f32[2,1024]{1,0:T(2,128)S(1)} %get-tuple-element.70), channel_id=1, source_target_pairs={{0,2},{2,0},{4,6},{6,4},{1,3},{3,1},{5,7},{7,5},{8,10},{10,8},{12,... | collective-permute-start | bytes 24584 | tf_op jit(solution)/shard_map/ppermute | solution.py:391
  99.5 4.1 %collective-permute-start.8 = (f32[2,1024]{1,0:T(2,128)S(1)}, f32[2,1024]{1,0:T(2,128)S(1)}, u32[]{:S(2)}, u32[]{:S(2)}) collective-permute-start(f32[2,1024]{1,0:T(2,128)S(1)} %add.65.near_ref), channel_id=1, source_target_pairs={{0,6},{2,4},{4,2},{6,0},{1,7},{3,5},{5,3},{7,1},{8,14},{10,12},{12... | collective-permute-start | bytes 24584 | tf_op jit(solution)/shard_map/ppermute | solution.py:391
  105.7 3.0 %collective-permute-start.9 = (f32[2,1024]{1,0:T(2,128)S(1)}, f32[2,1024]{1,0:T(2,128)S(1)}, u32[]{:S(2)}, u32[]{:S(2)}) collective-permute-start(f32[2,1024]{1,0:T(2,128)S(1)} %get-tuple-element.79), channel_id=1, source_target_pairs={{0,2},{2,0},{4,6},{6,4},{1,3},{3,1},{5,7},{7,5},{8,10},{10,8},{12,... | collective-permute-start | bytes 24584 | tf_op jit(solution)/shard_map/ppermute | solution.py:391
  108.7 4.1 %collective-permute-start.10 = (f32[2,1024]{1,0:T(2,128)S(1)}, f32[2,1024]{1,0:T(2,128)S(1)}, u32[]{:S(2)}, u32[]{:S(2)}) collective-permute-start(f32[2,1024]{1,0:T(2,128)S(1)} %add.66.near_ref), channel_id=1, source_target_pairs={{0,6},{2,4},{4,2},{6,0},{1,7},{3,5},{5,3},{7,1},{8,14},{10,12},{12... | collective-permute-start | bytes 24584 | tf_op jit(solution)/shard_map/ppermute | solution.py:391
  112.8 19.6 %collective-permute-start.14 = (bf16[2,512,256]{2,1,0:T(8,128)(2,1)}, bf16[2,512,256]{2,1,0:T(8,128)(2,1)S(1)}, u32[]{:S(2)}, u32[]{:S(2)}) collective-permute-start(bf16[2,512,256]{2,1,0:T(8,128)(2,1)} %correlate.6), channel_id=1, source_target_pairs={{0,4},{2,6},{4,0},{6,2},{1,5},{3,7},{5,1},{7,3},{8,12},{10,14},{12... | collective-permute-start | bytes 1572872 | tf_op jit(solution)/shard_map/ppermute | solution.py:391
  113.9 3.9 %collective-permute-start.11 = (f32[2,1024]{1,0:T(2,128)S(1)}, f32[2,1024]{1,0:T(2,128)S(1)}, u32[]{:S(2)}, u32[]{:S(2)}) collective-permute-start(f32[2,1024]{1,0:T(2,128)S(1)} %finish.1.refs_0_), channel_id=1, source_target_pairs={{0,1},{1,0},{8,9},{9,8},{16,17},{17,16},{24,25},{25,24},{32,33},{3... | collective-permute-start | bytes 24584 | tf_op jit(solution)/shard_map/ppermute | solution.py:391
  115.2 4.4 %collective-permute-start.12 = (f32[2,1024]{1,0:T(2,128)S(1)}, f32[2,1024]{1,0:T(2,128)S(1)}, u32[]{:S(2)}, u32[]{:S(2)}) collective-permute-start(f32[2,1024]{1,0:T(2,128)S(1)} %finish.1.refs_0_), channel_id=1, source_target_pairs={{0,128},{1,129},{8,136},{9,137},{16,144},{17,145},{24,152},{25,153... | collective-permute-start | bytes 24584 | tf_op jit(solution)/shard_map/ppermute | solution.py:391
  117.7 4.2 %collective-permute-start.13 = (f32[2,1024]{1,0:T(2,128)S(1)}, f32[2,1024]{1,0:T(2,128)S(1)}, u32[]{:S(2)}, u32[]{:S(2)}) collective-permute-start(f32[2,1024]{1,0:T(2,128)S(1)} %finish.1.refs_0_), channel_id=1, source_target_pairs={{0,129},{1,128},{8,137},{9,136},{16,145},{17,144},{24,153},{25,152... | collective-permute-start | bytes 24584 | tf_op jit(solution)/shard_map/ppermute | solution.py:391
  124.3 12.6 %all-to-all-start.2 = ((f32[8,2,1024]{2,1,0:T(2,128)}), f32[8,2,1024]{2,1,0:T(2,128)S(1)}, u32[]{:S(2)}, u32[]{:S(2)}) async-start(f32[8,2,1024]{2,1,0:T(2,128)} %get-tuple-element.93), calls=%async_computation.2 | async-start | bytes 131072 | tf_op jit(solution)/shard_map/all_to_all | solution.py:496
  129.7 11.0 %collective-permute-start.15 = (bf16[2,512,256]{2,1,0:T(8,128)(2,1)}, bf16[2,512,256]{2,1,0:T(8,128)(2,1)S(1)}, u32[]{:S(2)}, u32[]{:S(2)}) collective-permute-start(bf16[2,512,256]{2,1,0:T(8,128)(2,1)} %correlate.4), channel_id=1, source_target_pairs={{0,2},{2,0},{4,6},{6,4},{1,3},{3,1},{5,7},{7,5},{8,10},{10,8},{12,... | collective-permute-start | bytes 1572872 | tf_op jit(solution)/shard_map/ppermute | solution.py:391
  130.7 9.9 %collective-permute-start.16 = (bf16[2,512,256]{2,1,0:T(8,128)(2,1)}, bf16[2,512,256]{2,1,0:T(8,128)(2,1)S(1)}, u32[]{:S(2)}, u32[]{:S(2)}) collective-permute-start(bf16[2,512,256]{2,1,0:T(8,128)(2,1)} %correlate.7), channel_id=1, source_target_pairs={{0,6},{2,4},{4,2},{6,0},{1,7},{3,5},{5,3},{7,1},{8,14},{10,12},{12... | collective-permute-start | bytes 1572872 | tf_op jit(solution)/shard_map/ppermute | solution.py:391
  139.3 16.2 %collective-permute-start.18 = (bf16[2,2,128,512]{3,2,1,0:T(8,128)(2,1)S(1)}, bf16[2,2,128,512]{3,2,1,0:T(8,128)(2,1)S(1)}, u32[]{:S(2)}, u32[]{:S(2)}) collective-permute-start(bf16[2,2,128,512]{3,2,1,0:T(8,128)(2,1)S(1)} %beamform.3), channel_id=1, source_target_pairs={{0,1},{1,0},{2,3},{3,2},{4,5},{5,4},{6,7},{7,6},{8,9},{9,8},{10,11... | collective-permute-start | bytes 1572872 | tf_op jit(solution)/shard_map/ppermute | solution.py:391
  141.9 19.7 %collective-permute-start.17 = (bf16[2,512,256]{2,1,0:T(8,128)(2,1)S(1)}, bf16[2,512,256]{2,1,0:T(8,128)(2,1)S(1)}, u32[]{:S(2)}, u32[]{:S(2)}) collective-permute-start(bf16[2,512,256]{2,1,0:T(8,128)(2,1)S(1)} %gather.8), channel_id=1, source_target_pairs={{0,0},{1,8},{8,1},{9,9},{16,16},{17,24},{24,17},{25,25},{32,32},{3... | collective-permute-start | bytes 1572872 | tf_op jit(solution)/shard_map/ppermute | solution.py:400

commit v11 on v10

--- a/solution.py
+++ b/solution.py
@@ -155,7 +155,9 @@
         functools.partial(correlate_kernel, scale, mask),
         in_specs=[whole(SMEM)] + [whole(VMEM)] * len(ys),
         out_specs=whole(VMEM),
-        out_shape=pltpu.HBM((2, inputs // 2, inputs // n_time), BF16),
+        out_shape=(pltpu.VMEM if mask in (1,3,) else pltpu.HBM)(
+            (2, inputs // 2, inputs // n_time), BF16
+        ),
         compiler_params=params(16),
         name="correlate",
     )(me, *ys)
@@ -343,7 +345,14 @@
         compiler_params=params(16),
         cost_estimate=LONG,
         name="beamform",
-    )(source, me, line, cosine, sine, y)
+    )(
+        source,
+        me,
+        line,
+        pltpu.with_memory_space_constraint(cosine, pltpu.HBM),
+        pltpu.with_memory_space_constraint(sine, pltpu.HBM),
+        y,
+    )
 
 
 def place_kernel(me_ref, own_hbm, other_ref, out_hbm, sem):

time: 164 us -> 164 us (level)
  transfers between devices with their start and end apart: 22 -> 22, of which waited for: 12 -> 13; matrix products, arithmetic and copies ran while one was open for 3% -> 3% of each run, Pallas kernels for 18% -> 18%
where the time goes in v11:
time: 164 us; the launch traced here: 163 us
  waiting for transfers between devices  62.1 us (38%)
  starting transfers between devices  61 us (37%)
  Pallas kernels  33.1 us (20%)
  other arithmetic  3.44 us (2%)
  local copies, waits for them, and re-layouts  2.12 us (1%)
    all_to_all x1, waiting for transfers between devices, body(): lax.all_to_all(corr_send, WIDE, split_axis=0, concat_axis=0, tiled=True)  37.1 us
    ppermute x17, starting transfers between devices, swap(): return lax.ppermute(x, axis, [(i, i ^ mask) for i in range(n)])  20.9 us
    ppermute x17, waiting for transfers between devices, swap(): return lax.ppermute(x, axis, [(i, i ^ mask) for i in range(n)])  14.4 us
    ppermute x2, starting transfers between devices, cross(): return lax.ppermute(x, WIDE, pairs)  14.3 us
    all_to_all x1, starting transfers between devices, body(): lax.all_to_all(corr_send, WIDE, split_axis=0, concat_axis=0, tiled=True)  13.3 us
    pallas_call x4, Pallas kernels, correlate(): pl.pallas_call(functools.partial(correlate_kernel, scale, mask), in_specs...  8.88 us
    all_to_all x1, starting transfers between devices, body(): lax.all_to_all(beam_send, WIDE, split_axis=0, concat_axis=0, tiled=True)  7.35 us
    pallas_call x2, Pallas kernels, ingest(): pl.pallas_call(functools.partial(ingest_kernel, stations, pick), in_specs...  6.09 us
  transfers between devices with their start and end apart: 22, of which 13 were waited for; matrix products, arithmetic and copies ran while one was open for 3% of the time, Pallas kernels for 18%

profile of v11, /device:TPU:1, one launch (start us, length us, event | category | flops | bytes accessed | tf_op | source)
XLA Modules:
  0.0 163.3 jit_solution(5334929421472011402)
XLA Ops:
  0.6 3.1 %ingest.3 = bf16[32,2,2,16,512]{4,3,2,1,0:T(8,128)(2,1)} custom-call(s32[1]{0:T(128)} %bitcast.base_ref, s32[32]{0:T(128)} %chan_hbm.3, s32[512]{0:T(512)} %map_hbm.3, s32[512]{0:T(512)} %flag_hbm.3, bf16[32,2,16,1024]{3,2,1,0:T(8,128)(2,1)} %volts_hbm.3), custom_call_target="tpu_custom_call" | custom-call | tf_op jit(solution)/shard_map/ingest/pallas_call | solution.py:94
  3.8 13.3 %all-to-all-start = ((bf16[64,2,16,512]{3,2,1,0:T(8,128)(2,1)}), bf16[64,2,16,512]{3,2,1,0:T(8,128)(2,1)S(1)}, u32[]{:S(2)}, u32[]{:S(2)}) async-start(bf16[64,2,16,512]{3,2,1,0:T(8,128)(2,1)} %bitcast.15), calls=%async_computation | async-start | bytes 4194304 | tf_op jit(solution)/shard_map/all_to_all | solution.py:439
  17.1 3.5 %collective-permute-start = (f32[2,1024]{1,0:T(2,128)S(1)}, f32[2,1024]{1,0:T(2,128)S(1)}, u32[]{:S(2)}, u32[]{:S(2)}) collective-permute-start(f32[2,1024]{1,0:T(2,128)S(1)} %bitcast.21), channel_id=1, source_target_pairs={{0,0},{1,8},{8,1},{9,9},{16,16},{17,24},{24,17},{25,25},{32,32},{3... | collective-permute-start | bytes 24584 | tf_op jit(solution)/shard_map/ppermute | solution.py:409
  23.7 3.1 %fusion = (f32[256,512]{1,0:T(8,128)}, f32[256,512]{1,0:T(8,128)}) fusion(f32[512]{0:T(512)S(1)} %get-tuple-element.110, f32[256]{0:T(256)S(1)} %bitcast.20, f32[512]{0:T(512)S(1)} %get-tuple-element.109, f32[256]{0:T(256)S(1)} %bitcast.19, f32[]{:T(128)} %bitcast.4), kind=kLoop, calls=%fused_computation.2 | loop fusion | flops 524288 | bytes 1054724 | tf_op jit(solution)/shard_map/sin | solution.py:452
  26.9 3.0 %ingest.2 = bf16[32,2,2,16,512]{4,3,2,1,0:T(8,128)(2,1)} custom-call(s32[1]{0:T(128)} %bitcast.base_ref, s32[32]{0:T(128)} %chan_hbm.2, s32[512]{0:T(512)} %map_hbm.3, s32[512]{0:T(512)} %flag_hbm.3, bf16[32,2,16,1024]{3,2,1,0:T(8,128)(2,1)} %volts_hbm.3), custom_call_target="tpu_custom_call" | custom-call | tf_op jit(solution)/shard_map/ingest/pallas_call | solution.py:94
  29.9 37.1 %all-to-all-done.y_ref.mine_ref.refs_0_ = bf16[64,2,16,512]{3,2,1,0:T(8,128)(2,1)S(1)} async-done(((bf16[64,2,16,512]{3,2,1,0:T(8,128)(2,1)}), bf16[64,2,16,512]{3,2,1,0:T(8,128)(2,1)S(1)}, u32[]{:S(2)}, u32[]{:S(2)}) %all-to-all-start) | async-done | bytes 2097184 | tf_op jit(solution)/shard_map/all_to_all | solution.py:439
  67.1 7.3 %all-to-all-start.1 = ((bf16[64,2,16,512]{3,2,1,0:T(8,128)(2,1)}), bf16[64,2,16,512]{3,2,1,0:T(8,128)(2,1)}, u32[]{:S(2)}, u32[]{:S(2)}) async-start(bf16[64,2,16,512]{3,2,1,0:T(8,128)(2,1)} %bitcast.14), calls=%async_computation.1 | async-start | bytes 4194304 | tf_op jit(solution)/shard_map/all_to_all | solution.py:462
  78.4 1.7 %collective-permute-done.3 = f32[2,1024]{1,0:T(2,128)S(1)} collective-permute-done((f32[2,1024]{1,0:T(2,128)S(1)}, f32[2,1024]{1,0:T(2,128)S(1)}, u32[]{:S(2)}, u32[]{:S(2)}) %collective-permute-start.3) | collective-permute-done | bytes 8224 | tf_op jit(solution)/shard_map/ppermute | solution.py:400
  80.1 2.5 %collective-permute-start.4 = (f32[2,1024]{1,0:T(2,128)S(1)}, f32[2,1024]{1,0:T(2,128)S(1)}, u32[]{:S(2)}, u32[]{:S(2)}) collective-permute-start(f32[2,1024]{1,0:T(2,128)S(1)} %add.63.near_ref), channel_id=1, source_target_pairs={{0,6},{2,4},{4,2},{6,0},{1,7},{3,5},{5,3},{7,1},{8,14},{10,12},{12... | collective-permute-start | bytes 24584 | tf_op jit(solution)/shard_map/ppermute | solution.py:400
  82.6 1.6 %collective-permute-done.4.far_ref = f32[2,1024]{1,0:T(2,128)S(1)} collective-permute-done((f32[2,1024]{1,0:T(2,128)S(1)}, f32[2,1024]{1,0:T(2,128)S(1)}, u32[]{:S(2)}, u32[]{:S(2)}) %collective-permute-start.4) | collective-permute-done | bytes 8224 | tf_op jit(solution)/shard_map/ppermute | solution.py:400
  84.2 2.0 %apply.3 = (f32[2,1024]{1,0:T(2,128)S(1)}, f32[2,1024]{1,0:T(2,128)S(1)}) custom-call(bf16[64,2,16,512]{3,2,1,0:T(8,128)(2,1)S(1)} %all-to-all-done.y_ref.mine_ref.refs_0_, bf16[64,2,16,512]{3,2,1,0:T(8,128)(2,1)S(1)} %collective-permute-done.2.other_ref.refs_1_, f32[2,1024]{1,0:T(2,128)S(1)} %collective-permute-done.z_ref, f32[2,1024]{1,0:T(2,128)S(1)} %add.63.near_ref, ...), custom_call_target="tpu_custom_call" | custom-call | tf_op jit(solution)/shard_map/apply/pallas_call | solution.py:225
  86.3 2.9 %collective-permute-done.5 = f32[2,1024]{1,0:T(2,128)S(1)} collective-permute-done((f32[2,1024]{1,0:T(2,128)S(1)}, f32[2,1024]{1,0:T(2,128)S(1)}, u32[]{:S(2)}, u32[]{:S(2)}) %collective-permute-start.5) | collective-permute-done | bytes 8224 | tf_op jit(solution)/shard_map/ppermute | solution.py:400
  89.2 2.5 %collective-permute-start.6 = (f32[2,1024]{1,0:T(2,128)S(1)}, f32[2,1024]{1,0:T(2,128)S(1)}, u32[]{:S(2)}, u32[]{:S(2)}) collective-permute-start(f32[2,1024]{1,0:T(2,128)S(1)} %add.64.near_ref), channel_id=1, source_target_pairs={{0,6},{2,4},{4,2},{6,0},{1,7},{3,5},{5,3},{7,1},{8,14},{10,12},{12... | collective-permute-start | bytes 24584 | tf_op jit(solution)/shard_map/ppermute | solution.py:400
  91.7 1.8 %correlate.4 = bf16[2,512,256]{2,1,0:T(8,128)(2,1)S(1)} custom-call(s32[3]{0:T(128)S(1)} %pad_add_fusion.me_ref, bf16[64,2,16,512]{3,2,1,0:T(8,128)(2,1)S(1)} %all-to-all-done.y_ref.mine_ref.refs_0_, bf16[64,2,16,512]{3,2,1,0:T(8,128)(2,1)S(1)} %collective-permute-done.2.other_ref.refs_1_), custom_call_target="tpu_custom_call" | custom-call | tf_op jit(solution)/shard_map/correlate/pallas_call | solution.py:154
  93.6 2.0 %apply.4 = (f32[2,1024]{1,0:T(2,128)S(1)}, f32[2,1024]{1,0:T(2,128)S(1)}) custom-call(bf16[64,2,16,512]{3,2,1,0:T(8,128)(2,1)S(1)} %all-to-all-done.y_ref.mine_ref.refs_0_, bf16[64,2,16,512]{3,2,1,0:T(8,128)(2,1)S(1)} %collective-permute-done.2.other_ref.refs_1_, f32[2,1024]{1,0:T(2,128)S(1)} %get-tuple-element.62.z_ref, f32[2,1024]{1,0:T(2,128)S(1)} %add.64.near_ref, ...), custom_call_target="tpu_custom_call" | custom-call | tf_op jit(solution)/shard_map/apply/pallas_call | solution.py:225
  95.7 2.6 %correlate.5.refs_0_ = bf16[2,512,256]{2,1,0:T(8,128)(2,1)} custom-call(s32[3]{0:T(128)S(1)} %pad_add_fusion.me_ref, bf16[64,2,16,512]{3,2,1,0:T(8,128)(2,1)S(1)} %all-to-all-done.y_ref.mine_ref.refs_0_, bf16[64,2,16,512]{3,2,1,0:T(8,128)(2,1)S(1)} %collective-permute-done.2.other_ref.refs_1_), custom_call_target="tpu_custom_call" | custom-call | tf_op jit(solution)/shard_map/correlate/pallas_call | solution.py:154
  98.6 2.4 %collective-permute-start.8 = (f32[2,1024]{1,0:T(2,128)S(1)}, f32[2,1024]{1,0:T(2,128)S(1)}, u32[]{:S(2)}, u32[]{:S(2)}) collective-permute-start(f32[2,1024]{1,0:T(2,128)S(1)} %add.65.near_ref), channel_id=1, source_target_pairs={{0,6},{2,4},{4,2},{6,0},{1,7},{3,5},{5,3},{7,1},{8,14},{10,12},{12... | collective-permute-start | bytes 24584 | tf_op jit(solution)/shard_map/ppermute | solution.py:400
  101.0 2.6 %correlate.6 = bf16[2,512,256]{2,1,0:T(8,128)(2,1)} custom-call(s32[3]{0:T(128)S(1)} %pad_add_fusion.me_ref, bf16[64,2,16,512]{3,2,1,0:T(8,128)(2,1)S(1)} %all-to-all-done.y_ref.mine_ref.refs_0_, bf16[64,2,16,512]{3,2,1,0:T(8,128)(2,1)S(1)} %collective-permute-done.2.other_ref.refs_1_), custom_call_target="tpu_custom_call" | custom-call | tf_op jit(solution)/shard_map/correlate/pallas_call | solution.py:154
  103.6 2.0 %apply.5 = (f32[2,1024]{1,0:T(2,128)S(1)}, f32[2,1024]{1,0:T(2,128)S(1)}) custom-call(bf16[64,2,16,512]{3,2,1,0:T(8,128)(2,1)S(1)} %all-to-all-done.y_ref.mine_ref.refs_0_, bf16[64,2,16,512]{3,2,1,0:T(8,128)(2,1)S(1)} %collective-permute-done.2.other_ref.refs_1_, f32[2,1024]{1,0:T(2,128)S(1)} %get-tuple-element.68.z_ref, f32[2,1024]{1,0:T(2,128)S(1)} %add.65.near_ref, ...), custom_call_target="tpu_custom_call" | custom-call | tf_op jit(solution)/shard_map/apply/pallas_call | solution.py:225
  106.4 2.2 %collective-permute-done.9 = f32[2,1024]{1,0:T(2,128)S(1)} collective-permute-done((f32[2,1024]{1,0:T(2,128)S(1)}, f32[2,1024]{1,0:T(2,128)S(1)}, u32[]{:S(2)}, u32[]{:S(2)}) %collective-permute-start.9) | collective-permute-done | bytes 8224 | tf_op jit(solution)/shard_map/ppermute | solution.py:400
  110.1 1.8 %correlate.7 = bf16[2,512,256]{2,1,0:T(8,128)(2,1)S(1)} custom-call(s32[3]{0:T(128)S(1)} %pad_add_fusion.me_ref, bf16[64,2,16,512]{3,2,1,0:T(8,128)(2,1)S(1)} %all-to-all-done.y_ref.mine_ref.refs_0_, bf16[64,2,16,512]{3,2,1,0:T(8,128)(2,1)S(1)} %collective-permute-done.2.other_ref.refs_1_), custom_call_target="tpu_custom_call" | custom-call | tf_op jit(solution)/shard_map/correlate/pallas_call | solution.py:154
  114.5 2.5 %collective-permute-start.12 = (f32[2,1024]{1,0:T(2,128)S(1)}, f32[2,1024]{1,0:T(2,128)S(1)}, u32[]{:S(2)}, u32[]{:S(2)}) collective-permute-start(f32[2,1024]{1,0:T(2,128)S(1)} %finish.1.refs_0_), channel_id=1, source_target_pairs={{0,128},{1,129},{8,136},{9,137},{16,144},{17,145},{24,152},{25,153... | collective-permute-start | bytes 24584 | tf_op jit(solution)/shard_map/ppermute | solution.py:400
  117.1 1.8 %collective-permute-done.12.refs_2_ = f32[2,1024]{1,0:T(2,128)S(1)} collective-permute-done((f32[2,1024]{1,0:T(2,128)S(1)}, f32[2,1024]{1,0:T(2,128)S(1)}, u32[]{:S(2)}, u32[]{:S(2)}) %collective-permute-start.12) | collective-permute-done | bytes 8224 | tf_op jit(solution)/shard_map/ppermute | solution.py:400
  118.9 2.3 %collective-permute-done.13.refs_3_ = f32[2,1024]{1,0:T(2,128)S(1)} collective-permute-done((f32[2,1024]{1,0:T(2,128)S(1)}, f32[2,1024]{1,0:T(2,128)S(1)}, u32[]{:S(2)}, u32[]{:S(2)}) %collective-permute-start.13) | collective-permute-done | bytes 8224 | tf_op jit(solution)/shard_map/ppermute | solution.py:400
  122.4 1.8 %all-to-all-done.1.y_ref = bf16[64,2,16,512]{3,2,1,0:T(8,128)(2,1)} async-done(((bf16[64,2,16,512]{3,2,1,0:T(8,128)(2,1)}), bf16[64,2,16,512]{3,2,1,0:T(8,128)(2,1)}, u32[]{:S(2)}, u32[]{:S(2)}) %all-to-all-start.1) | async-done | bytes 2097184 | tf_op jit(solution)/shard_map/all_to_all | solution.py:462
  124.3 5.1 %all-to-all-start.2 = ((f32[8,2,1024]{2,1,0:T(2,128)}), f32[8,2,1024]{2,1,0:T(2,128)S(1)}, u32[]{:S(2)}, u32[]{:S(2)}) async-start(f32[8,2,1024]{2,1,0:T(2,128)} %get-tuple-element.93), calls=%async_computation.2 | async-start | bytes 131072 | tf_op jit(solution)/shard_map/all_to_all | solution.py:505
  130.7 1.7 %collective-permute-start.16 = (bf16[2,512,256]{2,1,0:T(8,128)(2,1)S(1)}, bf16[2,512,256]{2,1,0:T(8,128)(2,1)S(1)}, u32[]{:S(2)}, u32[]{:S(2)}) collective-permute-start(bf16[2,512,256]{2,1,0:T(8,128)(2,1)S(1)} %correlate.7), channel_id=1, source_target_pairs={{0,6},{2,4},{4,2},{6,0},{1,7},{3,5},{5,3},{7,1},{8,14},{10,12},{12... | collective-permute-start | bytes 1572872 | tf_op jit(solution)/shard_map/ppermute | solution.py:400
  132.4 4.2 %all-to-all-done.2.line_ref = f32[8,2,1024]{2,1,0:T(2,128)S(1)} async-done(((f32[8,2,1024]{2,1,0:T(2,128)}), f32[8,2,1024]{2,1,0:T(2,128)S(1)}, u32[]{:S(2)}, u32[]{:S(2)}) %all-to-all-start.2) | async-done | bytes 65568 | tf_op jit(solution)/shard_map/all_to_all | solution.py:505
  136.6 2.7 %beamform.3 = bf16[2,2,128,512]{3,2,1,0:T(8,128)(2,1)S(1)} custom-call(s32[32]{0:T(128)S(1)} %select_reduce_fusion.source_ref, s32[3]{0:T(128)S(1)} %pad_add_fusion.me_ref, f32[8,2,1024]{2,1,0:T(2,128)S(1)} %all-to-all-done.2.line_ref, f32[256,512]{1,0:T(8,128)} %get-tuple-element.106.cos_ref, f32[256,512]{1,0:T(8,128)} %get-tuple-element.107.sin_ref, ...), custom_call_target="tpu_custom_call" | custom-call | flops 42949672960 | bytes 67108864 | tf_op jit(solution)/shard_map/beamform/pallas_call | solution.py:339
  142.2 10.8 %collective-permute-start.17 = (bf16[2,512,256]{2,1,0:T(8,128)(2,1)S(1)}, bf16[2,512,256]{2,1,0:T(8,128)(2,1)S(1)}, u32[]{:S(2)}, u32[]{:S(2)}) collective-permute-start(bf16[2,512,256]{2,1,0:T(8,128)(2,1)S(1)} %gather.8), channel_id=1, source_target_pairs={{0,0},{1,8},{8,1},{9,9},{16,16},{17,24},{24,17},{25,25},{32,32},{3... | collective-permute-start | bytes 1572872 | tf_op jit(solution)/shard_map/ppermute | solution.py:409
  152.9 3.4 %beamform.2.own_hbm = bf16[2,2,128,1024]{3,2,1,0:T(8,128)(2,1)} custom-call(s32[32]{0:T(128)S(1)} %select_reduce_fusion.source_ref, s32[3]{0:T(128)S(1)} %pad_add_fusion.me_ref, f32[8,2,1024]{2,1,0:T(2,128)S(1)} %all-to-all-done.2.line_ref, f32[256,512]{1,0:T(8,128)} %get-tuple-element.106.cos_ref, f32[256,512]{1,0:T(8,128)} %get-tuple-element.107.sin_ref, ...), custom_call_target="tpu_custom_call" | custom-call | flops 42949672960 | bytes 67108864 | tf_op jit(solution)/shard_map/beamform/pallas_call | solution.py:339
  157.7 4.5 %collective-permute-done.17.in_ref = bf16[2,512,256]{2,1,0:T(8,128)(2,1)S(1)} collective-permute-done((bf16[2,512,256]{2,1,0:T(8,128)(2,1)S(1)}, bf16[2,512,256]{2,1,0:T(8,128)(2,1)S(1)}, u32[]{:S(2)}, u32[]{:S(2)}) %collective-permute-start.17) | collective-permute-done | bytes 524320 | tf_op jit(solution)/shard_map/ppermute | solution.py:409
  (55 shorter events, 19.7 us)
Async XLA Ops:
  3.7 13.4 %copy-start.5 = (f32[1,2,1024]{2,1,0:T(2,128)S(1)}, f32[1,2,1024]{2,1,0:T(2,128)}, u32[]{:S(2)}) copy-start(f32[1,2,1024]{2,1,0:T(2,128)} %param.9) | copy-start | bytes 24580
  3.7 16.9 %copy-start.4 = (s32[32]{0:T(128)S(1)}, s32[32]{0:T(128)}, u32[]{:S(2)}) copy-start(s32[32]{0:T(128)} %chan_hbm.2) | copy-start | bytes 388
  3.7 18.2 %copy-start.1 = (f32[2,512]{1,0:T(2,128)S(1)}, f32[2,512]{1,0:T(2,128)}, u32[]{:S(2)}) copy-start(f32[2,512]{1,0:T(2,128)} %param.12) | copy-start | bytes 12292
  3.7 18.3 %copy-start = (s32[512]{0:T(512)S(1)}, s32[512]{0:T(512)}, u32[]{:S(2)}) copy-start(s32[512]{0:T(512)} %map_hbm.3) | copy-start | bytes 6148
  3.8 19.4 %copy-start.3 = (s32[32]{0:T(128)S(1)}, s32[32]{0:T(128)}, u32[]{:S(2)}) copy-start(s32[32]{0:T(128)} %chan_hbm.3) | copy-start | bytes 388
  3.8 19.9 %copy-start.2 = (s32[2,256]{1,0:T(2,128)S(1)}, s32[2,256]{1,0:T(2,128)}, u32[]{:S(2)}) copy-start(s32[2,256]{1,0:T(2,128)} %param.13) | copy-start | bytes 6148
  3.8 63.3 %all-to-all-start = ((bf16[64,2,16,512]{3,2,1,0:T(8,128)(2,1)}), bf16[64,2,16,512]{3,2,1,0:T(8,128)(2,1)S(1)}, u32[]{:S(2)}, u32[]{:S(2)}) async-start(bf16[64,2,16,512]{3,2,1,0:T(8,128)(2,1)} %bitcast.15), calls=%async_computation | async-start | bytes 4194304 | tf_op jit(solution)/shard_map/all_to_all | solution.py:439
  17.1 12.8 %collective-permute-start = (f32[2,1024]{1,0:T(2,128)S(1)}, f32[2,1024]{1,0:T(2,128)S(1)}, u32[]{:S(2)}, u32[]{:S(2)}) collective-permute-start(f32[2,1024]{1,0:T(2,128)S(1)} %bitcast.21), channel_id=1, source_target_pairs={{0,0},{1,8},{8,1},{9,9},{16,16},{17,24},{24,17},{25,25},{32,32},{3... | collective-permute-start | bytes 24584 | tf_op jit(solution)/shard_map/ppermute | solution.py:409
  67.1 57.2 %all-to-all-start.1 = ((bf16[64,2,16,512]{3,2,1,0:T(8,128)(2,1)}), bf16[64,2,16,512]{3,2,1,0:T(8,128)(2,1)}, u32[]{:S(2)}, u32[]{:S(2)}) async-start(bf16[64,2,16,512]{3,2,1,0:T(8,128)(2,1)} %bitcast.14), calls=%async_computation.1 | async-start | bytes 4194304 | tf_op jit(solution)/shard_map/all_to_all | solution.py:462
  75.4 1.4 collective-permute-start.1
  76.9 7.4 %collective-permute-start.2 = (bf16[64,2,16,512]{3,2,1,0:T(8,128)(2,1)S(1)}, bf16[64,2,16,512]{3,2,1,0:T(8,128)(2,1)S(1)}, u32[]{:S(2)}, u32[]{:S(2)}) collective-permute-start(bf16[64,2,16,512]{3,2,1,0:T(8,128)(2,1)S(1)} %all-to-all-done.y_ref.mine_ref.refs_0_), channel_id=1, source_target_pairs={{0,8},{8,0},{16,24},{24,16},{32,40},{40,32},{48,56},{56,48},{64,72... | collective-permute-start | bytes 6291464 | tf_op jit(solution)/shard_map/ppermute | solution.py:400
  77.2 2.9 %collective-permute-start.3 = (f32[2,1024]{1,0:T(2,128)S(1)}, f32[2,1024]{1,0:T(2,128)S(1)}, u32[]{:S(2)}, u32[]{:S(2)}) collective-permute-start(f32[2,1024]{1,0:T(2,128)S(1)} %add.62), channel_id=1, source_target_pairs={{0,2},{2,0},{4,6},{6,4},{1,3},{3,1},{5,7},{7,5},{8,10},{10,8},{12,... | collective-permute-start | bytes 24584 | tf_op jit(solution)/shard_map/ppermute | solution.py:400
  80.1 4.1 %collective-permute-start.4 = (f32[2,1024]{1,0:T(2,128)S(1)}, f32[2,1024]{1,0:T(2,128)S(1)}, u32[]{:S(2)}, u32[]{:S(2)}) collective-permute-start(f32[2,1024]{1,0:T(2,128)S(1)} %add.63.near_ref), channel_id=1, source_target_pairs={{0,6},{2,4},{4,2},{6,0},{1,7},{3,5},{5,3},{7,1},{8,14},{10,12},{12... | collective-permute-start | bytes 24584 | tf_op jit(solution)/shard_map/ppermute | solution.py:400
  86.2 3.0 %collective-permute-start.5 = (f32[2,1024]{1,0:T(2,128)S(1)}, f32[2,1024]{1,0:T(2,128)S(1)}, u32[]{:S(2)}, u32[]{:S(2)}) collective-permute-start(f32[2,1024]{1,0:T(2,128)S(1)} %get-tuple-element.63), channel_id=1, source_target_pairs={{0,2},{2,0},{4,6},{6,4},{1,3},{3,1},{5,7},{7,5},{8,10},{10,8},{12,... | collective-permute-start | bytes 24584 | tf_op jit(solution)/shard_map/ppermute | solution.py:400
  89.2 4.3 %collective-permute-start.6 = (f32[2,1024]{1,0:T(2,128)S(1)}, f32[2,1024]{1,0:T(2,128)S(1)}, u32[]{:S(2)}, u32[]{:S(2)}) collective-permute-start(f32[2,1024]{1,0:T(2,128)S(1)} %add.64.near_ref), channel_id=1, source_target_pairs={{0,6},{2,4},{4,2},{6,0},{1,7},{3,5},{5,3},{7,1},{8,14},{10,12},{12... | collective-permute-start | bytes 24584 | tf_op jit(solution)/shard_map/ppermute | solution.py:400
  95.6 3.0 %collective-permute-start.7 = (f32[2,1024]{1,0:T(2,128)S(1)}, f32[2,1024]{1,0:T(2,128)S(1)}, u32[]{:S(2)}, u32[]{:S(2)}) collective-permute-start(f32[2,1024]{1,0:T(2,128)S(1)} %get-tuple-element.70), channel_id=1, source_target_pairs={{0,2},{2,0},{4,6},{6,4},{1,3},{3,1},{5,7},{7,5},{8,10},{10,8},{12,... | collective-permute-start | bytes 24584 | tf_op jit(solution)/shard_map/ppermute | solution.py:400
  98.6 5.0 %collective-permute-start.8 = (f32[2,1024]{1,0:T(2,128)S(1)}, f32[2,1024]{1,0:T(2,128)S(1)}, u32[]{:S(2)}, u32[]{:S(2)}) collective-permute-start(f32[2,1024]{1,0:T(2,128)S(1)} %add.65.near_ref), channel_id=1, source_target_pairs={{0,6},{2,4},{4,2},{6,0},{1,7},{3,5},{5,3},{7,1},{8,14},{10,12},{12... | collective-permute-start | bytes 24584 | tf_op jit(solution)/shard_map/ppermute | solution.py:400
  105.6 3.0 %collective-permute-start.9 = (f32[2,1024]{1,0:T(2,128)S(1)}, f32[2,1024]{1,0:T(2,128)S(1)}, u32[]{:S(2)}, u32[]{:S(2)}) collective-permute-start(f32[2,1024]{1,0:T(2,128)S(1)} %get-tuple-element.79), channel_id=1, source_target_pairs={{0,2},{2,0},{4,6},{6,4},{1,3},{3,1},{5,7},{7,5},{8,10},{10,8},{12,... | collective-permute-start | bytes 24584 | tf_op jit(solution)/shard_map/ppermute | solution.py:400
  108.6 4.1 %collective-permute-start.10 = (f32[2,1024]{1,0:T(2,128)S(1)}, f32[2,1024]{1,0:T(2,128)S(1)}, u32[]{:S(2)}, u32[]{:S(2)}) collective-permute-start(f32[2,1024]{1,0:T(2,128)S(1)} %add.66.near_ref), channel_id=1, source_target_pairs={{0,6},{2,4},{4,2},{6,0},{1,7},{3,5},{5,3},{7,1},{8,14},{10,12},{12... | collective-permute-start | bytes 24584 | tf_op jit(solution)/shard_map/ppermute | solution.py:400
  112.7 19.7 %collective-permute-start.14 = (bf16[2,512,256]{2,1,0:T(8,128)(2,1)}, bf16[2,512,256]{2,1,0:T(8,128)(2,1)S(1)}, u32[]{:S(2)}, u32[]{:S(2)}) collective-permute-start(bf16[2,512,256]{2,1,0:T(8,128)(2,1)} %correlate.6), channel_id=1, source_target_pairs={{0,4},{2,6},{4,0},{6,2},{1,5},{3,7},{5,1},{7,3},{8,12},{10,14},{12... | collective-permute-start | bytes 1572872 | tf_op jit(solution)/shard_map/ppermute | solution.py:400
  113.2 3.9 %collective-permute-start.11 = (f32[2,1024]{1,0:T(2,128)S(1)}, f32[2,1024]{1,0:T(2,128)S(1)}, u32[]{:S(2)}, u32[]{:S(2)}) collective-permute-start(f32[2,1024]{1,0:T(2,128)S(1)} %finish.1.refs_0_), channel_id=1, source_target_pairs={{0,1},{1,0},{8,9},{9,8},{16,17},{17,16},{24,25},{25,24},{32,33},{3... | collective-permute-start | bytes 24584 | tf_op jit(solution)/shard_map/ppermute | solution.py:400
  114.5 4.4 %collective-permute-start.12 = (f32[2,1024]{1,0:T(2,128)S(1)}, f32[2,1024]{1,0:T(2,128)S(1)}, u32[]{:S(2)}, u32[]{:S(2)}) collective-permute-start(f32[2,1024]{1,0:T(2,128)S(1)} %finish.1.refs_0_), channel_id=1, source_target_pairs={{0,128},{1,129},{8,136},{9,137},{16,144},{17,145},{24,152},{25,153... | collective-permute-start | bytes 24584 | tf_op jit(solution)/shard_map/ppermute | solution.py:400
  117.0 4.2 %collective-permute-start.13 = (f32[2,1024]{1,0:T(2,128)S(1)}, f32[2,1024]{1,0:T(2,128)S(1)}, u32[]{:S(2)}, u32[]{:S(2)}) collective-permute-start(f32[2,1024]{1,0:T(2,128)S(1)} %finish.1.refs_0_), channel_id=1, source_target_pairs={{0,129},{1,128},{8,137},{9,136},{16,145},{17,144},{24,153},{25,152... | collective-permute-start | bytes 24584 | tf_op jit(solution)/shard_map/ppermute | solution.py:400
  124.3 12.3 %all-to-all-start.2 = ((f32[8,2,1024]{2,1,0:T(2,128)}), f32[8,2,1024]{2,1,0:T(2,128)S(1)}, u32[]{:S(2)}, u32[]{:S(2)}) async-start(f32[8,2,1024]{2,1,0:T(2,128)} %get-tuple-element.93), calls=%async_computation.2 | async-start | bytes 131072 | tf_op jit(solution)/shard_map/all_to_all | solution.py:505
  129.4 11.5 %collective-permute-start.15 = (bf16[2,512,256]{2,1,0:T(8,128)(2,1)S(1)}, bf16[2,512,256]{2,1,0:T(8,128)(2,1)S(1)}, u32[]{:S(2)}, u32[]{:S(2)}) collective-permute-start(bf16[2,512,256]{2,1,0:T(8,128)(2,1)S(1)} %correlate.4), channel_id=1, source_target_pairs={{0,2},{2,0},{4,6},{6,4},{1,3},{3,1},{5,7},{7,5},{8,10},{10,8},{12,... | collective-permute-start | bytes 1572872 | tf_op jit(solution)/shard_map/ppermute | solution.py:400
  130.7 10.2 %collective-permute-start.16 = (bf16[2,512,256]{2,1,0:T(8,128)(2,1)S(1)}, bf16[2,512,256]{2,1,0:T(8,128)(2,1)S(1)}, u32[]{:S(2)}, u32[]{:S(2)}) collective-permute-start(bf16[2,512,256]{2,1,0:T(8,128)(2,1)S(1)} %correlate.7), channel_id=1, source_target_pairs={{0,6},{2,4},{4,2},{6,0},{1,7},{3,5},{5,3},{7,1},{8,14},{10,12},{12... | collective-permute-start | bytes 1572872 | tf_op jit(solution)/shard_map/ppermute | solution.py:400
  139.3 17.0 %collective-permute-start.18 = (bf16[2,2,128,512]{3,2,1,0:T(8,128)(2,1)S(1)}, bf16[2,2,128,512]{3,2,1,0:T(8,128)(2,1)S(1)}, u32[]{:S(2)}, u32[]{:S(2)}) collective-permute-start(bf16[2,2,128,512]{3,2,1,0:T(8,128)(2,1)S(1)} %beamform.3), channel_id=1, source_target_pairs={{0,1},{1,0},{2,3},{3,2},{4,5},{5,4},{6,7},{7,6},{8,9},{9,8},{10,11... | collective-permute-start | bytes 1572872 | tf_op jit(solution)/shard_map/ppermute | solution.py:400
  142.2 20.0 %collective-permute-start.17 = (bf16[2,512,256]{2,1,0:T(8,128)(2,1)S(1)}, bf16[2,512,256]{2,1,0:T(8,128)(2,1)S(1)}, u32[]{:S(2)}, u32[]{:S(2)}) collective-permute-start(bf16[2,512,256]{2,1,0:T(8,128)(2,1)S(1)} %gather.8), channel_id=1, source_target_pairs={{0,0},{1,8},{8,1},{9,9},{16,16},{17,24},{24,17},{25,25},{32,32},{3... | collective-permute-start | bytes 1572872 | tf_op jit(solution)/shard_map/ppermute | solution.py:409

commit v12 on v9

--- a/solution.py
+++ b/solution.py
@@ -341,7 +341,6 @@
         out_shape=out_shape,
         scratch_shapes=scratch,
         compiler_params=params(16),
-        cost_estimate=LONG,
         name="beamform",
     )(source, me, line, cosine, sine, y)
 
@@ -482,9 +481,7 @@
     half_ring = slots // 2 * n_group
     vectors = [z] + [swap(z, WIDE, high * half_ring + low) for high, low in reach[1:]]
     copies, solved = choose(source, me, vectors, reach, depth)
-    copies, beam_y, *bulk = lax.optimization_barrier(
-        (copies, beam_y, pieces[1], pieces[3])
-    )
+    copies, *bulk = lax.optimization_barrier((copies, pieces[1], pieces[3]))
     pieces[1], pieces[3] = swap(bulk[0], "tm", 1), swap(bulk[1], "tm", 3)
     pieces = [pieces[m] for m in range(n_time)]
     copies, beam_y = lax.optimization_barrier((copies, beam_y))
@@ -499,9 +496,8 @@
 
     away = beamform(1, source, me, line, cosine, sine, beam_y, n_group)
     other = swap(away, "grp", 1)
+    visibilities = widen(cross(gather(pieces)))
     own = beamform(0, source, me, line, cosine, sine, beam_y, n_group)
-    own, *pieces = lax.optimization_barrier((own, *pieces))
-    visibilities = widen(cross(gather(pieces)))
     beams = place(me, own, other)
     return visibilities[None], solved[None], beams[None]
 

time: 170 us -> 168 us (0.988)
  starting transfers between devices: 56.1 us -> 53.9 us
    all_to_all x1, waiting for transfers between devices: 3.62 us -> 0.01 us  [body(): lax.all_to_all(copies, 'freq', split_axis=0, concat_axis=0, axis_index_gr...]
    ppermute x17, starting transfers between devices: 20.4 us -> 17.6 us  [swap(): return lax.ppermute(x, axis, [(i, i ^ mask) for i in range(n)])]
    ppermute x17, waiting for transfers between devices: 23.8 us -> 26.4 us  [swap(): return lax.ppermute(x, axis, [(i, i ^ mask) for i in range(n)])]
where the time goes in v12:
time: 168 us; the launch traced here: 167 us
  waiting for transfers between devices  72 us (43%)
  starting transfers between devices  53.9 us (32%)
  Pallas kernels  34.9 us (21%)
  other arithmetic  2.26 us (1%)
  local copies, waits for them, and re-layouts  2.12 us (1%)
  between operations  1.76 us (1%)
    all_to_all x1, waiting for transfers between devices, body(): lax.all_to_all(corr_send, WIDE, split_axis=0, concat_axis=0, tiled=True)  38.3 us
    ppermute x17, waiting for transfers between devices, swap(): return lax.ppermute(x, axis, [(i, i ^ mask) for i in range(n)])  26.4 us
    ppermute x17, starting transfers between devices, swap(): return lax.ppermute(x, axis, [(i, i ^ mask) for i in range(n)])  17.6 us
    all_to_all x1, starting transfers between devices, body(): lax.all_to_all(corr_send, WIDE, split_axis=0, concat_axis=0, tiled=True)  13.3 us
    pallas_call x4, Pallas kernels, correlate(): pl.pallas_call(functools.partial(correlate_kernel, scale, mask), in_specs...  10.5 us
    ppermute x2, starting transfers between devices, cross(): return lax.ppermute(x, WIDE, pairs)  9.89 us
    all_to_all x1, starting transfers between devices, body(): lax.all_to_all(beam_send, WIDE, split_axis=0, concat_axis=0, tiled=True)  7.35 us
    ppermute x2, waiting for transfers between devices, cross(): return lax.ppermute(x, WIDE, pairs)  6.56 us
  transfers between devices with their start and end apart: 22, of which 14 were waited for; matrix products, arithmetic and copies ran while one was open for 3% of the time, Pallas kernels for 18%

profile of v12, /device:TPU:1, one launch (start us, length us, event | category | flops | bytes accessed | tf_op | source)
XLA Modules:
  0.0 166.9 jit_solution(1923176637597989080)
XLA Ops:
  0.6 3.1 %ingest.3 = bf16[32,2,2,16,512]{4,3,2,1,0:T(8,128)(2,1)} custom-call(s32[1]{0:T(128)} %bitcast.base_ref, s32[32]{0:T(128)} %chan_hbm.3, s32[512]{0:T(512)} %map_hbm.3, s32[512]{0:T(512)} %flag_hbm.3, bf16[32,2,16,1024]{3,2,1,0:T(8,128)(2,1)} %volts_hbm.3), custom_call_target="tpu_custom_call" | custom-call | tf_op jit(solution)/shard_map/ingest/pallas_call | solution.py:94
  3.8 13.3 %all-to-all-start = ((bf16[64,2,16,512]{3,2,1,0:T(8,128)(2,1)}), bf16[64,2,16,512]{3,2,1,0:T(8,128)(2,1)S(1)}, u32[]{:S(2)}, u32[]{:S(2)}) async-start(bf16[64,2,16,512]{3,2,1,0:T(8,128)(2,1)} %bitcast.15), calls=%async_computation | async-start | bytes 4194304 | tf_op jit(solution)/shard_map/all_to_all | solution.py:429
  17.1 3.5 %collective-permute-start = (f32[2,1024]{1,0:T(2,128)S(1)}, f32[2,1024]{1,0:T(2,128)S(1)}, u32[]{:S(2)}, u32[]{:S(2)}) collective-permute-start(f32[2,1024]{1,0:T(2,128)S(1)} %bitcast.21), channel_id=1, source_target_pairs={{0,0},{1,8},{8,1},{9,9},{16,16},{17,24},{24,17},{25,25},{32,32},{3... | collective-permute-start | bytes 24584 | tf_op jit(solution)/shard_map/ppermute | solution.py:399
  23.7 2.0 %fusion = (f32[256,512]{1,0:T(8,128)S(1)}, f32[256,512]{1,0:T(8,128)S(1)}) fusion(f32[512]{0:T(512)S(1)} %get-tuple-element.94, f32[256]{0:T(256)S(1)} %bitcast.20, f32[512]{0:T(512)S(1)} %get-tuple-element.93, f32[256]{0:T(256)S(1)} %bitcast.19, f32[]{:T(128)} %bitcast.4), kind=kLoop, calls=%fused_computation.2 | loop fusion | flops 524288 | bytes 1054724 | tf_op jit(solution)/shard_map/sin | solution.py:442
  25.7 3.0 %ingest.2 = bf16[32,2,2,16,512]{4,3,2,1,0:T(8,128)(2,1)} custom-call(s32[1]{0:T(128)} %bitcast.base_ref, s32[32]{0:T(128)} %chan_hbm.2, s32[512]{0:T(512)} %map_hbm.3, s32[512]{0:T(512)} %flag_hbm.3, bf16[32,2,16,1024]{3,2,1,0:T(8,128)(2,1)} %volts_hbm.3), custom_call_target="tpu_custom_call" | custom-call | tf_op jit(solution)/shard_map/ingest/pallas_call | solution.py:94
  28.7 38.3 %all-to-all-done.y_ref.mine_ref.refs_0_ = bf16[64,2,16,512]{3,2,1,0:T(8,128)(2,1)S(1)} async-done(((bf16[64,2,16,512]{3,2,1,0:T(8,128)(2,1)}), bf16[64,2,16,512]{3,2,1,0:T(8,128)(2,1)S(1)}, u32[]{:S(2)}, u32[]{:S(2)}) %all-to-all-start) | async-done | bytes 2097184 | tf_op jit(solution)/shard_map/all_to_all | solution.py:429
  67.1 7.3 %all-to-all-start.1 = ((bf16[64,2,16,512]{3,2,1,0:T(8,128)(2,1)}), bf16[64,2,16,512]{3,2,1,0:T(8,128)(2,1)}, u32[]{:S(2)}, u32[]{:S(2)}) async-start(bf16[64,2,16,512]{3,2,1,0:T(8,128)(2,1)} %bitcast.14), calls=%async_computation.1 | async-start | bytes 4194304 | tf_op jit(solution)/shard_map/all_to_all | solution.py:452
  78.4 1.7 %collective-permute-done.3 = f32[2,1024]{1,0:T(2,128)S(1)} collective-permute-done((f32[2,1024]{1,0:T(2,128)S(1)}, f32[2,1024]{1,0:T(2,128)S(1)}, u32[]{:S(2)}, u32[]{:S(2)}) %collective-permute-start.3) | collective-permute-done | bytes 8224 | tf_op jit(solution)/shard_map/ppermute | solution.py:390
  80.1 2.5 %collective-permute-start.4 = (f32[2,1024]{1,0:T(2,128)S(1)}, f32[2,1024]{1,0:T(2,128)S(1)}, u32[]{:S(2)}, u32[]{:S(2)}) collective-permute-start(f32[2,1024]{1,0:T(2,128)S(1)} %add.63.near_ref), channel_id=1, source_target_pairs={{0,6},{2,4},{4,2},{6,0},{1,7},{3,5},{5,3},{7,1},{8,14},{10,12},{12... | collective-permute-start | bytes 24584 | tf_op jit(solution)/shard_map/ppermute | solution.py:390
  82.6 1.6 collective-permute-done.4.far_ref
  84.2 2.0 %apply.3 = (f32[2,1024]{1,0:T(2,128)S(1)}, f32[2,1024]{1,0:T(2,128)S(1)}) custom-call(bf16[64,2,16,512]{3,2,1,0:T(8,128)(2,1)S(1)} %all-to-all-done.y_ref.mine_ref.refs_0_, bf16[64,2,16,512]{3,2,1,0:T(8,128)(2,1)S(1)} %collective-permute-done.2.other_ref.refs_1_, f32[2,1024]{1,0:T(2,128)S(1)} %collective-permute-done.z_ref, f32[2,1024]{1,0:T(2,128)S(1)} %add.63.near_ref, ...), custom_call_target="tpu_custom_call" | custom-call | tf_op jit(solution)/shard_map/apply/pallas_call | solution.py:223
  86.3 2.9 %collective-permute-done.5 = f32[2,1024]{1,0:T(2,128)S(1)} collective-permute-done((f32[2,1024]{1,0:T(2,128)S(1)}, f32[2,1024]{1,0:T(2,128)S(1)}, u32[]{:S(2)}, u32[]{:S(2)}) %collective-permute-start.5) | collective-permute-done | bytes 8224 | tf_op jit(solution)/shard_map/ppermute | solution.py:390
  89.2 2.5 %collective-permute-start.6 = (f32[2,1024]{1,0:T(2,128)S(1)}, f32[2,1024]{1,0:T(2,128)S(1)}, u32[]{:S(2)}, u32[]{:S(2)}) collective-permute-start(f32[2,1024]{1,0:T(2,128)S(1)} %add.64.near_ref), channel_id=1, source_target_pairs={{0,6},{2,4},{4,2},{6,0},{1,7},{3,5},{5,3},{7,1},{8,14},{10,12},{12... | collective-permute-start | bytes 24584 | tf_op jit(solution)/shard_map/ppermute | solution.py:390
  91.7 2.6 %correlate.4 = bf16[2,512,256]{2,1,0:T(8,128)(2,1)} custom-call(s32[3]{0:T(128)S(1)} %pad_add_fusion.me_ref, bf16[64,2,16,512]{3,2,1,0:T(8,128)(2,1)S(1)} %all-to-all-done.y_ref.mine_ref.refs_0_, bf16[64,2,16,512]{3,2,1,0:T(8,128)(2,1)S(1)} %collective-permute-done.2.other_ref.refs_1_), custom_call_target="tpu_custom_call" | custom-call | tf_op jit(solution)/shard_map/correlate/pallas_call | solution.py:154
  94.3 2.0 %apply.4 = (f32[2,1024]{1,0:T(2,128)S(1)}, f32[2,1024]{1,0:T(2,128)S(1)}) custom-call(bf16[64,2,16,512]{3,2,1,0:T(8,128)(2,1)S(1)} %all-to-all-done.y_ref.mine_ref.refs_0_, bf16[64,2,16,512]{3,2,1,0:T(8,128)(2,1)S(1)} %collective-permute-done.2.other_ref.refs_1_, f32[2,1024]{1,0:T(2,128)S(1)} %get-tuple-element.52.z_ref, f32[2,1024]{1,0:T(2,128)S(1)} %add.64.near_ref, ...), custom_call_target="tpu_custom_call" | custom-call | tf_op jit(solution)/shard_map/apply/pallas_call | solution.py:223
  96.6 2.6 %correlate.5.refs_0_ = bf16[2,512,256]{2,1,0:T(8,128)(2,1)} custom-call(s32[3]{0:T(128)S(1)} %pad_add_fusion.me_ref, bf16[64,2,16,512]{3,2,1,0:T(8,128)(2,1)S(1)} %all-to-all-done.y_ref.mine_ref.refs_0_, bf16[64,2,16,512]{3,2,1,0:T(8,128)(2,1)S(1)} %collective-permute-done.2.other_ref.refs_1_), custom_call_target="tpu_custom_call" | custom-call | tf_op jit(solution)/shard_map/correlate/pallas_call | solution.py:154
  99.5 1.5 collective-permute-start.8
  101.0 2.6 %correlate.6 = bf16[2,512,256]{2,1,0:T(8,128)(2,1)} custom-call(s32[3]{0:T(128)S(1)} %pad_add_fusion.me_ref, bf16[64,2,16,512]{3,2,1,0:T(8,128)(2,1)S(1)} %all-to-all-done.y_ref.mine_ref.refs_0_, bf16[64,2,16,512]{3,2,1,0:T(8,128)(2,1)S(1)} %collective-permute-done.2.other_ref.refs_1_), custom_call_target="tpu_custom_call" | custom-call | tf_op jit(solution)/shard_map/correlate/pallas_call | solution.py:154
  103.7 2.0 %apply.5 = (f32[2,1024]{1,0:T(2,128)S(1)}, f32[2,1024]{1,0:T(2,128)S(1)}) custom-call(bf16[64,2,16,512]{3,2,1,0:T(8,128)(2,1)S(1)} %all-to-all-done.y_ref.mine_ref.refs_0_, bf16[64,2,16,512]{3,2,1,0:T(8,128)(2,1)S(1)} %collective-permute-done.2.other_ref.refs_1_, f32[2,1024]{1,0:T(2,128)S(1)} %get-tuple-element.64.z_ref, f32[2,1024]{1,0:T(2,128)S(1)} %add.65.near_ref, ...), custom_call_target="tpu_custom_call" | custom-call | tf_op jit(solution)/shard_map/apply/pallas_call | solution.py:223
  106.4 2.2 %collective-permute-done.9 = f32[2,1024]{1,0:T(2,128)S(1)} collective-permute-done((f32[2,1024]{1,0:T(2,128)S(1)}, f32[2,1024]{1,0:T(2,128)S(1)}, u32[]{:S(2)}, u32[]{:S(2)}) %collective-permute-start.9) | collective-permute-done | bytes 8224 | tf_op jit(solution)/shard_map/ppermute | solution.py:390
  110.1 2.6 %correlate.7 = bf16[2,512,256]{2,1,0:T(8,128)(2,1)} custom-call(s32[3]{0:T(128)S(1)} %pad_add_fusion.me_ref, bf16[64,2,16,512]{3,2,1,0:T(8,128)(2,1)S(1)} %all-to-all-done.y_ref.mine_ref.refs_0_, bf16[64,2,16,512]{3,2,1,0:T(8,128)(2,1)S(1)} %collective-permute-done.2.other_ref.refs_1_), custom_call_target="tpu_custom_call" | custom-call | tf_op jit(solution)/shard_map/correlate/pallas_call | solution.py:154
  114.2 2.5 %collective-permute-start.12 = (f32[2,1024]{1,0:T(2,128)S(1)}, f32[2,1024]{1,0:T(2,128)S(1)}, u32[]{:S(2)}, u32[]{:S(2)}) collective-permute-start(f32[2,1024]{1,0:T(2,128)S(1)} %finish.1.refs_0_), channel_id=1, source_target_pairs={{0,128},{1,129},{8,136},{9,137},{16,144},{17,145},{24,152},{25,153... | collective-permute-start | bytes 24584 | tf_op jit(solution)/shard_map/ppermute | solution.py:390
  118.7 2.3 %collective-permute-done.13.refs_3_ = f32[2,1024]{1,0:T(2,128)S(1)} collective-permute-done((f32[2,1024]{1,0:T(2,128)S(1)}, f32[2,1024]{1,0:T(2,128)S(1)}, u32[]{:S(2)}, u32[]{:S(2)}) %collective-permute-start.13) | collective-permute-done | bytes 8224 | tf_op jit(solution)/shard_map/ppermute | solution.py:390
  124.3 5.8 %all-to-all-start.2 = ((f32[8,2,1024]{2,1,0:T(2,128)}), f32[8,2,1024]{2,1,0:T(2,128)S(1)}, u32[]{:S(2)}, u32[]{:S(2)}) async-start(f32[8,2,1024]{2,1,0:T(2,128)} %get-tuple-element.89), calls=%async_computation.2 | async-start | bytes 131072 | tf_op jit(solution)/shard_map/all_to_all | solution.py:493
  130.1 5.2 %collective-permute-done.14.refs_1_ = bf16[2,512,256]{2,1,0:T(8,128)(2,1)S(1)} collective-permute-done((bf16[2,512,256]{2,1,0:T(8,128)(2,1)}, bf16[2,512,256]{2,1,0:T(8,128)(2,1)S(1)}, u32[]{:S(2)}, u32[]{:S(2)}) %collective-permute-start.14) | collective-permute-done | bytes 524320 | tf_op jit(solution)/shard_map/ppermute | solution.py:390
  135.3 4.3 %collective-permute-done.16.refs_3_ = bf16[2,512,256]{2,1,0:T(8,128)(2,1)S(1)} collective-permute-done((bf16[2,512,256]{2,1,0:T(8,128)(2,1)}, bf16[2,512,256]{2,1,0:T(8,128)(2,1)S(1)}, u32[]{:S(2)}, u32[]{:S(2)}) %collective-permute-start.16) | collective-permute-done | bytes 524320 | tf_op jit(solution)/shard_map/ppermute | solution.py:390
  139.6 1.9 %gather.8 = bf16[2,512,256]{2,1,0:T(8,128)(2,1)} custom-call(bf16[2,512,256]{2,1,0:T(8,128)(2,1)} %correlate.5.refs_0_, bf16[2,512,256]{2,1,0:T(8,128)(2,1)S(1)} %collective-permute-done.14.refs_1_, bf16[2,512,256]{2,1,0:T(8,128)(2,1)S(1)} %collective-permute-done.15.refs_2_, bf16[2,512,256]{2,1,0:T(8,128)(2,1)S(1)} %collective-permute-done.16.refs_3_), custom_call_target="tpu_custom_call" | custom-call | tf_op jit(solution)/shard_map/gather/pallas_call | solution.py:175
  141.5 6.3 %collective-permute-start.17 = (bf16[2,512,256]{2,1,0:T(8,128)(2,1)}, bf16[2,512,256]{2,1,0:T(8,128)(2,1)S(1)}, u32[]{:S(2)}, u32[]{:S(2)}) collective-permute-start(bf16[2,512,256]{2,1,0:T(8,128)(2,1)} %gather.8), channel_id=1, source_target_pairs={{0,0},{1,8},{8,1},{9,9},{16,16},{17,24},{24,17},{25,25},{32,32},{3... | collective-permute-start | bytes 1572872 | tf_op jit(solution)/shard_map/ppermute | solution.py:399
  147.9 2.4 %beamform.3 = bf16[2,2,128,512]{3,2,1,0:T(8,128)(2,1)S(1)} custom-call(s32[32]{0:T(128)S(1)} %select_reduce_fusion.source_ref, s32[3]{0:T(128)S(1)} %pad_add_fusion.me_ref, f32[8,2,1024]{2,1,0:T(2,128)S(1)} %all-to-all-done.2.line_ref, f32[256,512]{1,0:T(8,128)S(1)} %get-tuple-element.90.cos_ref, f32[256,512]{1,0:T(8,128)S(1)} %get-tuple-element.91.sin_ref, ...), custom_call_target="tpu_custom_call" | custom-call | tf_op jit(solution)/shard_map/beamform/pallas_call | solution.py:337
  150.4 6.6 %collective-permute-done.17.in_ref = bf16[2,512,256]{2,1,0:T(8,128)(2,1)S(1)} collective-permute-done((bf16[2,512,256]{2,1,0:T(8,128)(2,1)}, bf16[2,512,256]{2,1,0:T(8,128)(2,1)S(1)}, u32[]{:S(2)}, u32[]{:S(2)}) %collective-permute-start.17) | collective-permute-done | bytes 524320 | tf_op jit(solution)/shard_map/ppermute | solution.py:399
  158.0 3.1 %beamform.2.own_hbm = bf16[2,2,128,1024]{3,2,1,0:T(8,128)(2,1)} custom-call(s32[32]{0:T(128)S(1)} %select_reduce_fusion.source_ref, s32[3]{0:T(128)S(1)} %pad_add_fusion.me_ref, f32[8,2,1024]{2,1,0:T(2,128)S(1)} %all-to-all-done.2.line_ref, f32[256,512]{1,0:T(8,128)S(1)} %get-tuple-element.90.cos_ref, f32[256,512]{1,0:T(8,128)S(1)} %get-tuple-element.91.sin_ref, ...), custom_call_target="tpu_custom_call" | custom-call | tf_op jit(solution)/shard_map/beamform/pallas_call | solution.py:337
  161.2 4.2 %collective-permute-done.18.other_ref = bf16[2,2,128,512]{3,2,1,0:T(8,128)(2,1)S(1)} collective-permute-done((bf16[2,2,128,512]{3,2,1,0:T(8,128)(2,1)S(1)}, bf16[2,2,128,512]{3,2,1,0:T(8,128)(2,1)S(1)}, u32[]{:S(2)}, u32[]{:S(2)}) %collective-permute-start.18) | collective-permute-done | bytes 524320 | tf_op jit(solution)/shard_map/ppermute | solution.py:390
  (55 shorter events, 18.5 us)
Async XLA Ops:
  3.7 13.4 %copy-start.5 = (f32[1,2,1024]{2,1,0:T(2,128)S(1)}, f32[1,2,1024]{2,1,0:T(2,128)}, u32[]{:S(2)}) copy-start(f32[1,2,1024]{2,1,0:T(2,128)} %param.9) | copy-start | bytes 24580
  3.7 16.9 %copy-start.4 = (s32[32]{0:T(128)S(1)}, s32[32]{0:T(128)}, u32[]{:S(2)}) copy-start(s32[32]{0:T(128)} %chan_hbm.2) | copy-start | bytes 388
  3.7 18.2 %copy-start.1 = (f32[2,512]{1,0:T(2,128)S(1)}, f32[2,512]{1,0:T(2,128)}, u32[]{:S(2)}) copy-start(f32[2,512]{1,0:T(2,128)} %param.12) | copy-start | bytes 12292
  3.7 18.3 %copy-start = (s32[512]{0:T(512)S(1)}, s32[512]{0:T(512)}, u32[]{:S(2)}) copy-start(s32[512]{0:T(512)} %map_hbm.3) | copy-start | bytes 6148
  3.8 19.4 %copy-start.3 = (s32[32]{0:T(128)S(1)}, s32[32]{0:T(128)}, u32[]{:S(2)}) copy-start(s32[32]{0:T(128)} %chan_hbm.3) | copy-start | bytes 388
  3.8 19.9 %copy-start.2 = (s32[2,256]{1,0:T(2,128)S(1)}, s32[2,256]{1,0:T(2,128)}, u32[]{:S(2)}) copy-start(s32[2,256]{1,0:T(2,128)} %param.13) | copy-start | bytes 6148
  3.8 63.3 %all-to-all-start = ((bf16[64,2,16,512]{3,2,1,0:T(8,128)(2,1)}), bf16[64,2,16,512]{3,2,1,0:T(8,128)(2,1)S(1)}, u32[]{:S(2)}, u32[]{:S(2)}) async-start(bf16[64,2,16,512]{3,2,1,0:T(8,128)(2,1)} %bitcast.15), calls=%async_computation | async-start | bytes 4194304 | tf_op jit(solution)/shard_map/all_to_all | solution.py:429
  17.1 11.6 %collective-permute-start = (f32[2,1024]{1,0:T(2,128)S(1)}, f32[2,1024]{1,0:T(2,128)S(1)}, u32[]{:S(2)}, u32[]{:S(2)}) collective-permute-start(f32[2,1024]{1,0:T(2,128)S(1)} %bitcast.21), channel_id=1, source_target_pairs={{0,0},{1,8},{8,1},{9,9},{16,16},{17,24},{24,17},{25,25},{32,32},{3... | collective-permute-start | bytes 24584 | tf_op jit(solution)/shard_map/ppermute | solution.py:399
  67.1 57.2 %all-to-all-start.1 = ((bf16[64,2,16,512]{3,2,1,0:T(8,128)(2,1)}), bf16[64,2,16,512]{3,2,1,0:T(8,128)(2,1)}, u32[]{:S(2)}, u32[]{:S(2)}) async-start(bf16[64,2,16,512]{3,2,1,0:T(8,128)(2,1)} %bitcast.14), calls=%async_computation.1 | async-start | bytes 4194304 | tf_op jit(solution)/shard_map/all_to_all | solution.py:452
  75.4 1.4 collective-permute-start.1
  76.9 7.4 %collective-permute-start.2 = (bf16[64,2,16,512]{3,2,1,0:T(8,128)(2,1)S(1)}, bf16[64,2,16,512]{3,2,1,0:T(8,128)(2,1)S(1)}, u32[]{:S(2)}, u32[]{:S(2)}) collective-permute-start(bf16[64,2,16,512]{3,2,1,0:T(8,128)(2,1)S(1)} %all-to-all-done.y_ref.mine_ref.refs_0_), channel_id=1, source_target_pairs={{0,8},{8,0},{16,24},{24,16},{32,40},{40,32},{48,56},{56,48},{64,72... | collective-permute-start | bytes 6291464 | tf_op jit(solution)/shard_map/ppermute | solution.py:390
  77.2 2.9 %collective-permute-start.3 = (f32[2,1024]{1,0:T(2,128)S(1)}, f32[2,1024]{1,0:T(2,128)S(1)}, u32[]{:S(2)}, u32[]{:S(2)}) collective-permute-start(f32[2,1024]{1,0:T(2,128)S(1)} %add.62), channel_id=1, source_target_pairs={{0,2},{2,0},{4,6},{6,4},{1,3},{3,1},{5,7},{7,5},{8,10},{10,8},{12,... | collective-permute-start | bytes 24584 | tf_op jit(solution)/shard_map/ppermute | solution.py:390
  80.1 4.1 %collective-permute-start.4 = (f32[2,1024]{1,0:T(2,128)S(1)}, f32[2,1024]{1,0:T(2,128)S(1)}, u32[]{:S(2)}, u32[]{:S(2)}) collective-permute-start(f32[2,1024]{1,0:T(2,128)S(1)} %add.63.near_ref), channel_id=1, source_target_pairs={{0,6},{2,4},{4,2},{6,0},{1,7},{3,5},{5,3},{7,1},{8,14},{10,12},{12... | collective-permute-start | bytes 24584 | tf_op jit(solution)/shard_map/ppermute | solution.py:390
  86.2 3.0 %collective-permute-start.5 = (f32[2,1024]{1,0:T(2,128)S(1)}, f32[2,1024]{1,0:T(2,128)S(1)}, u32[]{:S(2)}, u32[]{:S(2)}) collective-permute-start(f32[2,1024]{1,0:T(2,128)S(1)} %get-tuple-element.53), channel_id=1, source_target_pairs={{0,2},{2,0},{4,6},{6,4},{1,3},{3,1},{5,7},{7,5},{8,10},{10,8},{12,... | collective-permute-start | bytes 24584 | tf_op jit(solution)/shard_map/ppermute | solution.py:390
  89.2 5.1 %collective-permute-start.6 = (f32[2,1024]{1,0:T(2,128)S(1)}, f32[2,1024]{1,0:T(2,128)S(1)}, u32[]{:S(2)}, u32[]{:S(2)}) collective-permute-start(f32[2,1024]{1,0:T(2,128)S(1)} %add.64.near_ref), channel_id=1, source_target_pairs={{0,6},{2,4},{4,2},{6,0},{1,7},{3,5},{5,3},{7,1},{8,14},{10,12},{12... | collective-permute-start | bytes 24584 | tf_op jit(solution)/shard_map/ppermute | solution.py:390
  96.4 3.2 %collective-permute-start.7 = (f32[2,1024]{1,0:T(2,128)S(1)}, f32[2,1024]{1,0:T(2,128)S(1)}, u32[]{:S(2)}, u32[]{:S(2)}) collective-permute-start(f32[2,1024]{1,0:T(2,128)S(1)} %get-tuple-element.65), channel_id=1, source_target_pairs={{0,2},{2,0},{4,6},{6,4},{1,3},{3,1},{5,7},{7,5},{8,10},{10,8},{12,... | collective-permute-start | bytes 24584 | tf_op jit(solution)/shard_map/ppermute | solution.py:390
  99.5 4.1 %collective-permute-start.8 = (f32[2,1024]{1,0:T(2,128)S(1)}, f32[2,1024]{1,0:T(2,128)S(1)}, u32[]{:S(2)}, u32[]{:S(2)}) collective-permute-start(f32[2,1024]{1,0:T(2,128)S(1)} %add.65.near_ref), channel_id=1, source_target_pairs={{0,6},{2,4},{4,2},{6,0},{1,7},{3,5},{5,3},{7,1},{8,14},{10,12},{12... | collective-permute-start | bytes 24584 | tf_op jit(solution)/shard_map/ppermute | solution.py:390
  105.7 3.0 %collective-permute-start.9 = (f32[2,1024]{1,0:T(2,128)S(1)}, f32[2,1024]{1,0:T(2,128)S(1)}, u32[]{:S(2)}, u32[]{:S(2)}) collective-permute-start(f32[2,1024]{1,0:T(2,128)S(1)} %get-tuple-element.72), channel_id=1, source_target_pairs={{0,2},{2,0},{4,6},{6,4},{1,3},{3,1},{5,7},{7,5},{8,10},{10,8},{12,... | collective-permute-start | bytes 24584 | tf_op jit(solution)/shard_map/ppermute | solution.py:390
  108.7 4.1 %collective-permute-start.10 = (f32[2,1024]{1,0:T(2,128)S(1)}, f32[2,1024]{1,0:T(2,128)S(1)}, u32[]{:S(2)}, u32[]{:S(2)}) collective-permute-start(f32[2,1024]{1,0:T(2,128)S(1)} %add.66.near_ref), channel_id=1, source_target_pairs={{0,6},{2,4},{4,2},{6,0},{1,7},{3,5},{5,3},{7,1},{8,14},{10,12},{12... | collective-permute-start | bytes 24584 | tf_op jit(solution)/shard_map/ppermute | solution.py:390
  112.9 4.9 %collective-permute-start.11 = (f32[2,1024]{1,0:T(2,128)S(1)}, f32[2,1024]{1,0:T(2,128)S(1)}, u32[]{:S(2)}, u32[]{:S(2)}) collective-permute-start(f32[2,1024]{1,0:T(2,128)S(1)} %finish.1.refs_0_), channel_id=1, source_target_pairs={{0,1},{1,0},{8,9},{9,8},{16,17},{17,16},{24,25},{25,24},{32,33},{3... | collective-permute-start | bytes 24584 | tf_op jit(solution)/shard_map/ppermute | solution.py:390
  114.2 4.5 %collective-permute-start.12 = (f32[2,1024]{1,0:T(2,128)S(1)}, f32[2,1024]{1,0:T(2,128)S(1)}, u32[]{:S(2)}, u32[]{:S(2)}) collective-permute-start(f32[2,1024]{1,0:T(2,128)S(1)} %finish.1.refs_0_), channel_id=1, source_target_pairs={{0,128},{1,129},{8,136},{9,137},{16,144},{17,145},{24,152},{25,153... | collective-permute-start | bytes 24584 | tf_op jit(solution)/shard_map/ppermute | solution.py:390
  116.7 4.3 %collective-permute-start.13 = (f32[2,1024]{1,0:T(2,128)S(1)}, f32[2,1024]{1,0:T(2,128)S(1)}, u32[]{:S(2)}, u32[]{:S(2)}) collective-permute-start(f32[2,1024]{1,0:T(2,128)S(1)} %finish.1.refs_0_), channel_id=1, source_target_pairs={{0,129},{1,128},{8,137},{9,136},{16,145},{17,144},{24,153},{25,152... | collective-permute-start | bytes 24584 | tf_op jit(solution)/shard_map/ppermute | solution.py:390
  116.9 13.2 %collective-permute-start.15 = (bf16[2,512,256]{2,1,0:T(8,128)(2,1)}, bf16[2,512,256]{2,1,0:T(8,128)(2,1)S(1)}, u32[]{:S(2)}, u32[]{:S(2)}) collective-permute-start(bf16[2,512,256]{2,1,0:T(8,128)(2,1)} %correlate.6), channel_id=1, source_target_pairs={{0,4},{2,6},{4,0},{6,2},{1,5},{3,7},{5,1},{7,3},{8,12},{10,14},{12... | collective-permute-start | bytes 1572872 | tf_op jit(solution)/shard_map/ppermute | solution.py:390
  122.2 13.1 %collective-permute-start.14 = (bf16[2,512,256]{2,1,0:T(8,128)(2,1)}, bf16[2,512,256]{2,1,0:T(8,128)(2,1)S(1)}, u32[]{:S(2)}, u32[]{:S(2)}) collective-permute-start(bf16[2,512,256]{2,1,0:T(8,128)(2,1)} %correlate.4), channel_id=1, source_target_pairs={{0,2},{2,0},{4,6},{6,4},{1,3},{3,1},{5,7},{7,5},{8,10},{10,8},{12,... | collective-permute-start | bytes 1572872 | tf_op jit(solution)/shard_map/ppermute | solution.py:390
  122.2 17.4 %collective-permute-start.16 = (bf16[2,512,256]{2,1,0:T(8,128)(2,1)}, bf16[2,512,256]{2,1,0:T(8,128)(2,1)S(1)}, u32[]{:S(2)}, u32[]{:S(2)}) collective-permute-start(bf16[2,512,256]{2,1,0:T(8,128)(2,1)} %correlate.7), channel_id=1, source_target_pairs={{0,6},{2,4},{4,2},{6,0},{1,7},{3,5},{5,3},{7,1},{8,14},{10,12},{12... | collective-permute-start | bytes 1572872 | tf_op jit(solution)/shard_map/ppermute | solution.py:390
  124.3 23.6 %all-to-all-start.2 = ((f32[8,2,1024]{2,1,0:T(2,128)}), f32[8,2,1024]{2,1,0:T(2,128)S(1)}, u32[]{:S(2)}, u32[]{:S(2)}) async-start(f32[8,2,1024]{2,1,0:T(2,128)} %get-tuple-element.89), calls=%async_computation.2 | async-start | bytes 131072 | tf_op jit(solution)/shard_map/all_to_all | solution.py:493
  141.5 15.5 %collective-permute-start.17 = (bf16[2,512,256]{2,1,0:T(8,128)(2,1)}, bf16[2,512,256]{2,1,0:T(8,128)(2,1)S(1)}, u32[]{:S(2)}, u32[]{:S(2)}) collective-permute-start(bf16[2,512,256]{2,1,0:T(8,128)(2,1)} %gather.8), channel_id=1, source_target_pairs={{0,0},{1,8},{8,1},{9,9},{16,16},{17,24},{24,17},{25,25},{32,32},{3... | collective-permute-start | bytes 1572872 | tf_op jit(solution)/shard_map/ppermute | solution.py:399
  150.3 15.1 %collective-permute-start.18 = (bf16[2,2,128,512]{3,2,1,0:T(8,128)(2,1)S(1)}, bf16[2,2,128,512]{3,2,1,0:T(8,128)(2,1)S(1)}, u32[]{:S(2)}, u32[]{:S(2)}) collective-permute-start(bf16[2,2,128,512]{3,2,1,0:T(8,128)(2,1)S(1)} %beamform.3), channel_id=1, source_target_pairs={{0,1},{1,0},{2,3},{3,2},{4,5},{5,4},{6,7},{7,6},{8,9},{9,8},{10,11... | collective-permute-start | bytes 1572872 | tf_op jit(solution)/shard_map/ppermute | solution.py:390

commit v13 on v11

--- a/solution.py
+++ b/solution.py
@@ -155,9 +155,7 @@
         functools.partial(correlate_kernel, scale, mask),
         in_specs=[whole(SMEM)] + [whole(VMEM)] * len(ys),
         out_specs=whole(VMEM),
-        out_shape=(pltpu.VMEM if mask in (1,3,) else pltpu.HBM)(
-            (2, inputs // 2, inputs // n_time), BF16
-        ),
+        out_shape=pltpu.HBM((2, inputs // 2, inputs // n_time), BF16),
         compiler_params=params(16),
         name="correlate",
     )(me, *ys)
@@ -376,6 +374,25 @@
     )(me, own, other)
 
 
+def stage_kernel(in_ref, out_ref):
+    out_ref[...] = in_ref[...]
+
+
+def stage(y):
+    blocks = y.shape[0]
+    steps = 4
+    spec = pl.BlockSpec((blocks // steps,) + y.shape[1:], lambda i: (i, 0, 0, 0))
+    return pl.pallas_call(
+        stage_kernel,
+        grid=(steps,),
+        in_specs=[spec],
+        out_specs=spec,
+        out_shape=pltpu.VMEM(y.shape, BF16),
+        compiler_params=params(8),
+        name="stage",
+    )(y)
+
+
 def widen_kernel(in_ref, out_ref):
     out_ref[...] = in_ref[...].astype(F32)
 
@@ -506,7 +523,8 @@
         copies, "freq", split_axis=0, concat_axis=0, axis_index_groups=groups, tiled=True
     )
 
-    line, pieces[2] = lax.optimization_barrier((line, pieces[2]))
+    beam_y = stage(beam_y)
+    line, pieces[2], beam_y = lax.optimization_barrier((line, pieces[2], beam_y))
     away = beamform(1, source, me, line, cosine, sine, beam_y, n_group)
     other = swap(away, "grp", 1)
     late, *pieces = lax.optimization_barrier((line, *pieces))

time: 164 us -> 163 us (level)
  waiting for transfers between devices: 62.1 us -> 59.3 us
  Pallas kernels: 33.1 us -> 35.7 us
    pallas_call x0 -> x1, Pallas kernels: none -> 2.38 us  [stage(): pl.pallas_call(stage_kernel, grid=(steps,), in_specs=[spec], out_specs=sp...]
    all_to_all x1, waiting for transfers between devices: 4.2 us -> 1.94 us  [body(): lax.all_to_all(copies, 'freq', split_axis=0, concat_axis=0, axis_index_gr...]
    ppermute x17, waiting for transfers between devices: 14.4 us -> 16.2 us  [swap(): return lax.ppermute(x, axis, [(i, i ^ mask) for i in range(n)])]
    ppermute x2, waiting for transfers between devices: 4.52 us -> 2.81 us  [cross(): return lax.ppermute(x, WIDE, pairs)]
  transfers between devices with their start and end apart: 22 -> 22, of which waited for: 13 -> 14; matrix products, arithmetic and copies ran while one was open for 3% -> 3% of each run, Pallas kernels for 18% -> 19%
where the time goes in v13:
time: 163 us
  starting transfers between devices  60.4 us (37%)
  waiting for transfers between devices  59.3 us (36%)
  Pallas kernels  35.7 us (22%)
  other arithmetic  3.44 us (2%)
  local copies, waits for them, and re-layouts  2.12 us (1%)
    all_to_all x1, waiting for transfers between devices, body(): lax.all_to_all(corr_send, WIDE, split_axis=0, concat_axis=0, tiled=True)  37.1 us
    ppermute x17, starting transfers between devices, swap(): return lax.ppermute(x, axis, [(i, i ^ mask) for i in range(n)])  20.5 us
    ppermute x17, waiting for transfers between devices, swap(): return lax.ppermute(x, axis, [(i, i ^ mask) for i in range(n)])  16.2 us
    ppermute x2, starting transfers between devices, cross(): return lax.ppermute(x, WIDE, pairs)  13.9 us
    all_to_all x1, starting transfers between devices, body(): lax.all_to_all(corr_send, WIDE, split_axis=0, concat_axis=0, tiled=True)  13.3 us
    pallas_call x4, Pallas kernels, correlate(): pl.pallas_call(functools.partial(correlate_kernel, scale, mask), in_specs...  10.5 us
    all_to_all x1, starting transfers between devices, body(): lax.all_to_all(beam_send, WIDE, split_axis=0, concat_axis=0, tiled=True)  7.35 us
    pallas_call x2, Pallas kernels, ingest(): pl.pallas_call(functools.partial(ingest_kernel, stations, pick), in_specs...  6.09 us
  transfers between devices with their start and end apart: 22, of which 14 were waited for; matrix products, arithmetic and copies ran while one was open for 3% of the time, Pallas kernels for 19%

profile of v13, /device:TPU:1, one launch (start us, length us, event | category | flops | bytes accessed | tf_op | source)
XLA Modules:
  0.0 162.6 jit_solution(16408453899572252195)
XLA Ops:
  0.6 3.1 %ingest.3 = bf16[32,2,2,16,512]{4,3,2,1,0:T(8,128)(2,1)} custom-call(s32[1]{0:T(128)} %bitcast.base_ref, s32[32]{0:T(128)} %chan_hbm.3, s32[512]{0:T(512)} %map_hbm.3, s32[512]{0:T(512)} %flag_hbm.3, bf16[32,2,16,1024]{3,2,1,0:T(8,128)(2,1)} %volts_hbm.3), custom_call_target="tpu_custom_call" | custom-call | tf_op jit(solution)/shard_map/ingest/pallas_call | solution.py:94
  3.8 13.3 %all-to-all-start = ((bf16[64,2,16,512]{3,2,1,0:T(8,128)(2,1)}), bf16[64,2,16,512]{3,2,1,0:T(8,128)(2,1)S(1)}, u32[]{:S(2)}, u32[]{:S(2)}) async-start(bf16[64,2,16,512]{3,2,1,0:T(8,128)(2,1)} %bitcast.15), calls=%async_computation | async-start | bytes 4194304 | tf_op jit(solution)/shard_map/all_to_all | solution.py:456
  17.1 3.5 %collective-permute-start = (f32[2,1024]{1,0:T(2,128)S(1)}, f32[2,1024]{1,0:T(2,128)S(1)}, u32[]{:S(2)}, u32[]{:S(2)}) collective-permute-start(f32[2,1024]{1,0:T(2,128)S(1)} %bitcast.21), channel_id=1, source_target_pairs={{0,0},{1,8},{8,1},{9,9},{16,16},{17,24},{24,17},{25,25},{32,32},{3... | collective-permute-start | bytes 24584 | tf_op jit(solution)/shard_map/ppermute | solution.py:426
  23.7 3.1 %fusion = (f32[256,512]{1,0:T(8,128)}, f32[256,512]{1,0:T(8,128)}) fusion(f32[512]{0:T(512)S(1)} %get-tuple-element.112, f32[256]{0:T(256)S(1)} %bitcast.20, f32[512]{0:T(512)S(1)} %get-tuple-element.111, f32[256]{0:T(256)S(1)} %bitcast.19, f32[]{:T(128)} %bitcast.4), kind=kLoop, calls=%fused_computation.2 | loop fusion | flops 524288 | bytes 1054724 | tf_op jit(solution)/shard_map/sin | solution.py:469
  26.9 3.0 %ingest.2 = bf16[32,2,2,16,512]{4,3,2,1,0:T(8,128)(2,1)} custom-call(s32[1]{0:T(128)} %bitcast.base_ref, s32[32]{0:T(128)} %chan_hbm.2, s32[512]{0:T(512)} %map_hbm.3, s32[512]{0:T(512)} %flag_hbm.3, bf16[32,2,16,1024]{3,2,1,0:T(8,128)(2,1)} %volts_hbm.3), custom_call_target="tpu_custom_call" | custom-call | tf_op jit(solution)/shard_map/ingest/pallas_call | solution.py:94
  29.9 37.1 %all-to-all-done.y_ref.mine_ref.refs_0_ = bf16[64,2,16,512]{3,2,1,0:T(8,128)(2,1)S(1)} async-done(((bf16[64,2,16,512]{3,2,1,0:T(8,128)(2,1)}), bf16[64,2,16,512]{3,2,1,0:T(8,128)(2,1)S(1)}, u32[]{:S(2)}, u32[]{:S(2)}) %all-to-all-start) | async-done | bytes 2097184 | tf_op jit(solution)/shard_map/all_to_all | solution.py:456
  67.1 7.3 %all-to-all-start.1 = ((bf16[64,2,16,512]{3,2,1,0:T(8,128)(2,1)}), bf16[64,2,16,512]{3,2,1,0:T(8,128)(2,1)}, u32[]{:S(2)}, u32[]{:S(2)}) async-start(bf16[64,2,16,512]{3,2,1,0:T(8,128)(2,1)} %bitcast.14), calls=%async_computation.1 | async-start | bytes 4194304 | tf_op jit(solution)/shard_map/all_to_all | solution.py:479
  78.4 1.7 %collective-permute-done.3 = f32[2,1024]{1,0:T(2,128)S(1)} collective-permute-done((f32[2,1024]{1,0:T(2,128)S(1)}, f32[2,1024]{1,0:T(2,128)S(1)}, u32[]{:S(2)}, u32[]{:S(2)}) %collective-permute-start.3) | collective-permute-done | bytes 8224 | tf_op jit(solution)/shard_map/ppermute | solution.py:417
  80.1 2.5 %collective-permute-start.4 = (f32[2,1024]{1,0:T(2,128)S(1)}, f32[2,1024]{1,0:T(2,128)S(1)}, u32[]{:S(2)}, u32[]{:S(2)}) collective-permute-start(f32[2,1024]{1,0:T(2,128)S(1)} %add.63.near_ref), channel_id=1, source_target_pairs={{0,6},{2,4},{4,2},{6,0},{1,7},{3,5},{5,3},{7,1},{8,14},{10,12},{12... | collective-permute-start | bytes 24584 | tf_op jit(solution)/shard_map/ppermute | solution.py:417
  82.6 1.6 %collective-permute-done.4.far_ref = f32[2,1024]{1,0:T(2,128)S(1)} collective-permute-done((f32[2,1024]{1,0:T(2,128)S(1)}, f32[2,1024]{1,0:T(2,128)S(1)}, u32[]{:S(2)}, u32[]{:S(2)}) %collective-permute-start.4) | collective-permute-done | bytes 8224 | tf_op jit(solution)/shard_map/ppermute | solution.py:417
  84.2 2.0 %apply.3 = (f32[2,1024]{1,0:T(2,128)S(1)}, f32[2,1024]{1,0:T(2,128)S(1)}) custom-call(bf16[64,2,16,512]{3,2,1,0:T(8,128)(2,1)S(1)} %all-to-all-done.y_ref.mine_ref.refs_0_, bf16[64,2,16,512]{3,2,1,0:T(8,128)(2,1)S(1)} %collective-permute-done.2.other_ref.refs_1_, f32[2,1024]{1,0:T(2,128)S(1)} %collective-permute-done.z_ref, f32[2,1024]{1,0:T(2,128)S(1)} %add.63.near_ref, ...), custom_call_target="tpu_custom_call" | custom-call | tf_op jit(solution)/shard_map/apply/pallas_call | solution.py:223
  86.3 2.9 %collective-permute-done.5 = f32[2,1024]{1,0:T(2,128)S(1)} collective-permute-done((f32[2,1024]{1,0:T(2,128)S(1)}, f32[2,1024]{1,0:T(2,128)S(1)}, u32[]{:S(2)}, u32[]{:S(2)}) %collective-permute-start.5) | collective-permute-done | bytes 8224 | tf_op jit(solution)/shard_map/ppermute | solution.py:417
  89.2 2.5 %collective-permute-start.6 = (f32[2,1024]{1,0:T(2,128)S(1)}, f32[2,1024]{1,0:T(2,128)S(1)}, u32[]{:S(2)}, u32[]{:S(2)}) collective-permute-start(f32[2,1024]{1,0:T(2,128)S(1)} %add.64.near_ref), channel_id=1, source_target_pairs={{0,6},{2,4},{4,2},{6,0},{1,7},{3,5},{5,3},{7,1},{8,14},{10,12},{12... | collective-permute-start | bytes 24584 | tf_op jit(solution)/shard_map/ppermute | solution.py:417
  91.7 2.6 %correlate.4 = bf16[2,512,256]{2,1,0:T(8,128)(2,1)} custom-call(s32[3]{0:T(128)S(1)} %pad_add_fusion.me_ref, bf16[64,2,16,512]{3,2,1,0:T(8,128)(2,1)S(1)} %all-to-all-done.y_ref.mine_ref.refs_0_, bf16[64,2,16,512]{3,2,1,0:T(8,128)(2,1)S(1)} %collective-permute-done.2.other_ref.refs_1_), custom_call_target="tpu_custom_call" | custom-call | tf_op jit(solution)/shard_map/correlate/pallas_call | solution.py:154
  94.3 2.0 %apply.4 = (f32[2,1024]{1,0:T(2,128)S(1)}, f32[2,1024]{1,0:T(2,128)S(1)}) custom-call(bf16[64,2,16,512]{3,2,1,0:T(8,128)(2,1)S(1)} %all-to-all-done.y_ref.mine_ref.refs_0_, bf16[64,2,16,512]{3,2,1,0:T(8,128)(2,1)S(1)} %collective-permute-done.2.other_ref.refs_1_, f32[2,1024]{1,0:T(2,128)S(1)} %get-tuple-element.63.z_ref, f32[2,1024]{1,0:T(2,128)S(1)} %add.64.near_ref, ...), custom_call_target="tpu_custom_call" | custom-call | tf_op jit(solution)/shard_map/apply/pallas_call | solution.py:223
  96.4 2.6 %correlate.5.refs_0_ = bf16[2,512,256]{2,1,0:T(8,128)(2,1)} custom-call(s32[3]{0:T(128)S(1)} %pad_add_fusion.me_ref, bf16[64,2,16,512]{3,2,1,0:T(8,128)(2,1)S(1)} %all-to-all-done.y_ref.mine_ref.refs_0_, bf16[64,2,16,512]{3,2,1,0:T(8,128)(2,1)S(1)} %collective-permute-done.2.other_ref.refs_1_), custom_call_target="tpu_custom_call" | custom-call | tf_op jit(solution)/shard_map/correlate/pallas_call | solution.py:154
  101.0 2.6 %correlate.6 = bf16[2,512,256]{2,1,0:T(8,128)(2,1)} custom-call(s32[3]{0:T(128)S(1)} %pad_add_fusion.me_ref, bf16[64,2,16,512]{3,2,1,0:T(8,128)(2,1)S(1)} %all-to-all-done.y_ref.mine_ref.refs_0_, bf16[64,2,16,512]{3,2,1,0:T(8,128)(2,1)S(1)} %collective-permute-done.2.other_ref.refs_1_), custom_call_target="tpu_custom_call" | custom-call | tf_op jit(solution)/shard_map/correlate/pallas_call | solution.py:154
  103.6 2.0 %apply.5 = (f32[2,1024]{1,0:T(2,128)S(1)}, f32[2,1024]{1,0:T(2,128)S(1)}) custom-call(bf16[64,2,16,512]{3,2,1,0:T(8,128)(2,1)S(1)} %all-to-all-done.y_ref.mine_ref.refs_0_, bf16[64,2,16,512]{3,2,1,0:T(8,128)(2,1)S(1)} %collective-permute-done.2.other_ref.refs_1_, f32[2,1024]{1,0:T(2,128)S(1)} %get-tuple-element.69.z_ref, f32[2,1024]{1,0:T(2,128)S(1)} %add.65.near_ref, ...), custom_call_target="tpu_custom_call" | custom-call | tf_op jit(solution)/shard_map/apply/pallas_call | solution.py:223
  106.4 2.2 %collective-permute-done.9 = f32[2,1024]{1,0:T(2,128)S(1)} collective-permute-done((f32[2,1024]{1,0:T(2,128)S(1)}, f32[2,1024]{1,0:T(2,128)S(1)}, u32[]{:S(2)}, u32[]{:S(2)}) %collective-permute-start.9) | collective-permute-done | bytes 8224 | tf_op jit(solution)/shard_map/ppermute | solution.py:417
  110.1 2.6 %correlate.7 = bf16[2,512,256]{2,1,0:T(8,128)(2,1)} custom-call(s32[3]{0:T(128)S(1)} %pad_add_fusion.me_ref, bf16[64,2,16,512]{3,2,1,0:T(8,128)(2,1)S(1)} %all-to-all-done.y_ref.mine_ref.refs_0_, bf16[64,2,16,512]{3,2,1,0:T(8,128)(2,1)S(1)} %collective-permute-done.2.other_ref.refs_1_), custom_call_target="tpu_custom_call" | custom-call | tf_op jit(solution)/shard_map/correlate/pallas_call | solution.py:154
  115.2 2.5 %collective-permute-start.12 = (f32[2,1024]{1,0:T(2,128)S(1)}, f32[2,1024]{1,0:T(2,128)S(1)}, u32[]{:S(2)}, u32[]{:S(2)}) collective-permute-start(f32[2,1024]{1,0:T(2,128)S(1)} %finish.1.refs_0_), channel_id=1, source_target_pairs={{0,128},{1,129},{8,136},{9,137},{16,144},{17,145},{24,152},{25,153... | collective-permute-start | bytes 24584 | tf_op jit(solution)/shard_map/ppermute | solution.py:417
  117.8 1.8 %collective-permute-done.12.refs_2_ = f32[2,1024]{1,0:T(2,128)S(1)} collective-permute-done((f32[2,1024]{1,0:T(2,128)S(1)}, f32[2,1024]{1,0:T(2,128)S(1)}, u32[]{:S(2)}, u32[]{:S(2)}) %collective-permute-start.12) | collective-permute-done | bytes 8224 | tf_op jit(solution)/shard_map/ppermute | solution.py:417
  119.6 2.2 %collective-permute-done.13.refs_3_ = f32[2,1024]{1,0:T(2,128)S(1)} collective-permute-done((f32[2,1024]{1,0:T(2,128)S(1)}, f32[2,1024]{1,0:T(2,128)S(1)}, u32[]{:S(2)}, u32[]{:S(2)}) %collective-permute-start.13) | collective-permute-done | bytes 8224 | tf_op jit(solution)/shard_map/ppermute | solution.py:417
  124.3 5.3 %all-to-all-start.2 = ((f32[8,2,1024]{2,1,0:T(2,128)}), f32[8,2,1024]{2,1,0:T(2,128)S(1)}, u32[]{:S(2)}, u32[]{:S(2)}) async-start(f32[8,2,1024]{2,1,0:T(2,128)} %get-tuple-element.94), calls=%async_computation.2 | async-start | bytes 131072 | tf_op jit(solution)/shard_map/all_to_all | solution.py:522
  129.6 2.4 %stage.1.y_ref = bf16[64,2,16,512]{3,2,1,0:T(8,128)(2,1)S(1)} custom-call(bf16[64,2,16,512]{3,2,1,0:T(8,128)(2,1)} %all-to-all-done.1.in_ref), custom_call_target="tpu_custom_call" | custom-call | tf_op jit(solution)/shard_map/stage/pallas_call | solution.py:385
  133.1 1.8 %collective-permute-start.16 = (bf16[2,512,256]{2,1,0:T(8,128)(2,1)}, bf16[2,512,256]{2,1,0:T(8,128)(2,1)}, u32[]{:S(2)}, u32[]{:S(2)}) collective-permute-start(bf16[2,512,256]{2,1,0:T(8,128)(2,1)} %correlate.7), channel_id=1, source_target_pairs={{0,6},{2,4},{4,2},{6,0},{1,7},{3,5},{5,3},{7,1},{8,14},{10,12},{12... | collective-permute-start | bytes 1572872 | tf_op jit(solution)/shard_map/ppermute | solution.py:417
  134.9 1.9 %all-to-all-done.2.line_ref = f32[8,2,1024]{2,1,0:T(2,128)S(1)} async-done(((f32[8,2,1024]{2,1,0:T(2,128)}), f32[8,2,1024]{2,1,0:T(2,128)S(1)}, u32[]{:S(2)}, u32[]{:S(2)}) %all-to-all-start.2) | async-done | bytes 65568 | tf_op jit(solution)/shard_map/all_to_all | solution.py:522
  136.8 1.9 %beamform.3 = bf16[2,2,128,512]{3,2,1,0:T(8,128)(2,1)S(1)} custom-call(s32[32]{0:T(128)S(1)} %select_reduce_fusion.source_ref, s32[3]{0:T(128)S(1)} %pad_add_fusion.me_ref, f32[8,2,1024]{2,1,0:T(2,128)S(1)} %all-to-all-done.2.line_ref, f32[256,512]{1,0:T(8,128)} %get-tuple-element.108.cos_ref, f32[256,512]{1,0:T(8,128)} %get-tuple-element.109.sin_ref, ...), custom_call_target="tpu_custom_call" | custom-call | flops 42949672960 | bytes 67108864 | tf_op jit(solution)/shard_map/beamform/pallas_call | solution.py:337
  140.6 2.3 %collective-permute-done.16.refs_3_ = bf16[2,512,256]{2,1,0:T(8,128)(2,1)} collective-permute-done((bf16[2,512,256]{2,1,0:T(8,128)(2,1)}, bf16[2,512,256]{2,1,0:T(8,128)(2,1)}, u32[]{:S(2)}, u32[]{:S(2)}) %collective-permute-start.16) | collective-permute-done | bytes 524320 | tf_op jit(solution)/shard_map/ppermute | solution.py:417
  144.3 10.4 %collective-permute-start.17 = (bf16[2,512,256]{2,1,0:T(8,128)(2,1)S(1)}, bf16[2,512,256]{2,1,0:T(8,128)(2,1)S(1)}, u32[]{:S(2)}, u32[]{:S(2)}) collective-permute-start(bf16[2,512,256]{2,1,0:T(8,128)(2,1)S(1)} %gather.8), channel_id=1, source_target_pairs={{0,0},{1,8},{8,1},{9,9},{16,16},{17,24},{24,17},{25,25},{32,32},{3... | collective-permute-start | bytes 1572872 | tf_op jit(solution)/shard_map/ppermute | solution.py:426
  154.7 2.7 %beamform.2.own_hbm = bf16[2,2,128,1024]{3,2,1,0:T(8,128)(2,1)} custom-call(s32[32]{0:T(128)S(1)} %select_reduce_fusion.source_ref, s32[3]{0:T(128)S(1)} %pad_add_fusion.me_ref, f32[8,2,1024]{2,1,0:T(2,128)S(1)} %all-to-all-done.2.line_ref, f32[256,512]{1,0:T(8,128)} %get-tuple-element.108.cos_ref, f32[256,512]{1,0:T(8,128)} %get-tuple-element.109.sin_ref, ...), custom_call_target="tpu_custom_call" | custom-call | flops 42949672960 | bytes 67108864 | tf_op jit(solution)/shard_map/beamform/pallas_call | solution.py:337
  158.7 2.8 %collective-permute-done.17.in_ref = bf16[2,512,256]{2,1,0:T(8,128)(2,1)S(1)} collective-permute-done((bf16[2,512,256]{2,1,0:T(8,128)(2,1)S(1)}, bf16[2,512,256]{2,1,0:T(8,128)(2,1)S(1)}, u32[]{:S(2)}, u32[]{:S(2)}) %collective-permute-start.17) | collective-permute-done | bytes 524320 | tf_op jit(solution)/shard_map/ppermute | solution.py:426
  (56 shorter events, 22.6 us)
Async XLA Ops:
  3.7 13.4 %copy-start.5 = (f32[1,2,1024]{2,1,0:T(2,128)S(1)}, f32[1,2,1024]{2,1,0:T(2,128)}, u32[]{:S(2)}) copy-start(f32[1,2,1024]{2,1,0:T(2,128)} %param.9) | copy-start | bytes 24580
  3.7 16.9 %copy-start.4 = (s32[32]{0:T(128)S(1)}, s32[32]{0:T(128)}, u32[]{:S(2)}) copy-start(s32[32]{0:T(128)} %chan_hbm.2) | copy-start | bytes 388
  3.7 18.2 %copy-start.1 = (f32[2,512]{1,0:T(2,128)S(1)}, f32[2,512]{1,0:T(2,128)}, u32[]{:S(2)}) copy-start(f32[2,512]{1,0:T(2,128)} %param.12) | copy-start | bytes 12292
  3.7 18.3 %copy-start = (s32[512]{0:T(512)S(1)}, s32[512]{0:T(512)}, u32[]{:S(2)}) copy-start(s32[512]{0:T(512)} %map_hbm.3) | copy-start | bytes 6148
  3.8 19.4 %copy-start.3 = (s32[32]{0:T(128)S(1)}, s32[32]{0:T(128)}, u32[]{:S(2)}) copy-start(s32[32]{0:T(128)} %chan_hbm.3) | copy-start | bytes 388
  3.8 19.9 %copy-start.2 = (s32[2,256]{1,0:T(2,128)S(1)}, s32[2,256]{1,0:T(2,128)}, u32[]{:S(2)}) copy-start(s32[2,256]{1,0:T(2,128)} %param.13) | copy-start | bytes 6148
  3.8 63.3 %all-to-all-start = ((bf16[64,2,16,512]{3,2,1,0:T(8,128)(2,1)}), bf16[64,2,16,512]{3,2,1,0:T(8,128)(2,1)S(1)}, u32[]{:S(2)}, u32[]{:S(2)}) async-start(bf16[64,2,16,512]{3,2,1,0:T(8,128)(2,1)} %bitcast.15), calls=%async_computation | async-start | bytes 4194304 | tf_op jit(solution)/shard_map/all_to_all | solution.py:456
  17.1 12.8 %collective-permute-start = (f32[2,1024]{1,0:T(2,128)S(1)}, f32[2,1024]{1,0:T(2,128)S(1)}, u32[]{:S(2)}, u32[]{:S(2)}) collective-permute-start(f32[2,1024]{1,0:T(2,128)S(1)} %bitcast.21), channel_id=1, source_target_pairs={{0,0},{1,8},{8,1},{9,9},{16,16},{17,24},{24,17},{25,25},{32,32},{3... | collective-permute-start | bytes 24584 | tf_op jit(solution)/shard_map/ppermute | solution.py:426
  67.1 57.2 %all-to-all-start.1 = ((bf16[64,2,16,512]{3,2,1,0:T(8,128)(2,1)}), bf16[64,2,16,512]{3,2,1,0:T(8,128)(2,1)}, u32[]{:S(2)}, u32[]{:S(2)}) async-start(bf16[64,2,16,512]{3,2,1,0:T(8,128)(2,1)} %bitcast.14), calls=%async_computation.1 | async-start | bytes 4194304 | tf_op jit(solution)/shard_map/all_to_all | solution.py:479
  75.4 1.4 collective-permute-start.1
  76.9 7.4 %collective-permute-start.2 = (bf16[64,2,16,512]{3,2,1,0:T(8,128)(2,1)S(1)}, bf16[64,2,16,512]{3,2,1,0:T(8,128)(2,1)S(1)}, u32[]{:S(2)}, u32[]{:S(2)}) collective-permute-start(bf16[64,2,16,512]{3,2,1,0:T(8,128)(2,1)S(1)} %all-to-all-done.y_ref.mine_ref.refs_0_), channel_id=1, source_target_pairs={{0,8},{8,0},{16,24},{24,16},{32,40},{40,32},{48,56},{56,48},{64,72... | collective-permute-start | bytes 6291464 | tf_op jit(solution)/shard_map/ppermute | solution.py:417
  77.2 2.9 %collective-permute-start.3 = (f32[2,1024]{1,0:T(2,128)S(1)}, f32[2,1024]{1,0:T(2,128)S(1)}, u32[]{:S(2)}, u32[]{:S(2)}) collective-permute-start(f32[2,1024]{1,0:T(2,128)S(1)} %add.62), channel_id=1, source_target_pairs={{0,2},{2,0},{4,6},{6,4},{1,3},{3,1},{5,7},{7,5},{8,10},{10,8},{12,... | collective-permute-start | bytes 24584 | tf_op jit(solution)/shard_map/ppermute | solution.py:417
  80.1 4.1 %collective-permute-start.4 = (f32[2,1024]{1,0:T(2,128)S(1)}, f32[2,1024]{1,0:T(2,128)S(1)}, u32[]{:S(2)}, u32[]{:S(2)}) collective-permute-start(f32[2,1024]{1,0:T(2,128)S(1)} %add.63.near_ref), channel_id=1, source_target_pairs={{0,6},{2,4},{4,2},{6,0},{1,7},{3,5},{5,3},{7,1},{8,14},{10,12},{12... | collective-permute-start | bytes 24584 | tf_op jit(solution)/shard_map/ppermute | solution.py:417
  86.2 3.0 %collective-permute-start.5 = (f32[2,1024]{1,0:T(2,128)S(1)}, f32[2,1024]{1,0:T(2,128)S(1)}, u32[]{:S(2)}, u32[]{:S(2)}) collective-permute-start(f32[2,1024]{1,0:T(2,128)S(1)} %get-tuple-element.64), channel_id=1, source_target_pairs={{0,2},{2,0},{4,6},{6,4},{1,3},{3,1},{5,7},{7,5},{8,10},{10,8},{12,... | collective-permute-start | bytes 24584 | tf_op jit(solution)/shard_map/ppermute | solution.py:417
  89.2 5.1 %collective-permute-start.6 = (f32[2,1024]{1,0:T(2,128)S(1)}, f32[2,1024]{1,0:T(2,128)S(1)}, u32[]{:S(2)}, u32[]{:S(2)}) collective-permute-start(f32[2,1024]{1,0:T(2,128)S(1)} %add.64.near_ref), channel_id=1, source_target_pairs={{0,6},{2,4},{4,2},{6,0},{1,7},{3,5},{5,3},{7,1},{8,14},{10,12},{12... | collective-permute-start | bytes 24584 | tf_op jit(solution)/shard_map/ppermute | solution.py:417
  96.3 3.0 %collective-permute-start.7 = (f32[2,1024]{1,0:T(2,128)S(1)}, f32[2,1024]{1,0:T(2,128)S(1)}, u32[]{:S(2)}, u32[]{:S(2)}) collective-permute-start(f32[2,1024]{1,0:T(2,128)S(1)} %get-tuple-element.71), channel_id=1, source_target_pairs={{0,2},{2,0},{4,6},{6,4},{1,3},{3,1},{5,7},{7,5},{8,10},{10,8},{12,... | collective-permute-start | bytes 24584 | tf_op jit(solution)/shard_map/ppermute | solution.py:417
  99.3 4.3 %collective-permute-start.8 = (f32[2,1024]{1,0:T(2,128)S(1)}, f32[2,1024]{1,0:T(2,128)S(1)}, u32[]{:S(2)}, u32[]{:S(2)}) collective-permute-start(f32[2,1024]{1,0:T(2,128)S(1)} %add.65.near_ref), channel_id=1, source_target_pairs={{0,6},{2,4},{4,2},{6,0},{1,7},{3,5},{5,3},{7,1},{8,14},{10,12},{12... | collective-permute-start | bytes 24584 | tf_op jit(solution)/shard_map/ppermute | solution.py:417
  105.6 3.0 %collective-permute-start.9 = (f32[2,1024]{1,0:T(2,128)S(1)}, f32[2,1024]{1,0:T(2,128)S(1)}, u32[]{:S(2)}, u32[]{:S(2)}) collective-permute-start(f32[2,1024]{1,0:T(2,128)S(1)} %get-tuple-element.80), channel_id=1, source_target_pairs={{0,2},{2,0},{4,6},{6,4},{1,3},{3,1},{5,7},{7,5},{8,10},{10,8},{12,... | collective-permute-start | bytes 24584 | tf_op jit(solution)/shard_map/ppermute | solution.py:417
  108.6 4.1 %collective-permute-start.10 = (f32[2,1024]{1,0:T(2,128)S(1)}, f32[2,1024]{1,0:T(2,128)S(1)}, u32[]{:S(2)}, u32[]{:S(2)}) collective-permute-start(f32[2,1024]{1,0:T(2,128)S(1)} %add.66.near_ref), channel_id=1, source_target_pairs={{0,6},{2,4},{4,2},{6,0},{1,7},{3,5},{5,3},{7,1},{8,14},{10,12},{12... | collective-permute-start | bytes 24584 | tf_op jit(solution)/shard_map/ppermute | solution.py:417
  112.7 22.2 %collective-permute-start.14 = (bf16[2,512,256]{2,1,0:T(8,128)(2,1)}, bf16[2,512,256]{2,1,0:T(8,128)(2,1)S(1)}, u32[]{:S(2)}, u32[]{:S(2)}) collective-permute-start(bf16[2,512,256]{2,1,0:T(8,128)(2,1)} %correlate.6), channel_id=1, source_target_pairs={{0,4},{2,6},{4,0},{6,2},{1,5},{3,7},{5,1},{7,3},{8,12},{10,14},{12... | collective-permute-start | bytes 1572872 | tf_op jit(solution)/shard_map/ppermute | solution.py:417
  113.9 3.9 %collective-permute-start.11 = (f32[2,1024]{1,0:T(2,128)S(1)}, f32[2,1024]{1,0:T(2,128)S(1)}, u32[]{:S(2)}, u32[]{:S(2)}) collective-permute-start(f32[2,1024]{1,0:T(2,128)S(1)} %finish.1.refs_0_), channel_id=1, source_target_pairs={{0,1},{1,0},{8,9},{9,8},{16,17},{17,16},{24,25},{25,24},{32,33},{3... | collective-permute-start | bytes 24584 | tf_op jit(solution)/shard_map/ppermute | solution.py:417
  115.2 4.4 %collective-permute-start.12 = (f32[2,1024]{1,0:T(2,128)S(1)}, f32[2,1024]{1,0:T(2,128)S(1)}, u32[]{:S(2)}, u32[]{:S(2)}) collective-permute-start(f32[2,1024]{1,0:T(2,128)S(1)} %finish.1.refs_0_), channel_id=1, source_target_pairs={{0,128},{1,129},{8,136},{9,137},{16,144},{17,145},{24,152},{25,153... | collective-permute-start | bytes 24584 | tf_op jit(solution)/shard_map/ppermute | solution.py:417
  117.7 4.2 %collective-permute-start.13 = (f32[2,1024]{1,0:T(2,128)S(1)}, f32[2,1024]{1,0:T(2,128)S(1)}, u32[]{:S(2)}, u32[]{:S(2)}) collective-permute-start(f32[2,1024]{1,0:T(2,128)S(1)} %finish.1.refs_0_), channel_id=1, source_target_pairs={{0,129},{1,128},{8,137},{9,136},{16,145},{17,144},{24,153},{25,152... | collective-permute-start | bytes 24584 | tf_op jit(solution)/shard_map/ppermute | solution.py:417
  124.3 12.5 %all-to-all-start.2 = ((f32[8,2,1024]{2,1,0:T(2,128)}), f32[8,2,1024]{2,1,0:T(2,128)S(1)}, u32[]{:S(2)}, u32[]{:S(2)}) async-start(f32[8,2,1024]{2,1,0:T(2,128)} %get-tuple-element.94), calls=%async_computation.2 | async-start | bytes 131072 | tf_op jit(solution)/shard_map/all_to_all | solution.py:522
  132.0 8.6 %collective-permute-start.15 = (bf16[2,512,256]{2,1,0:T(8,128)(2,1)}, bf16[2,512,256]{2,1,0:T(8,128)(2,1)S(1)}, u32[]{:S(2)}, u32[]{:S(2)}) collective-permute-start(bf16[2,512,256]{2,1,0:T(8,128)(2,1)} %correlate.4), channel_id=1, source_target_pairs={{0,2},{2,0},{4,6},{6,4},{1,3},{3,1},{5,7},{7,5},{8,10},{10,8},{12,... | collective-permute-start | bytes 1572872 | tf_op jit(solution)/shard_map/ppermute | solution.py:417
  133.1 9.7 %collective-permute-start.16 = (bf16[2,512,256]{2,1,0:T(8,128)(2,1)}, bf16[2,512,256]{2,1,0:T(8,128)(2,1)}, u32[]{:S(2)}, u32[]{:S(2)}) collective-permute-start(bf16[2,512,256]{2,1,0:T(8,128)(2,1)} %correlate.7), channel_id=1, source_target_pairs={{0,6},{2,4},{4,2},{6,0},{1,7},{3,5},{5,3},{7,1},{8,14},{10,12},{12... | collective-permute-start | bytes 1572872 | tf_op jit(solution)/shard_map/ppermute | solution.py:417
  138.8 18.6 %collective-permute-start.18 = (bf16[2,2,128,512]{3,2,1,0:T(8,128)(2,1)S(1)}, bf16[2,2,128,512]{3,2,1,0:T(8,128)(2,1)S(1)}, u32[]{:S(2)}, u32[]{:S(2)}) collective-permute-start(bf16[2,2,128,512]{3,2,1,0:T(8,128)(2,1)S(1)} %beamform.3), channel_id=1, source_target_pairs={{0,1},{1,0},{2,3},{3,2},{4,5},{5,4},{6,7},{7,6},{8,9},{9,8},{10,11... | collective-permute-start | bytes 1572872 | tf_op jit(solution)/shard_map/ppermute | solution.py:417
  144.3 17.2 %collective-permute-start.17 = (bf16[2,512,256]{2,1,0:T(8,128)(2,1)S(1)}, bf16[2,512,256]{2,1,0:T(8,128)(2,1)S(1)}, u32[]{:S(2)}, u32[]{:S(2)}) collective-permute-start(bf16[2,512,256]{2,1,0:T(8,128)(2,1)S(1)} %gather.8), channel_id=1, source_target_pairs={{0,0},{1,8},{8,1},{9,9},{16,16},{17,24},{24,17},{25,25},{32,32},{3... | collective-permute-start | bytes 1572872 | tf_op jit(solution)/shard_map/ppermute | solution.py:426
